TPU v7x, 32 devices: a whole 2x2x4 slice. The times are simulated.
32 devices in a mesh: epoch: 4 (over y, x), strip: 8 (over z, core).
Axes of the slice: x: 2, y: 2, z: 4, core: 2. Of those that a mesh axis runs over, the one named last changes fastest.
Arguments:
- raw_tiles: float32 [4, 96, 256, 512], P('epoch', 'strip'), may hold values from -6 to 6
- tile_kind: int32 [4, 96], P('epoch', 'strip'), may hold values from 0 to 3
- tile_invvar: float32 [4, 96], P('epoch', 'strip'), may hold values from 0.2 to 5
- tile_heights: int32 [4, 8, 12], P('epoch'), may hold values from 1 to 256, 2048 in all within a row
- row_interp: float32 [4, 256, 256], replicated, may hold values from -0.4 to 1.9
- col_interp: float32 [4, 512, 512], replicated, may hold values from -0.4 to 1.9
- psf_profiles: float32 [2, 2, 31], replicated, may hold values from -1 to 1
- psf_poly: float32 [4, 2, 6], replicated, may hold values from -1 to 1
Outputs:
- difference: float32 [4, 2048, 4096], P('epoch', 'strip')
Inputs may be any that keep to these rules, and one draw needn't show every extreme that they name: `tile_heights`: along the last dimension, the heights of one column block's tiles from the top of the patch down; they sum to 2048, and the tallest is exactly 256.
All inputs are finite; a program needn't handle non-finite values.
Results may differ from a plain program's by a relative error of at most 0.0003.
Values sent between devices are 32-bit elements; how exact they have to be, the bound alone decides.
No kernel may reach another device: no remote copies, remote signals or barrier semaphores. Data moves between devices by JAX's collectives and lax.ppermute only.
A program may use at most 128 MiB of HBM per device.

v0:
```python
import functools

import jax
import jax.numpy as jnp
from jax import lax
from jax.experimental import pallas as pl
from jax.experimental.pallas import tpu as pltpu
from jax.sharding import PartitionSpec as P


ROWS_DEV = 256
HALO = 16
FIRST_PART = 3
LANES = 128
F32 = jnp.float32
BF16 = jnp.bfloat16


def split(x):
    hi = x.astype(BF16)
    lo = (x - hi.astype(F32)).astype(BF16)
    return hi, lo


def dot(a, b, trans_b=False):
    dims = (((1,), (1 if trans_b else 0,)), ((), ()))
    return lax.dot_general(a, b, dims, preferred_element_type=F32)


def dot3(a, b, trans_b=False):
    a_hi, a_lo = a
    b_hi, b_lo = b
    both = dot(jnp.concatenate([a_hi, a_lo], axis=0), b_hi, trans_b)
    rows = a_hi.shape[0]
    return both[:rows] + (both[rows:] + dot(a_hi, b_lo, trans_b))


def start_and_wait(copies):
    for copy in copies:
        copy.start()
    for copy in copies:
        copy.wait()


def slot_order(count, order):
    bits = len(order)
    key = lambda j: sum(((j >> order[i]) & 1) << (bits - 1 - i) for i in range(bits))
    slots = sorted(range(count), key=key)
    return slots[: count // 2], slots[count // 2 :]


def warp_kernel(
    geom, kind_ref, heights_ref, invvar_ref, raw_ref, rmat_ref, cmat_ref,
    sci_a, sci_b, keep_a, send_a, keep_b, send_b,
    sci_s, num_s, wt_s, chi_s, clo_s, top_s, sems,
):
    epochs, nrow, share, orders, tiles = geom
    step = pl.program_id(0)
    together, tile_rows, tile_cols = raw_ref.shape
    per_col = heights_ref.shape[2]
    span = tile_rows + 8
    me = lax.axis_index("epoch")
    first_tile = lax.axis_index("strip") * tiles
    block = lax.div(first_tile, per_col)
    offset_in = lax.rem(first_tile, per_col)

    @pl.when(step == 0)
    def _():
        top_s[0] = lax.fori_loop(
            0, offset_in, lambda i, total: total + heights_ref[0, block, i], jnp.int32(0)
        )

        def divide(i, carry):
            k = lax.div(i, 4)
            here = pl.ds(pl.multiple_of(lax.rem(i, 4) * (tile_cols // 4), tile_cols // 4), tile_cols // 4)
            chi_s[k, here, :], clo_s[k, here, :] = split(cmat_ref[k, here, :])
            return carry

        lax.fori_loop(0, 4 * cmat_ref.shape[0], divide, 0)
        if tiles != per_col:
            sci_s[...] = jnp.zeros_like(sci_s)
            num_s[...] = jnp.zeros_like(num_s)
            wt_s[...] = jnp.zeros_like(wt_s)

    def warped(i, top):
        t = step * together + i
        kind = kind_ref[0, t]
        height = heights_ref[0, block, offset_in + t]
        start = pl.multiple_of(jnp.minimum(lax.div(top, 8) * 8, nrow - span), 8)
        off = top - start
        across = dot3(split(raw_ref[i]), (chi_s[kind], clo_s[kind]), trans_b=True)
        live = lax.broadcasted_iota(jnp.int32, (tile_rows, tile_rows), 1) < height
        rows = jnp.concatenate(
            [jnp.where(live, rmat_ref[kind], 0.0), jnp.zeros((8, tile_rows), F32)], axis=0
        )
        return t, height, start, off, dot3(split(pltpu.roll(rows, off, 0)), split(across))

    top = top_s[0]
    results = []
    for i in range(together):
        results.append((top, warped(i, top)))
        top = top + results[-1][1][1]
    top_s[0] = top

    for top, (t, height, start, off, placed) in results:
        weight = invvar_ref[0, t]
        local = lax.broadcasted_iota(jnp.int32, (span, share), 0) - off
        own = (local >= 0) & (local < height)
        here = pl.ds(start, span)
        for q in range(epochs):
            columns = pl.ds(q * share, share)
            piece = placed[:, q * share : (q + 1) * share]
            slot = jnp.bitwise_xor(me, q)
            sci_s[here, columns] = jnp.where(own, piece, sci_s[here, columns])
            num_s[slot, here, :] = jnp.where(own, weight * piece, num_s[slot, here, :])
        flat = lax.broadcasted_iota(jnp.int32, wt_s.shape, 0) * share + lax.broadcasted_iota(
            jnp.int32, wt_s.shape, 1
        )
        wt_s[...] = jnp.where((flat >= top) & (flat < top + height), weight, wt_s[...])

    @pl.when(step == pl.num_programs(0) - 1)
    def _():
        strips, rows_a, _ = sci_a.shape
        rows_b = sci_b.shape[1]
        pairs = []
        nhalf = nrow // 2
        whalf = wt_s.shape[0] // 2
        for i, (order, outs) in enumerate(zip(orders, ((keep_a, send_a), (keep_b, send_b)))):
            for slots, out in zip(slot_order(epochs, order), outs):
                for place, j in enumerate(slots):
                    pairs.append((num_s.at[j, pl.ds(i * nhalf, nhalf)], out.at[place, pl.ds(0, nhalf)]))
                    pairs.append((wt_s.at[pl.ds(i * whalf, whalf)], out.at[place, pl.ds(nhalf, whalf)]))
        for s in range(strips):
            base = s * (rows_a + rows_b)
            pairs.append((sci_s.at[pl.ds(base, rows_a)], sci_a.at[s]))
            pairs.append((sci_s.at[pl.ds(base + rows_a, rows_b)], sci_b.at[s]))
        start_and_wait([pltpu.make_async_copy(a, b, sems.at[n]) for n, (a, b) in enumerate(pairs)])


def template_kernel(terms, *refs):
    term_refs, out_ref, pad_s = refs[:-2], refs[-2], refs[-1]
    strips, long, share = out_ref.shape
    rows_dev = long - 2 * HALO
    nrow = strips * rows_dev
    nhalf = nrow // 2
    whalf = nhalf // share
    edge = jnp.zeros((HALO, share), F32)
    pad_s[pl.ds(0, HALO), :] = edge
    pad_s[pl.ds(HALO + nrow, HALO), :] = edge
    for part in range(2):
        own = term_refs[part * terms : (part + 1) * terms]
        add = lambda place: functools.reduce(lambda a, b: a + b, [ref[0, place, :] for ref in own])
        weights = add(pl.ds(nhalf, whalf))
        for i in range(whalf):
            below = jnp.transpose(jnp.broadcast_to(weights[i : i + 1, :], (share, share)))
            pad_s[pl.ds(HALO + part * nhalf + i * share, share), :] = add(pl.ds(i * share, share)) / below
    for s in range(strips):
        out_ref[s] = pad_s[pl.ds(s * rows_dev, long), :]


def bands_kernel(psf_ref, toep_hi, toep_lo, band_ref):
    basis, _, ksize = psf_ref.shape
    margin = ksize // 2
    for k in range(basis):
        shape = (2 * LANES, LANES)
        tap = lax.broadcasted_iota(jnp.int32, shape, 0) - lax.broadcasted_iota(jnp.int32, shape, 1)
        tap = tap - (LANES // 2 - margin)
        value = jnp.zeros(shape, F32)
        for j in range(ksize):
            value = jnp.where(tap == j, psf_ref[k, 1, j], value)
        toep_hi[:, pl.ds(k * LANES, LANES)], toep_lo[:, pl.ds(k * LANES, LANES)] = split(value)
        shape = (LANES, LANES + 2 * HALO)
        tap = lax.broadcasted_iota(jnp.int32, shape, 1) - lax.broadcasted_iota(jnp.int32, shape, 0)
        tap = tap - (HALO - margin)
        value = jnp.zeros(shape, F32)
        for j in range(ksize):
            value = jnp.where(tap == j, psf_ref[k, 0, j], value)
        band_ref[k, pl.ds(0, LANES), :], band_ref[k, pl.ds(LANES, LANES), :] = split(value)


def match_kernel(geom, *refs):
    pieces, nrow, ncol = geom
    count = len(pieces)
    tile_refs = refs[:count]
    poly_ref, toep_hi, toep_lo, band_ref, out_ref, pad_s, row_s, sems = refs[count:]
    step = pl.program_id(0)
    tiles = pad_s.shape[0] - 2
    rows_dev = pad_s.shape[1] - 2 * HALO
    me = lax.axis_index("epoch")
    strip = lax.axis_index("strip")
    per_step = out_ref.shape[1] // LANES

    @pl.when(step == 0)
    def _():
        copies = []
        for ref, (slot, first, stride) in zip(tile_refs, pieces):
            place = first if slot is None else jnp.bitwise_xor(me, slot) + first
            for i in range(ref.shape[0]):
                copies.append(
                    pltpu.make_async_copy(ref.at[i], pad_s.at[1 + place + i * stride], sems.at[len(copies)])
                )
        for copy in copies:
            copy.start()
        pad_s[0] = jnp.zeros(pad_s.shape[1:], F32)
        pad_s[tiles + 1] = jnp.zeros(pad_s.shape[1:], F32)
        shape = (rows_dev, LANES)
        counter = (strip * rows_dev + lax.broadcasted_iota(jnp.int32, shape, 0)).astype(F32)
        u = (2.0 * counter + 1.0) / nrow - 1.0
        for k in range(2):
            p = [poly_ref[me, k, i] for i in range(6)]
            row_s[k, 0] = p[0] + u * (p[1] + p[3] * u)
            row_s[k, 1] = p[2] + p[4] * u
        for copy in copies:
            copy.wait()

    lane = lax.broadcasted_iota(jnp.int32, pad_s.shape[1:], 1)
    base = step * per_step
    shifted = []
    for m in range(per_step + 1):
        mixed = jnp.where(lane < LANES // 2, pad_s[base + m + 1], pad_s[base + m])
        shifted.append(split(pltpu.roll(mixed, LANES // 2, 1)))
    toep = (toep_hi[...], toep_lo[...])
    for pair in range(per_step // 2):
        across = []
        for c in (2 * pair, 2 * pair + 1):
            window = tuple(
                jnp.concatenate([shifted[c][i], shifted[c + 1][i]], axis=1) for i in range(2)
            )
            across.append(dot3(window, toep))
        width = 2 * LANES
        cols = lax.broadcasted_iota(jnp.int32, (1, width), 1) + (base + 2 * pair) * LANES
        v = (2.0 * cols.astype(F32) + 1.0) / ncol - 1.0
        for part in range(rows_dev // LANES):
            total = 0.0
            for k in range(2):
                both = jnp.concatenate(
                    [a[part * LANES : part * LANES + LANES + 2 * HALO, k * LANES : (k + 1) * LANES] for a in across],
                    axis=1,
                )
                hi, lo = split(both)
                wide = dot(band_ref[k], hi)
                done = wide[:LANES] + (wide[LANES:] + dot(band_ref[k, pl.ds(0, LANES), :], lo))
                place = pl.ds(part * LANES, LANES)
                one = jnp.concatenate([row_s[k, 0, place, :]] * 2, axis=1)
                two = jnp.concatenate([row_s[k, 1, place, :]] * 2, axis=1)
                coeff = one + v * (two + poly_ref[me, k, 5] * v)
                total = total + coeff * done
            out_ref[pl.ds(part * LANES, LANES), pl.ds(pair * width, width)] = total


def subtract_kernel(sci_a, sci_b, matched_ref, out_ref):
    rows = sci_a.shape[1]
    out_ref[0, pl.ds(0, rows), :] = sci_a[0] - matched_ref[pl.ds(0, rows), :]
    rest = pl.ds(rows, sci_b.shape[1])
    out_ref[0, rest, :] = sci_b[0] - matched_ref[rest, :]


def swap(value, axis, bit):
    count = lax.axis_size(axis)
    return lax.ppermute(value, axis, [(i, i ^ (1 << bit)) for i in range(count)])


def shards(
    raw_tiles, tile_kind, tile_invvar, tile_heights, row_interp, col_interp, psf_profiles, psf_poly
):
    strips, epochs = lax.axis_size("strip"), lax.axis_size("epoch")
    _, tiles, tile_rows, tile_cols = raw_tiles.shape
    _, blocks, _ = tile_heights.shape
    ncol, nrow = blocks * tile_cols, ROWS_DEV * strips
    sources = strips // blocks
    share = tile_cols // epochs
    bits = epochs.bit_length() - 1
    orders = (tuple(range(bits)), tuple(reversed(range(bits))))
    nhalf = nrow // 2
    wrows = nrow // share
    long_half = nhalf + wrows // 2
    smem = pl.BlockSpec(memory_space=pltpu.SMEM)
    hbm = pl.BlockSpec(memory_space=pl.ANY)
    vmem = pl.BlockSpec(memory_space=pltpu.VMEM)
    kinds = col_interp.shape[0]

    first_rows = ROWS_DEV * FIRST_PART // 8
    sci_shapes = [
        jax.ShapeDtypeStruct((strips, rows, tile_cols), F32) for rows in (first_rows, ROWS_DEV - first_rows)
    ]
    send_shape = jax.ShapeDtypeStruct((epochs // 2, long_half, share), F32)
    together = 2 if tiles % 2 == 0 else 1
    once = pl.Buffered(1)
    sci_a, sci_b, keep_a, send_a, keep_b, send_b = pl.pallas_call(
        functools.partial(warp_kernel, (epochs, nrow, share, orders, tiles)),
        grid=(tiles // together,),
        in_specs=[
            smem,
            smem,
            smem,
            pl.BlockSpec((together, tile_rows, tile_cols), lambda t: (t, 0, 0)),
            pl.BlockSpec((kinds, tile_rows, tile_rows), lambda t: (0, 0, 0), pipeline_mode=once),
            pl.BlockSpec((kinds, tile_cols, tile_cols), lambda t: (0, 0, 0), pipeline_mode=once),
        ],
        out_specs=[hbm] * 6,
        out_shape=sci_shapes + [send_shape] * 4,
        scratch_shapes=[
            pltpu.VMEM((nrow, tile_cols), F32),
            pltpu.VMEM((epochs, nrow, share), F32),
            pltpu.VMEM((wrows, share), F32),
            pltpu.VMEM((kinds, tile_cols, tile_cols), BF16),
            pltpu.VMEM((kinds, tile_cols, tile_cols), BF16),
            pltpu.SMEM((1,), jnp.int32),
            pltpu.SemaphoreType.DMA((2 * strips + 4 * epochs,)),
        ],
        name="warp",
        cost_estimate=pl.CostEstimate(flops=8_000_000_000, bytes_accessed=20_000_000, transcendentals=0),
    )(tile_kind, tile_heights, tile_invvar, raw_tiles[0], row_interp, col_interp)

    got_a = lax.all_to_all(sci_a, "strip", split_axis=0, concat_axis=0, tiled=True)

    basis, _, _ = psf_profiles.shape
    build_bands = pl.pallas_call(
        bands_kernel,
        in_specs=[smem],
        out_specs=[vmem] * 3,
        out_shape=[
            jax.ShapeDtypeStruct((2 * LANES, 2 * LANES), BF16),
            jax.ShapeDtypeStruct((2 * LANES, 2 * LANES), BF16),
            jax.ShapeDtypeStruct((basis, 2 * LANES, LANES + 2 * HALO), BF16),
        ],
        name="bands",
        cost_estimate=pl.CostEstimate(flops=10_000_000, bytes_accessed=500_000, transcendentals=0),
    )
    toep_hi, toep_lo, band = build_bands(psf_profiles)

    terms = [[keep_a], [keep_b]]
    sends = [send_a, send_b]
    for i in range(bits):
        for part in range(2):
            terms[part].append(swap(sends[part], "epoch", orders[part][i]))
        left = epochs >> (i + 1)
        if left > 1:
            sends = [
                functools.reduce(lambda a, b: a + b, [t[left // 2 : left] for t in own]) for own in terms
            ]
    if sources > 1:
        fixed = []
        for own in terms:
            total = functools.reduce(lambda a, b: a + b, [t[:1] for t in own])
            around = total
            for k in range(1, sources):
                ring = [(i, i // sources * sources + (i + k) % sources) for i in range(strips)]
                around = around + lax.ppermute(total, "strip", ring)
            fixed.append([around])
        terms = fixed

    long = ROWS_DEV + 2 * HALO
    first_slot = pl.BlockSpec((1, long_half, share), lambda i: (0, 0, 0))
    strips_out = pl.pallas_call(
        functools.partial(template_kernel, len(terms[0])),
        grid=(1,),
        in_specs=[first_slot] * (2 * len(terms[0])),
        out_specs=pl.BlockSpec((strips, long, share), lambda i: (0, 0, 0)),
        out_shape=jax.ShapeDtypeStruct((strips, long, share), F32),
        scratch_shapes=[pltpu.VMEM((nrow + 2 * HALO, share), F32)],
        name="template",
        cost_estimate=pl.CostEstimate(flops=2_000_000, bytes_accessed=5_000_000, transcendentals=0),
    )(*terms[0], *terms[1])
    strips_out, got_a = lax.optimization_barrier((strips_out, got_a))
    mine = lax.all_to_all(strips_out, "strip", split_axis=0, concat_axis=0, tiled=True)
    sci_b, mine = lax.optimization_barrier((sci_b, mine))
    got_b = lax.all_to_all(sci_b, "strip", split_axis=0, concat_axis=0, tiled=True)
    if sources > 1:
        mine = mine[::sources]
        got_a = jnp.sum(got_a.reshape((blocks, sources) + got_a.shape[1:]), axis=1)
        got_b = jnp.sum(got_b.reshape((blocks, sources) + got_b.shape[1:]), axis=1)

    per_block = tile_cols // LANES
    if epochs == 4 and share == LANES:
        near = [swap(mine, "epoch", b) for b in range(2)]
        cut = blocks // 2
        far_low = swap(near[1][:cut], "epoch", 0)
        far_high = swap(near[0][cut:], "epoch", 1)
        arrays = [mine, near[0], near[1], far_low, far_high]
        pieces = [(0, 0, per_block), (1, 0, per_block), (2, 0, per_block), (3, 0, per_block), (3, cut * per_block, per_block)]
    else:
        slots = [mine]
        for b in range(bits):
            slots = slots + [swap(s, "epoch", b) for s in slots]
        me = lax.axis_index("epoch")
        every = jnp.take(jnp.stack(slots), jnp.bitwise_xor(jnp.arange(epochs), me), axis=0)
        flat = jnp.transpose(every, (1, 2, 0, 3)).reshape(blocks, long, per_block, LANES)
        arrays = [jnp.transpose(flat, (0, 2, 1, 3)).reshape(blocks * per_block, long, LANES)]
        pieces = [(None, 0, 1)]

    const = lambda b: (0, 0)
    convolve = pl.pallas_call(
        functools.partial(match_kernel, (pieces, nrow, ncol)),
        grid=(blocks,),
        in_specs=[hbm] * len(arrays)
        + [
            smem,
            pl.BlockSpec(toep_hi.shape, const),
            pl.BlockSpec(toep_lo.shape, const),
            pl.BlockSpec(band.shape, lambda b: (0, 0, 0)),
        ],
        out_specs=pl.BlockSpec((ROWS_DEV, tile_cols), lambda b: (0, b)),
        out_shape=jax.ShapeDtypeStruct((ROWS_DEV, ncol), F32),
        scratch_shapes=[
            pltpu.VMEM((blocks * per_block + 2, long, LANES), F32),
            pltpu.VMEM((2, 2, ROWS_DEV, LANES), F32),
            pltpu.SemaphoreType.DMA((sum(a.shape[0] for a in arrays),)),
        ],
        name="convolve",
        cost_estimate=pl.CostEstimate(flops=15_000_000_000, bytes_accessed=10_000_000, transcendentals=0),
    )
    matched = convolve(*arrays, psf_poly, toep_hi, toep_lo, band)
    return pl.pallas_call(
        subtract_kernel,
        grid=(blocks,),
        in_specs=[
            pl.BlockSpec((1,) + got_a.shape[1:], lambda b: (b, 0, 0)),
            pl.BlockSpec((1,) + got_b.shape[1:], lambda b: (b, 0, 0)),
            pl.BlockSpec((ROWS_DEV, tile_cols), lambda b: (0, b)),
        ],
        out_specs=pl.BlockSpec((1, ROWS_DEV, tile_cols), lambda b: (0, 0, b)),
        out_shape=jax.ShapeDtypeStruct((1, ROWS_DEV, ncol), F32),
        name="subtract",
        cost_estimate=pl.CostEstimate(flops=1_000_000, bytes_accessed=12_000_000, transcendentals=0),
    )(got_a, got_b, matched)


def solution(mesh):
    in_specs = (
        P("epoch", "strip", None, None),
        P("epoch", "strip"),
        P("epoch", "strip"),
        P("epoch", None, None),
        P(),
        P(),
        P(),
        P(),
    )
    out_specs = P("epoch", "strip", None)

    return jax.shard_map(shards, mesh=mesh, in_specs=in_specs, out_specs=out_specs, check_vma=False)
```

profile of v0, /device:TPU:0, one launch (start us, length us, event | category | flops | bytes accessed | tf_op | source)
XLA Modules:
  0.0 180.1 jit_solution(15469056660844623601)
XLA Ops:
  0.0 19.7 %warp.1 = (f32[8,96,512]{2,1,0:T(8,128)}, f32[8,160,512]{2,1,0:T(8,128)}, f32[2,1032,128]{2,1,0:T(8,128)}, f32[2,1032,128]{2,1,0:T(8,128)}, f32[2,1032,128]{2,1,0:T(8,128)}, /*index=5*/f32[2,1032,128]{2,1,0:T(8,128)}) custom-call(s32[1,12]{1,0:T(1,128)} %kind_ref.1, s32[1,8,12]{2,1,0:T(8,128)} %heights_ref.1, f32[1,12]{1,0:T(1,128)} %invvar_ref.1, ...), custom_call_target="tpu_custom_call" | custom-call | flops 8000000000 | bytes 20000000 | tf_op jit(solution)/shard_map/warp/pallas_call | solution.py:289
  19.7 6.4 %all-to-all-start = ((f32[8,96,512]{2,1,0:T(8,128)}), f32[8,96,512]{2,1,0:T(8,128)S(1)}, u32[]{:S(2)}, u32[]{:S(2)}) async-start(f32[8,96,512]{2,1,0:T(8,128)} %get-tuple-element.22), calls=%async_computation | async-start | bytes 3145728 | tf_op jit(solution)/shard_map/all_to_all | solution.py:315
  26.1 1.6 collective-permute-start
  27.7 1.5 collective-permute-start.2
  29.2 22.9 %collective-permute-done.refs_1_ = f32[2,1032,128]{2,1,0:T(8,128)S(1)} collective-permute-done((f32[2,1032,128]{2,1,0:T(8,128)}, f32[2,1032,128]{2,1,0:T(8,128)S(1)}, u32[]{:S(2)}, u32[]{:S(2)}) %collective-permute-start) | collective-permute-done | bytes 1056800 | tf_op jit(solution)/shard_map/ppermute | solution.py:260
  52.2 1.6 collective-permute-start.1
  53.9 1.5 collective-permute-start.3
  55.4 10.3 %collective-permute-done.1.refs_2_ = f32[1,1032,128]{2,1,0:T(8,128)S(1)} collective-permute-done((f32[1,1032,128]{2,1,0:T(8,128)S(1)}, f32[1,1032,128]{2,1,0:T(8,128)S(1)}, u32[]{:S(2)}, u32[]{:S(2)}) %collective-permute-start.1) | collective-permute-done | bytes 528416 | tf_op jit(solution)/shard_map/ppermute | solution.py:260
  65.7 1.4 collective-permute-done.3.refs_5_
  68.0 3.2 %template.1 = f32[8,288,128]{2,1,0:T(8,128)} custom-call(f32[2,1032,128]{2,1,0:T(8,128)} %get-tuple-element.18.refs_0_, f32[2,1032,128]{2,1,0:T(8,128)} %copy-done.4, f32[1,1032,128]{2,1,0:T(8,128)} %copy-done.6, f32[2,1032,128]{2,1,0:T(8,128)} %get-tuple-element.20.refs_3_, f32[2,1032,128]{2,1,0:T(8,128)} %copy-done.5, f32[1,1032,128]{2,1,0:T(8,128)} %copy-done.7), custom_call_target="tpu_custom_call" | custom-call | flops 2000000 | bytes 5000000 | tf_op jit(solution)/shard_map/template/pallas_call | solution.py:355
  71.3 33.9 %all_to_all.15.refs_0_ = f32[8,288,128]{2,1,0:T(8,128)} all-to-all(f32[8,288,128]{2,1,0:T(8,128)} %template.1), channel_id=1, replica_groups=mesh['epoch'=4,'strip'=8] {'strip'}, dimensions={0} | all-to-all | bytes 2359296 | tf_op jit(solution)/shard_map/all_to_all | solution.py:366
  105.1 3.6 %all-to-all-start.2 = ((f32[8,160,512]{2,1,0:T(8,128)}), f32[8,160,512]{2,1,0:T(8,128)S(1)}, u32[]{:S(2)}, u32[]{:S(2)}) async-start(f32[8,160,512]{2,1,0:T(8,128)} %get-tuple-element.26), calls=%async_computation.2 | async-start | bytes 5242880 | tf_op jit(solution)/shard_map/all_to_all | solution.py:368
  108.8 1.1 collective-permute-start.5
  109.9 1.4 collective-permute-start.4
  111.3 26.0 %collective-permute-done.5.refs_2_ = f32[8,288,128]{2,1,0:T(8,128)S(1)} collective-permute-done((f32[8,288,128]{2,1,0:T(8,128)}, f32[8,288,128]{2,1,0:T(8,128)S(1)}, u32[]{:S(2)}, u32[]{:S(2)}) %collective-permute-start.5) | collective-permute-done | bytes 1179680 | tf_op jit(solution)/shard_map/ppermute | solution.py:260
  137.3 1.5 collective-permute-start.6
  138.8 1.0 copy-done.9
  140.7 1.0 collective-permute-start.7
  141.7 2.4 %bands.1 = (bf16[256,256]{1,0:T(8,128)(2,1)}, bf16[256,256]{1,0:T(8,128)(2,1)}, bf16[2,256,160]{2,1,0:T(8,128)(2,1)}) custom-call(f32[2,2,31]{2,1,0:T(2,128)} %psf_ref.1), custom_call_target="tpu_custom_call" | custom-call | flops 10000000 | bytes 500000 | tf_op jit(solution)/shard_map/bands/pallas_call | solution.py:330
  144.1 8.1 %collective-permute-done.6.refs_3_ = f32[4,288,128]{2,1,0:T(8,128)} collective-permute-done((f32[4,288,128]{2,1,0:T(8,128)S(1)}, f32[4,288,128]{2,1,0:T(8,128)}, u32[]{:S(2)}, u32[]{:S(2)}) %collective-permute-start.6) | collective-permute-done | bytes 589856 | tf_op jit(solution)/shard_map/ppermute | solution.py:260
  152.2 3.3 %collective-permute-done.7.refs_4_ = f32[4,288,128]{2,1,0:T(8,128)} collective-permute-done((f32[4,288,128]{2,1,0:T(8,128)}, f32[4,288,128]{2,1,0:T(8,128)}, u32[]{:S(2)}, u32[]{:S(2)}) %collective-permute-start.7) | collective-permute-done | bytes 589856 | tf_op jit(solution)/shard_map/ppermute | solution.py:260
  155.5 15.5 %convolve.1.matched_ref = f32[256,4096]{1,0:T(8,128)} custom-call(f32[8,288,128]{2,1,0:T(8,128)} %all_to_all.15.refs_0_, f32[8,288,128]{2,1,0:T(8,128)} %copy-done.9, f32[8,288,128]{2,1,0:T(8,128)} %copy-done.8, f32[4,288,128]{2,1,0:T(8,128)} %collective-permute-done.6.refs_3_, f32[4,288,128]{2,1,0:T(8,128)} %collective-permute-done.7.refs_4_, ...), custom_call_target="tpu_custom_call" | custom-call | flops 15000000512 | bytes 10000000 | tf_op jit(solution)/shard_map/convolve/pallas_call | solution.py:413
  171.0 1.5 copy-done
  172.5 7.6 %subtract.1 = f32[1,256,4096]{2,1,0:T(8,128)} custom-call(f32[8,96,512]{2,1,0:T(8,128)} %copy-done.1, f32[8,160,512]{2,1,0:T(8,128)} %copy-done, f32[256,4096]{1,0:T(8,128)} %convolve.1.matched_ref), custom_call_target="tpu_custom_call" | custom-call | flops 1000000 | bytes 12000000 | tf_op jit(solution)/shard_map/subtract/pallas_call | solution.py:414
  (26 shorter events, 1.9 us)
Async XLA Ops:
  19.7 32.4 %copy-start.2 = (f32[2,1032,128]{2,1,0:T(8,128)S(1)}, f32[2,1032,128]{2,1,0:T(8,128)}, u32[]{:S(2)}) copy-start(f32[2,1032,128]{2,1,0:T(8,128)} %get-tuple-element.18.refs_0_) | copy-start | bytes 3170308
  19.7 51.6 %all-to-all-start = ((f32[8,96,512]{2,1,0:T(8,128)}), f32[8,96,512]{2,1,0:T(8,128)S(1)}, u32[]{:S(2)}, u32[]{:S(2)}) async-start(f32[8,96,512]{2,1,0:T(8,128)} %get-tuple-element.22), calls=%async_computation | async-start | bytes 3145728 | tf_op jit(solution)/shard_map/all_to_all | solution.py:315
  26.1 27.7 %copy-start.3 = (f32[2,1032,128]{2,1,0:T(8,128)S(1)}, f32[2,1032,128]{2,1,0:T(8,128)}, u32[]{:S(2)}) copy-start(f32[2,1032,128]{2,1,0:T(8,128)} %get-tuple-element.20.refs_3_) | copy-start | bytes 3170308
  26.1 26.0 %collective-permute-start = (f32[2,1032,128]{2,1,0:T(8,128)}, f32[2,1032,128]{2,1,0:T(8,128)S(1)}, u32[]{:S(2)}, u32[]{:S(2)}) collective-permute-start(f32[2,1032,128]{2,1,0:T(8,128)} %get-tuple-element.19), channel_id=1, source_target_pairs={{0,8},{8,0},{16,24},{24,16},{1,9},{9,1},{17,25},{25,17},{2,10},{10... | collective-permute-start | bytes 3170312 | tf_op jit(solution)/shard_map/ppermute | solution.py:260
  27.7 26.1 %collective-permute-start.2 = (f32[2,1032,128]{2,1,0:T(8,128)}, f32[2,1032,128]{2,1,0:T(8,128)S(1)}, u32[]{:S(2)}, u32[]{:S(2)}) collective-permute-start(f32[2,1032,128]{2,1,0:T(8,128)} %get-tuple-element.21), channel_id=1, source_target_pairs={{0,16},{8,24},{16,0},{24,8},{1,17},{9,25},{17,1},{25,9},{2,18},{10... | collective-permute-start | bytes 3170312 | tf_op jit(solution)/shard_map/ppermute | solution.py:260
  52.1 1.8 copy-start.4
  52.2 13.6 %collective-permute-start.1 = (f32[1,1032,128]{2,1,0:T(8,128)S(1)}, f32[1,1032,128]{2,1,0:T(8,128)S(1)}, u32[]{:S(2)}, u32[]{:S(2)}) collective-permute-start(f32[1,1032,128]{2,1,0:T(8,128)S(1)} %slice_add_fusion.1), channel_id=1, source_target_pairs={{0,16},{8,24},{16,0},{24,8},{1,17},{9,25},{17,1},{25,9},{2,18},{10... | collective-permute-start | bytes 1585160 | tf_op jit(solution)/shard_map/ppermute | solution.py:260
  53.8 1.6 copy-start.5
  53.9 13.3 %collective-permute-start.3 = (f32[1,1032,128]{2,1,0:T(8,128)S(1)}, f32[1,1032,128]{2,1,0:T(8,128)S(1)}, u32[]{:S(2)}, u32[]{:S(2)}) collective-permute-start(f32[1,1032,128]{2,1,0:T(8,128)S(1)} %slice_add_fusion), channel_id=1, source_target_pairs={{0,8},{8,0},{16,24},{24,16},{1,9},{9,1},{17,25},{25,17},{2,10},{10... | collective-permute-start | bytes 1585160 | tf_op jit(solution)/shard_map/ppermute | solution.py:260
  65.7 1.4 copy-start.6
  67.2 0.9 copy-start.7
  71.3 33.9 %copy-start.1 = (f32[8,96,512]{2,1,0:T(8,128)}, f32[8,96,512]{2,1,0:T(8,128)S(1)}, u32[]{:S(2)}) copy-start(f32[8,96,512]{2,1,0:T(8,128)S(1)} %all-to-all-done.sci_a) | copy-start | bytes 4718596
  105.1 65.8 %all-to-all-start.2 = ((f32[8,160,512]{2,1,0:T(8,128)}), f32[8,160,512]{2,1,0:T(8,128)S(1)}, u32[]{:S(2)}, u32[]{:S(2)}) async-start(f32[8,160,512]{2,1,0:T(8,128)} %get-tuple-element.26), calls=%async_computation.2 | async-start | bytes 5242880 | tf_op jit(solution)/shard_map/all_to_all | solution.py:368
  108.8 28.5 %collective-permute-start.5 = (f32[8,288,128]{2,1,0:T(8,128)}, f32[8,288,128]{2,1,0:T(8,128)S(1)}, u32[]{:S(2)}, u32[]{:S(2)}) collective-permute-start(f32[8,288,128]{2,1,0:T(8,128)} %all_to_all.15.refs_0_), channel_id=1, source_target_pairs={{0,16},{8,24},{16,0},{24,8},{1,17},{9,25},{17,1},{25,9},{2,18},{10... | collective-permute-start | bytes 3538952 | tf_op jit(solution)/shard_map/ppermute | solution.py:260
  109.9 28.9 %collective-permute-start.4 = (f32[8,288,128]{2,1,0:T(8,128)}, f32[8,288,128]{2,1,0:T(8,128)S(1)}, u32[]{:S(2)}, u32[]{:S(2)}) collective-permute-start(f32[8,288,128]{2,1,0:T(8,128)} %all_to_all.15.refs_0_), channel_id=1, source_target_pairs={{0,8},{8,0},{16,24},{24,16},{1,9},{9,1},{17,25},{25,17},{2,10},{10... | collective-permute-start | bytes 3538952 | tf_op jit(solution)/shard_map/ppermute | solution.py:260
  137.2 3.5 %copy-start.8 = (f32[8,288,128]{2,1,0:T(8,128)}, f32[8,288,128]{2,1,0:T(8,128)S(1)}, u32[]{:S(2)}) copy-start(f32[8,288,128]{2,1,0:T(8,128)S(1)} %collective-permute-done.5.refs_2_) | copy-start | bytes 3538948
  137.3 14.9 %collective-permute-start.6 = (f32[4,288,128]{2,1,0:T(8,128)S(1)}, f32[4,288,128]{2,1,0:T(8,128)}, u32[]{:S(2)}, u32[]{:S(2)}) collective-permute-start(f32[4,288,128]{2,1,0:T(8,128)S(1)} %slice.26), channel_id=1, source_target_pairs={{0,8},{8,0},{16,24},{24,16},{1,9},{9,1},{17,25},{25,17},{2,10},{10... | collective-permute-start | bytes 1769480 | tf_op jit(solution)/shard_map/ppermute | solution.py:260
  138.8 1.0 copy-start.9
  140.7 14.7 %collective-permute-start.7 = (f32[4,288,128]{2,1,0:T(8,128)}, f32[4,288,128]{2,1,0:T(8,128)}, u32[]{:S(2)}, u32[]{:S(2)}) collective-permute-start(f32[4,288,128]{2,1,0:T(8,128)} %slice.27), channel_id=1, source_target_pairs={{0,16},{8,24},{16,0},{24,8},{1,17},{9,25},{17,1},{25,9},{2,18},{10... | collective-permute-start | bytes 1769480 | tf_op jit(solution)/shard_map/ppermute | solution.py:260
  171.0 1.5 copy-start
where the time goes:
time: 181 us; the launch traced here: 180 us
  waiting for transfers between devices  72 us (40%)
  Pallas kernels  48.4 us (27%)
  blocking collectives  33.9 us (19%)
  starting transfers between devices  21.3 us (12%)
  local copies, waits for them, and re-layouts  4.35 us (2%)
    ppermute x8, waiting for transfers between devices, swap(): return lax.ppermute(value, axis, [(i, i ^ 1 << bit) for i in range(count)])  72 us
    all_to_all x1, blocking collectives, shards(): lax.all_to_all(strips_out, 'strip', split_axis=0, concat_axis=0, tiled=True)  33.9 us
    pallas_call x1, Pallas kernels, shards(): pl.pallas_call(functools.partial(warp_kernel, (epochs, nrow, share, order...  19.7 us
    pallas_call x1, Pallas kernels, shards(): matched = convolve(*arrays, psf_poly, toep_hi, toep_lo, band)  15.5 us
    ppermute x8, starting transfers between devices, swap(): return lax.ppermute(value, axis, [(i, i ^ 1 << bit) for i in range(count)])  11.3 us
    pallas_call x1, Pallas kernels, shards(): pl.pallas_call(subtract_kernel, grid=(blocks,), in_specs=[pl.BlockSpec((1...  7.64 us
    all_to_all x1, starting transfers between devices, shards(): lax.all_to_all(sci_a, 'strip', split_axis=0, concat_axis=0, tiled=True)  6.44 us
    all_to_all x1, starting transfers between devices, shards(): lax.all_to_all(sci_b, 'strip', split_axis=0, concat_axis=0, tiled=True)  3.63 us
  transfers between devices with their start and end apart: 10, of which 6 were waited for; matrix products, arithmetic and copies ran while one was open for 1% of the time, Pallas kernels for 12%

commit v1 on v0

--- a/solution.py
+++ b/solution.py
@@ -138,8 +138,9 @@
 
 
 def template_kernel(terms, *refs):
-    term_refs, out_ref, pad_s = refs[:-2], refs[-2], refs[-1]
-    strips, long, share = out_ref.shape
+    term_refs, out_refs, pad_s = refs[: 2 * terms], refs[2 * terms : -1], refs[-1]
+    strips = len(out_refs)
+    long, share = out_refs[0].shape
     rows_dev = long - 2 * HALO
     nrow = strips * rows_dev
     nhalf = nrow // 2
@@ -154,8 +155,9 @@
         for i in range(whalf):
             below = jnp.transpose(jnp.broadcast_to(weights[i : i + 1, :], (share, share)))
             pad_s[pl.ds(HALO + part * nhalf + i * share, share), :] = add(pl.ds(i * share, share)) / below
-    for s in range(strips):
-        out_ref[s] = pad_s[pl.ds(s * rows_dev, long), :]
+    for k in range(strips):
+        strip = jnp.bitwise_xor(lax.axis_index("strip"), k)
+        out_refs[k][...] = pad_s[pl.ds(pl.multiple_of(strip * rows_dev, rows_dev), long), :]
 
 
 def bands_kernel(psf_ref, toep_hi, toep_lo, band_ref):
@@ -193,12 +195,14 @@
     @pl.when(step == 0)
     def _():
         copies = []
-        for ref, (slot, first, stride) in zip(tile_refs, pieces):
-            place = first if slot is None else jnp.bitwise_xor(me, slot) + first
+        for ref, (slot, first) in zip(tile_refs, pieces):
             for i in range(ref.shape[0]):
-                copies.append(
-                    pltpu.make_async_copy(ref.at[i], pad_s.at[1 + place + i * stride], sems.at[len(copies)])
-                )
+                if slot is None:
+                    place = i
+                else:
+                    block = jnp.bitwise_xor(strip, first + i)
+                    place = block * per_step + jnp.bitwise_xor(me, slot)
+                copies.append(pltpu.make_async_copy(ref.at[i], pad_s.at[1 + place], sems.at[len(copies)]))
         for copy in copies:
             copy.start()
         pad_s[0] = jnp.zeros(pad_s.shape[1:], F32)
@@ -249,10 +253,12 @@
 
 
 def subtract_kernel(sci_a, sci_b, matched_ref, out_ref):
-    rows = sci_a.shape[1]
-    out_ref[0, pl.ds(0, rows), :] = sci_a[0] - matched_ref[pl.ds(0, rows), :]
+    b = pl.program_id(0)
+    rows, width = sci_a.shape[1:]
+    columns = pl.ds(pl.multiple_of(b * width, width), width)
+    out_ref[0, pl.ds(0, rows), :] = sci_a[b] - matched_ref[pl.ds(0, rows), columns]
     rest = pl.ds(rows, sci_b.shape[1])
-    out_ref[0, rest, :] = sci_b[0] - matched_ref[rest, :]
+    out_ref[0, rest, :] = sci_b[b] - matched_ref[rest, columns]
 
 
 def swap(value, axis, bit):
@@ -351,23 +357,23 @@
         terms = fixed
 
     long = ROWS_DEV + 2 * HALO
-    first_slot = pl.BlockSpec((1, long_half, share), lambda i: (0, 0, 0))
-    strips_out = pl.pallas_call(
+    parts = pl.pallas_call(
         functools.partial(template_kernel, len(terms[0])),
-        grid=(1,),
-        in_specs=[first_slot] * (2 * len(terms[0])),
-        out_specs=pl.BlockSpec((strips, long, share), lambda i: (0, 0, 0)),
-        out_shape=jax.ShapeDtypeStruct((strips, long, share), F32),
+        in_specs=[vmem] * (2 * len(terms[0])),
+        out_specs=[vmem] * strips,
+        out_shape=[jax.ShapeDtypeStruct((long, share), F32)] * strips,
         scratch_shapes=[pltpu.VMEM((nrow + 2 * HALO, share), F32)],
         name="template",
         cost_estimate=pl.CostEstimate(flops=2_000_000, bytes_accessed=5_000_000, transcendentals=0),
     )(*terms[0], *terms[1])
-    strips_out, got_a = lax.optimization_barrier((strips_out, got_a))
-    mine = lax.all_to_all(strips_out, "strip", split_axis=0, concat_axis=0, tiled=True)
-    sci_b, mine = lax.optimization_barrier((sci_b, mine))
+    came = [None] * strips
+    came[0] = parts[0]
+    for k in reversed(range(1, strips)):
+        came[k] = lax.ppermute(parts[k], "strip", [(i, i ^ k) for i in range(strips)])
+    mine = jnp.stack(came[:: sources])
+    sci_b, got_a = lax.optimization_barrier((sci_b, got_a))
     got_b = lax.all_to_all(sci_b, "strip", split_axis=0, concat_axis=0, tiled=True)
     if sources > 1:
-        mine = mine[::sources]
         got_a = jnp.sum(got_a.reshape((blocks, sources) + got_a.shape[1:]), axis=1)
         got_b = jnp.sum(got_b.reshape((blocks, sources) + got_b.shape[1:]), axis=1)
 
@@ -378,16 +384,18 @@
         far_low = swap(near[1][:cut], "epoch", 0)
         far_high = swap(near[0][cut:], "epoch", 1)
         arrays = [mine, near[0], near[1], far_low, far_high]
-        pieces = [(0, 0, per_block), (1, 0, per_block), (2, 0, per_block), (3, 0, per_block), (3, cut * per_block, per_block)]
+        pieces = [(0, 0), (1, 0), (2, 0), (3, 0), (3, cut)]
     else:
         slots = [mine]
         for b in range(bits):
             slots = slots + [swap(s, "epoch", b) for s in slots]
         me = lax.axis_index("epoch")
         every = jnp.take(jnp.stack(slots), jnp.bitwise_xor(jnp.arange(epochs), me), axis=0)
+        home = lax.axis_index("strip") // sources
+        every = jnp.take(every, jnp.bitwise_xor(jnp.arange(blocks), home), axis=1)
         flat = jnp.transpose(every, (1, 2, 0, 3)).reshape(blocks, long, per_block, LANES)
         arrays = [jnp.transpose(flat, (0, 2, 1, 3)).reshape(blocks * per_block, long, LANES)]
-        pieces = [(None, 0, 1)]
+        pieces = [(None, 0)]
 
     const = lambda b: (0, 0)
     convolve = pl.pallas_call(
@@ -414,11 +422,7 @@
     return pl.pallas_call(
         subtract_kernel,
         grid=(blocks,),
-        in_specs=[
-            pl.BlockSpec((1,) + got_a.shape[1:], lambda b: (b, 0, 0)),
-            pl.BlockSpec((1,) + got_b.shape[1:], lambda b: (b, 0, 0)),
-            pl.BlockSpec((ROWS_DEV, tile_cols), lambda b: (0, b)),
-        ],
+        in_specs=[vmem] * 3,
         out_specs=pl.BlockSpec((1, ROWS_DEV, tile_cols), lambda b: (0, 0, b)),
         out_shape=jax.ShapeDtypeStruct((1, ROWS_DEV, ncol), F32),
         name="subtract",

time: 181 us -> 230 us (1.27)
  the two profiles are of different devices: /device:TPU:0 before, /device:TPU:9 now
where the time goes in v1:
time: 230 us; the launch traced here: 226 us
  waiting for transfers between devices  137 us (60%)
  Pallas kernels  48.6 us (21%)
  starting transfers between devices  26.7 us (12%)
  local copies, waits for them, and re-layouts  12.7 us (6%)
    ppermute x8, waiting for transfers between devices, swap(): return lax.ppermute(value, axis, [(i, i ^ 1 << bit) for i in range(count)])  69.2 us
    ppermute x7, waiting for transfers between devices, shards(): lax.ppermute(parts[k], 'strip', [(i, i ^ k) for i in range(strips)])  67.9 us
    pallas_call x1, Pallas kernels, shards(): pl.pallas_call(functools.partial(warp_kernel, (epochs, nrow, share, order...  19.7 us
    pallas_call x1, Pallas kernels, shards(): matched = convolve(*arrays, psf_poly, toep_hi, toep_lo, band)  15.6 us
    unnamed x27, local copies, waits for them, and re-layouts  11.2 us
    ppermute x7, starting transfers between devices, shards(): lax.ppermute(parts[k], 'strip', [(i, i ^ k) for i in range(strips)])  9.37 us
    pallas_call x1, Pallas kernels, shards(): pl.pallas_call(subtract_kernel, grid=(blocks,), in_specs=[vmem] * 3, out_...  7.02 us
    ppermute x8, starting transfers between devices, swap(): return lax.ppermute(value, axis, [(i, i ^ 1 << bit) for i in range(count)])  6.54 us
  transfers between devices with their start and end apart: 17, of which 11 were waited for; matrix products, arithmetic and copies ran while one was open for 4% of the time, Pallas kernels for 10%

profile of v1, /device:TPU:9, one launch (start us, length us, event | category | flops | bytes accessed | tf_op | source)
XLA Modules:
  0.0 226.3 jit_solution(14119407112315252624)
XLA Ops:
  0.0 19.7 %warp.1 = (f32[8,96,512]{2,1,0:T(8,128)}, f32[8,160,512]{2,1,0:T(8,128)}, f32[2,1032,128]{2,1,0:T(8,128)}, f32[2,1032,128]{2,1,0:T(8,128)}, f32[2,1032,128]{2,1,0:T(8,128)}, /*index=5*/f32[2,1032,128]{2,1,0:T(8,128)}) custom-call(s32[1,12]{1,0:T(1,128)} %kind_ref.1, s32[1,8,12]{2,1,0:T(8,128)} %heights_ref.1, f32[1,12]{1,0:T(1,128)} %invvar_ref.1, ...), custom_call_target="tpu_custom_call" | custom-call | flops 8000000000 | bytes 20000000 | tf_op jit(solution)/shard_map/warp/pallas_call | solution.py:295
  19.7 1.2 collective-permute-start
  20.9 6.0 %all-to-all-start = ((f32[8,96,512]{2,1,0:T(8,128)}), f32[8,96,512]{2,1,0:T(8,128)S(1)}, u32[]{:S(2)}, u32[]{:S(2)}) async-start(f32[8,96,512]{2,1,0:T(8,128)} %get-tuple-element.25), calls=%async_computation | async-start | bytes 3145728 | tf_op jit(solution)/shard_map/all_to_all | solution.py:321
  26.9 1.3 collective-permute-start.2
  28.2 16.1 %collective-permute-done.refs_1_ = f32[2,1032,128]{2,1,0:T(8,128)} collective-permute-done((f32[2,1032,128]{2,1,0:T(8,128)}, f32[2,1032,128]{2,1,0:T(8,128)}, u32[]{:S(2)}, u32[]{:S(2)}) %collective-permute-start) | collective-permute-done | bytes 1056800 | tf_op jit(solution)/shard_map/ppermute | solution.py:266
  46.6 5.0 %collective-permute-done.2.refs_4_ = f32[2,1032,128]{2,1,0:T(8,128)S(1)} collective-permute-done((f32[2,1032,128]{2,1,0:T(8,128)}, f32[2,1032,128]{2,1,0:T(8,128)S(1)}, u32[]{:S(2)}, u32[]{:S(2)}) %collective-permute-start.2) | collective-permute-done | bytes 1056800 | tf_op jit(solution)/shard_map/ppermute | solution.py:266
  52.9 10.1 %collective-permute-done.1.refs_2_ = f32[1,1032,128]{2,1,0:T(8,128)S(1)} collective-permute-done((f32[1,1032,128]{2,1,0:T(8,128)S(1)}, f32[1,1032,128]{2,1,0:T(8,128)S(1)}, u32[]{:S(2)}, u32[]{:S(2)}) %collective-permute-start.1) | collective-permute-done | bytes 528416 | tf_op jit(solution)/shard_map/ppermute | solution.py:266
  64.9 3.9 %template.1 = (f32[288,128]{1,0:T(8,128)}, f32[288,128]{1,0:T(8,128)}, f32[288,128]{1,0:T(8,128)}, f32[288,128]{1,0:T(8,128)}, f32[288,128]{1,0:T(8,128)}, /*ind...) custom-call(f32[2,1032,128]{2,1,0:T(8,128)} %get-tuple-element.28.refs_0_, ...), custom_call_target="tpu_custom_call" | custom-call | flops 2000000 | bytes 5000000 | tf_op jit(solution)/shard_map/template/pallas_call | solution.py:360
  68.8 3.0 %collective-permute-start.4 = (f32[288,128]{1,0:T(8,128)}, f32[288,128]{1,0:T(8,128)S(1)}, u32[]{:S(2)}, u32[]{:S(2)}) collective-permute-start(f32[288,128]{1,0:T(8,128)} %get-tuple-element.33), channel_id=1, source_target_pairs={{0,1},{1,0},{2,3},{3,2},{4,5},{5,4},{6,7},{7,6},{8,9},{9,8},{10,11... | collective-permute-start | bytes 442376 | tf_op jit(solution)/shard_map/ppermute | solution.py:372
  72.2 1.2 collective-permute-start.6
  73.4 2.1 collective-permute-start.7
  76.2 1.6 bitcast_dynamic-update-slice_fusion.7
  79.0 4.8 %all-to-all-start.1 = ((f32[8,160,512]{2,1,0:T(8,128)}), f32[8,160,512]{2,1,0:T(8,128)S(1)}, u32[]{:S(2)}, u32[]{:S(2)}) async-start(f32[8,160,512]{2,1,0:T(8,128)} %get-tuple-element.27), calls=%async_computation.1 | async-start | bytes 5242880 | tf_op jit(solution)/shard_map/all_to_all | solution.py:375
  88.5 8.9 %collective-permute-done.8 = f32[288,128]{1,0:T(8,128)S(1)} collective-permute-done((f32[288,128]{1,0:T(8,128)}, f32[288,128]{1,0:T(8,128)S(1)}, u32[]{:S(2)}, u32[]{:S(2)}) %collective-permute-start.8) | collective-permute-done | bytes 147488 | tf_op jit(solution)/shard_map/ppermute | solution.py:372
  98.1 56.1 %collective-permute-done.9 = f32[288,128]{1,0:T(8,128)S(1)} collective-permute-done((f32[288,128]{1,0:T(8,128)}, f32[288,128]{1,0:T(8,128)S(1)}, u32[]{:S(2)}, u32[]{:S(2)}) %collective-permute-start.9) | collective-permute-done | bytes 147488 | tf_op jit(solution)/shard_map/ppermute | solution.py:372
  154.9 2.8 %collective-permute-done.10 = f32[288,128]{1,0:T(8,128)S(1)} collective-permute-done((f32[288,128]{1,0:T(8,128)S(1)}, f32[288,128]{1,0:T(8,128)S(1)}, u32[]{:S(2)}, u32[]{:S(2)}) %collective-permute-start.10) | collective-permute-done | bytes 147488 | tf_op jit(solution)/shard_map/ppermute | solution.py:372
  158.4 1.3 collective-permute-start.12
  159.9 25.7 %collective-permute-done.12.refs_2_ = f32[8,288,128]{2,1,0:T(8,128)S(1)} collective-permute-done((f32[8,288,128]{2,1,0:T(8,128)}, f32[8,288,128]{2,1,0:T(8,128)S(1)}, u32[]{:S(2)}, u32[]{:S(2)}) %collective-permute-start.12) | collective-permute-done | bytes 1179680 | tf_op jit(solution)/shard_map/ppermute | solution.py:266
  189.2 2.4 %bands.1 = (bf16[256,256]{1,0:T(8,128)(2,1)}, bf16[256,256]{1,0:T(8,128)(2,1)}, bf16[2,256,160]{2,1,0:T(8,128)(2,1)}) custom-call(f32[2,2,31]{2,1,0:T(2,128)} %psf_ref.1), custom_call_target="tpu_custom_call" | custom-call | flops 10000000 | bytes 500000 | tf_op jit(solution)/shard_map/bands/pallas_call | solution.py:336
  191.6 7.8 %collective-permute-done.13.refs_3_ = f32[4,288,128]{2,1,0:T(8,128)} collective-permute-done((f32[4,288,128]{2,1,0:T(8,128)S(1)}, f32[4,288,128]{2,1,0:T(8,128)}, u32[]{:S(2)}, u32[]{:S(2)}) %collective-permute-start.13) | collective-permute-done | bytes 589856 | tf_op jit(solution)/shard_map/ppermute | solution.py:266
  199.4 2.7 %collective-permute-done.14.refs_4_ = f32[4,288,128]{2,1,0:T(8,128)} collective-permute-done((f32[4,288,128]{2,1,0:T(8,128)}, f32[4,288,128]{2,1,0:T(8,128)}, u32[]{:S(2)}, u32[]{:S(2)}) %collective-permute-start.14) | collective-permute-done | bytes 589856 | tf_op jit(solution)/shard_map/ppermute | solution.py:266
  202.1 15.6 %convolve.1.matched_ref = f32[256,4096]{1,0:T(8,128)} custom-call(f32[8,288,128]{2,1,0:T(8,128)} %bitcast_dynamic-update-slice_fusion.refs_0_, f32[8,288,128]{2,1,0:T(8,128)} %copy-done.8, f32[8,288,128]{2,1,0:T(8,128)} %copy-done.7, f32[4,288,128]{2,1,0:T(8,128)} %collective-permute-done.13.refs_3_, f32[4,288,128]{2,1,0:T(8,128)} %collective-permute-done.14.refs_4_, ...), custom_call_target="tpu_custom_call" | custom-call | flops 15000000512 | bytes 10000000 | tf_op jit(solution)/shard_map/convolve/pallas_call | solution.py:421
  217.8 1.5 copy-done
  219.3 7.0 %subtract.1 = f32[1,256,4096]{2,1,0:T(8,128)} custom-call(f32[8,96,512]{2,1,0:T(8,128)} %copy-done.1, f32[8,160,512]{2,1,0:T(8,128)} %copy-done, f32[256,4096]{1,0:T(8,128)} %convolve.1.matched_ref), custom_call_target="tpu_custom_call" | custom-call | flops 1000000 | bytes 12000000 | tf_op jit(solution)/shard_map/subtract/pallas_call | solution.py:422
  (47 shorter events, 18.4 us)
Async XLA Ops:
  19.7 24.6 %collective-permute-start = (f32[2,1032,128]{2,1,0:T(8,128)}, f32[2,1032,128]{2,1,0:T(8,128)}, u32[]{:S(2)}, u32[]{:S(2)}) collective-permute-start(f32[2,1032,128]{2,1,0:T(8,128)} %get-tuple-element.29), channel_id=1, source_target_pairs={{0,8},{8,0},{16,24},{24,16},{1,9},{9,1},{17,25},{25,17},{2,10},{10... | collective-permute-start | bytes 3170312 | tf_op jit(solution)/shard_map/ppermute | solution.py:266
  20.9 23.4 %copy-start.2 = (f32[2,1032,128]{2,1,0:T(8,128)S(1)}, f32[2,1032,128]{2,1,0:T(8,128)}, u32[]{:S(2)}) copy-start(f32[2,1032,128]{2,1,0:T(8,128)} %get-tuple-element.28.refs_0_) | copy-start | bytes 3170308
  20.9 56.8 %all-to-all-start = ((f32[8,96,512]{2,1,0:T(8,128)}), f32[8,96,512]{2,1,0:T(8,128)S(1)}, u32[]{:S(2)}, u32[]{:S(2)}) async-start(f32[8,96,512]{2,1,0:T(8,128)} %get-tuple-element.25), calls=%async_computation | async-start | bytes 3145728 | tf_op jit(solution)/shard_map/all_to_all | solution.py:321
  26.9 24.7 %copy-start.3 = (f32[2,1032,128]{2,1,0:T(8,128)S(1)}, f32[2,1032,128]{2,1,0:T(8,128)}, u32[]{:S(2)}) copy-start(f32[2,1032,128]{2,1,0:T(8,128)} %get-tuple-element.30.refs_3_) | copy-start | bytes 3170308
  26.9 24.7 %collective-permute-start.2 = (f32[2,1032,128]{2,1,0:T(8,128)}, f32[2,1032,128]{2,1,0:T(8,128)S(1)}, u32[]{:S(2)}, u32[]{:S(2)}) collective-permute-start(f32[2,1032,128]{2,1,0:T(8,128)} %get-tuple-element.31), channel_id=1, source_target_pairs={{0,16},{8,24},{16,0},{24,8},{1,17},{9,25},{17,1},{25,9},{2,18},{10... | collective-permute-start | bytes 3170312 | tf_op jit(solution)/shard_map/ppermute | solution.py:266
  45.4 17.5 %collective-permute-start.1 = (f32[1,1032,128]{2,1,0:T(8,128)S(1)}, f32[1,1032,128]{2,1,0:T(8,128)S(1)}, u32[]{:S(2)}, u32[]{:S(2)}) collective-permute-start(f32[1,1032,128]{2,1,0:T(8,128)S(1)} %slice_add_fusion.1), channel_id=1, source_target_pairs={{0,16},{8,24},{16,0},{24,8},{1,17},{9,25},{17,1},{25,9},{2,18},{10... | collective-permute-start | bytes 1585160 | tf_op jit(solution)/shard_map/ppermute | solution.py:266
  52.6 11.5 %collective-permute-start.3 = (f32[1,1032,128]{2,1,0:T(8,128)S(1)}, f32[1,1032,128]{2,1,0:T(8,128)S(1)}, u32[]{:S(2)}, u32[]{:S(2)}) collective-permute-start(f32[1,1032,128]{2,1,0:T(8,128)S(1)} %slice_add_fusion), channel_id=1, source_target_pairs={{0,8},{8,0},{16,24},{24,16},{1,9},{9,1},{17,25},{25,17},{2,10},{10... | collective-permute-start | bytes 1585160 | tf_op jit(solution)/shard_map/ppermute | solution.py:266
  63.0 1.2 copy-start.5
  68.8 15.0 %collective-permute-start.4 = (f32[288,128]{1,0:T(8,128)}, f32[288,128]{1,0:T(8,128)S(1)}, u32[]{:S(2)}, u32[]{:S(2)}) collective-permute-start(f32[288,128]{1,0:T(8,128)} %get-tuple-element.33), channel_id=1, source_target_pairs={{0,1},{1,0},{2,3},{3,2},{4,5},{5,4},{6,7},{7,6},{8,9},{9,8},{10,11... | collective-permute-start | bytes 442376 | tf_op jit(solution)/shard_map/ppermute | solution.py:372
  71.8 13.9 %collective-permute-start.5 = (f32[288,128]{1,0:T(8,128)}, f32[288,128]{1,0:T(8,128)S(1)}, u32[]{:S(2)}, u32[]{:S(2)}) collective-permute-start(f32[288,128]{1,0:T(8,128)} %get-tuple-element.34), channel_id=1, source_target_pairs={{0,2},{1,3},{2,0},{3,1},{4,6},{5,7},{6,4},{7,5},{8,10},{9,11},{10,... | collective-permute-start | bytes 442376 | tf_op jit(solution)/shard_map/ppermute | solution.py:372
  72.2 15.0 %collective-permute-start.6 = (f32[288,128]{1,0:T(8,128)}, f32[288,128]{1,0:T(8,128)S(1)}, u32[]{:S(2)}, u32[]{:S(2)}) collective-permute-start(f32[288,128]{1,0:T(8,128)} %get-tuple-element.35), channel_id=1, source_target_pairs={{0,3},{1,2},{2,1},{3,0},{4,7},{5,6},{6,5},{7,4},{8,11},{9,10},{10,... | collective-permute-start | bytes 442376 | tf_op jit(solution)/shard_map/ppermute | solution.py:372
  73.4 14.4 %collective-permute-start.7 = (f32[288,128]{1,0:T(8,128)}, f32[288,128]{1,0:T(8,128)S(1)}, u32[]{:S(2)}, u32[]{:S(2)}) collective-permute-start(f32[288,128]{1,0:T(8,128)} %get-tuple-element.36), channel_id=1, source_target_pairs={{0,4},{1,5},{2,6},{3,7},{4,0},{5,1},{6,2},{7,3},{8,12},{9,13},{10,... | collective-permute-start | bytes 442376 | tf_op jit(solution)/shard_map/ppermute | solution.py:372
  75.5 21.9 %collective-permute-start.8 = (f32[288,128]{1,0:T(8,128)}, f32[288,128]{1,0:T(8,128)S(1)}, u32[]{:S(2)}, u32[]{:S(2)}) collective-permute-start(f32[288,128]{1,0:T(8,128)} %get-tuple-element.37), channel_id=1, source_target_pairs={{0,5},{1,4},{2,7},{3,6},{4,1},{5,0},{6,3},{7,2},{8,13},{9,12},{10,... | collective-permute-start | bytes 442376 | tf_op jit(solution)/shard_map/ppermute | solution.py:372
  77.7 1.2 copy-start.1
  77.7 7.9 %copy-start.9 = (f32[288,128]{1,0:T(8,128)S(1)}, f32[288,128]{1,0:T(8,128)}, u32[]{:S(2)}) copy-start(f32[288,128]{1,0:T(8,128)} %get-tuple-element.39) | copy-start | bytes 442372
  79.0 138.8 %all-to-all-start.1 = ((f32[8,160,512]{2,1,0:T(8,128)}), f32[8,160,512]{2,1,0:T(8,128)S(1)}, u32[]{:S(2)}, u32[]{:S(2)}) async-start(f32[8,160,512]{2,1,0:T(8,128)} %get-tuple-element.27), calls=%async_computation.1 | async-start | bytes 5242880 | tf_op jit(solution)/shard_map/all_to_all | solution.py:375
  83.8 70.4 %collective-permute-start.9 = (f32[288,128]{1,0:T(8,128)}, f32[288,128]{1,0:T(8,128)S(1)}, u32[]{:S(2)}, u32[]{:S(2)}) collective-permute-start(f32[288,128]{1,0:T(8,128)} %get-tuple-element.38), channel_id=1, source_target_pairs={{0,6},{1,7},{2,4},{3,5},{4,2},{5,3},{6,0},{7,1},{8,14},{9,15},{10,... | collective-permute-start | bytes 442376 | tf_op jit(solution)/shard_map/ppermute | solution.py:372
  85.7 72.1 %collective-permute-start.10 = (f32[288,128]{1,0:T(8,128)S(1)}, f32[288,128]{1,0:T(8,128)S(1)}, u32[]{:S(2)}, u32[]{:S(2)}) collective-permute-start(f32[288,128]{1,0:T(8,128)S(1)} %copy-done.9), channel_id=1, source_target_pairs={{0,7},{1,6},{2,5},{3,4},{4,3},{5,2},{6,1},{7,0},{8,15},{9,14},{10,... | collective-permute-start | bytes 442376 | tf_op jit(solution)/shard_map/ppermute | solution.py:372
  158.4 27.3 %collective-permute-start.12 = (f32[8,288,128]{2,1,0:T(8,128)}, f32[8,288,128]{2,1,0:T(8,128)S(1)}, u32[]{:S(2)}, u32[]{:S(2)}) collective-permute-start(f32[8,288,128]{2,1,0:T(8,128)} %bitcast_dynamic-update-slice_fusion.refs_0_), channel_id=1, source_target_pairs={{0,16},{8,24},{16,0},{24,8},{1,17},{9,25},{17,1},{25,9},{2,18},{10... | collective-permute-start | bytes 3538952 | tf_op jit(solution)/shard_map/ppermute | solution.py:266
  159.7 27.0 %collective-permute-start.11 = (f32[8,288,128]{2,1,0:T(8,128)}, f32[8,288,128]{2,1,0:T(8,128)S(1)}, u32[]{:S(2)}, u32[]{:S(2)}) collective-permute-start(f32[8,288,128]{2,1,0:T(8,128)} %bitcast_dynamic-update-slice_fusion.refs_0_), channel_id=1, source_target_pairs={{0,8},{8,0},{16,24},{24,16},{1,9},{9,1},{17,25},{25,17},{2,10},{10... | collective-permute-start | bytes 3538952 | tf_op jit(solution)/shard_map/ppermute | solution.py:266
  185.7 2.9 %copy-start.7 = (f32[8,288,128]{2,1,0:T(8,128)}, f32[8,288,128]{2,1,0:T(8,128)S(1)}, u32[]{:S(2)}) copy-start(f32[8,288,128]{2,1,0:T(8,128)S(1)} %collective-permute-done.12.refs_2_) | copy-start | bytes 3538948
  185.7 13.7 %collective-permute-start.13 = (f32[4,288,128]{2,1,0:T(8,128)S(1)}, f32[4,288,128]{2,1,0:T(8,128)}, u32[]{:S(2)}, u32[]{:S(2)}) collective-permute-start(f32[4,288,128]{2,1,0:T(8,128)S(1)} %slice.26), channel_id=1, source_target_pairs={{0,8},{8,0},{16,24},{24,16},{1,9},{9,1},{17,25},{25,17},{2,10},{10... | collective-permute-start | bytes 1769480 | tf_op jit(solution)/shard_map/ppermute | solution.py:266
  188.5 13.6 %collective-permute-start.14 = (f32[4,288,128]{2,1,0:T(8,128)}, f32[4,288,128]{2,1,0:T(8,128)}, u32[]{:S(2)}, u32[]{:S(2)}) collective-permute-start(f32[4,288,128]{2,1,0:T(8,128)} %slice.27), channel_id=1, source_target_pairs={{0,16},{8,24},{16,0},{24,8},{1,17},{9,25},{17,1},{25,9},{2,18},{10... | collective-permute-start | bytes 1769480 | tf_op jit(solution)/shard_map/ppermute | solution.py:266
  217.8 1.5 copy-start
  (3 other events, 2.9 us)

commit v2 on v1

--- a/solution.py
+++ b/solution.py
@@ -371,7 +371,7 @@
     for k in reversed(range(1, strips)):
         came[k] = lax.ppermute(parts[k], "strip", [(i, i ^ k) for i in range(strips)])
     mine = jnp.stack(came[:: sources])
-    sci_b, got_a = lax.optimization_barrier((sci_b, got_a))
+    sci_b, got_a, mine = lax.optimization_barrier((sci_b, got_a, mine))
     got_b = lax.all_to_all(sci_b, "strip", split_axis=0, concat_axis=0, tiled=True)
     if sources > 1:
         got_a = jnp.sum(got_a.reshape((blocks, sources) + got_a.shape[1:]), axis=1)
@@ -379,7 +379,9 @@
 
     per_block = tile_cols // LANES
     if epochs == 4 and share == LANES:
-        near = [swap(mine, "epoch", b) for b in range(2)]
+        near = []
+        for b in range(2):
+            near.append(swap(mine, "epoch", b))
         cut = blocks // 2
         far_low = swap(near[1][:cut], "epoch", 0)
         far_high = swap(near[0][cut:], "epoch", 1)

time: 230 us -> 176 us (0.77)
  the two profiles are of different devices: /device:TPU:9 before, /device:TPU:0 now
where the time goes in v2:
time: 176 us
  waiting for transfers between devices  77.1 us (44%)
  Pallas kernels  48.6 us (28%)
  starting transfers between devices  35.7 us (20%)
  local copies, waits for them, and re-layouts  11.8 us (7%)
  other arithmetic  2.19 us (1%)
    ppermute x8, waiting for transfers between devices, swap(): return lax.ppermute(value, axis, [(i, i ^ 1 << bit) for i in range(count)])  66.8 us
    pallas_call x1, Pallas kernels, shards(): pl.pallas_call(functools.partial(warp_kernel, (epochs, nrow, share, order...  19.7 us
    pallas_call x1, Pallas kernels, shards(): matched = convolve(*arrays, psf_poly, toep_hi, toep_lo, band)  15.6 us
    ppermute x8, starting transfers between devices, swap(): return lax.ppermute(value, axis, [(i, i ^ 1 << bit) for i in range(count)])  11.9 us
    all_to_all x1, starting transfers between devices, shards(): lax.all_to_all(sci_b, 'strip', split_axis=0, concat_axis=0, tiled=True)  10.6 us
    ppermute x7, waiting for transfers between devices, shards(): lax.ppermute(parts[k], 'strip', [(i, i ^ k) for i in range(strips)])  10.3 us
    unnamed x23, local copies, waits for them, and re-layouts  10.2 us
    ppermute x7, starting transfers between devices, shards(): lax.ppermute(parts[k], 'strip', [(i, i ^ k) for i in range(strips)])  8.12 us
  transfers between devices with their start and end apart: 17, of which 10 were waited for; matrix products, arithmetic and copies ran while one was open for 5% of the time, Pallas kernels for 12%

profile of v2, /device:TPU:0, one launch (start us, length us, event | category | flops | bytes accessed | tf_op | source)
XLA Modules:
  0.0 175.5 jit_solution(11998932971515563131)
XLA Ops:
  0.0 19.7 %warp.1 = (f32[8,96,512]{2,1,0:T(8,128)}, f32[8,160,512]{2,1,0:T(8,128)}, f32[2,1032,128]{2,1,0:T(8,128)}, f32[2,1032,128]{2,1,0:T(8,128)}, f32[2,1032,128]{2,1,0:T(8,128)}, /*index=5*/f32[2,1032,128]{2,1,0:T(8,128)}) custom-call(s32[1,12]{1,0:T(1,128)} %kind_ref.1, s32[1,8,12]{2,1,0:T(8,128)} %heights_ref.1, f32[1,12]{1,0:T(1,128)} %invvar_ref.1, ...), custom_call_target="tpu_custom_call" | custom-call | flops 8000000000 | bytes 20000000 | tf_op jit(solution)/shard_map/warp/pallas_call | solution.py:295
  19.7 3.0 %collective-permute-start = (f32[2,1032,128]{2,1,0:T(8,128)}, f32[2,1032,128]{2,1,0:T(8,128)}, u32[]{:S(2)}, u32[]{:S(2)}) collective-permute-start(f32[2,1032,128]{2,1,0:T(8,128)} %get-tuple-element.28), channel_id=1, source_target_pairs={{0,8},{8,0},{16,24},{24,16},{1,9},{9,1},{17,25},{25,17},{2,10},{10... | collective-permute-start | bytes 3170312 | tf_op jit(solution)/shard_map/ppermute | solution.py:266
  24.2 5.0 %all-to-all-start = ((f32[8,96,512]{2,1,0:T(8,128)}), f32[8,96,512]{2,1,0:T(8,128)S(1)}, u32[]{:S(2)}, u32[]{:S(2)}) async-start(f32[8,96,512]{2,1,0:T(8,128)} %get-tuple-element.26), calls=%async_computation | async-start | bytes 3145728 | tf_op jit(solution)/shard_map/all_to_all | solution.py:321
  29.2 17.1 %collective-permute-done.refs_1_ = f32[2,1032,128]{2,1,0:T(8,128)} collective-permute-done((f32[2,1032,128]{2,1,0:T(8,128)}, f32[2,1032,128]{2,1,0:T(8,128)}, u32[]{:S(2)}, u32[]{:S(2)}) %collective-permute-start) | collective-permute-done | bytes 1056800 | tf_op jit(solution)/shard_map/ppermute | solution.py:266
  47.4 1.8 %collective-permute-start.1 = (f32[1,1032,128]{2,1,0:T(8,128)S(1)}, f32[1,1032,128]{2,1,0:T(8,128)S(1)}, u32[]{:S(2)}, u32[]{:S(2)}) collective-permute-start(f32[1,1032,128]{2,1,0:T(8,128)S(1)} %slice_add_fusion.1), channel_id=1, source_target_pairs={{0,16},{8,24},{16,0},{24,8},{1,17},{9,25},{17,1},{25,9},{2,18},{10... | collective-permute-start | bytes 1585160 | tf_op jit(solution)/shard_map/ppermute | solution.py:266
  50.3 1.6 collective-permute-start.3
  51.9 8.7 %collective-permute-done.1.refs_2_ = f32[1,1032,128]{2,1,0:T(8,128)S(1)} collective-permute-done((f32[1,1032,128]{2,1,0:T(8,128)S(1)}, f32[1,1032,128]{2,1,0:T(8,128)S(1)}, u32[]{:S(2)}, u32[]{:S(2)}) %collective-permute-start.1) | collective-permute-done | bytes 528416 | tf_op jit(solution)/shard_map/ppermute | solution.py:266
  60.6 2.4 %collective-permute-done.3.refs_5_ = f32[1,1032,128]{2,1,0:T(8,128)S(1)} collective-permute-done((f32[1,1032,128]{2,1,0:T(8,128)S(1)}, f32[1,1032,128]{2,1,0:T(8,128)S(1)}, u32[]{:S(2)}, u32[]{:S(2)}) %collective-permute-start.3) | collective-permute-done | bytes 528416 | tf_op jit(solution)/shard_map/ppermute | solution.py:266
  63.8 3.9 %template.1 = (f32[288,128]{1,0:T(8,128)}, f32[288,128]{1,0:T(8,128)}, f32[288,128]{1,0:T(8,128)}, f32[288,128]{1,0:T(8,128)}, f32[288,128]{1,0:T(8,128)}, /*ind...) custom-call(f32[2,1032,128]{2,1,0:T(8,128)} %get-tuple-element.27.refs_0_, ...), custom_call_target="tpu_custom_call" | custom-call | flops 2000000 | bytes 5000000 | tf_op jit(solution)/shard_map/template/pallas_call | solution.py:360
  67.6 1.7 collective-permute-start.5
  69.5 2.8 %collective-permute-start.7 = (f32[288,128]{1,0:T(8,128)}, f32[288,128]{1,0:T(8,128)S(1)}, u32[]{:S(2)}, u32[]{:S(2)}) collective-permute-start(f32[288,128]{1,0:T(8,128)} %get-tuple-element.35), channel_id=1, source_target_pairs={{0,4},{1,5},{2,6},{3,7},{4,0},{5,1},{6,2},{7,3},{8,12},{9,13},{10,... | collective-permute-start | bytes 442376 | tf_op jit(solution)/shard_map/ppermute | solution.py:372
  72.3 1.6 bitcast_dynamic-update-slice_fusion.7
  73.9 3.5 %collective-permute-start.9 = (f32[288,128]{1,0:T(8,128)}, f32[288,128]{1,0:T(8,128)S(1)}, u32[]{:S(2)}, u32[]{:S(2)}) collective-permute-start(f32[288,128]{1,0:T(8,128)} %get-tuple-element.37), channel_id=1, source_target_pairs={{0,6},{1,7},{2,4},{3,5},{4,2},{5,3},{6,0},{7,1},{8,14},{9,15},{10,... | collective-permute-start | bytes 442376 | tf_op jit(solution)/shard_map/ppermute | solution.py:372
  78.0 2.4 %collective-permute-done.5 = f32[288,128]{1,0:T(8,128)S(1)} collective-permute-done((f32[288,128]{1,0:T(8,128)}, f32[288,128]{1,0:T(8,128)S(1)}, u32[]{:S(2)}, u32[]{:S(2)}) %collective-permute-start.5) | collective-permute-done | bytes 147488 | tf_op jit(solution)/shard_map/ppermute | solution.py:372
  84.6 4.9 %collective-permute-done.9 = f32[288,128]{1,0:T(8,128)S(1)} collective-permute-done((f32[288,128]{1,0:T(8,128)}, f32[288,128]{1,0:T(8,128)S(1)}, u32[]{:S(2)}, u32[]{:S(2)}) %collective-permute-start.9) | collective-permute-done | bytes 147488 | tf_op jit(solution)/shard_map/ppermute | solution.py:372
  93.6 10.6 %all-to-all-start.1 = ((f32[8,160,512]{2,1,0:T(8,128)}), f32[8,160,512]{2,1,0:T(8,128)S(1)}, u32[]{:S(2)}, u32[]{:S(2)}) async-start(f32[8,160,512]{2,1,0:T(8,128)} %get-tuple-element.40), calls=%async_computation.1 | async-start | bytes 5242880 | tf_op jit(solution)/shard_map/all_to_all | solution.py:375
  106.2 26.6 %collective-permute-done.12.refs_2_ = f32[8,288,128]{2,1,0:T(8,128)S(1)} collective-permute-done((f32[8,288,128]{2,1,0:T(8,128)}, f32[8,288,128]{2,1,0:T(8,128)S(1)}, u32[]{:S(2)}, u32[]{:S(2)}) %collective-permute-start.12) | collective-permute-done | bytes 1179680 | tf_op jit(solution)/shard_map/ppermute | solution.py:266
  132.9 1.6 collective-permute-start.13
  136.9 2.4 %bands.1 = (bf16[256,256]{1,0:T(8,128)(2,1)}, bf16[256,256]{1,0:T(8,128)(2,1)}, bf16[2,256,160]{2,1,0:T(8,128)(2,1)}) custom-call(f32[2,2,31]{2,1,0:T(2,128)} %psf_ref.1), custom_call_target="tpu_custom_call" | custom-call | flops 10000000 | bytes 500000 | tf_op jit(solution)/shard_map/bands/pallas_call | solution.py:336
  139.3 8.7 %collective-permute-done.13.refs_3_ = f32[4,288,128]{2,1,0:T(8,128)} collective-permute-done((f32[4,288,128]{2,1,0:T(8,128)S(1)}, f32[4,288,128]{2,1,0:T(8,128)}, u32[]{:S(2)}, u32[]{:S(2)}) %collective-permute-start.13) | collective-permute-done | bytes 589856 | tf_op jit(solution)/shard_map/ppermute | solution.py:266
  147.9 3.4 %collective-permute-done.14.refs_4_ = f32[4,288,128]{2,1,0:T(8,128)} collective-permute-done((f32[4,288,128]{2,1,0:T(8,128)}, f32[4,288,128]{2,1,0:T(8,128)}, u32[]{:S(2)}, u32[]{:S(2)}) %collective-permute-start.14) | collective-permute-done | bytes 589856 | tf_op jit(solution)/shard_map/ppermute | solution.py:266
  151.3 15.6 %convolve.1.matched_ref = f32[256,4096]{1,0:T(8,128)} custom-call(f32[8,288,128]{2,1,0:T(8,128)} %bitcast_dynamic-update-slice_fusion.refs_0_, f32[8,288,128]{2,1,0:T(8,128)} %copy-done.7, f32[8,288,128]{2,1,0:T(8,128)} %copy-done.6, f32[4,288,128]{2,1,0:T(8,128)} %collective-permute-done.13.refs_3_, f32[4,288,128]{2,1,0:T(8,128)} %collective-permute-done.14.refs_4_, ...), custom_call_target="tpu_custom_call" | custom-call | flops 15000000512 | bytes 10000000 | tf_op jit(solution)/shard_map/convolve/pallas_call | solution.py:423
  167.0 1.5 copy-done
  168.5 7.0 %subtract.1 = f32[1,256,4096]{2,1,0:T(8,128)} custom-call(f32[8,96,512]{2,1,0:T(8,128)} %copy-done.1, f32[8,160,512]{2,1,0:T(8,128)} %copy-done, f32[256,4096]{1,0:T(8,128)} %convolve.1.matched_ref), custom_call_target="tpu_custom_call" | custom-call | flops 1000000 | bytes 12000000 | tf_op jit(solution)/shard_map/subtract/pallas_call | solution.py:424
  (43 shorter events, 17.9 us)
Async XLA Ops:
  19.7 26.6 %collective-permute-start = (f32[2,1032,128]{2,1,0:T(8,128)}, f32[2,1032,128]{2,1,0:T(8,128)}, u32[]{:S(2)}, u32[]{:S(2)}) collective-permute-start(f32[2,1032,128]{2,1,0:T(8,128)} %get-tuple-element.28), channel_id=1, source_target_pairs={{0,8},{8,0},{16,24},{24,16},{1,9},{9,1},{17,25},{25,17},{2,10},{10... | collective-permute-start | bytes 3170312 | tf_op jit(solution)/shard_map/ppermute | solution.py:266
  22.7 26.5 %collective-permute-start.2 = (f32[2,1032,128]{2,1,0:T(8,128)}, f32[2,1032,128]{2,1,0:T(8,128)}, u32[]{:S(2)}, u32[]{:S(2)}) collective-permute-start(f32[2,1032,128]{2,1,0:T(8,128)} %get-tuple-element.30), channel_id=1, source_target_pairs={{0,16},{8,24},{16,0},{24,8},{1,17},{9,25},{17,1},{25,9},{2,18},{10... | collective-permute-start | bytes 3170312 | tf_op jit(solution)/shard_map/ppermute | solution.py:266
  24.2 22.1 %copy-start.2 = (f32[2,1032,128]{2,1,0:T(8,128)S(1)}, f32[2,1032,128]{2,1,0:T(8,128)}, u32[]{:S(2)}) copy-start(f32[2,1032,128]{2,1,0:T(8,128)} %get-tuple-element.27.refs_0_) | copy-start | bytes 3170308
  24.2 68.2 %all-to-all-start = ((f32[8,96,512]{2,1,0:T(8,128)}), f32[8,96,512]{2,1,0:T(8,128)S(1)}, u32[]{:S(2)}, u32[]{:S(2)}) async-start(f32[8,96,512]{2,1,0:T(8,128)} %get-tuple-element.26), calls=%async_computation | async-start | bytes 3145728 | tf_op jit(solution)/shard_map/all_to_all | solution.py:321
  29.2 20.0 %copy-start.3 = (f32[2,1032,128]{2,1,0:T(8,128)S(1)}, f32[2,1032,128]{2,1,0:T(8,128)}, u32[]{:S(2)}) copy-start(f32[2,1032,128]{2,1,0:T(8,128)} %get-tuple-element.29.refs_3_) | copy-start | bytes 3170308
  47.4 13.2 %collective-permute-start.1 = (f32[1,1032,128]{2,1,0:T(8,128)S(1)}, f32[1,1032,128]{2,1,0:T(8,128)S(1)}, u32[]{:S(2)}, u32[]{:S(2)}) collective-permute-start(f32[1,1032,128]{2,1,0:T(8,128)S(1)} %slice_add_fusion.1), channel_id=1, source_target_pairs={{0,16},{8,24},{16,0},{24,8},{1,17},{9,25},{17,1},{25,9},{2,18},{10... | collective-permute-start | bytes 1585160 | tf_op jit(solution)/shard_map/ppermute | solution.py:266
  50.3 12.6 %collective-permute-start.3 = (f32[1,1032,128]{2,1,0:T(8,128)S(1)}, f32[1,1032,128]{2,1,0:T(8,128)S(1)}, u32[]{:S(2)}, u32[]{:S(2)}) collective-permute-start(f32[1,1032,128]{2,1,0:T(8,128)S(1)} %slice_add_fusion), channel_id=1, source_target_pairs={{0,8},{8,0},{16,24},{24,16},{1,9},{9,1},{17,25},{25,17},{2,10},{10... | collective-permute-start | bytes 1585160 | tf_op jit(solution)/shard_map/ppermute | solution.py:266
  60.6 2.4 %copy-start.4 = (f32[1,1032,128]{2,1,0:T(8,128)}, f32[1,1032,128]{2,1,0:T(8,128)S(1)}, u32[]{:S(2)}) copy-start(f32[1,1032,128]{2,1,0:T(8,128)S(1)} %collective-permute-done.1.refs_2_) | copy-start | bytes 1585156
  67.6 6.2 %collective-permute-start.4 = (f32[288,128]{1,0:T(8,128)}, f32[288,128]{1,0:T(8,128)S(1)}, u32[]{:S(2)}, u32[]{:S(2)}) collective-permute-start(f32[288,128]{1,0:T(8,128)} %get-tuple-element.32), channel_id=1, source_target_pairs={{0,1},{1,0},{2,3},{3,2},{4,5},{5,4},{6,7},{7,6},{8,9},{9,8},{10,11... | collective-permute-start | bytes 442376 | tf_op jit(solution)/shard_map/ppermute | solution.py:372
  67.6 12.8 %collective-permute-start.5 = (f32[288,128]{1,0:T(8,128)}, f32[288,128]{1,0:T(8,128)S(1)}, u32[]{:S(2)}, u32[]{:S(2)}) collective-permute-start(f32[288,128]{1,0:T(8,128)} %get-tuple-element.33), channel_id=1, source_target_pairs={{0,2},{1,3},{2,0},{3,1},{4,6},{5,7},{6,4},{7,5},{8,10},{9,11},{10,... | collective-permute-start | bytes 442376 | tf_op jit(solution)/shard_map/ppermute | solution.py:372
  69.3 13.3 %collective-permute-start.6 = (f32[288,128]{1,0:T(8,128)}, f32[288,128]{1,0:T(8,128)S(1)}, u32[]{:S(2)}, u32[]{:S(2)}) collective-permute-start(f32[288,128]{1,0:T(8,128)} %get-tuple-element.34), channel_id=1, source_target_pairs={{0,3},{1,2},{2,1},{3,0},{4,7},{5,6},{6,5},{7,4},{8,11},{9,10},{10,... | collective-permute-start | bytes 442376 | tf_op jit(solution)/shard_map/ppermute | solution.py:372
  69.5 13.8 %collective-permute-start.7 = (f32[288,128]{1,0:T(8,128)}, f32[288,128]{1,0:T(8,128)S(1)}, u32[]{:S(2)}, u32[]{:S(2)}) collective-permute-start(f32[288,128]{1,0:T(8,128)} %get-tuple-element.35), channel_id=1, source_target_pairs={{0,4},{1,5},{2,6},{3,7},{4,0},{5,1},{6,2},{7,3},{8,12},{9,13},{10,... | collective-permute-start | bytes 442376 | tf_op jit(solution)/shard_map/ppermute | solution.py:372
  72.3 11.7 %collective-permute-start.8 = (f32[288,128]{1,0:T(8,128)}, f32[288,128]{1,0:T(8,128)S(1)}, u32[]{:S(2)}, u32[]{:S(2)}) collective-permute-start(f32[288,128]{1,0:T(8,128)} %get-tuple-element.36), channel_id=1, source_target_pairs={{0,5},{1,4},{2,7},{3,6},{4,1},{5,0},{6,3},{7,2},{8,13},{9,12},{10,... | collective-permute-start | bytes 442376 | tf_op jit(solution)/shard_map/ppermute | solution.py:372
  73.9 15.7 %collective-permute-start.9 = (f32[288,128]{1,0:T(8,128)}, f32[288,128]{1,0:T(8,128)S(1)}, u32[]{:S(2)}, u32[]{:S(2)}) collective-permute-start(f32[288,128]{1,0:T(8,128)} %get-tuple-element.37), channel_id=1, source_target_pairs={{0,6},{1,7},{2,4},{3,5},{4,2},{5,3},{6,0},{7,1},{8,14},{9,15},{10,... | collective-permute-start | bytes 442376 | tf_op jit(solution)/shard_map/ppermute | solution.py:372
  80.5 11.2 %collective-permute-start.10 = (f32[288,128]{1,0:T(8,128)}, f32[288,128]{1,0:T(8,128)S(1)}, u32[]{:S(2)}, u32[]{:S(2)}) collective-permute-start(f32[288,128]{1,0:T(8,128)} %get-tuple-element.38), channel_id=1, source_target_pairs={{0,7},{1,6},{2,5},{3,4},{4,3},{5,2},{6,1},{7,0},{8,15},{9,14},{10,... | collective-permute-start | bytes 442376 | tf_op jit(solution)/shard_map/ppermute | solution.py:372
  92.4 1.2 copy-start.1
  93.6 73.3 %all-to-all-start.1 = ((f32[8,160,512]{2,1,0:T(8,128)}), f32[8,160,512]{2,1,0:T(8,128)S(1)}, u32[]{:S(2)}, u32[]{:S(2)}) async-start(f32[8,160,512]{2,1,0:T(8,128)} %get-tuple-element.40), calls=%async_computation.1 | async-start | bytes 5242880 | tf_op jit(solution)/shard_map/all_to_all | solution.py:375
  104.3 28.6 %collective-permute-start.12 = (f32[8,288,128]{2,1,0:T(8,128)}, f32[8,288,128]{2,1,0:T(8,128)S(1)}, u32[]{:S(2)}, u32[]{:S(2)}) collective-permute-start(f32[8,288,128]{2,1,0:T(8,128)} %bitcast_dynamic-update-slice_fusion.refs_0_), channel_id=1, source_target_pairs={{0,16},{8,24},{16,0},{24,8},{1,17},{9,25},{17,1},{25,9},{2,18},{10... | collective-permute-start | bytes 3538952 | tf_op jit(solution)/shard_map/ppermute | solution.py:266
  104.9 29.6 %collective-permute-start.11 = (f32[8,288,128]{2,1,0:T(8,128)}, f32[8,288,128]{2,1,0:T(8,128)S(1)}, u32[]{:S(2)}, u32[]{:S(2)}) collective-permute-start(f32[8,288,128]{2,1,0:T(8,128)} %bitcast_dynamic-update-slice_fusion.refs_0_), channel_id=1, source_target_pairs={{0,8},{8,0},{16,24},{24,16},{1,9},{9,1},{17,25},{25,17},{2,10},{10... | collective-permute-start | bytes 3538952 | tf_op jit(solution)/shard_map/ppermute | solution.py:266
  132.8 3.6 %copy-start.6 = (f32[8,288,128]{2,1,0:T(8,128)}, f32[8,288,128]{2,1,0:T(8,128)S(1)}, u32[]{:S(2)}) copy-start(f32[8,288,128]{2,1,0:T(8,128)S(1)} %collective-permute-done.12.refs_2_) | copy-start | bytes 3538948
  132.9 15.1 %collective-permute-start.13 = (f32[4,288,128]{2,1,0:T(8,128)S(1)}, f32[4,288,128]{2,1,0:T(8,128)}, u32[]{:S(2)}, u32[]{:S(2)}) collective-permute-start(f32[4,288,128]{2,1,0:T(8,128)S(1)} %slice.26), channel_id=1, source_target_pairs={{0,8},{8,0},{16,24},{24,16},{1,9},{9,1},{17,25},{25,17},{2,10},{10... | collective-permute-start | bytes 1769480 | tf_op jit(solution)/shard_map/ppermute | solution.py:266
  134.5 1.1 copy-start.7
  136.4 14.9 %collective-permute-start.14 = (f32[4,288,128]{2,1,0:T(8,128)}, f32[4,288,128]{2,1,0:T(8,128)}, u32[]{:S(2)}, u32[]{:S(2)}) collective-permute-start(f32[4,288,128]{2,1,0:T(8,128)} %slice.27), channel_id=1, source_target_pairs={{0,16},{8,24},{16,0},{24,8},{1,17},{9,25},{17,1},{25,9},{2,18},{10... | collective-permute-start | bytes 1769480 | tf_op jit(solution)/shard_map/ppermute | solution.py:266
  167.0 1.5 copy-start
  (1 other events, 0.8 us)

commit v3 on v2

--- a/solution.py
+++ b/solution.py
@@ -52,31 +52,55 @@
 def warp_kernel(
     geom, kind_ref, heights_ref, invvar_ref, raw_ref, rmat_ref, cmat_ref,
     sci_a, sci_b, keep_a, send_a, keep_b, send_b,
-    sci_s, num_s, wt_s, chi_s, clo_s, top_s, sems,
+    sci_s, num_s, wt_s, rmat_s, cmat_s, chi_s, clo_s, top_s, ready_s, fetch_sems, sems, wt_sems,
 ):
     epochs, nrow, share, orders, tiles = geom
     step = pl.program_id(0)
     together, tile_rows, tile_cols = raw_ref.shape
+    last = pl.num_programs(0) - 1
     per_col = heights_ref.shape[2]
     span = tile_rows + 8
     me = lax.axis_index("epoch")
     first_tile = lax.axis_index("strip") * tiles
     block = lax.div(first_tile, per_col)
     offset_in = lax.rem(first_tile, per_col)
+    kinds = cmat_ref.shape[0]
+    strips, rows_a, _ = sci_a.shape
+    rows_dev = rows_a + sci_b.shape[1]
+    nhalf = nrow // 2
+    outs = (keep_a, send_a), (keep_b, send_b)
+
+    def fetches(k):
+        return [
+            pltpu.make_async_copy(cmat_ref.at[k], cmat_s.at[k], fetch_sems.at[k, 0]),
+            pltpu.make_async_copy(rmat_ref.at[k], rmat_s.at[k], fetch_sems.at[k, 1]),
+        ]
+
+    def strip_copies(s):
+        base = s * rows_dev
+        part = base // nhalf
+        pairs = [
+            (sci_s.at[pl.ds(base, rows_a)], sci_a.at[s]),
+            (sci_s.at[pl.ds(base + rows_a, rows_dev - rows_a)], sci_b.at[s]),
+        ]
+        for slots, out in zip(slot_order(epochs, orders[part]), outs[part]):
+            for place, j in enumerate(slots):
+                pairs.append(
+                    (num_s.at[j, pl.ds(base, rows_dev)], out.at[place, pl.ds(base - part * nhalf, rows_dev)])
+                )
+        return [pltpu.make_async_copy(a, b, sems.at[s, n]) for n, (a, b) in enumerate(pairs)]
 
     @pl.when(step == 0)
     def _():
         top_s[0] = lax.fori_loop(
             0, offset_in, lambda i, total: total + heights_ref[0, block, i], jnp.int32(0)
         )
-
-        def divide(i, carry):
-            k = lax.div(i, 4)
-            here = pl.ds(pl.multiple_of(lax.rem(i, 4) * (tile_cols // 4), tile_cols // 4), tile_cols // 4)
-            chi_s[k, here, :], clo_s[k, here, :] = split(cmat_ref[k, here, :])
-            return carry
-
-        lax.fori_loop(0, 4 * cmat_ref.shape[0], divide, 0)
+        top_s[1] = 0
+        first = kind_ref[0, 0]
+        for i in range(kinds):
+            ready_s[i] = 0
+            for copy in fetches(lax.rem(first + i, kinds)):
+                copy.start()
         if tiles != per_col:
             sci_s[...] = jnp.zeros_like(sci_s)
             num_s[...] = jnp.zeros_like(num_s)
@@ -91,9 +115,25 @@
         across = dot3(split(raw_ref[i]), (chi_s[kind], clo_s[kind]), trans_b=True)
         live = lax.broadcasted_iota(jnp.int32, (tile_rows, tile_rows), 1) < height
         rows = jnp.concatenate(
-            [jnp.where(live, rmat_ref[kind], 0.0), jnp.zeros((8, tile_rows), F32)], axis=0
+            [jnp.where(live, rmat_s[kind], 0.0), jnp.zeros((8, tile_rows), F32)], axis=0
         )
         return t, height, start, off, dot3(split(pltpu.roll(rows, off, 0)), split(across))
+
+    for i in range(together):
+        kind = kind_ref[0, step * together + i]
+
+        @pl.when(ready_s[kind] == 0)
+        def _():
+            for copy in fetches(kind):
+                copy.wait()
+            ready_s[kind] = 1
+
+            def divide(n, carry):
+                here = pl.ds(pl.multiple_of(n * (tile_cols // 8), tile_cols // 8), tile_cols // 8)
+                chi_s[kind, here, :], clo_s[kind, here, :] = split(cmat_s[kind, here, :])
+                return carry
+
+            lax.fori_loop(0, 8, divide, 0)
 
     top = top_s[0]
     results = []
@@ -101,6 +141,7 @@
         results.append((top, warped(i, top)))
         top = top + results[-1][1][1]
     top_s[0] = top
+    after = top
 
     for top, (t, height, start, off, placed) in results:
         weight = invvar_ref[0, t]
@@ -118,23 +159,41 @@
         )
         wt_s[...] = jnp.where((flat >= top) & (flat < top + height), weight, wt_s[...])
 
-    @pl.when(step == pl.num_programs(0) - 1)
+    before = top_s[1]
+    final = jnp.where(step == last, nrow, jnp.minimum(lax.div(after, 8) * 8, nrow - span))
+    top_s[1] = final
+    for s in range(strips):
+        end = (s + 1) * rows_dev
+
+        @pl.when((before < end) & (end <= final))
+        def _():
+            for copy in strip_copies(s):
+                copy.start()
+
+    @pl.when(step == last)
     def _():
-        strips, rows_a, _ = sci_a.shape
-        rows_b = sci_b.shape[1]
-        pairs = []
-        nhalf = nrow // 2
         whalf = wt_s.shape[0] // 2
-        for i, (order, outs) in enumerate(zip(orders, ((keep_a, send_a), (keep_b, send_b)))):
-            for slots, out in zip(slot_order(epochs, order), outs):
-                for place, j in enumerate(slots):
-                    pairs.append((num_s.at[j, pl.ds(i * nhalf, nhalf)], out.at[place, pl.ds(0, nhalf)]))
-                    pairs.append((wt_s.at[pl.ds(i * whalf, whalf)], out.at[place, pl.ds(nhalf, whalf)]))
+        copies = []
+        for part, order in enumerate(orders):
+            for slots, out in zip(slot_order(epochs, order), outs[part]):
+                for place in range(len(slots)):
+                    copies.append(
+                        pltpu.make_async_copy(
+                            wt_s.at[pl.ds(part * whalf, whalf)],
+                            out.at[place, pl.ds(nhalf, whalf)],
+                            wt_sems.at[len(copies)],
+                        )
+                    )
+        start_and_wait(copies)
         for s in range(strips):
-            base = s * (rows_a + rows_b)
-            pairs.append((sci_s.at[pl.ds(base, rows_a)], sci_a.at[s]))
-            pairs.append((sci_s.at[pl.ds(base + rows_a, rows_b)], sci_b.at[s]))
-        start_and_wait([pltpu.make_async_copy(a, b, sems.at[n]) for n, (a, b) in enumerate(pairs)])
+            for copy in strip_copies(s):
+                copy.wait()
+        for k in range(kinds):
+
+            @pl.when(ready_s[k] == 0)
+            def _():
+                for copy in fetches(k):
+                    copy.wait()
 
 
 def template_kernel(terms, *refs):
@@ -181,30 +240,48 @@
 
 
 def match_kernel(geom, *refs):
-    pieces, nrow, ncol = geom
-    count = len(pieces)
+    slots, nrow, ncol = geom
+    count = max(len(slots), 1) + (len(slots) > 1)
     tile_refs = refs[:count]
-    poly_ref, toep_hi, toep_lo, band_ref, out_ref, pad_s, row_s, sems = refs[count:]
+    poly_ref, toep_hi, toep_lo, band_ref, sci_ref, out_ref, pad_s, row_s, sems = refs[count:]
     step = pl.program_id(0)
+    blocks = pl.num_programs(0)
     tiles = pad_s.shape[0] - 2
     rows_dev = pad_s.shape[1] - 2 * HALO
     me = lax.axis_index("epoch")
     strip = lax.axis_index("strip")
     per_step = out_ref.shape[1] // LANES
 
+    def bring(b):
+        if not slots:
+            for i in range(per_step):
+                place = b * per_step + i
+                pltpu.make_async_copy(tile_refs[0].at[place], pad_s.at[1 + place], sems.at[b, i]).start()
+            return
+        at = jnp.bitwise_xor(strip, b)
+        for n, slot in enumerate(slots):
+            target = pad_s.at[1 + b * per_step + jnp.bitwise_xor(me, slot)]
+            if n < len(slots) - 1:
+                pltpu.make_async_copy(tile_refs[n].at[at], target, sems.at[b, n]).start()
+                continue
+            cut = tile_refs[n].shape[0]
+
+            @pl.when(at < cut)
+            def _():
+                pltpu.make_async_copy(tile_refs[n].at[at], target, sems.at[b, n]).start()
+
+            @pl.when(at >= cut)
+            def _():
+                pltpu.make_async_copy(tile_refs[n + 1].at[at - cut], target, sems.at[b, n]).start()
+
+    def await_block(b):
+        for i in range(per_step):
+            pltpu.make_async_copy(tile_refs[0].at[0], pad_s.at[1], sems.at[b, i]).wait()
+
     @pl.when(step == 0)
     def _():
-        copies = []
-        for ref, (slot, first) in zip(tile_refs, pieces):
-            for i in range(ref.shape[0]):
-                if slot is None:
-                    place = i
-                else:
-                    block = jnp.bitwise_xor(strip, first + i)
-                    place = block * per_step + jnp.bitwise_xor(me, slot)
-                copies.append(pltpu.make_async_copy(ref.at[i], pad_s.at[1 + place], sems.at[len(copies)]))
-        for copy in copies:
-            copy.start()
+        for b in range(tiles // per_step):
+            bring(b)
         pad_s[0] = jnp.zeros(pad_s.shape[1:], F32)
         pad_s[tiles + 1] = jnp.zeros(pad_s.shape[1:], F32)
         shape = (rows_dev, LANES)
@@ -214,8 +291,11 @@
             p = [poly_ref[me, k, i] for i in range(6)]
             row_s[k, 0] = p[0] + u * (p[1] + p[3] * u)
             row_s[k, 1] = p[2] + p[4] * u
-        for copy in copies:
-            copy.wait()
+        await_block(0)
+
+    @pl.when(step < blocks - 1)
+    def _():
+        await_block(step + 1)
 
     lane = lax.broadcasted_iota(jnp.int32, pad_s.shape[1:], 1)
     base = step * per_step
@@ -249,16 +329,23 @@
                 two = jnp.concatenate([row_s[k, 1, place, :]] * 2, axis=1)
                 coeff = one + v * (two + poly_ref[me, k, 5] * v)
                 total = total + coeff * done
-            out_ref[pl.ds(part * LANES, LANES), pl.ds(pair * width, width)] = total
-
-
-def subtract_kernel(sci_a, sci_b, matched_ref, out_ref):
-    b = pl.program_id(0)
-    rows, width = sci_a.shape[1:]
-    columns = pl.ds(pl.multiple_of(b * width, width), width)
-    out_ref[0, pl.ds(0, rows), :] = sci_a[b] - matched_ref[pl.ds(0, rows), columns]
-    rest = pl.ds(rows, sci_b.shape[1])
-    out_ref[0, rest, :] = sci_b[b] - matched_ref[rest, columns]
+            columns = pl.ds(pair * width, width)
+            ready = min(max(sci_ref.shape[1] - part * LANES, 0), LANES)
+            if ready:
+                here = pl.ds(part * LANES, ready)
+                out_ref[here, columns] = sci_ref[0, here, columns] - total[:ready]
+            if ready < LANES:
+                out_ref[pl.ds(part * LANES + ready, LANES - ready), columns] = total[ready:]
+
+
+def subtract_kernel(sci_ref, matched_ref, out_ref):
+    i = pl.program_id(0)
+    blocks, _, width = sci_ref.shape
+    rows = out_ref.shape[1]
+    for b in range(blocks):
+        columns = pl.ds(b * width, width)
+        science = sci_ref[b, pl.ds(pl.multiple_of(i * rows, rows), rows), :]
+        out_ref[0, :, columns] = science - matched_ref[0, :, columns]
 
 
 def swap(value, axis, bit):
@@ -291,7 +378,6 @@
     ]
     send_shape = jax.ShapeDtypeStruct((epochs // 2, long_half, share), F32)
     together = 2 if tiles % 2 == 0 else 1
-    once = pl.Buffered(1)
     sci_a, sci_b, keep_a, send_a, keep_b, send_b = pl.pallas_call(
         functools.partial(warp_kernel, (epochs, nrow, share, orders, tiles)),
         grid=(tiles // together,),
@@ -300,8 +386,8 @@
             smem,
             smem,
             pl.BlockSpec((together, tile_rows, tile_cols), lambda t: (t, 0, 0)),
-            pl.BlockSpec((kinds, tile_rows, tile_rows), lambda t: (0, 0, 0), pipeline_mode=once),
-            pl.BlockSpec((kinds, tile_cols, tile_cols), lambda t: (0, 0, 0), pipeline_mode=once),
+            hbm,
+            hbm,
         ],
         out_specs=[hbm] * 6,
         out_shape=sci_shapes + [send_shape] * 4,
@@ -309,10 +395,15 @@
             pltpu.VMEM((nrow, tile_cols), F32),
             pltpu.VMEM((epochs, nrow, share), F32),
             pltpu.VMEM((wrows, share), F32),
+            pltpu.VMEM((kinds, tile_rows, tile_rows), F32),
+            pltpu.VMEM((kinds, tile_cols, tile_cols), F32),
             pltpu.VMEM((kinds, tile_cols, tile_cols), BF16),
             pltpu.VMEM((kinds, tile_cols, tile_cols), BF16),
-            pltpu.SMEM((1,), jnp.int32),
-            pltpu.SemaphoreType.DMA((2 * strips + 4 * epochs,)),
+            pltpu.SMEM((2,), jnp.int32),
+            pltpu.SMEM((kinds,), jnp.int32),
+            pltpu.SemaphoreType.DMA((kinds, 2)),
+            pltpu.SemaphoreType.DMA((strips, 2 + epochs)),
+            pltpu.SemaphoreType.DMA((2 * epochs,)),
         ],
         name="warp",
         cost_estimate=pl.CostEstimate(flops=8_000_000_000, bytes_accessed=20_000_000, transcendentals=0),
@@ -386,7 +477,7 @@
         far_low = swap(near[1][:cut], "epoch", 0)
         far_high = swap(near[0][cut:], "epoch", 1)
         arrays = [mine, near[0], near[1], far_low, far_high]
-        pieces = [(0, 0), (1, 0), (2, 0), (3, 0), (3, cut)]
+        held = (0, 1, 2, 3)
     else:
         slots = [mine]
         for b in range(bits):
@@ -397,11 +488,11 @@
         every = jnp.take(every, jnp.bitwise_xor(jnp.arange(blocks), home), axis=1)
         flat = jnp.transpose(every, (1, 2, 0, 3)).reshape(blocks, long, per_block, LANES)
         arrays = [jnp.transpose(flat, (0, 2, 1, 3)).reshape(blocks * per_block, long, LANES)]
-        pieces = [(None, 0)]
+        held = ()
 
     const = lambda b: (0, 0)
     convolve = pl.pallas_call(
-        functools.partial(match_kernel, (pieces, nrow, ncol)),
+        functools.partial(match_kernel, (held, nrow, ncol)),
         grid=(blocks,),
         in_specs=[hbm] * len(arrays)
         + [
@@ -409,27 +500,33 @@
             pl.BlockSpec(toep_hi.shape, const),
             pl.BlockSpec(toep_lo.shape, const),
             pl.BlockSpec(band.shape, lambda b: (0, 0, 0)),
+            pl.BlockSpec((1,) + got_a.shape[1:], lambda b: (b, 0, 0)),
         ],
         out_specs=pl.BlockSpec((ROWS_DEV, tile_cols), lambda b: (0, b)),
         out_shape=jax.ShapeDtypeStruct((ROWS_DEV, ncol), F32),
         scratch_shapes=[
             pltpu.VMEM((blocks * per_block + 2, long, LANES), F32),
             pltpu.VMEM((2, 2, ROWS_DEV, LANES), F32),
-            pltpu.SemaphoreType.DMA((sum(a.shape[0] for a in arrays),)),
+            pltpu.SemaphoreType.DMA((blocks, per_block)),
         ],
         name="convolve",
+        compiler_params=pltpu.CompilerParams(vmem_limit_bytes=32 << 20),
         cost_estimate=pl.CostEstimate(flops=15_000_000_000, bytes_accessed=10_000_000, transcendentals=0),
     )
-    matched = convolve(*arrays, psf_poly, toep_hi, toep_lo, band)
+    matched = convolve(*arrays, psf_poly, toep_hi, toep_lo, band, got_a)
+    unit = ROWS_DEV // 8
+    rest = pl.BlockSpec((1, unit, ncol), lambda i: (0, FIRST_PART + i, 0))
     return pl.pallas_call(
         subtract_kernel,
-        grid=(blocks,),
-        in_specs=[vmem] * 3,
-        out_specs=pl.BlockSpec((1, ROWS_DEV, tile_cols), lambda b: (0, 0, b)),
+        grid=(8 - FIRST_PART,),
+        in_specs=[vmem, rest],
+        out_specs=rest,
         out_shape=jax.ShapeDtypeStruct((1, ROWS_DEV, ncol), F32),
+        input_output_aliases={1: 0},
         name="subtract",
-        cost_estimate=pl.CostEstimate(flops=1_000_000, bytes_accessed=12_000_000, transcendentals=0),
-    )(got_a, got_b, matched)
+        compiler_params=pltpu.CompilerParams(vmem_limit_bytes=16 << 20),
+        cost_estimate=pl.CostEstimate(flops=1_000_000, bytes_accessed=6_000_000, transcendentals=0),
+    )(pltpu.with_memory_space_constraint(got_b, pltpu.VMEM), matched[None])
 
 
 def solution(mesh):

time: 176 us -> 180 us (1.023)
  local copies, waits for them, and re-layouts: 11.8 us -> 17.8 us
  starting transfers between devices: 35.7 us -> 32 us
  waiting for transfers between devices: 77.1 us -> 80.7 us
    unnamed x23 -> x35, local copies, waits for them, and re-layouts: 10.2 us -> 15.3 us
    ppermute x7, waiting for transfers between devices: 10.3 us -> 12.5 us  [shards(): lax.ppermute(parts[k], 'strip', [(i, i ^ k) for i in range(strips)])]
    all_to_all x1, starting transfers between devices: 10.6 us -> 8.49 us  [shards(): lax.all_to_all(sci_b, 'strip', split_axis=0, concat_axis=0, tiled=True)]
  transfers between devices with their start and end apart: 17 -> 17, of which waited for: 10 -> 9; matrix products, arithmetic and copies ran while one was open for 5% -> 6% of each run, Pallas kernels for 12% -> 13%
where the time goes in v3:
time: 180 us
  waiting for transfers between devices  80.7 us (45%)
  Pallas kernels  47.1 us (26%)
  starting transfers between devices  32 us (18%)
  local copies, waits for them, and re-layouts  17.8 us (10%)
  other arithmetic  2.19 us (1%)
    ppermute x8, waiting for transfers between devices, swap(): return lax.ppermute(value, axis, [(i, i ^ 1 << bit) for i in range(count)])  68.2 us
    pallas_call x1, Pallas kernels, shards(): pl.pallas_call(functools.partial(warp_kernel, (epochs, nrow, share, order...  19.3 us
    pallas_call x1, Pallas kernels, shards(): matched = convolve(*arrays, psf_poly, toep_hi, toep_lo, band, got_a)  16.7 us
    unnamed x35, local copies, waits for them, and re-layouts  15.3 us
    ppermute x7, waiting for transfers between devices, shards(): lax.ppermute(parts[k], 'strip', [(i, i ^ k) for i in range(strips)])  12.5 us
    ppermute x8, starting transfers between devices, swap(): return lax.ppermute(value, axis, [(i, i ^ 1 << bit) for i in range(count)])  10.6 us
    all_to_all x1, starting transfers between devices, shards(): lax.all_to_all(sci_b, 'strip', split_axis=0, concat_axis=0, tiled=True)  8.49 us
    ppermute x7, starting transfers between devices, shards(): lax.ppermute(parts[k], 'strip', [(i, i ^ k) for i in range(strips)])  7.52 us
  transfers between devices with their start and end apart: 17, of which 9 were waited for; matrix products, arithmetic and copies ran while one was open for 6% of the time, Pallas kernels for 13%

profile of v3, /device:TPU:0, one launch (start us, length us, event | category | flops | bytes accessed | tf_op | source)
XLA Modules:
  0.0 179.8 jit_solution(18431372930332523111)
XLA Ops:
  0.0 19.3 %warp.1 = (f32[8,96,512]{2,1,0:T(8,128)}, f32[8,160,512]{2,1,0:T(8,128)}, f32[2,1032,128]{2,1,0:T(8,128)}, f32[2,1032,128]{2,1,0:T(8,128)}, f32[2,1032,128]{2,1,0:T(8,128)}, /*index=5*/f32[2,1032,128]{2,1,0:T(8,128)}) custom-call(s32[1,12]{1,0:T(1,128)} %kind_ref.1, s32[1,8,12]{2,1,0:T(8,128)} %heights_ref.1, f32[1,12]{1,0:T(1,128)} %invvar_ref.1, ...), custom_call_target="tpu_custom_call" | custom-call | flops 8000000000 | bytes 20000000 | tf_op jit(solution)/shard_map/warp/pallas_call | solution.py:381
  19.4 2.6 %collective-permute-start = (f32[2,1032,128]{2,1,0:T(8,128)}, f32[2,1032,128]{2,1,0:T(8,128)}, u32[]{:S(2)}, u32[]{:S(2)}) collective-permute-start(f32[2,1032,128]{2,1,0:T(8,128)} %get-tuple-element.28), channel_id=1, source_target_pairs={{0,8},{8,0},{16,24},{24,16},{1,9},{9,1},{17,25},{25,17},{2,10},{10... | collective-permute-start | bytes 3170312 | tf_op jit(solution)/shard_map/ppermute | solution.py:353
  22.0 1.5 collective-permute-start.2
  23.4 5.4 %all-to-all-start = ((f32[8,96,512]{2,1,0:T(8,128)}), f32[8,96,512]{2,1,0:T(8,128)S(1)}, u32[]{:S(2)}, u32[]{:S(2)}) async-start(f32[8,96,512]{2,1,0:T(8,128)} %get-tuple-element.26), calls=%async_computation | async-start | bytes 3145728 | tf_op jit(solution)/shard_map/all_to_all | solution.py:412
  28.9 17.3 %collective-permute-done.refs_1_ = f32[2,1032,128]{2,1,0:T(8,128)} collective-permute-done((f32[2,1032,128]{2,1,0:T(8,128)}, f32[2,1032,128]{2,1,0:T(8,128)}, u32[]{:S(2)}, u32[]{:S(2)}) %collective-permute-start) | collective-permute-done | bytes 1056800 | tf_op jit(solution)/shard_map/ppermute | solution.py:353
  47.3 2.0 %collective-permute-start.1 = (f32[1,1032,128]{2,1,0:T(8,128)S(1)}, f32[1,1032,128]{2,1,0:T(8,128)S(1)}, u32[]{:S(2)}, u32[]{:S(2)}) collective-permute-start(f32[1,1032,128]{2,1,0:T(8,128)S(1)} %slice_add_fusion.1), channel_id=1, source_target_pairs={{0,16},{8,24},{16,0},{24,8},{1,17},{9,25},{17,1},{25,9},{2,18},{10... | collective-permute-start | bytes 1585160 | tf_op jit(solution)/shard_map/ppermute | solution.py:353
  50.4 1.6 collective-permute-start.3
  51.9 9.1 %collective-permute-done.1.refs_2_ = f32[1,1032,128]{2,1,0:T(8,128)S(1)} collective-permute-done((f32[1,1032,128]{2,1,0:T(8,128)S(1)}, f32[1,1032,128]{2,1,0:T(8,128)S(1)}, u32[]{:S(2)}, u32[]{:S(2)}) %collective-permute-start.1) | collective-permute-done | bytes 528416 | tf_op jit(solution)/shard_map/ppermute | solution.py:353
  61.0 2.5 %collective-permute-done.3.refs_5_ = f32[1,1032,128]{2,1,0:T(8,128)S(1)} collective-permute-done((f32[1,1032,128]{2,1,0:T(8,128)S(1)}, f32[1,1032,128]{2,1,0:T(8,128)S(1)}, u32[]{:S(2)}, u32[]{:S(2)}) %collective-permute-start.3) | collective-permute-done | bytes 528416 | tf_op jit(solution)/shard_map/ppermute | solution.py:353
  64.4 3.9 %template.1 = (f32[288,128]{1,0:T(8,128)}, f32[288,128]{1,0:T(8,128)}, f32[288,128]{1,0:T(8,128)}, f32[288,128]{1,0:T(8,128)}, f32[288,128]{1,0:T(8,128)}, /*ind...) custom-call(f32[2,1032,128]{2,1,0:T(8,128)} %get-tuple-element.27.refs_0_, ...), custom_call_target="tpu_custom_call" | custom-call | flops 2000000 | bytes 5000000 | tf_op jit(solution)/shard_map/template/pallas_call | solution.py:451
  70.2 1.9 %collective-permute-start.7 = (f32[288,128]{1,0:T(8,128)}, f32[288,128]{1,0:T(8,128)S(1)}, u32[]{:S(2)}, u32[]{:S(2)}) collective-permute-start(f32[288,128]{1,0:T(8,128)} %get-tuple-element.35), channel_id=1, source_target_pairs={{0,4},{1,5},{2,6},{3,7},{4,0},{5,1},{6,2},{7,3},{8,12},{9,13},{10,... | collective-permute-start | bytes 442376 | tf_op jit(solution)/shard_map/ppermute | solution.py:463
  72.8 1.6 bitcast_dynamic-update-slice_fusion.7
  74.4 3.1 %collective-permute-start.9 = (f32[288,128]{1,0:T(8,128)}, f32[288,128]{1,0:T(8,128)S(1)}, u32[]{:S(2)}, u32[]{:S(2)}) collective-permute-start(f32[288,128]{1,0:T(8,128)} %get-tuple-element.37), channel_id=1, source_target_pairs={{0,6},{1,7},{2,4},{3,5},{4,2},{5,3},{6,0},{7,1},{8,14},{9,15},{10,... | collective-permute-start | bytes 442376 | tf_op jit(solution)/shard_map/ppermute | solution.py:463
  78.1 2.3 %collective-permute-done.5 = f32[288,128]{1,0:T(8,128)S(1)} collective-permute-done((f32[288,128]{1,0:T(8,128)}, f32[288,128]{1,0:T(8,128)S(1)}, u32[]{:S(2)}, u32[]{:S(2)}) %collective-permute-start.5) | collective-permute-done | bytes 147488 | tf_op jit(solution)/shard_map/ppermute | solution.py:463
  81.1 1.4 collective-permute-done.6
  83.9 8.7 %collective-permute-done.8 = f32[288,128]{1,0:T(8,128)S(1)} collective-permute-done((f32[288,128]{1,0:T(8,128)}, f32[288,128]{1,0:T(8,128)S(1)}, u32[]{:S(2)}, u32[]{:S(2)}) %collective-permute-start.8) | collective-permute-done | bytes 147488 | tf_op jit(solution)/shard_map/ppermute | solution.py:463
  95.8 8.5 %all-to-all-start.1 = ((f32[8,160,512]{2,1,0:T(8,128)}), f32[8,160,512]{2,1,0:T(8,128)S(1)}, u32[]{:S(2)}, u32[]{:S(2)}) async-start(f32[8,160,512]{2,1,0:T(8,128)} %get-tuple-element.39), calls=%async_computation.1 | async-start | bytes 5242880 | tf_op jit(solution)/shard_map/all_to_all | solution.py:466
  105.8 27.1 %collective-permute-done.12.refs_2_ = f32[8,288,128]{2,1,0:T(8,128)S(1)} collective-permute-done((f32[8,288,128]{2,1,0:T(8,128)}, f32[8,288,128]{2,1,0:T(8,128)S(1)}, u32[]{:S(2)}, u32[]{:S(2)}) %collective-permute-start.12) | collective-permute-done | bytes 1179680 | tf_op jit(solution)/shard_map/ppermute | solution.py:353
  137.1 2.4 %bands.1 = (bf16[256,256]{1,0:T(8,128)(2,1)}, bf16[256,256]{1,0:T(8,128)(2,1)}, bf16[2,256,160]{2,1,0:T(8,128)(2,1)}) custom-call(f32[2,2,31]{2,1,0:T(2,128)} %psf_ref.1), custom_call_target="tpu_custom_call" | custom-call | flops 10000000 | bytes 500000 | tf_op jit(solution)/shard_map/bands/pallas_call | solution.py:427
  139.5 9.3 %collective-permute-done.13.refs_3_ = f32[4,288,128]{2,1,0:T(8,128)S(1)} collective-permute-done((f32[4,288,128]{2,1,0:T(8,128)}, f32[4,288,128]{2,1,0:T(8,128)S(1)}, u32[]{:S(2)}, u32[]{:S(2)}) %collective-permute-start.13) | collective-permute-done | bytes 589856 | tf_op jit(solution)/shard_map/ppermute | solution.py:353
  148.8 2.9 %collective-permute-done.14.refs_4_ = f32[4,288,128]{2,1,0:T(8,128)} collective-permute-done((f32[4,288,128]{2,1,0:T(8,128)}, f32[4,288,128]{2,1,0:T(8,128)}, u32[]{:S(2)}, u32[]{:S(2)}) %collective-permute-start.14) | collective-permute-done | bytes 589856 | tf_op jit(solution)/shard_map/ppermute | solution.py:353
  151.6 1.4 copy-done.1
  158.3 16.7 %convolve.1 = f32[256,4096]{1,0:T(8,128)} custom-call(f32[8,288,128]{2,1,0:T(8,128)} %bitcast_dynamic-update-slice_fusion.refs_0_, f32[8,288,128]{2,1,0:T(8,128)S(1)} %copy-done.5, f32[8,288,128]{2,1,0:T(8,128)S(1)} %copy-done.3, f32[4,288,128]{2,1,0:T(8,128)S(1)} %collective-permute-done.13.refs_3_, f32[4,288,128]{2,1,0:T(8,128)} %collective-permute-done.14.refs_4_, ...), custom_call_target="tpu_custom_call" | custom-call | flops 15000000512 | bytes 10000000 | tf_op jit(solution)/shard_map/convolve/pallas_call | solution.py:516
  175.1 4.7 %subtract.1 = f32[1,256,4096]{2,1,0:T(8,128)} custom-call(f32[8,160,512]{2,1,0:T(8,128)S(1)} %all-to-all-done.1.sci_ref, f32[1,256,4096]{2,1,0:T(8,128)} %bitcast.18), custom_call_target="tpu_custom_call", output_to_operand_aliasing={{}: (1, {})} | custom-call | flops 1000000 | bytes 6000000 | tf_op jit(solution)/shard_map/subtract/pallas_call | solution.py:519
  (55 shorter events, 22.5 us)
Async XLA Ops:
  19.4 26.8 %collective-permute-start = (f32[2,1032,128]{2,1,0:T(8,128)}, f32[2,1032,128]{2,1,0:T(8,128)}, u32[]{:S(2)}, u32[]{:S(2)}) collective-permute-start(f32[2,1032,128]{2,1,0:T(8,128)} %get-tuple-element.28), channel_id=1, source_target_pairs={{0,8},{8,0},{16,24},{24,16},{1,9},{9,1},{17,25},{25,17},{2,10},{10... | collective-permute-start | bytes 3170312 | tf_op jit(solution)/shard_map/ppermute | solution.py:353
  22.0 27.3 %collective-permute-start.2 = (f32[2,1032,128]{2,1,0:T(8,128)}, f32[2,1032,128]{2,1,0:T(8,128)}, u32[]{:S(2)}, u32[]{:S(2)}) collective-permute-start(f32[2,1032,128]{2,1,0:T(8,128)} %get-tuple-element.30), channel_id=1, source_target_pairs={{0,16},{8,24},{16,0},{24,8},{1,17},{9,25},{17,1},{25,9},{2,18},{10... | collective-permute-start | bytes 3170312 | tf_op jit(solution)/shard_map/ppermute | solution.py:353
  23.4 22.7 %copy-start.10 = (f32[2,1032,128]{2,1,0:T(8,128)S(1)}, f32[2,1032,128]{2,1,0:T(8,128)}, u32[]{:S(2)}) copy-start(f32[2,1032,128]{2,1,0:T(8,128)} %get-tuple-element.27.refs_0_) | copy-start | bytes 3170308
  23.4 71.2 %all-to-all-start = ((f32[8,96,512]{2,1,0:T(8,128)}), f32[8,96,512]{2,1,0:T(8,128)S(1)}, u32[]{:S(2)}, u32[]{:S(2)}) async-start(f32[8,96,512]{2,1,0:T(8,128)} %get-tuple-element.26), calls=%async_computation | async-start | bytes 3145728 | tf_op jit(solution)/shard_map/all_to_all | solution.py:412
  28.9 20.4 %copy-start.11 = (f32[2,1032,128]{2,1,0:T(8,128)S(1)}, f32[2,1032,128]{2,1,0:T(8,128)}, u32[]{:S(2)}) copy-start(f32[2,1032,128]{2,1,0:T(8,128)} %get-tuple-element.29.refs_3_) | copy-start | bytes 3170308
  47.3 13.8 %collective-permute-start.1 = (f32[1,1032,128]{2,1,0:T(8,128)S(1)}, f32[1,1032,128]{2,1,0:T(8,128)S(1)}, u32[]{:S(2)}, u32[]{:S(2)}) collective-permute-start(f32[1,1032,128]{2,1,0:T(8,128)S(1)} %slice_add_fusion.1), channel_id=1, source_target_pairs={{0,16},{8,24},{16,0},{24,8},{1,17},{9,25},{17,1},{25,9},{2,18},{10... | collective-permute-start | bytes 1585160 | tf_op jit(solution)/shard_map/ppermute | solution.py:353
  50.4 13.2 %collective-permute-start.3 = (f32[1,1032,128]{2,1,0:T(8,128)S(1)}, f32[1,1032,128]{2,1,0:T(8,128)S(1)}, u32[]{:S(2)}, u32[]{:S(2)}) collective-permute-start(f32[1,1032,128]{2,1,0:T(8,128)S(1)} %slice_add_fusion), channel_id=1, source_target_pairs={{0,8},{8,0},{16,24},{24,16},{1,9},{9,1},{17,25},{25,17},{2,10},{10... | collective-permute-start | bytes 1585160 | tf_op jit(solution)/shard_map/ppermute | solution.py:353
  61.0 2.5 %copy-start.12 = (f32[1,1032,128]{2,1,0:T(8,128)}, f32[1,1032,128]{2,1,0:T(8,128)S(1)}, u32[]{:S(2)}) copy-start(f32[1,1032,128]{2,1,0:T(8,128)S(1)} %collective-permute-done.1.refs_2_) | copy-start | bytes 1585156
  68.3 6.0 %collective-permute-start.4 = (f32[288,128]{1,0:T(8,128)}, f32[288,128]{1,0:T(8,128)S(1)}, u32[]{:S(2)}, u32[]{:S(2)}) collective-permute-start(f32[288,128]{1,0:T(8,128)} %get-tuple-element.32), channel_id=1, source_target_pairs={{0,1},{1,0},{2,3},{3,2},{4,5},{5,4},{6,7},{7,6},{8,9},{9,8},{10,11... | collective-permute-start | bytes 442376 | tf_op jit(solution)/shard_map/ppermute | solution.py:463
  68.4 12.1 %collective-permute-start.5 = (f32[288,128]{1,0:T(8,128)}, f32[288,128]{1,0:T(8,128)S(1)}, u32[]{:S(2)}, u32[]{:S(2)}) collective-permute-start(f32[288,128]{1,0:T(8,128)} %get-tuple-element.33), channel_id=1, source_target_pairs={{0,2},{1,3},{2,0},{3,1},{4,6},{5,7},{6,4},{7,5},{8,10},{9,11},{10,... | collective-permute-start | bytes 442376 | tf_op jit(solution)/shard_map/ppermute | solution.py:463
  68.8 13.8 %collective-permute-start.6 = (f32[288,128]{1,0:T(8,128)}, f32[288,128]{1,0:T(8,128)S(1)}, u32[]{:S(2)}, u32[]{:S(2)}) collective-permute-start(f32[288,128]{1,0:T(8,128)} %get-tuple-element.34), channel_id=1, source_target_pairs={{0,3},{1,2},{2,1},{3,0},{4,7},{5,6},{6,5},{7,4},{8,11},{9,10},{10,... | collective-permute-start | bytes 442376 | tf_op jit(solution)/shard_map/ppermute | solution.py:463
  70.2 13.0 %collective-permute-start.7 = (f32[288,128]{1,0:T(8,128)}, f32[288,128]{1,0:T(8,128)S(1)}, u32[]{:S(2)}, u32[]{:S(2)}) collective-permute-start(f32[288,128]{1,0:T(8,128)} %get-tuple-element.35), channel_id=1, source_target_pairs={{0,4},{1,5},{2,6},{3,7},{4,0},{5,1},{6,2},{7,3},{8,12},{9,13},{10,... | collective-permute-start | bytes 442376 | tf_op jit(solution)/shard_map/ppermute | solution.py:463
  72.1 20.5 %collective-permute-start.8 = (f32[288,128]{1,0:T(8,128)}, f32[288,128]{1,0:T(8,128)S(1)}, u32[]{:S(2)}, u32[]{:S(2)}) collective-permute-start(f32[288,128]{1,0:T(8,128)} %get-tuple-element.36), channel_id=1, source_target_pairs={{0,5},{1,4},{2,7},{3,6},{4,1},{5,0},{6,3},{7,2},{8,13},{9,12},{10,... | collective-permute-start | bytes 442376 | tf_op jit(solution)/shard_map/ppermute | solution.py:463
  74.4 18.9 %collective-permute-start.9 = (f32[288,128]{1,0:T(8,128)}, f32[288,128]{1,0:T(8,128)S(1)}, u32[]{:S(2)}, u32[]{:S(2)}) collective-permute-start(f32[288,128]{1,0:T(8,128)} %get-tuple-element.37), channel_id=1, source_target_pairs={{0,6},{1,7},{2,4},{3,5},{4,2},{5,3},{6,0},{7,1},{8,14},{9,15},{10,... | collective-permute-start | bytes 442376 | tf_op jit(solution)/shard_map/ppermute | solution.py:463
  80.4 13.5 %collective-permute-start.10 = (f32[288,128]{1,0:T(8,128)}, f32[288,128]{1,0:T(8,128)S(1)}, u32[]{:S(2)}, u32[]{:S(2)}) collective-permute-start(f32[288,128]{1,0:T(8,128)} %get-tuple-element.38), channel_id=1, source_target_pairs={{0,7},{1,6},{2,5},{3,4},{4,3},{5,2},{6,1},{7,0},{8,15},{9,14},{10,... | collective-permute-start | bytes 442376 | tf_op jit(solution)/shard_map/ppermute | solution.py:463
  95.8 79.3 %all-to-all-start.1 = ((f32[8,160,512]{2,1,0:T(8,128)}), f32[8,160,512]{2,1,0:T(8,128)S(1)}, u32[]{:S(2)}, u32[]{:S(2)}) async-start(f32[8,160,512]{2,1,0:T(8,128)} %get-tuple-element.39), calls=%async_computation.1 | async-start | bytes 5242880 | tf_op jit(solution)/shard_map/all_to_all | solution.py:466
  104.3 47.4 %copy-start.6 = (f32[4,2,6]{2,1,0:T(2,128)S(1)}, f32[4,2,6]{2,1,0:T(2,128)}, u32[]{:S(2)}) copy-start(f32[4,2,6]{2,1,0:T(2,128)} %refs_5_.1) | copy-start | bytes 580
  104.3 28.6 %collective-permute-start.12 = (f32[8,288,128]{2,1,0:T(8,128)}, f32[8,288,128]{2,1,0:T(8,128)S(1)}, u32[]{:S(2)}, u32[]{:S(2)}) collective-permute-start(f32[8,288,128]{2,1,0:T(8,128)} %bitcast_dynamic-update-slice_fusion.refs_0_), channel_id=1, source_target_pairs={{0,16},{8,24},{16,0},{24,8},{1,17},{9,25},{17,1},{25,9},{2,18},{10... | collective-permute-start | bytes 3538952 | tf_op jit(solution)/shard_map/ppermute | solution.py:353
  105.3 29.5 %collective-permute-start.11 = (f32[8,288,128]{2,1,0:T(8,128)}, f32[8,288,128]{2,1,0:T(8,128)S(1)}, u32[]{:S(2)}, u32[]{:S(2)}) collective-permute-start(f32[8,288,128]{2,1,0:T(8,128)} %bitcast_dynamic-update-slice_fusion.refs_0_), channel_id=1, source_target_pairs={{0,8},{8,0},{16,24},{24,16},{1,9},{9,1},{17,25},{25,17},{2,10},{10... | collective-permute-start | bytes 3538952 | tf_op jit(solution)/shard_map/ppermute | solution.py:353
  132.9 2.9 %copy-start.2 = (f32[8,288,128]{2,1,0:T(8,128)}, f32[8,288,128]{2,1,0:T(8,128)S(1)}, u32[]{:S(2)}) copy-start(f32[8,288,128]{2,1,0:T(8,128)S(1)} %collective-permute-done.12.refs_2_) | copy-start | bytes 3538948
  133.8 15.0 %collective-permute-start.13 = (f32[4,288,128]{2,1,0:T(8,128)}, f32[4,288,128]{2,1,0:T(8,128)S(1)}, u32[]{:S(2)}, u32[]{:S(2)}) collective-permute-start(f32[4,288,128]{2,1,0:T(8,128)} %slice.26), channel_id=1, source_target_pairs={{0,8},{8,0},{16,24},{24,16},{1,9},{9,1},{17,25},{25,17},{2,10},{10... | collective-permute-start | bytes 1769480 | tf_op jit(solution)/shard_map/ppermute | solution.py:353
  136.8 14.8 %collective-permute-start.14 = (f32[4,288,128]{2,1,0:T(8,128)}, f32[4,288,128]{2,1,0:T(8,128)}, u32[]{:S(2)}, u32[]{:S(2)}) collective-permute-start(f32[4,288,128]{2,1,0:T(8,128)} %slice.27), channel_id=1, source_target_pairs={{0,16},{8,24},{16,0},{24,8},{1,17},{9,25},{17,1},{25,9},{2,18},{10... | collective-permute-start | bytes 1769480 | tf_op jit(solution)/shard_map/ppermute | solution.py:353
  151.6 1.4 copy-start.1
  153.0 1.3 copy-start.3
  (7 other events, 7.0 us)

commit v4 on v3

--- a/solution.py
+++ b/solution.py
@@ -10,7 +10,7 @@
 
 ROWS_DEV = 256
 HALO = 16
-FIRST_PART = 3
+EDGE = 96
 LANES = 128
 F32 = jnp.float32
 BF16 = jnp.bfloat16
@@ -66,8 +66,11 @@
     offset_in = lax.rem(first_tile, per_col)
     kinds = cmat_ref.shape[0]
     strips, rows_a, _ = sci_a.shape
-    rows_dev = rows_a + sci_b.shape[1]
+    rows_b = sci_b.shape[1]
+    edge = rows_b // 2
+    rows_dev = rows_a + rows_b
     nhalf = nrow // 2
+    bhalf = strips // 2 * rows_b
     outs = (keep_a, send_a), (keep_b, send_b)
 
     def fetches(k):
@@ -79,15 +82,14 @@
     def strip_copies(s):
         base = s * rows_dev
         part = base // nhalf
-        pairs = [
-            (sci_s.at[pl.ds(base, rows_a)], sci_a.at[s]),
-            (sci_s.at[pl.ds(base + rows_a, rows_dev - rows_a)], sci_b.at[s]),
-        ]
-        for slots, out in zip(slot_order(epochs, orders[part]), outs[part]):
-            for place, j in enumerate(slots):
-                pairs.append(
-                    (num_s.at[j, pl.ds(base, rows_dev)], out.at[place, pl.ds(base - part * nhalf, rows_dev)])
-                )
+        pairs = [(sci_s.at[pl.ds(base + edge, rows_a)], sci_a.at[s])]
+        for i in range(2):
+            source = pl.ds(base + i * (rows_dev - edge), edge)
+            pairs.append((sci_s.at[source], sci_b.at[s, pl.ds(i * edge, edge)]))
+            target = pl.ds((s - part * (strips // 2)) * rows_b + i * edge, edge)
+            for slots, out in zip(slot_order(epochs, orders[part]), outs[part]):
+                for place, j in enumerate(slots):
+                    pairs.append((num_s.at[j, source], out.at[place, target]))
         return [pltpu.make_async_copy(a, b, sems.at[s, n]) for n, (a, b) in enumerate(pairs)]
 
     @pl.when(step == 0)
@@ -180,7 +182,7 @@
                     copies.append(
                         pltpu.make_async_copy(
                             wt_s.at[pl.ds(part * whalf, whalf)],
-                            out.at[place, pl.ds(nhalf, whalf)],
+                            out.at[place, pl.ds(bhalf, whalf)],
                             wt_sems.at[len(copies)],
                         )
                     )
@@ -196,30 +198,105 @@
                     copy.wait()
 
 
+def added(refs, place):
+    return functools.reduce(lambda a, b: a + b, [ref[0, place, :] for ref in refs])
+
+
+def upright(row, width):
+    return jnp.transpose(jnp.broadcast_to(row, (width, width)))
+
+
 def template_kernel(terms, *refs):
     term_refs, out_refs, pad_s = refs[: 2 * terms], refs[2 * terms : -1], refs[-1]
     strips = len(out_refs)
     long, share = out_refs[0].shape
-    rows_dev = long - 2 * HALO
-    nrow = strips * rows_dev
-    nhalf = nrow // 2
-    whalf = nhalf // share
-    edge = jnp.zeros((HALO, share), F32)
-    pad_s[pl.ds(0, HALO), :] = edge
-    pad_s[pl.ds(HALO + nrow, HALO), :] = edge
+    rows_b = long - 2 * HALO
+    edge = rows_b // 2
+    half = strips // 2
+    total = strips * rows_b
+    blank = jnp.zeros((HALO, share), F32)
+    pad_s[pl.ds(0, HALO), :] = blank
+    pad_s[pl.ds(HALO + total, HALO), :] = blank
+    per_strip = ROWS_DEV // share
     for part in range(2):
         own = term_refs[part * terms : (part + 1) * terms]
-        add = lambda place: functools.reduce(lambda a, b: a + b, [ref[0, place, :] for ref in own])
-        weights = add(pl.ds(nhalf, whalf))
-        for i in range(whalf):
-            below = jnp.transpose(jnp.broadcast_to(weights[i : i + 1, :], (share, share)))
-            pad_s[pl.ds(HALO + part * nhalf + i * share, share), :] = add(pl.ds(i * share, share)) / below
+        weights = added(own, pl.ds(half * rows_b, half * per_strip))
+        for s in range(half):
+            below = jnp.concatenate(
+                [upright(weights[s * per_strip + i : s * per_strip + i + 1, :], share) for i in range(per_strip)],
+                axis=0,
+            )
+            for i in range(2):
+                first = s * rows_b + i * edge
+                under = below[i * (ROWS_DEV - edge) : i * (ROWS_DEV - edge) + edge]
+                pad_s[pl.ds(HALO + part * half * rows_b + first, edge), :] = added(own, pl.ds(first, edge)) / under
     for k in range(strips):
         strip = jnp.bitwise_xor(lax.axis_index("strip"), k)
-        out_refs[k][...] = pad_s[pl.ds(pl.multiple_of(strip * rows_dev, rows_dev), long), :]
-
-
-def bands_kernel(psf_ref, toep_hi, toep_lo, band_ref):
+        out_refs[k][...] = pad_s[pl.ds(pl.multiple_of(strip * rows_b, 8), long), :]
+
+
+def weigh_kernel(geom, heights_ref, invvar_ref, sci_ref, *refs):
+    epochs, orders, share = geom
+    outs, num_s = refs[:4], refs[4]
+    blocks, rows_a, _ = sci_ref.shape
+    per_col = heights_ref.shape[2]
+    tiles = invvar_ref.shape[1]
+    sources = per_col // tiles
+    me, strip = lax.axis_index("epoch"), lax.axis_index("strip")
+    first = strip * ROWS_DEV + EDGE
+    half = blocks // 2
+    long = outs[0].shape[1]
+    flat_shape = (long - half * rows_a, share)
+    flat = lax.broadcasted_iota(jnp.int32, flat_shape, 0) * share + lax.broadcasted_iota(jnp.int32, flat_shape, 1)
+    row = lax.broadcasted_iota(jnp.int32, (rows_a, share), 0) + first
+    for part in range(2):
+        wide = jnp.zeros(flat_shape, F32)
+        for b in range(half):
+            block = part * half + b
+            sky = flat - b * rows_a
+            mine = (sky >= 0) & (sky < rows_a)
+            sky = sky + first
+            weight = jnp.zeros((rows_a, share), F32)
+            top = jnp.int32(0)
+            for t in range(per_col):
+                height = heights_ref[0, block, t]
+                value = invvar_ref[jnp.bitwise_xor(block * sources + t // tiles, strip), t % tiles]
+                weight = jnp.where((row >= top) & (row < top + height), value, weight)
+                wide = jnp.where(mine & (sky >= top) & (sky < top + height), value, wide)
+                top = top + height
+            for q in range(epochs):
+                piece = sci_ref[block, :, pl.ds(q * share, share)]
+                num_s[jnp.bitwise_xor(me, q), pl.ds(b * rows_a, rows_a), :] = weight * piece
+        for j in range(epochs):
+            num_s[j, pl.ds(half * rows_a, flat_shape[0]), :] = wide
+        for slots, out in zip(slot_order(epochs, orders[part]), outs[2 * part : 2 * part + 2]):
+            for place, j in enumerate(slots):
+                out[place] = num_s[j]
+
+
+def middle_kernel(terms, *refs):
+    term_refs, outer_refs, out_ref = refs[: 2 * terms], refs[2 * terms : -1], refs[-1]
+    blocks, long, share = out_ref.shape
+    above = EDGE + HALO
+    rows_a = long - 2 * above
+    home = lax.div(lax.axis_index("strip"), lax.axis_size("strip") // blocks)
+    half = blocks // 2
+    for k, ref in enumerate(outer_refs):
+        out_ref[k, pl.ds(0, above), :] = ref[pl.ds(0, above), :]
+        out_ref[k, pl.ds(above + rows_a, above), :] = ref[pl.ds(above, above), :]
+    for part in range(2):
+        own = term_refs[part * terms : (part + 1) * terms]
+        weights = added(own, pl.ds(half * rows_a, own[0].shape[1] - half * rows_a))
+        together = share // rows_a
+        for n in range(half // together):
+            below = upright(weights[n : n + 1, :], share)
+            for i in range(together):
+                b = n * together + i
+                value = added(own, pl.ds(b * rows_a, rows_a)) / below[i * rows_a : (i + 1) * rows_a]
+                out_ref[jnp.bitwise_xor(home, part * half + b), pl.ds(above, rows_a), :] = value
+
+
+def bands_kernel(psf_ref, _, toep_hi, toep_lo, band_ref):
     basis, _, ksize = psf_ref.shape
     margin = ksize // 2
     for k in range(basis):
@@ -330,12 +407,16 @@
                 coeff = one + v * (two + poly_ref[me, k, 5] * v)
                 total = total + coeff * done
             columns = pl.ds(pair * width, width)
-            ready = min(max(sci_ref.shape[1] - part * LANES, 0), LANES)
-            if ready:
-                here = pl.ds(part * LANES, ready)
-                out_ref[here, columns] = sci_ref[0, here, columns] - total[:ready]
-            if ready < LANES:
-                out_ref[pl.ds(part * LANES + ready, LANES - ready), columns] = total[ready:]
+            low = min(max(EDGE - part * LANES, 0), LANES)
+            high = min(max(rows_dev - EDGE - part * LANES, 0), LANES)
+            for begin, end, final in ((0, low, False), (low, high, True), (high, LANES, False)):
+                if begin == end:
+                    continue
+                piece = total[begin:end]
+                if final:
+                    own = pl.ds(part * LANES + begin - EDGE, end - begin)
+                    piece = sci_ref[0, own, columns] - piece
+                out_ref[pl.ds(part * LANES + begin, end - begin), columns] = piece
 
 
 def subtract_kernel(sci_ref, matched_ref, out_ref):
@@ -364,18 +445,16 @@
     share = tile_cols // epochs
     bits = epochs.bit_length() - 1
     orders = (tuple(range(bits)), tuple(reversed(range(bits))))
-    nhalf = nrow // 2
     wrows = nrow // share
-    long_half = nhalf + wrows // 2
+    rows_b = 2 * EDGE
+    rows_a = ROWS_DEV - rows_b
+    long_half = strips // 2 * rows_b + wrows // 2
     smem = pl.BlockSpec(memory_space=pltpu.SMEM)
     hbm = pl.BlockSpec(memory_space=pl.ANY)
     vmem = pl.BlockSpec(memory_space=pltpu.VMEM)
     kinds = col_interp.shape[0]
 
-    first_rows = ROWS_DEV * FIRST_PART // 8
-    sci_shapes = [
-        jax.ShapeDtypeStruct((strips, rows, tile_cols), F32) for rows in (first_rows, ROWS_DEV - first_rows)
-    ]
+    sci_shapes = [jax.ShapeDtypeStruct((strips, rows, tile_cols), F32) for rows in (rows_a, rows_b)]
     send_shape = jax.ShapeDtypeStruct((epochs // 2, long_half, share), F32)
     together = 2 if tiles % 2 == 0 else 1
     sci_a, sci_b, keep_a, send_a, keep_b, send_b = pl.pallas_call(
@@ -402,7 +481,7 @@
             pltpu.SMEM((2,), jnp.int32),
             pltpu.SMEM((kinds,), jnp.int32),
             pltpu.SemaphoreType.DMA((kinds, 2)),
-            pltpu.SemaphoreType.DMA((strips, 2 + epochs)),
+            pltpu.SemaphoreType.DMA((strips, 3 + 2 * epochs)),
             pltpu.SemaphoreType.DMA((2 * epochs,)),
         ],
         name="warp",
@@ -410,11 +489,14 @@
     )(tile_kind, tile_heights, tile_invvar, raw_tiles[0], row_interp, col_interp)
 
     got_a = lax.all_to_all(sci_a, "strip", split_axis=0, concat_axis=0, tiled=True)
+    invvars = tile_invvar
+    for bit in range(strips.bit_length() - 1):
+        invvars = jnp.concatenate([invvars, swap(invvars, "strip", bit)], axis=0)
 
     basis, _, _ = psf_profiles.shape
     build_bands = pl.pallas_call(
         bands_kernel,
-        in_specs=[smem],
+        in_specs=[smem, smem],
         out_specs=[vmem] * 3,
         out_shape=[
             jax.ShapeDtypeStruct((2 * LANES, 2 * LANES), BF16),
@@ -424,18 +506,21 @@
         name="bands",
         cost_estimate=pl.CostEstimate(flops=10_000_000, bytes_accessed=500_000, transcendentals=0),
     )
-    toep_hi, toep_lo, band = build_bands(psf_profiles)
-
-    terms = [[keep_a], [keep_b]]
-    sends = [send_a, send_b]
-    for i in range(bits):
-        for part in range(2):
-            terms[part].append(swap(sends[part], "epoch", orders[part][i]))
-        left = epochs >> (i + 1)
-        if left > 1:
-            sends = [
-                functools.reduce(lambda a, b: a + b, [t[left // 2 : left] for t in own]) for own in terms
-            ]
+    toep_hi, toep_lo, band = build_bands(psf_profiles, invvars)
+
+    def reduced(keeps, sends):
+        terms = [[keep] for keep in keeps]
+        for i in range(bits):
+            for part in range(2):
+                terms[part].append(swap(sends[part], "epoch", orders[part][i]))
+            left = epochs >> (i + 1)
+            if left > 1:
+                sends = [
+                    functools.reduce(lambda a, b: a + b, [t[left // 2 : left] for t in own]) for own in terms
+                ]
+        return terms
+
+    terms = reduced([keep_a, keep_b], [send_a, send_b])
     if sources > 1:
         fixed = []
         for own in terms:
@@ -448,12 +533,13 @@
         terms = fixed
 
     long = ROWS_DEV + 2 * HALO
+    long_b = rows_b + 2 * HALO
     parts = pl.pallas_call(
         functools.partial(template_kernel, len(terms[0])),
         in_specs=[vmem] * (2 * len(terms[0])),
         out_specs=[vmem] * strips,
-        out_shape=[jax.ShapeDtypeStruct((long, share), F32)] * strips,
-        scratch_shapes=[pltpu.VMEM((nrow + 2 * HALO, share), F32)],
+        out_shape=[jax.ShapeDtypeStruct((long_b, share), F32)] * strips,
+        scratch_shapes=[pltpu.VMEM((strips * rows_b + 2 * HALO, share), F32)],
         name="template",
         cost_estimate=pl.CostEstimate(flops=2_000_000, bytes_accessed=5_000_000, transcendentals=0),
     )(*terms[0], *terms[1])
@@ -461,11 +547,35 @@
     came[0] = parts[0]
     for k in reversed(range(1, strips)):
         came[k] = lax.ppermute(parts[k], "strip", [(i, i ^ k) for i in range(strips)])
-    mine = jnp.stack(came[:: sources])
+    side_a = got_a
+    if sources > 1:
+        side_a = jnp.sum(got_a.reshape((blocks, sources) + got_a.shape[1:]), axis=1)
+    long_a = blocks // 2 * rows_a + 8 * pl.cdiv(blocks // 2 * rows_a, 8 * share)
+    weighted_shape = jax.ShapeDtypeStruct((epochs // 2, long_a, share), F32)
+    weigh = pl.pallas_call(
+        functools.partial(weigh_kernel, (epochs, orders, share)),
+        in_specs=[smem, smem, vmem],
+        out_specs=[vmem] * 4,
+        out_shape=[weighted_shape] * 4,
+        scratch_shapes=[pltpu.VMEM((epochs, long_a, share), F32)],
+        name="weigh",
+        cost_estimate=pl.CostEstimate(flops=2_000_000, bytes_accessed=2_500_000, transcendentals=0),
+    )
+    weighted = weigh(tile_heights, invvars, side_a)
+    middle_terms = reduced(weighted[0::2], weighted[1::2])
+    outer = came[::sources]
+    mine = pl.pallas_call(
+        functools.partial(middle_kernel, len(middle_terms[0])),
+        in_specs=[vmem] * (2 * len(middle_terms[0]) + blocks),
+        out_specs=vmem,
+        out_shape=jax.ShapeDtypeStruct((blocks, long, share), F32),
+        name="middle",
+        cost_estimate=pl.CostEstimate(flops=500_000, bytes_accessed=4_000_000, transcendentals=0),
+    )(*middle_terms[0], *middle_terms[1], *outer)
     sci_b, got_a, mine = lax.optimization_barrier((sci_b, got_a, mine))
     got_b = lax.all_to_all(sci_b, "strip", split_axis=0, concat_axis=0, tiled=True)
+    got_a = got_a if sources == 1 else side_a
     if sources > 1:
-        got_a = jnp.sum(got_a.reshape((blocks, sources) + got_a.shape[1:]), axis=1)
         got_b = jnp.sum(got_b.reshape((blocks, sources) + got_b.shape[1:]), axis=1)
 
     per_block = tile_cols // LANES
@@ -515,10 +625,13 @@
     )
     matched = convolve(*arrays, psf_poly, toep_hi, toep_lo, band, got_a)
     unit = ROWS_DEV // 8
-    rest = pl.BlockSpec((1, unit, ncol), lambda i: (0, FIRST_PART + i, 0))
+    outside = EDGE // unit
+    rest = pl.BlockSpec(
+        (1, unit, ncol), lambda i: (0, jnp.where(i < outside, i, i + rows_a // unit), 0)
+    )
     return pl.pallas_call(
         subtract_kernel,
-        grid=(8 - FIRST_PART,),
+        grid=(2 * outside,),
         in_specs=[vmem, rest],
         out_specs=rest,
         out_shape=jax.ShapeDtypeStruct((1, ROWS_DEV, ncol), F32),

time: 180 us -> 179 us (level)
  waiting for transfers between devices: 80.7 us -> 64.7 us
  starting transfers between devices: 32 us -> 42.4 us
  Pallas kernels: 47.1 us -> 53.2 us
  local copies, waits for them, and re-layouts: 17.8 us -> 14.1 us
    ppermute x8 -> x15, waiting for transfers between devices: 68.2 us -> 53.5 us  [swap(): return lax.ppermute(value, axis, [(i, i ^ 1 << bit) for i in range(count)])]
    ppermute x8 -> x15, starting transfers between devices: 10.6 us -> 20.9 us  [swap(): return lax.ppermute(value, axis, [(i, i ^ 1 << bit) for i in range(count)])]
    pallas_call x2 -> x4, Pallas kernels: 7.16 us -> 13.1 us  [the longest x1 5.34 us: shards(): pl.pallas_call(subtract_kernel, grid=(2 * outside,), in_specs=[vmem, rest...]
    unnamed x35 -> x58, local copies, waits for them, and re-layouts: 15.3 us -> 12.3 us
  transfers between devices with their start and end apart: 17 -> 24, of which waited for: 9 -> 9; matrix products, arithmetic and copies ran while one was open for 6% -> 3% of each run, Pallas kernels for 13% -> 14%
where the time goes in v4:
time: 179 us; the launch traced here: 178 us
  waiting for transfers between devices  64.7 us (36%)
  Pallas kernels  53.2 us (30%)
  starting transfers between devices  42.4 us (24%)
  local copies, waits for them, and re-layouts  14.1 us (8%)
  other arithmetic  3.61 us (2%)
    ppermute x15, waiting for transfers between devices, swap(): return lax.ppermute(value, axis, [(i, i ^ 1 << bit) for i in range(count)])  53.5 us
    ppermute x15, starting transfers between devices, swap(): return lax.ppermute(value, axis, [(i, i ^ 1 << bit) for i in range(count)])  20.9 us
    pallas_call x1, Pallas kernels, shards(): pl.pallas_call(functools.partial(warp_kernel, (epochs, nrow, share, order...  19.4 us
    pallas_call x1, Pallas kernels, shards(): matched = convolve(*arrays, psf_poly, toep_hi, toep_lo, band, got_a)  17.3 us
    unnamed x58, local copies, waits for them, and re-layouts  12.3 us
    ppermute x7, waiting for transfers between devices, shards(): lax.ppermute(parts[k], 'strip', [(i, i ^ k) for i in range(strips)])  11.2 us
    ppermute x7, starting transfers between devices, shards(): lax.ppermute(parts[k], 'strip', [(i, i ^ k) for i in range(strips)])  8.17 us
    all_to_all x1, starting transfers between devices, shards(): lax.all_to_all(sci_b, 'strip', split_axis=0, concat_axis=0, tiled=True)  6.81 us
  transfers between devices with their start and end apart: 24, of which 9 were waited for; matrix products, arithmetic and copies ran while one was open for 3% of the time, Pallas kernels for 14%

profile of v4, /device:TPU:0, one launch (start us, length us, event | category | flops | bytes accessed | tf_op | source)
XLA Modules:
  0.0 178.3 jit_solution(14351078266128423116)
XLA Ops:
  0.0 19.4 %warp.1 = (f32[8,64,512]{2,1,0:T(8,128)}, f32[8,192,512]{2,1,0:T(8,128)}, f32[2,776,128]{2,1,0:T(8,128)}, f32[2,776,128]{2,1,0:T(8,128)}, f32[2,776,128]{2,1,0:T(8,128)}, /*index=5*/f32[2,776,128]{2,1,0:T(8,128)}) custom-call(s32[1,12]{1,0:T(1,128)} %kind_ref.1, s32[1,8,12]{2,1,0:T(8,128)} %heights_ref.3, f32[1,12]{1,0:T(1,128)} %invvar_ref.1, ...), custom_call_target="tpu_custom_call" | custom-call | flops 8000000000 | bytes 20000000 | tf_op jit(solution)/shard_map/warp/pallas_call | solution.py:460
  19.4 6.4 %all-to-all-start = ((f32[8,64,512]{2,1,0:T(8,128)}), f32[8,64,512]{2,1,0:T(8,128)S(1)}, u32[]{:S(2)}, u32[]{:S(2)}) async-start(f32[8,64,512]{2,1,0:T(8,128)} %get-tuple-element.30), calls=%async_computation | async-start | bytes 2097152 | tf_op jit(solution)/shard_map/all_to_all | solution.py:491
  26.9 2.0 %collective-permute-start.9 = (f32[2,776,128]{2,1,0:T(8,128)}, f32[2,776,128]{2,1,0:T(8,128)S(1)}, u32[]{:S(2)}, u32[]{:S(2)}) collective-permute-start(f32[2,776,128]{2,1,0:T(8,128)} %get-tuple-element.38), channel_id=1, source_target_pairs={{0,16},{8,24},{16,0},{24,8},{1,17},{9,25},{17,1},{25,9},{2,18},{10... | collective-permute-start | bytes 2383880 | tf_op jit(solution)/shard_map/ppermute | solution.py:434
  30.1 2.1 %collective-permute-start.1 = (f32[2,12]{1,0:T(2,128)S(1)}, f32[2,12]{1,0:T(2,128)S(1)}, u32[]{:S(2)}, u32[]{:S(2)}) collective-permute-start(f32[2,12]{1,0:T(2,128)S(1)} %pad_maximum_fusion.2), channel_id=1, source_target_pairs={{0,2},{1,3},{2,0},{3,1},{4,6},{5,7},{6,4},{7,5},{8,10},{9,11},{10,... | collective-permute-start | bytes 296 | tf_op jit(solution)/shard_map/ppermute | solution.py:434
  32.1 14.1 %collective-permute-done.7.refs_1_ = f32[2,776,128]{2,1,0:T(8,128)S(1)} collective-permute-done((f32[2,776,128]{2,1,0:T(8,128)}, f32[2,776,128]{2,1,0:T(8,128)S(1)}, u32[]{:S(2)}, u32[]{:S(2)}) %collective-permute-start.7) | collective-permute-done | bytes 794656 | tf_op jit(solution)/shard_map/ppermute | solution.py:434
  46.2 2.0 %slice_add_fusion.1 = f32[1,776,128]{2,1,0:T(8,128)} fusion(f32[2,776,128]{2,1,0:T(8,128)S(1)} %collective-permute-done.7.refs_1_, f32[2,776,128]{2,1,0:T(8,128)} %get-tuple-element.35.refs_0_), kind=kLoop, calls=%fused_computation.1 | loop fusion | flops 99328 | bytes 1191936 | tf_op jit(solution)/shard_map/add | solution.py:519
  50.5 1.7 collective-permute-start.10
  52.2 2.6 %collective-permute-start.2 = (f32[4,12]{1,0:T(4,128)S(1)}, f32[4,12]{1,0:T(4,128)S(1)}, u32[]{:S(2)}, u32[]{:S(2)}) collective-permute-start(f32[4,12]{1,0:T(4,128)S(1)} %pad_maximum_fusion.1), channel_id=1, source_target_pairs={{0,4},{1,5},{2,6},{3,7},{4,0},{5,1},{6,2},{7,3},{8,12},{9,13},{10,... | collective-permute-start | bytes 584 | tf_op jit(solution)/shard_map/ppermute | solution.py:434
  54.8 2.0 %collective-permute-done.2 = f32[4,12]{1,0:T(4,128)S(1)} collective-permute-done((f32[4,12]{1,0:T(4,128)S(1)}, f32[4,12]{1,0:T(4,128)S(1)}, u32[]{:S(2)}, u32[]{:S(2)}) %collective-permute-start.2) | collective-permute-done | bytes 224 | tf_op jit(solution)/shard_map/ppermute | solution.py:434
  58.4 2.6 %weigh.1 = (f32[2,264,128]{2,1,0:T(8,128)}, f32[2,264,128]{2,1,0:T(8,128)}, f32[2,264,128]{2,1,0:T(8,128)}, f32[2,264,128]{2,1,0:T(8,128)}) custom-call(s32[1,8,12]{2,1,0:T(8,128)} %heights_ref.3, f32[8,12]{1,0:T(8,128)} %pad_maximum_fusion.invvar_ref._, f32[8,64,512]{2,1,0:T(8,128)} %copy-done), custom_call_target="tpu_custom_call" | custom-call | flops 2000000 | bytes 2500000 | tf_op jit(solution)/shard_map/weigh/pallas_call | solution.py:564
  62.8 3.4 %template.1 = (f32[224,128]{1,0:T(8,128)}, f32[224,128]{1,0:T(8,128)}, f32[224,128]{1,0:T(8,128)}, f32[224,128]{1,0:T(8,128)}, f32[224,128]{1,0:T(8,128)}, /*ind...) custom-call(f32[2,776,128]{2,1,0:T(8,128)} %get-tuple-element.35.refs_0_, f32[2,776,128]{2,1,0:T(8,128)} %copy-done.12, ...), custom_call_target="tpu_custom_call" | custom-call | flops 2000000 | bytes 5000000 | tf_op jit(solution)/shard_map/template/pallas_call | solution.py:537
  68.1 2.5 %collective-permute-start.14 = (f32[224,128]{1,0:T(8,128)}, f32[224,128]{1,0:T(8,128)S(1)}, u32[]{:S(2)}, u32[]{:S(2)}) collective-permute-start(f32[224,128]{1,0:T(8,128)} %get-tuple-element.43), channel_id=1, source_target_pairs={{0,4},{1,5},{2,6},{3,7},{4,0},{5,1},{6,2},{7,3},{8,12},{9,13},{10,... | collective-permute-start | bytes 344072 | tf_op jit(solution)/shard_map/ppermute | solution.py:549
  72.0 1.8 %collective-permute-start.6 = (f32[1,264,128]{2,1,0:T(8,128)S(1)}, f32[1,264,128]{2,1,0:T(8,128)S(1)}, u32[]{:S(2)}, u32[]{:S(2)}) collective-permute-start(f32[1,264,128]{2,1,0:T(8,128)S(1)} %slice_add_fusion.2), channel_id=1, source_target_pairs={{0,8},{8,0},{16,24},{24,16},{1,9},{9,1},{17,25},{25,17},{2,10},{10... | collective-permute-start | bytes 405512 | tf_op jit(solution)/shard_map/ppermute | solution.py:434
  76.4 3.4 %collective-permute-start.16 = (f32[224,128]{1,0:T(8,128)}, f32[224,128]{1,0:T(8,128)S(1)}, u32[]{:S(2)}, u32[]{:S(2)}) collective-permute-start(f32[224,128]{1,0:T(8,128)} %get-tuple-element.45), channel_id=1, source_target_pairs={{0,6},{1,7},{2,4},{3,5},{4,2},{5,3},{6,0},{7,1},{8,14},{9,15},{10,... | collective-permute-start | bytes 344072 | tf_op jit(solution)/shard_map/ppermute | solution.py:549
  80.2 8.6 %collective-permute-done.15.refs_11_ = f32[224,128]{1,0:T(8,128)S(1)} collective-permute-done((f32[224,128]{1,0:T(8,128)}, f32[224,128]{1,0:T(8,128)S(1)}, u32[]{:S(2)}, u32[]{:S(2)}) %collective-permute-start.15) | collective-permute-done | bytes 114720 | tf_op jit(solution)/shard_map/ppermute | solution.py:549
  89.6 2.7 %middle.1.refs_0_ = f32[8,288,128]{2,1,0:T(8,128)} custom-call(f32[2,264,128]{2,1,0:T(8,128)} %get-tuple-element.31.refs_0_, f32[2,264,128]{2,1,0:T(8,128)} %copy-done.16, f32[1,264,128]{2,1,0:T(8,128)} %copy-done.19, f32[2,264,128]{2,1,0:T(8,128)} %get-tuple-element.33.refs_3_, f32[2,264,128]{2,1,0:T(8,128)} %copy-done.17, f32[1,264,128]{2,1,0:T(8,128)} %copy-done.20, ...), custom_call_target="tpu_custom_call" | custom-call | flops 500000 | bytes 4000000 | tf_op jit(solution)/shard_map/middle/pallas_call | solution.py:567
  92.3 6.8 %all-to-all-start.1 = ((f32[8,192,512]{2,1,0:T(8,128)}), f32[8,192,512]{2,1,0:T(8,128)S(1)}, u32[]{:S(2)}, u32[]{:S(2)}) async-start(f32[8,192,512]{2,1,0:T(8,128)} %get-tuple-element.47), calls=%async_computation.1 | async-start | bytes 6291456 | tf_op jit(solution)/shard_map/all_to_all | solution.py:576
  100.4 1.7 collective-permute-start.18
  102.1 25.6 %collective-permute-done.19.refs_2_ = f32[8,288,128]{2,1,0:T(8,128)S(1)} collective-permute-done((f32[8,288,128]{2,1,0:T(8,128)}, f32[8,288,128]{2,1,0:T(8,128)S(1)}, u32[]{:S(2)}, u32[]{:S(2)}) %collective-permute-start.19) | collective-permute-done | bytes 1179680 | tf_op jit(solution)/shard_map/ppermute | solution.py:434
  134.6 2.5 %bands.1 = (bf16[256,256]{1,0:T(8,128)(2,1)}, bf16[256,256]{1,0:T(8,128)(2,1)}, bf16[2,256,160]{2,1,0:T(8,128)(2,1)}) custom-call(f32[2,2,31]{2,1,0:T(2,128)} %psf_ref.1, f32[8,12]{1,0:T(8,128)} %pad_maximum_fusion.invvar_ref._), custom_call_target="tpu_custom_call" | custom-call | flops 10000000 | bytes 500000 | tf_op jit(solution)/shard_map/bands/pallas_call | solution.py:509
  137.0 7.8 %collective-permute-done.20.refs_3_ = f32[4,288,128]{2,1,0:T(8,128)} collective-permute-done((f32[4,288,128]{2,1,0:T(8,128)}, f32[4,288,128]{2,1,0:T(8,128)}, u32[]{:S(2)}, u32[]{:S(2)}) %collective-permute-start.20) | collective-permute-done | bytes 589856 | tf_op jit(solution)/shard_map/ppermute | solution.py:434
  144.8 2.9 %collective-permute-done.21.refs_4_ = f32[4,288,128]{2,1,0:T(8,128)} collective-permute-done((f32[4,288,128]{2,1,0:T(8,128)}, f32[4,288,128]{2,1,0:T(8,128)}, u32[]{:S(2)}, u32[]{:S(2)}) %collective-permute-start.21) | collective-permute-done | bytes 589856 | tf_op jit(solution)/shard_map/ppermute | solution.py:434
  155.6 17.3 %convolve.1 = f32[256,4096]{1,0:T(8,128)} custom-call(f32[8,288,128]{2,1,0:T(8,128)S(1)} %copy-done.2, f32[8,288,128]{2,1,0:T(8,128)S(1)} %copy-done.6, f32[8,288,128]{2,1,0:T(8,128)S(1)} %copy-done.4, f32[4,288,128]{2,1,0:T(8,128)} %collective-permute-done.20.refs_3_, f32[4,288,128]{2,1,0:T(8,128)} %collective-permute-done.21.refs_4_, ...), custom_call_target="tpu_custom_call" | custom-call | flops 15000000512 | bytes 10000000 | tf_op jit(solution)/shard_map/convolve/pallas_call | solution.py:626
  172.9 5.3 %subtract.1 = f32[1,256,4096]{2,1,0:T(8,128)} custom-call(f32[8,192,512]{2,1,0:T(8,128)S(1)} %all-to-all-done.1.sci_ref, f32[1,256,4096]{2,1,0:T(8,128)} %bitcast.2), custom_call_target="tpu_custom_call", output_to_operand_aliasing={{}: (1, {})} | custom-call | flops 1000000 | bytes 6000000 | tf_op jit(solution)/shard_map/subtract/pallas_call | solution.py:632
  (98 shorter events, 30.7 us)
Async XLA Ops:
  19.4 37.9 %all-to-all-start = ((f32[8,64,512]{2,1,0:T(8,128)}), f32[8,64,512]{2,1,0:T(8,128)S(1)}, u32[]{:S(2)}, u32[]{:S(2)}) async-start(f32[8,64,512]{2,1,0:T(8,128)} %get-tuple-element.30), calls=%async_computation | async-start | bytes 2097152 | tf_op jit(solution)/shard_map/all_to_all | solution.py:491
  25.9 20.3 %collective-permute-start.7 = (f32[2,776,128]{2,1,0:T(8,128)}, f32[2,776,128]{2,1,0:T(8,128)S(1)}, u32[]{:S(2)}, u32[]{:S(2)}) collective-permute-start(f32[2,776,128]{2,1,0:T(8,128)} %get-tuple-element.36), channel_id=1, source_target_pairs={{0,8},{8,0},{16,24},{24,16},{1,9},{9,1},{17,25},{25,17},{2,10},{10... | collective-permute-start | bytes 2383880 | tf_op jit(solution)/shard_map/ppermute | solution.py:434
  26.9 22.6 %collective-permute-start.9 = (f32[2,776,128]{2,1,0:T(8,128)}, f32[2,776,128]{2,1,0:T(8,128)S(1)}, u32[]{:S(2)}, u32[]{:S(2)}) collective-permute-start(f32[2,776,128]{2,1,0:T(8,128)} %get-tuple-element.38), channel_id=1, source_target_pairs={{0,16},{8,24},{16,0},{24,8},{1,17},{9,25},{17,1},{25,9},{2,18},{10... | collective-permute-start | bytes 2383880 | tf_op jit(solution)/shard_map/ppermute | solution.py:434
  28.9 1.2 collective-permute-start
  30.1 22.1 %collective-permute-start.1 = (f32[2,12]{1,0:T(2,128)S(1)}, f32[2,12]{1,0:T(2,128)S(1)}, u32[]{:S(2)}, u32[]{:S(2)}) collective-permute-start(f32[2,12]{1,0:T(2,128)S(1)} %pad_maximum_fusion.2), channel_id=1, source_target_pairs={{0,2},{1,3},{2,0},{3,1},{4,6},{5,7},{6,4},{7,5},{8,10},{9,11},{10,... | collective-permute-start | bytes 296 | tf_op jit(solution)/shard_map/ppermute | solution.py:434
  48.3 13.8 %collective-permute-start.8 = (f32[1,776,128]{2,1,0:T(8,128)}, f32[1,776,128]{2,1,0:T(8,128)}, u32[]{:S(2)}, u32[]{:S(2)}) collective-permute-start(f32[1,776,128]{2,1,0:T(8,128)} %slice_add_fusion.1), channel_id=1, source_target_pairs={{0,16},{8,24},{16,0},{24,8},{1,17},{9,25},{17,1},{25,9},{2,18},{10... | collective-permute-start | bytes 1191944 | tf_op jit(solution)/shard_map/ppermute | solution.py:434
  50.5 11.6 %collective-permute-start.10 = (f32[1,776,128]{2,1,0:T(8,128)}, f32[1,776,128]{2,1,0:T(8,128)S(1)}, u32[]{:S(2)}, u32[]{:S(2)}) collective-permute-start(f32[1,776,128]{2,1,0:T(8,128)} %slice_add_fusion), channel_id=1, source_target_pairs={{0,8},{8,0},{16,24},{24,16},{1,9},{9,1},{17,25},{25,17},{2,10},{10... | collective-permute-start | bytes 1191944 | tf_op jit(solution)/shard_map/ppermute | solution.py:434
  52.2 4.5 %collective-permute-start.2 = (f32[4,12]{1,0:T(4,128)S(1)}, f32[4,12]{1,0:T(4,128)S(1)}, u32[]{:S(2)}, u32[]{:S(2)}) collective-permute-start(f32[4,12]{1,0:T(4,128)S(1)} %pad_maximum_fusion.1), channel_id=1, source_target_pairs={{0,4},{1,5},{2,6},{3,7},{4,0},{5,1},{6,2},{7,3},{8,12},{9,13},{10,... | collective-permute-start | bytes 584 | tf_op jit(solution)/shard_map/ppermute | solution.py:434
  61.0 7.1 %collective-permute-start.3 = (f32[2,264,128]{2,1,0:T(8,128)}, f32[2,264,128]{2,1,0:T(8,128)S(1)}, u32[]{:S(2)}, u32[]{:S(2)}) collective-permute-start(f32[2,264,128]{2,1,0:T(8,128)} %get-tuple-element.32), channel_id=1, source_target_pairs={{0,8},{8,0},{16,24},{24,16},{1,9},{9,1},{17,25},{25,17},{2,10},{10... | collective-permute-start | bytes 811016 | tf_op jit(solution)/shard_map/ppermute | solution.py:434
  61.3 9.3 %collective-permute-start.5 = (f32[2,264,128]{2,1,0:T(8,128)}, f32[2,264,128]{2,1,0:T(8,128)S(1)}, u32[]{:S(2)}, u32[]{:S(2)}) collective-permute-start(f32[2,264,128]{2,1,0:T(8,128)} %get-tuple-element.34), channel_id=1, source_target_pairs={{0,16},{8,24},{16,0},{24,8},{1,17},{9,25},{17,1},{25,9},{2,18},{10... | collective-permute-start | bytes 811016 | tf_op jit(solution)/shard_map/ppermute | solution.py:434
  66.2 5.8 %collective-permute-start.11 = (f32[224,128]{1,0:T(8,128)}, f32[224,128]{1,0:T(8,128)S(1)}, u32[]{:S(2)}, u32[]{:S(2)}) collective-permute-start(f32[224,128]{1,0:T(8,128)} %get-tuple-element.40), channel_id=1, source_target_pairs={{0,1},{1,0},{2,3},{3,2},{4,5},{5,4},{6,7},{7,6},{8,9},{9,8},{10,11... | collective-permute-start | bytes 344072 | tf_op jit(solution)/shard_map/ppermute | solution.py:549
  66.2 8.7 %collective-permute-start.12 = (f32[224,128]{1,0:T(8,128)}, f32[224,128]{1,0:T(8,128)S(1)}, u32[]{:S(2)}, u32[]{:S(2)}) collective-permute-start(f32[224,128]{1,0:T(8,128)} %get-tuple-element.41), channel_id=1, source_target_pairs={{0,2},{1,3},{2,0},{3,1},{4,6},{5,7},{6,4},{7,5},{8,10},{9,11},{10,... | collective-permute-start | bytes 344072 | tf_op jit(solution)/shard_map/ppermute | solution.py:549
  67.9 8.5 %collective-permute-start.13 = (f32[224,128]{1,0:T(8,128)}, f32[224,128]{1,0:T(8,128)S(1)}, u32[]{:S(2)}, u32[]{:S(2)}) collective-permute-start(f32[224,128]{1,0:T(8,128)} %get-tuple-element.42), channel_id=1, source_target_pairs={{0,3},{1,2},{2,1},{3,0},{4,7},{5,6},{6,5},{7,4},{8,11},{9,10},{10,... | collective-permute-start | bytes 344072 | tf_op jit(solution)/shard_map/ppermute | solution.py:549
  68.1 11.7 %collective-permute-start.14 = (f32[224,128]{1,0:T(8,128)}, f32[224,128]{1,0:T(8,128)S(1)}, u32[]{:S(2)}, u32[]{:S(2)}) collective-permute-start(f32[224,128]{1,0:T(8,128)} %get-tuple-element.43), channel_id=1, source_target_pairs={{0,4},{1,5},{2,6},{3,7},{4,0},{5,1},{6,2},{7,3},{8,12},{9,13},{10,... | collective-permute-start | bytes 344072 | tf_op jit(solution)/shard_map/ppermute | solution.py:549
  70.6 18.2 %collective-permute-start.4 = (f32[1,264,128]{2,1,0:T(8,128)S(1)}, f32[1,264,128]{2,1,0:T(8,128)S(1)}, u32[]{:S(2)}, u32[]{:S(2)}) collective-permute-start(f32[1,264,128]{2,1,0:T(8,128)S(1)} %slice_add_fusion.3), channel_id=1, source_target_pairs={{0,16},{8,24},{16,0},{24,8},{1,17},{9,25},{17,1},{25,9},{2,18},{10... | collective-permute-start | bytes 405512 | tf_op jit(solution)/shard_map/ppermute | solution.py:434
  72.0 16.8 %collective-permute-start.6 = (f32[1,264,128]{2,1,0:T(8,128)S(1)}, f32[1,264,128]{2,1,0:T(8,128)S(1)}, u32[]{:S(2)}, u32[]{:S(2)}) collective-permute-start(f32[1,264,128]{2,1,0:T(8,128)S(1)} %slice_add_fusion.2), channel_id=1, source_target_pairs={{0,8},{8,0},{16,24},{24,16},{1,9},{9,1},{17,25},{25,17},{2,10},{10... | collective-permute-start | bytes 405512 | tf_op jit(solution)/shard_map/ppermute | solution.py:434
  74.9 13.8 %collective-permute-start.15 = (f32[224,128]{1,0:T(8,128)}, f32[224,128]{1,0:T(8,128)S(1)}, u32[]{:S(2)}, u32[]{:S(2)}) collective-permute-start(f32[224,128]{1,0:T(8,128)} %get-tuple-element.44), channel_id=1, source_target_pairs={{0,5},{1,4},{2,7},{3,6},{4,1},{5,0},{6,3},{7,2},{8,13},{9,12},{10,... | collective-permute-start | bytes 344072 | tf_op jit(solution)/shard_map/ppermute | solution.py:549
  76.4 12.4 %collective-permute-start.16 = (f32[224,128]{1,0:T(8,128)}, f32[224,128]{1,0:T(8,128)S(1)}, u32[]{:S(2)}, u32[]{:S(2)}) collective-permute-start(f32[224,128]{1,0:T(8,128)} %get-tuple-element.45), channel_id=1, source_target_pairs={{0,6},{1,7},{2,4},{3,5},{4,2},{5,3},{6,0},{7,1},{8,14},{9,15},{10,... | collective-permute-start | bytes 344072 | tf_op jit(solution)/shard_map/ppermute | solution.py:549
  79.7 9.1 %collective-permute-start.17 = (f32[224,128]{1,0:T(8,128)}, f32[224,128]{1,0:T(8,128)S(1)}, u32[]{:S(2)}, u32[]{:S(2)}) collective-permute-start(f32[224,128]{1,0:T(8,128)} %get-tuple-element.46), channel_id=1, source_target_pairs={{0,7},{1,6},{2,5},{3,4},{4,3},{5,2},{6,1},{7,0},{8,15},{9,14},{10,... | collective-permute-start | bytes 344072 | tf_op jit(solution)/shard_map/ppermute | solution.py:549
  92.3 80.6 %all-to-all-start.1 = ((f32[8,192,512]{2,1,0:T(8,128)}), f32[8,192,512]{2,1,0:T(8,128)S(1)}, u32[]{:S(2)}, u32[]{:S(2)}) async-start(f32[8,192,512]{2,1,0:T(8,128)} %get-tuple-element.47), calls=%async_computation.1 | async-start | bytes 6291456 | tf_op jit(solution)/shard_map/all_to_all | solution.py:576
  99.1 28.6 %collective-permute-start.19 = (f32[8,288,128]{2,1,0:T(8,128)}, f32[8,288,128]{2,1,0:T(8,128)S(1)}, u32[]{:S(2)}, u32[]{:S(2)}) collective-permute-start(f32[8,288,128]{2,1,0:T(8,128)} %middle.1.refs_0_), channel_id=1, source_target_pairs={{0,16},{8,24},{16,0},{24,8},{1,17},{9,25},{17,1},{25,9},{2,18},{10... | collective-permute-start | bytes 3538952 | tf_op jit(solution)/shard_map/ppermute | solution.py:434
  100.4 30.5 %collective-permute-start.18 = (f32[8,288,128]{2,1,0:T(8,128)}, f32[8,288,128]{2,1,0:T(8,128)S(1)}, u32[]{:S(2)}, u32[]{:S(2)}) collective-permute-start(f32[8,288,128]{2,1,0:T(8,128)} %middle.1.refs_0_), channel_id=1, source_target_pairs={{0,8},{8,0},{16,24},{24,16},{1,9},{9,1},{17,25},{25,17},{2,10},{10... | collective-permute-start | bytes 3538952 | tf_op jit(solution)/shard_map/ppermute | solution.py:434
  129.6 15.2 %collective-permute-start.20 = (f32[4,288,128]{2,1,0:T(8,128)}, f32[4,288,128]{2,1,0:T(8,128)}, u32[]{:S(2)}, u32[]{:S(2)}) collective-permute-start(f32[4,288,128]{2,1,0:T(8,128)} %slice.44), channel_id=1, source_target_pairs={{0,8},{8,0},{16,24},{24,16},{1,9},{9,1},{17,25},{25,17},{2,10},{10... | collective-permute-start | bytes 1769480 | tf_op jit(solution)/shard_map/ppermute | solution.py:434
  132.8 14.9 %collective-permute-start.21 = (f32[4,288,128]{2,1,0:T(8,128)}, f32[4,288,128]{2,1,0:T(8,128)}, u32[]{:S(2)}, u32[]{:S(2)}) collective-permute-start(f32[4,288,128]{2,1,0:T(8,128)} %slice.45), channel_id=1, source_target_pairs={{0,16},{8,24},{16,0},{24,8},{1,17},{9,25},{17,1},{25,9},{2,18},{10... | collective-permute-start | bytes 1769480 | tf_op jit(solution)/shard_map/ppermute | solution.py:434
  (29 other events, 270.1 us)

commit v5 on v4

--- a/solution.py
+++ b/solution.py
@@ -10,7 +10,7 @@
 
 ROWS_DEV = 256
 HALO = 16
-EDGE = 96
+EDGE = 80
 LANES = 128
 F32 = jnp.float32
 BF16 = jnp.bfloat16
@@ -247,13 +247,14 @@
     half = blocks // 2
     long = outs[0].shape[1]
     flat_shape = (long - half * rows_a, share)
+    pitch = pl.cdiv(rows_a, share) * share
     flat = lax.broadcasted_iota(jnp.int32, flat_shape, 0) * share + lax.broadcasted_iota(jnp.int32, flat_shape, 1)
     row = lax.broadcasted_iota(jnp.int32, (rows_a, share), 0) + first
     for part in range(2):
         wide = jnp.zeros(flat_shape, F32)
         for b in range(half):
             block = part * half + b
-            sky = flat - b * rows_a
+            sky = flat - b * pitch
             mine = (sky >= 0) & (sky < rows_a)
             sky = sky + first
             weight = jnp.zeros((rows_a, share), F32)
@@ -287,16 +288,16 @@
     for part in range(2):
         own = term_refs[part * terms : (part + 1) * terms]
         weights = added(own, pl.ds(half * rows_a, own[0].shape[1] - half * rows_a))
-        together = share // rows_a
-        for n in range(half // together):
-            below = upright(weights[n : n + 1, :], share)
-            for i in range(together):
-                b = n * together + i
-                value = added(own, pl.ds(b * rows_a, rows_a)) / below[i * rows_a : (i + 1) * rows_a]
-                out_ref[jnp.bitwise_xor(home, part * half + b), pl.ds(above, rows_a), :] = value
-
-
-def bands_kernel(psf_ref, _, toep_hi, toep_lo, band_ref):
+        lines = pl.cdiv(rows_a, share)
+        for b in range(half):
+            below = jnp.concatenate(
+                [upright(weights[b * lines + i : b * lines + i + 1, :], share) for i in range(lines)], axis=0
+            )
+            value = added(own, pl.ds(b * rows_a, rows_a)) / below[:rows_a]
+            out_ref[jnp.bitwise_xor(home, part * half + b), pl.ds(above, rows_a), :] = value
+
+
+def bands_kernel(psf_ref, toep_hi, toep_lo, band_ref):
     basis, _, ksize = psf_ref.shape
     margin = ksize // 2
     for k in range(basis):
@@ -489,14 +490,15 @@
     )(tile_kind, tile_heights, tile_invvar, raw_tiles[0], row_interp, col_interp)
 
     got_a = lax.all_to_all(sci_a, "strip", split_axis=0, concat_axis=0, tiled=True)
-    invvars = tile_invvar
-    for bit in range(strips.bit_length() - 1):
-        invvars = jnp.concatenate([invvars, swap(invvars, "strip", bit)], axis=0)
+    invvars = [tile_invvar]
+    for k in range(1, strips):
+        invvars.append(lax.ppermute(tile_invvar, "strip", [(i, i ^ k) for i in range(strips)]))
+    invvars = jnp.concatenate(invvars, axis=0)
 
     basis, _, _ = psf_profiles.shape
     build_bands = pl.pallas_call(
         bands_kernel,
-        in_specs=[smem, smem],
+        in_specs=[smem],
         out_specs=[vmem] * 3,
         out_shape=[
             jax.ShapeDtypeStruct((2 * LANES, 2 * LANES), BF16),
@@ -506,18 +508,18 @@
         name="bands",
         cost_estimate=pl.CostEstimate(flops=10_000_000, bytes_accessed=500_000, transcendentals=0),
     )
-    toep_hi, toep_lo, band = build_bands(psf_profiles, invvars)
+    toep_hi, toep_lo, band = build_bands(psf_profiles)
 
     def reduced(keeps, sends):
         terms = [[keep] for keep in keeps]
+        sends = list(sends)
         for i in range(bits):
             for part in range(2):
                 terms[part].append(swap(sends[part], "epoch", orders[part][i]))
             left = epochs >> (i + 1)
             if left > 1:
-                sends = [
-                    functools.reduce(lambda a, b: a + b, [t[left // 2 : left] for t in own]) for own in terms
-                ]
+                for part, own in enumerate(terms):
+                    sends[part] = functools.reduce(lambda a, b: a + b, [t[left // 2 : left] for t in own])
         return terms
 
     terms = reduced([keep_a, keep_b], [send_a, send_b])
@@ -550,7 +552,7 @@
     side_a = got_a
     if sources > 1:
         side_a = jnp.sum(got_a.reshape((blocks, sources) + got_a.shape[1:]), axis=1)
-    long_a = blocks // 2 * rows_a + 8 * pl.cdiv(blocks // 2 * rows_a, 8 * share)
+    long_a = blocks // 2 * rows_a + 8 * pl.cdiv(blocks // 2 * pl.cdiv(rows_a, share), 8)
     weighted_shape = jax.ShapeDtypeStruct((epochs // 2, long_a, share), F32)
     weigh = pl.pallas_call(
         functools.partial(weigh_kernel, (epochs, orders, share)),
@@ -564,15 +566,18 @@
     weighted = weigh(tile_heights, invvars, side_a)
     middle_terms = reduced(weighted[0::2], weighted[1::2])
     outer = came[::sources]
-    mine = pl.pallas_call(
+    for part in range(2):
+        sci_b, middle_terms[part][-1] = lax.optimization_barrier((sci_b, middle_terms[part][-1]))
+    sci_b, got_a, *outer = lax.optimization_barrier((sci_b, got_a, *outer))
+    merge = pl.pallas_call(
         functools.partial(middle_kernel, len(middle_terms[0])),
         in_specs=[vmem] * (2 * len(middle_terms[0]) + blocks),
         out_specs=vmem,
         out_shape=jax.ShapeDtypeStruct((blocks, long, share), F32),
         name="middle",
         cost_estimate=pl.CostEstimate(flops=500_000, bytes_accessed=4_000_000, transcendentals=0),
-    )(*middle_terms[0], *middle_terms[1], *outer)
-    sci_b, got_a, mine = lax.optimization_barrier((sci_b, got_a, mine))
+    )
+    mine = merge(*middle_terms[0], *middle_terms[1], *outer)
     got_b = lax.all_to_all(sci_b, "strip", split_axis=0, concat_axis=0, tiled=True)
     got_a = got_a if sources == 1 else side_a
     if sources > 1:
@@ -624,7 +629,7 @@
         cost_estimate=pl.CostEstimate(flops=15_000_000_000, bytes_accessed=10_000_000, transcendentals=0),
     )
     matched = convolve(*arrays, psf_poly, toep_hi, toep_lo, band, got_a)
-    unit = ROWS_DEV // 8
+    unit = ROWS_DEV // 16
     outside = EDGE // unit
     rest = pl.BlockSpec(
         (1, unit, ncol), lambda i: (0, jnp.where(i < outside, i, i + rows_a // unit), 0)

time: 179 us -> 213 us (1.19)
  the two profiles are of different devices: /device:TPU:0 before, /device:TPU:9 now
where the time goes in v5:
time: 213 us; the launch traced here: 209 us
  waiting for transfers between devices  92.7 us (44%)
  Pallas kernels  55.7 us (26%)
  starting transfers between devices  41.1 us (19%)
  local copies, waits for them, and re-layouts  16.2 us (8%)
  other arithmetic  3.18 us (1%)
    ppermute x12, waiting for transfers between devices, swap(): return lax.ppermute(value, axis, [(i, i ^ 1 << bit) for i in range(count)])  46.5 us
    ppermute x7, waiting for transfers between devices, shards(): lax.ppermute(tile_invvar, 'strip', [(i, i ^ k) for i in range(strips)])  30.5 us
    pallas_call x1, Pallas kernels, shards(): pl.pallas_call(functools.partial(warp_kernel, (epochs, nrow, share, order...  19 us
    pallas_call x1, Pallas kernels, shards(): matched = convolve(*arrays, psf_poly, toep_hi, toep_lo, band, got_a)  18 us
    ppermute x7, waiting for transfers between devices, shards(): lax.ppermute(parts[k], 'strip', [(i, i ^ k) for i in range(strips)])  15.8 us
    unnamed x56, local copies, waits for them, and re-layouts  13.8 us
    ppermute x12, starting transfers between devices, swap(): return lax.ppermute(value, axis, [(i, i ^ 1 << bit) for i in range(count)])  11.9 us
    ppermute x7, starting transfers between devices, shards(): lax.ppermute(parts[k], 'strip', [(i, i ^ k) for i in range(strips)])  10.3 us
  transfers between devices with their start and end apart: 28, of which 13 were waited for; matrix products, arithmetic and copies ran while one was open for 3% of the time, Pallas kernels for 14%

profile of v5, /device:TPU:9, one launch (start us, length us, event | category | flops | bytes accessed | tf_op | source)
XLA Modules:
  0.0 209.0 jit_solution(13948827926468060742)
XLA Ops:
  0.0 19.0 %warp.1 = (f32[8,96,512]{2,1,0:T(8,128)}, f32[8,160,512]{2,1,0:T(8,128)}, f32[2,648,128]{2,1,0:T(8,128)}, f32[2,648,128]{2,1,0:T(8,128)}, f32[2,648,128]{2,1,0:T(8,128)}, /*index=5*/f32[2,648,128]{2,1,0:T(8,128)}) custom-call(s32[1,12]{1,0:T(1,128)} %kind_ref.1, s32[1,8,12]{2,1,0:T(8,128)} %heights_ref.3, f32[1,12]{1,0:T(1,128)} %invvar_ref.1, ...), custom_call_target="tpu_custom_call" | custom-call | flops 8000000000 | bytes 20000000 | tf_op jit(solution)/shard_map/warp/pallas_call | solution.py:461
  19.0 6.1 %all-to-all-start = ((f32[8,96,512]{2,1,0:T(8,128)}), f32[8,96,512]{2,1,0:T(8,128)S(1)}, u32[]{:S(2)}, u32[]{:S(2)}) async-start(f32[8,96,512]{2,1,0:T(8,128)} %get-tuple-element.41), calls=%async_computation | async-start | bytes 3145728 | tf_op jit(solution)/shard_map/all_to_all | solution.py:492
  28.7 1.7 collective-permute-start.4
  30.5 1.7 collective-permute-start.3
  32.2 28.4 %collective-permute-done.5 = f32[1,12]{1,0:T(1,128)S(1)} collective-permute-done((f32[1,12]{1,0:T(1,128)S(1)}, f32[1,12]{1,0:T(1,128)S(1)}, u32[]{:S(2)}, u32[]{:S(2)}) %collective-permute-start.5) | collective-permute-done | bytes 80 | tf_op jit(solution)/shard_map/ppermute | solution.py:495
  60.6 2.6 %collective-permute-start.1 = (f32[1,12]{1,0:T(1,128)S(1)}, f32[1,12]{1,0:T(1,128)S(1)}, u32[]{:S(2)}, u32[]{:S(2)}) collective-permute-start(f32[1,12]{1,0:T(1,128)S(1)} %copy-done.27), channel_id=1, source_target_pairs={{0,2},{1,3},{2,0},{3,1},{4,6},{5,7},{6,4},{7,5},{8,10},{9,11},{10,... | collective-permute-start | bytes 152 | tf_op jit(solution)/shard_map/ppermute | solution.py:495
  68.4 3.3 %weigh.1 = (f32[2,392,128]{2,1,0:T(8,128)}, f32[2,392,128]{2,1,0:T(8,128)}, f32[2,392,128]{2,1,0:T(8,128)}, f32[2,392,128]{2,1,0:T(8,128)}) custom-call(s32[1,8,12]{2,1,0:T(8,128)} %heights_ref.3, f32[8,12]{1,0:T(8,128)} %concatenate.3.invvar_ref, f32[8,96,512]{2,1,0:T(8,128)} %copy-done), custom_call_target="tpu_custom_call" | custom-call | flops 2000000 | bytes 2500000 | tf_op jit(solution)/shard_map/weigh/pallas_call | solution.py:566
  76.7 4.7 %collective-permute-done.7.refs_1_ = f32[2,392,128]{2,1,0:T(8,128)S(1)} collective-permute-done((f32[2,392,128]{2,1,0:T(8,128)}, f32[2,392,128]{2,1,0:T(8,128)S(1)}, u32[]{:S(2)}, u32[]{:S(2)}) %collective-permute-start.7) | collective-permute-done | bytes 401440 | tf_op jit(solution)/shard_map/ppermute | solution.py:435
  83.6 6.7 %collective-permute-done.9.refs_4_ = f32[2,392,128]{2,1,0:T(8,128)S(1)} collective-permute-done((f32[2,392,128]{2,1,0:T(8,128)}, f32[2,392,128]{2,1,0:T(8,128)S(1)}, u32[]{:S(2)}, u32[]{:S(2)}) %collective-permute-start.9) | collective-permute-done | bytes 401440 | tf_op jit(solution)/shard_map/ppermute | solution.py:435
  92.6 3.2 %template.1 = (f32[192,128]{1,0:T(8,128)}, f32[192,128]{1,0:T(8,128)}, f32[192,128]{1,0:T(8,128)}, f32[192,128]{1,0:T(8,128)}, f32[192,128]{1,0:T(8,128)}, /*ind...) custom-call(f32[2,648,128]{2,1,0:T(8,128)} %get-tuple-element.48.refs_0_, ...), custom_call_target="tpu_custom_call" | custom-call | flops 2000000 | bytes 5000000 | tf_op jit(solution)/shard_map/template/pallas_call | solution.py:539
  95.8 4.3 %collective-permute-start.15 = (f32[192,128]{1,0:T(8,128)}, f32[192,128]{1,0:T(8,128)S(1)}, u32[]{:S(2)}, u32[]{:S(2)}) collective-permute-start(f32[192,128]{1,0:T(8,128)} %get-tuple-element.53), channel_id=1, source_target_pairs={{0,1},{1,0},{2,3},{3,2},{4,5},{5,4},{6,7},{7,6},{8,9},{9,8},{10,11... | collective-permute-start | bytes 294920 | tf_op jit(solution)/shard_map/ppermute | solution.py:551
  102.8 1.8 collective-permute-done.16.refs_8_
  104.6 2.4 %collective-permute-start.19 = (f32[192,128]{1,0:T(8,128)}, f32[192,128]{1,0:T(8,128)S(1)}, u32[]{:S(2)}, u32[]{:S(2)}) collective-permute-start(f32[192,128]{1,0:T(8,128)} %get-tuple-element.57), channel_id=1, source_target_pairs={{0,5},{1,4},{2,7},{3,6},{4,1},{5,0},{6,3},{7,2},{8,13},{9,12},{10,... | collective-permute-start | bytes 294920 | tf_op jit(solution)/shard_map/ppermute | solution.py:551
  108.7 8.2 %collective-permute-done.19.refs_11_ = f32[192,128]{1,0:T(8,128)S(1)} collective-permute-done((f32[192,128]{1,0:T(8,128)}, f32[192,128]{1,0:T(8,128)S(1)}, u32[]{:S(2)}, u32[]{:S(2)}) %collective-permute-start.19) | collective-permute-done | bytes 98336 | tf_op jit(solution)/shard_map/ppermute | solution.py:551
  116.9 2.9 %collective-permute-done.20.refs_12_ = f32[192,128]{1,0:T(8,128)S(1)} collective-permute-done((f32[192,128]{1,0:T(8,128)}, f32[192,128]{1,0:T(8,128)S(1)}, u32[]{:S(2)}, u32[]{:S(2)}) %collective-permute-start.20) | collective-permute-done | bytes 98336 | tf_op jit(solution)/shard_map/ppermute | solution.py:551
  119.8 2.1 %collective-permute-done.21.refs_13_ = f32[192,128]{1,0:T(8,128)S(1)} collective-permute-done((f32[192,128]{1,0:T(8,128)}, f32[192,128]{1,0:T(8,128)S(1)}, u32[]{:S(2)}, u32[]{:S(2)}) %collective-permute-start.21) | collective-permute-done | bytes 98336 | tf_op jit(solution)/shard_map/ppermute | solution.py:551
  122.6 4.3 %all-to-all-start.1 = ((f32[8,160,512]{2,1,0:T(8,128)}), f32[8,160,512]{2,1,0:T(8,128)S(1)}, u32[]{:S(2)}, u32[]{:S(2)}) async-start(f32[8,160,512]{2,1,0:T(8,128)} %get-tuple-element.60), calls=%async_computation.1 | async-start | bytes 5242880 | tf_op jit(solution)/shard_map/all_to_all | solution.py:581
  126.9 2.9 %middle.1.refs_0_ = f32[8,288,128]{2,1,0:T(8,128)} custom-call(f32[2,392,128]{2,1,0:T(8,128)} %get-tuple-element.42.refs_0_, f32[2,392,128]{2,1,0:T(8,128)} %copy-done.14, f32[1,392,128]{2,1,0:T(8,128)} %copy-done.18, f32[2,392,128]{2,1,0:T(8,128)} %get-tuple-element.45.refs_3_, f32[2,392,128]{2,1,0:T(8,128)} %copy-done.15, f32[1,392,128]{2,1,0:T(8,128)} %copy-done.19, ...), custom_call_target="tpu_custom_call" | custom-call | flops 500000 | bytes 4000000 | tf_op jit(solution)/shard_map/middle/pallas_call | solution.py:580
  132.3 24.9 %collective-permute-done.23.refs_2_ = f32[8,288,128]{2,1,0:T(8,128)S(1)} collective-permute-done((f32[8,288,128]{2,1,0:T(8,128)}, f32[8,288,128]{2,1,0:T(8,128)S(1)}, u32[]{:S(2)}, u32[]{:S(2)}) %collective-permute-start.23) | collective-permute-done | bytes 1179680 | tf_op jit(solution)/shard_map/ppermute | solution.py:435
  163.5 2.4 %bands.1 = (bf16[256,256]{1,0:T(8,128)(2,1)}, bf16[256,256]{1,0:T(8,128)(2,1)}, bf16[2,256,160]{2,1,0:T(8,128)(2,1)}) custom-call(f32[2,2,31]{2,1,0:T(2,128)} %psf_ref.1), custom_call_target="tpu_custom_call" | custom-call | flops 10000000 | bytes 500000 | tf_op jit(solution)/shard_map/bands/pallas_call | solution.py:511
  165.9 7.1 %collective-permute-done.24.refs_3_ = f32[4,288,128]{2,1,0:T(8,128)S(1)} collective-permute-done((f32[4,288,128]{2,1,0:T(8,128)}, f32[4,288,128]{2,1,0:T(8,128)S(1)}, u32[]{:S(2)}, u32[]{:S(2)}) %collective-permute-start.24) | collective-permute-done | bytes 589856 | tf_op jit(solution)/shard_map/ppermute | solution.py:435
  173.1 3.1 %collective-permute-done.25.refs_4_ = f32[4,288,128]{2,1,0:T(8,128)} collective-permute-done((f32[4,288,128]{2,1,0:T(8,128)}, f32[4,288,128]{2,1,0:T(8,128)}, u32[]{:S(2)}, u32[]{:S(2)}) %collective-permute-start.25) | collective-permute-done | bytes 589856 | tf_op jit(solution)/shard_map/ppermute | solution.py:435
  184.1 18.0 %convolve.1 = f32[256,4096]{1,0:T(8,128)} custom-call(f32[8,288,128]{2,1,0:T(8,128)S(1)} %copy-done.2, f32[8,288,128]{2,1,0:T(8,128)S(1)} %copy-done.6, f32[8,288,128]{2,1,0:T(8,128)S(1)} %copy-done.4, f32[4,288,128]{2,1,0:T(8,128)S(1)} %collective-permute-done.24.refs_3_, f32[4,288,128]{2,1,0:T(8,128)} %collective-permute-done.25.refs_4_, ...), custom_call_target="tpu_custom_call" | custom-call | flops 15000000512 | bytes 10000000 | tf_op jit(solution)/shard_map/convolve/pallas_call | solution.py:631
  202.2 6.8 %subtract.1 = f32[1,256,4096]{2,1,0:T(8,128)} custom-call(f32[8,160,512]{2,1,0:T(8,128)S(1)} %all-to-all-done.1.sci_ref, f32[1,256,4096]{2,1,0:T(8,128)} %bitcast.2), custom_call_target="tpu_custom_call", output_to_operand_aliasing={{}: (1, {})} | custom-call | flops 1000000 | bytes 6000000 | tf_op jit(solution)/shard_map/subtract/pallas_call | solution.py:637
  (102 shorter events, 40.2 us)
Async XLA Ops:
  19.0 48.2 %all-to-all-start = ((f32[8,96,512]{2,1,0:T(8,128)}), f32[8,96,512]{2,1,0:T(8,128)S(1)}, u32[]{:S(2)}, u32[]{:S(2)}) async-start(f32[8,96,512]{2,1,0:T(8,128)} %get-tuple-element.41), calls=%async_computation | async-start | bytes 3145728 | tf_op jit(solution)/shard_map/all_to_all | solution.py:492
  25.1 47.3 %collective-permute-start.11 = (f32[2,648,128]{2,1,0:T(8,128)}, f32[2,648,128]{2,1,0:T(8,128)}, u32[]{:S(2)}, u32[]{:S(2)}) collective-permute-start(f32[2,648,128]{2,1,0:T(8,128)} %get-tuple-element.49), channel_id=1, source_target_pairs={{0,8},{8,0},{16,24},{24,16},{1,9},{9,1},{17,25},{25,17},{2,10},{10... | collective-permute-start | bytes 1990664 | tf_op jit(solution)/shard_map/ppermute | solution.py:435
  25.9 49.4 %collective-permute-start.13 = (f32[2,648,128]{2,1,0:T(8,128)}, f32[2,648,128]{2,1,0:T(8,128)}, u32[]{:S(2)}, u32[]{:S(2)}) collective-permute-start(f32[2,648,128]{2,1,0:T(8,128)} %get-tuple-element.51), channel_id=1, source_target_pairs={{0,16},{8,24},{16,0},{24,8},{1,17},{9,25},{17,1},{25,9},{2,18},{10... | collective-permute-start | bytes 1990664 | tf_op jit(solution)/shard_map/ppermute | solution.py:435
  27.5 33.1 %collective-permute-start.5 = (f32[1,12]{1,0:T(1,128)S(1)}, f32[1,12]{1,0:T(1,128)S(1)}, u32[]{:S(2)}, u32[]{:S(2)}) collective-permute-start(f32[1,12]{1,0:T(1,128)S(1)} %copy-done.27), channel_id=1, source_target_pairs={{0,6},{1,7},{2,4},{3,5},{4,2},{5,3},{6,0},{7,1},{8,14},{9,15},{10,... | collective-permute-start | bytes 152 | tf_op jit(solution)/shard_map/ppermute | solution.py:495
  28.7 31.9 %collective-permute-start.4 = (f32[1,12]{1,0:T(1,128)S(1)}, f32[1,12]{1,0:T(1,128)S(1)}, u32[]{:S(2)}, u32[]{:S(2)}) collective-permute-start(f32[1,12]{1,0:T(1,128)S(1)} %copy-done.27), channel_id=1, source_target_pairs={{0,5},{1,4},{2,7},{3,6},{4,1},{5,0},{6,3},{7,2},{8,13},{9,12},{10,... | collective-permute-start | bytes 152 | tf_op jit(solution)/shard_map/ppermute | solution.py:495
  30.5 32.8 %collective-permute-start.3 = (f32[1,12]{1,0:T(1,128)S(1)}, f32[1,12]{1,0:T(1,128)S(1)}, u32[]{:S(2)}, u32[]{:S(2)}) collective-permute-start(f32[1,12]{1,0:T(1,128)S(1)} %copy-done.27), channel_id=1, source_target_pairs={{0,4},{1,5},{2,6},{3,7},{4,0},{5,1},{6,2},{7,3},{8,12},{9,13},{10,... | collective-permute-start | bytes 152 | tf_op jit(solution)/shard_map/ppermute | solution.py:495
  71.6 9.8 %collective-permute-start.7 = (f32[2,392,128]{2,1,0:T(8,128)}, f32[2,392,128]{2,1,0:T(8,128)S(1)}, u32[]{:S(2)}, u32[]{:S(2)}) collective-permute-start(f32[2,392,128]{2,1,0:T(8,128)} %get-tuple-element.43), channel_id=1, source_target_pairs={{0,8},{8,0},{16,24},{24,16},{1,9},{9,1},{17,25},{25,17},{2,10},{10... | collective-permute-start | bytes 1204232 | tf_op jit(solution)/shard_map/ppermute | solution.py:435
  73.4 17.6 %collective-permute-start.12 = (f32[1,648,128]{2,1,0:T(8,128)S(1)}, f32[1,648,128]{2,1,0:T(8,128)S(1)}, u32[]{:S(2)}, u32[]{:S(2)}) collective-permute-start(f32[1,648,128]{2,1,0:T(8,128)S(1)} %slice_add_fusion.1), channel_id=1, source_target_pairs={{0,16},{8,24},{16,0},{24,8},{1,17},{9,25},{17,1},{25,9},{2,18},{10... | collective-permute-start | bytes 995336 | tf_op jit(solution)/shard_map/ppermute | solution.py:435
  75.2 15.1 %collective-permute-start.9 = (f32[2,392,128]{2,1,0:T(8,128)}, f32[2,392,128]{2,1,0:T(8,128)S(1)}, u32[]{:S(2)}, u32[]{:S(2)}) collective-permute-start(f32[2,392,128]{2,1,0:T(8,128)} %get-tuple-element.46), channel_id=1, source_target_pairs={{0,16},{8,24},{16,0},{24,8},{1,17},{9,25},{17,1},{25,9},{2,18},{10... | collective-permute-start | bytes 1204232 | tf_op jit(solution)/shard_map/ppermute | solution.py:435
  76.3 14.8 %collective-permute-start.14 = (f32[1,648,128]{2,1,0:T(8,128)S(1)}, f32[1,648,128]{2,1,0:T(8,128)S(1)}, u32[]{:S(2)}, u32[]{:S(2)}) collective-permute-start(f32[1,648,128]{2,1,0:T(8,128)S(1)} %slice_add_fusion), channel_id=1, source_target_pairs={{0,8},{8,0},{16,24},{24,16},{1,9},{9,1},{17,25},{25,17},{2,10},{10... | collective-permute-start | bytes 995336 | tf_op jit(solution)/shard_map/ppermute | solution.py:435
  82.5 24.5 %collective-permute-start.8 = (f32[1,392,128]{2,1,0:T(8,128)S(1)}, f32[1,392,128]{2,1,0:T(8,128)S(1)}, u32[]{:S(2)}, u32[]{:S(2)}) collective-permute-start(f32[1,392,128]{2,1,0:T(8,128)S(1)} %slice_add_fusion.3), channel_id=1, source_target_pairs={{0,16},{8,24},{16,0},{24,8},{1,17},{9,25},{17,1},{25,9},{2,18},{10... | collective-permute-start | bytes 602120 | tf_op jit(solution)/shard_map/ppermute | solution.py:435
  90.4 17.5 %collective-permute-start.10 = (f32[1,392,128]{2,1,0:T(8,128)S(1)}, f32[1,392,128]{2,1,0:T(8,128)S(1)}, u32[]{:S(2)}, u32[]{:S(2)}) collective-permute-start(f32[1,392,128]{2,1,0:T(8,128)S(1)} %slice_add_fusion.2), channel_id=1, source_target_pairs={{0,8},{8,0},{16,24},{24,16},{1,9},{9,1},{17,25},{25,17},{2,10},{10... | collective-permute-start | bytes 602120 | tf_op jit(solution)/shard_map/ppermute | solution.py:435
  95.8 6.0 %collective-permute-start.15 = (f32[192,128]{1,0:T(8,128)}, f32[192,128]{1,0:T(8,128)S(1)}, u32[]{:S(2)}, u32[]{:S(2)}) collective-permute-start(f32[192,128]{1,0:T(8,128)} %get-tuple-element.53), channel_id=1, source_target_pairs={{0,1},{1,0},{2,3},{3,2},{4,5},{5,4},{6,7},{7,6},{8,9},{9,8},{10,11... | collective-permute-start | bytes 294920 | tf_op jit(solution)/shard_map/ppermute | solution.py:551
  100.1 4.5 %collective-permute-start.16 = (f32[192,128]{1,0:T(8,128)}, f32[192,128]{1,0:T(8,128)S(1)}, u32[]{:S(2)}, u32[]{:S(2)}) collective-permute-start(f32[192,128]{1,0:T(8,128)} %get-tuple-element.54), channel_id=1, source_target_pairs={{0,2},{1,3},{2,0},{3,1},{4,6},{5,7},{6,4},{7,5},{8,10},{9,11},{10,... | collective-permute-start | bytes 294920 | tf_op jit(solution)/shard_map/ppermute | solution.py:551
  100.9 7.0 %collective-permute-start.17 = (f32[192,128]{1,0:T(8,128)}, f32[192,128]{1,0:T(8,128)S(1)}, u32[]{:S(2)}, u32[]{:S(2)}) collective-permute-start(f32[192,128]{1,0:T(8,128)} %get-tuple-element.55), channel_id=1, source_target_pairs={{0,3},{1,2},{2,1},{3,0},{4,7},{5,6},{6,5},{7,4},{8,11},{9,10},{10,... | collective-permute-start | bytes 294920 | tf_op jit(solution)/shard_map/ppermute | solution.py:551
  101.8 6.9 %collective-permute-start.18 = (f32[192,128]{1,0:T(8,128)}, f32[192,128]{1,0:T(8,128)S(1)}, u32[]{:S(2)}, u32[]{:S(2)}) collective-permute-start(f32[192,128]{1,0:T(8,128)} %get-tuple-element.56), channel_id=1, source_target_pairs={{0,4},{1,5},{2,6},{3,7},{4,0},{5,1},{6,2},{7,3},{8,12},{9,13},{10,... | collective-permute-start | bytes 294920 | tf_op jit(solution)/shard_map/ppermute | solution.py:551
  104.6 12.3 %collective-permute-start.19 = (f32[192,128]{1,0:T(8,128)}, f32[192,128]{1,0:T(8,128)S(1)}, u32[]{:S(2)}, u32[]{:S(2)}) collective-permute-start(f32[192,128]{1,0:T(8,128)} %get-tuple-element.57), channel_id=1, source_target_pairs={{0,5},{1,4},{2,7},{3,6},{4,1},{5,0},{6,3},{7,2},{8,13},{9,12},{10,... | collective-permute-start | bytes 294920 | tf_op jit(solution)/shard_map/ppermute | solution.py:551
  107.0 12.8 %collective-permute-start.20 = (f32[192,128]{1,0:T(8,128)}, f32[192,128]{1,0:T(8,128)S(1)}, u32[]{:S(2)}, u32[]{:S(2)}) collective-permute-start(f32[192,128]{1,0:T(8,128)} %get-tuple-element.58), channel_id=1, source_target_pairs={{0,6},{1,7},{2,4},{3,5},{4,2},{5,3},{6,0},{7,1},{8,14},{9,15},{10,... | collective-permute-start | bytes 294920 | tf_op jit(solution)/shard_map/ppermute | solution.py:551
  107.9 14.0 %collective-permute-start.21 = (f32[192,128]{1,0:T(8,128)}, f32[192,128]{1,0:T(8,128)S(1)}, u32[]{:S(2)}, u32[]{:S(2)}) collective-permute-start(f32[192,128]{1,0:T(8,128)} %get-tuple-element.59), channel_id=1, source_target_pairs={{0,7},{1,6},{2,5},{3,4},{4,3},{5,2},{6,1},{7,0},{8,15},{9,14},{10,... | collective-permute-start | bytes 294920 | tf_op jit(solution)/shard_map/ppermute | solution.py:551
  122.6 79.6 %all-to-all-start.1 = ((f32[8,160,512]{2,1,0:T(8,128)}), f32[8,160,512]{2,1,0:T(8,128)S(1)}, u32[]{:S(2)}, u32[]{:S(2)}) async-start(f32[8,160,512]{2,1,0:T(8,128)} %get-tuple-element.60), calls=%async_computation.1 | async-start | bytes 5242880 | tf_op jit(solution)/shard_map/all_to_all | solution.py:581
  129.8 27.3 %collective-permute-start.23 = (f32[8,288,128]{2,1,0:T(8,128)}, f32[8,288,128]{2,1,0:T(8,128)S(1)}, u32[]{:S(2)}, u32[]{:S(2)}) collective-permute-start(f32[8,288,128]{2,1,0:T(8,128)} %middle.1.refs_0_), channel_id=1, source_target_pairs={{0,16},{8,24},{16,0},{24,8},{1,17},{9,25},{17,1},{25,9},{2,18},{10... | collective-permute-start | bytes 3538952 | tf_op jit(solution)/shard_map/ppermute | solution.py:435
  131.2 29.1 %collective-permute-start.22 = (f32[8,288,128]{2,1,0:T(8,128)}, f32[8,288,128]{2,1,0:T(8,128)S(1)}, u32[]{:S(2)}, u32[]{:S(2)}) collective-permute-start(f32[8,288,128]{2,1,0:T(8,128)} %middle.1.refs_0_), channel_id=1, source_target_pairs={{0,8},{8,0},{16,24},{24,16},{1,9},{9,1},{17,25},{25,17},{2,10},{10... | collective-permute-start | bytes 3538952 | tf_op jit(solution)/shard_map/ppermute | solution.py:435
  159.1 14.0 %collective-permute-start.24 = (f32[4,288,128]{2,1,0:T(8,128)}, f32[4,288,128]{2,1,0:T(8,128)S(1)}, u32[]{:S(2)}, u32[]{:S(2)}) collective-permute-start(f32[4,288,128]{2,1,0:T(8,128)} %slice.44), channel_id=1, source_target_pairs={{0,8},{8,0},{16,24},{24,16},{1,9},{9,1},{17,25},{25,17},{2,10},{10... | collective-permute-start | bytes 1769480 | tf_op jit(solution)/shard_map/ppermute | solution.py:435
  162.2 13.9 %collective-permute-start.25 = (f32[4,288,128]{2,1,0:T(8,128)}, f32[4,288,128]{2,1,0:T(8,128)}, u32[]{:S(2)}, u32[]{:S(2)}) collective-permute-start(f32[4,288,128]{2,1,0:T(8,128)} %slice.45), channel_id=1, source_target_pairs={{0,16},{8,24},{16,0},{24,8},{1,17},{9,25},{17,1},{25,9},{2,18},{10... | collective-permute-start | bytes 1769480 | tf_op jit(solution)/shard_map/ppermute | solution.py:435
  (32 other events, 326.4 us)

commit v6 on v3

--- a/solution.py
+++ b/solution.py
@@ -14,6 +14,7 @@
 LANES = 128
 F32 = jnp.float32
 BF16 = jnp.bfloat16
+F8 = jnp.float8_e4m3fn
 
 
 def split(x):
@@ -33,6 +34,13 @@
     both = dot(jnp.concatenate([a_hi, a_lo], axis=0), b_hi, trans_b)
     rows = a_hi.shape[0]
     return both[:rows] + (both[rows:] + dot(a_hi, b_lo, trans_b))
+
+
+def split8(x, own, rest, swapped=False):
+    hi = x.astype(BF16)
+    wide = hi.astype(F32)
+    high, low = (wide * own).astype(F8), ((x - wide) * rest).astype(F8)
+    return hi, jnp.concatenate([high, low] if swapped else [low, high], axis=-1)
 
 
 def start_and_wait(copies):
@@ -112,7 +120,8 @@
         height = heights_ref[0, block, offset_in + t]
         start = pl.multiple_of(jnp.minimum(lax.div(top, 8) * 8, nrow - span), 8)
         off = top - start
-        across = dot3(split(raw_ref[i]), (chi_s[kind], clo_s[kind]), trans_b=True)
+        main, fine = split8(raw_ref[i], 1.0, 256.0)
+        across = dot(main, chi_s[kind], True) + dot(fine, clo_s[kind], True) * (1.0 / 4096.0)
         live = lax.broadcasted_iota(jnp.int32, (tile_rows, tile_rows), 1) < height
         rows = jnp.concatenate(
             [jnp.where(live, rmat_s[kind], 0.0), jnp.zeros((8, tile_rows), F32)], axis=0
@@ -130,7 +139,7 @@
 
             def divide(n, carry):
                 here = pl.ds(pl.multiple_of(n * (tile_cols // 8), tile_cols // 8), tile_cols // 8)
-                chi_s[kind, here, :], clo_s[kind, here, :] = split(cmat_s[kind, here, :])
+                chi_s[kind, here, :], clo_s[kind, here, :] = split8(cmat_s[kind, here, :], 16.0, 4096.0, True)
                 return carry
 
             lax.fori_loop(0, 8, divide, 0)
@@ -398,7 +407,7 @@
             pltpu.VMEM((kinds, tile_rows, tile_rows), F32),
             pltpu.VMEM((kinds, tile_cols, tile_cols), F32),
             pltpu.VMEM((kinds, tile_cols, tile_cols), BF16),
-            pltpu.VMEM((kinds, tile_cols, tile_cols), BF16),
+            pltpu.VMEM((kinds, tile_cols, 2 * tile_cols), F8),
             pltpu.SMEM((2,), jnp.int32),
             pltpu.SMEM((kinds,), jnp.int32),
             pltpu.SemaphoreType.DMA((kinds, 2)),

time: 180 us -> 180 us (level)
  no operation moved by 1% of the time
where the time goes in v6:
time: 180 us; the launch traced here: 179 us
  waiting for transfers between devices  80.5 us (45%)
  Pallas kernels  46.6 us (26%)
  starting transfers between devices  32.1 us (18%)
  local copies, waits for them, and re-layouts  17.8 us (10%)
  other arithmetic  2.19 us (1%)
    ppermute x8, waiting for transfers between devices, swap(): return lax.ppermute(value, axis, [(i, i ^ 1 << bit) for i in range(count)])  68 us
    pallas_call x1, Pallas kernels, shards(): pl.pallas_call(functools.partial(warp_kernel, (epochs, nrow, share, order...  18.8 us
    pallas_call x1, Pallas kernels, shards(): matched = convolve(*arrays, psf_poly, toep_hi, toep_lo, band, got_a)  16.7 us
    unnamed x35, local copies, waits for them, and re-layouts  15.3 us
    ppermute x7, waiting for transfers between devices, shards(): lax.ppermute(parts[k], 'strip', [(i, i ^ k) for i in range(strips)])  12.5 us
    ppermute x8, starting transfers between devices, swap(): return lax.ppermute(value, axis, [(i, i ^ 1 << bit) for i in range(count)])  10.8 us
    all_to_all x1, starting transfers between devices, shards(): lax.all_to_all(sci_b, 'strip', split_axis=0, concat_axis=0, tiled=True)  8.43 us
    ppermute x7, starting transfers between devices, shards(): lax.ppermute(parts[k], 'strip', [(i, i ^ k) for i in range(strips)])  7.46 us
  transfers between devices with their start and end apart: 17, of which 9 were waited for; matrix products, arithmetic and copies ran while one was open for 6% of the time, Pallas kernels for 13%

profile of v6, /device:TPU:0, one launch (start us, length us, event | category | flops | bytes accessed | tf_op | source)
XLA Modules:
  0.0 179.3 jit_solution(5043863020637336907)
XLA Ops:
  0.0 18.8 %warp.1 = (f32[8,96,512]{2,1,0:T(8,128)}, f32[8,160,512]{2,1,0:T(8,128)}, f32[2,1032,128]{2,1,0:T(8,128)}, f32[2,1032,128]{2,1,0:T(8,128)}, f32[2,1032,128]{2,1,0:T(8,128)}, /*index=5*/f32[2,1032,128]{2,1,0:T(8,128)}) custom-call(s32[1,12]{1,0:T(1,128)} %kind_ref.1, s32[1,8,12]{2,1,0:T(8,128)} %heights_ref.1, f32[1,12]{1,0:T(1,128)} %invvar_ref.1, ...), custom_call_target="tpu_custom_call" | custom-call | flops 8000000000 | bytes 20000000 | tf_op jit(solution)/shard_map/warp/pallas_call | solution.py:390
  18.8 2.6 %collective-permute-start = (f32[2,1032,128]{2,1,0:T(8,128)}, f32[2,1032,128]{2,1,0:T(8,128)}, u32[]{:S(2)}, u32[]{:S(2)}) collective-permute-start(f32[2,1032,128]{2,1,0:T(8,128)} %get-tuple-element.28), channel_id=1, source_target_pairs={{0,8},{8,0},{16,24},{24,16},{1,9},{9,1},{17,25},{25,17},{2,10},{10... | collective-permute-start | bytes 3170312 | tf_op jit(solution)/shard_map/ppermute | solution.py:362
  21.4 1.5 collective-permute-start.2
  22.9 5.4 %all-to-all-start = ((f32[8,96,512]{2,1,0:T(8,128)}), f32[8,96,512]{2,1,0:T(8,128)S(1)}, u32[]{:S(2)}, u32[]{:S(2)}) async-start(f32[8,96,512]{2,1,0:T(8,128)} %get-tuple-element.26), calls=%async_computation | async-start | bytes 3145728 | tf_op jit(solution)/shard_map/all_to_all | solution.py:421
  28.3 17.2 %collective-permute-done.refs_1_ = f32[2,1032,128]{2,1,0:T(8,128)} collective-permute-done((f32[2,1032,128]{2,1,0:T(8,128)}, f32[2,1032,128]{2,1,0:T(8,128)}, u32[]{:S(2)}, u32[]{:S(2)}) %collective-permute-start) | collective-permute-done | bytes 1056800 | tf_op jit(solution)/shard_map/ppermute | solution.py:362
  46.6 2.1 %collective-permute-start.1 = (f32[1,1032,128]{2,1,0:T(8,128)S(1)}, f32[1,1032,128]{2,1,0:T(8,128)S(1)}, u32[]{:S(2)}, u32[]{:S(2)}) collective-permute-start(f32[1,1032,128]{2,1,0:T(8,128)S(1)} %slice_add_fusion.1), channel_id=1, source_target_pairs={{0,16},{8,24},{16,0},{24,8},{1,17},{9,25},{17,1},{25,9},{2,18},{10... | collective-permute-start | bytes 1585160 | tf_op jit(solution)/shard_map/ppermute | solution.py:362
  49.8 1.5 collective-permute-start.3
  51.4 8.9 %collective-permute-done.1.refs_2_ = f32[1,1032,128]{2,1,0:T(8,128)S(1)} collective-permute-done((f32[1,1032,128]{2,1,0:T(8,128)S(1)}, f32[1,1032,128]{2,1,0:T(8,128)S(1)}, u32[]{:S(2)}, u32[]{:S(2)}) %collective-permute-start.1) | collective-permute-done | bytes 528416 | tf_op jit(solution)/shard_map/ppermute | solution.py:362
  60.3 2.7 %collective-permute-done.3.refs_5_ = f32[1,1032,128]{2,1,0:T(8,128)S(1)} collective-permute-done((f32[1,1032,128]{2,1,0:T(8,128)S(1)}, f32[1,1032,128]{2,1,0:T(8,128)S(1)}, u32[]{:S(2)}, u32[]{:S(2)}) %collective-permute-start.3) | collective-permute-done | bytes 528416 | tf_op jit(solution)/shard_map/ppermute | solution.py:362
  63.9 3.9 %template.1 = (f32[288,128]{1,0:T(8,128)}, f32[288,128]{1,0:T(8,128)}, f32[288,128]{1,0:T(8,128)}, f32[288,128]{1,0:T(8,128)}, f32[288,128]{1,0:T(8,128)}, /*ind...) custom-call(f32[2,1032,128]{2,1,0:T(8,128)} %get-tuple-element.27.refs_0_, ...), custom_call_target="tpu_custom_call" | custom-call | flops 2000000 | bytes 5000000 | tf_op jit(solution)/shard_map/template/pallas_call | solution.py:460
  69.6 1.8 %collective-permute-start.7 = (f32[288,128]{1,0:T(8,128)}, f32[288,128]{1,0:T(8,128)S(1)}, u32[]{:S(2)}, u32[]{:S(2)}) collective-permute-start(f32[288,128]{1,0:T(8,128)} %get-tuple-element.35), channel_id=1, source_target_pairs={{0,4},{1,5},{2,6},{3,7},{4,0},{5,1},{6,2},{7,3},{8,12},{9,13},{10,... | collective-permute-start | bytes 442376 | tf_op jit(solution)/shard_map/ppermute | solution.py:472
  72.2 1.6 bitcast_dynamic-update-slice_fusion.7
  73.8 3.0 %collective-permute-start.9 = (f32[288,128]{1,0:T(8,128)}, f32[288,128]{1,0:T(8,128)S(1)}, u32[]{:S(2)}, u32[]{:S(2)}) collective-permute-start(f32[288,128]{1,0:T(8,128)} %get-tuple-element.37), channel_id=1, source_target_pairs={{0,6},{1,7},{2,4},{3,5},{4,2},{5,3},{6,0},{7,1},{8,14},{9,15},{10,... | collective-permute-start | bytes 442376 | tf_op jit(solution)/shard_map/ppermute | solution.py:472
  77.5 2.3 %collective-permute-done.5 = f32[288,128]{1,0:T(8,128)S(1)} collective-permute-done((f32[288,128]{1,0:T(8,128)}, f32[288,128]{1,0:T(8,128)S(1)}, u32[]{:S(2)}, u32[]{:S(2)}) %collective-permute-start.5) | collective-permute-done | bytes 147488 | tf_op jit(solution)/shard_map/ppermute | solution.py:472
  80.5 1.4 collective-permute-done.6
  83.3 8.8 %collective-permute-done.8 = f32[288,128]{1,0:T(8,128)S(1)} collective-permute-done((f32[288,128]{1,0:T(8,128)}, f32[288,128]{1,0:T(8,128)S(1)}, u32[]{:S(2)}, u32[]{:S(2)}) %collective-permute-start.8) | collective-permute-done | bytes 147488 | tf_op jit(solution)/shard_map/ppermute | solution.py:472
  95.2 8.4 %all-to-all-start.1 = ((f32[8,160,512]{2,1,0:T(8,128)}), f32[8,160,512]{2,1,0:T(8,128)S(1)}, u32[]{:S(2)}, u32[]{:S(2)}) async-start(f32[8,160,512]{2,1,0:T(8,128)} %get-tuple-element.39), calls=%async_computation.1 | async-start | bytes 5242880 | tf_op jit(solution)/shard_map/all_to_all | solution.py:475
  105.2 27.0 %collective-permute-done.12.refs_2_ = f32[8,288,128]{2,1,0:T(8,128)S(1)} collective-permute-done((f32[8,288,128]{2,1,0:T(8,128)}, f32[8,288,128]{2,1,0:T(8,128)S(1)}, u32[]{:S(2)}, u32[]{:S(2)}) %collective-permute-start.12) | collective-permute-done | bytes 1179680 | tf_op jit(solution)/shard_map/ppermute | solution.py:362
  136.5 2.4 %bands.1 = (bf16[256,256]{1,0:T(8,128)(2,1)}, bf16[256,256]{1,0:T(8,128)(2,1)}, bf16[2,256,160]{2,1,0:T(8,128)(2,1)}) custom-call(f32[2,2,31]{2,1,0:T(2,128)} %psf_ref.1), custom_call_target="tpu_custom_call" | custom-call | flops 10000000 | bytes 500000 | tf_op jit(solution)/shard_map/bands/pallas_call | solution.py:436
  138.9 9.2 %collective-permute-done.13.refs_3_ = f32[4,288,128]{2,1,0:T(8,128)S(1)} collective-permute-done((f32[4,288,128]{2,1,0:T(8,128)}, f32[4,288,128]{2,1,0:T(8,128)S(1)}, u32[]{:S(2)}, u32[]{:S(2)}) %collective-permute-start.13) | collective-permute-done | bytes 589856 | tf_op jit(solution)/shard_map/ppermute | solution.py:362
  148.1 2.9 %collective-permute-done.14.refs_4_ = f32[4,288,128]{2,1,0:T(8,128)} collective-permute-done((f32[4,288,128]{2,1,0:T(8,128)}, f32[4,288,128]{2,1,0:T(8,128)}, u32[]{:S(2)}, u32[]{:S(2)}) %collective-permute-start.14) | collective-permute-done | bytes 589856 | tf_op jit(solution)/shard_map/ppermute | solution.py:362
  151.1 1.4 copy-done.1
  157.8 16.7 %convolve.1 = f32[256,4096]{1,0:T(8,128)} custom-call(f32[8,288,128]{2,1,0:T(8,128)} %bitcast_dynamic-update-slice_fusion.refs_0_, f32[8,288,128]{2,1,0:T(8,128)S(1)} %copy-done.5, f32[8,288,128]{2,1,0:T(8,128)S(1)} %copy-done.3, f32[4,288,128]{2,1,0:T(8,128)S(1)} %collective-permute-done.13.refs_3_, f32[4,288,128]{2,1,0:T(8,128)} %collective-permute-done.14.refs_4_, ...), custom_call_target="tpu_custom_call" | custom-call | flops 15000000512 | bytes 10000000 | tf_op jit(solution)/shard_map/convolve/pallas_call | solution.py:525
  174.5 4.7 %subtract.1 = f32[1,256,4096]{2,1,0:T(8,128)} custom-call(f32[8,160,512]{2,1,0:T(8,128)S(1)} %all-to-all-done.1.sci_ref, f32[1,256,4096]{2,1,0:T(8,128)} %bitcast.18), custom_call_target="tpu_custom_call", output_to_operand_aliasing={{}: (1, {})} | custom-call | flops 1000000 | bytes 6000000 | tf_op jit(solution)/shard_map/subtract/pallas_call | solution.py:528
  (55 shorter events, 22.7 us)
Async XLA Ops:
  18.8 26.7 %collective-permute-start = (f32[2,1032,128]{2,1,0:T(8,128)}, f32[2,1032,128]{2,1,0:T(8,128)}, u32[]{:S(2)}, u32[]{:S(2)}) collective-permute-start(f32[2,1032,128]{2,1,0:T(8,128)} %get-tuple-element.28), channel_id=1, source_target_pairs={{0,8},{8,0},{16,24},{24,16},{1,9},{9,1},{17,25},{25,17},{2,10},{10... | collective-permute-start | bytes 3170312 | tf_op jit(solution)/shard_map/ppermute | solution.py:362
  21.4 27.3 %collective-permute-start.2 = (f32[2,1032,128]{2,1,0:T(8,128)}, f32[2,1032,128]{2,1,0:T(8,128)}, u32[]{:S(2)}, u32[]{:S(2)}) collective-permute-start(f32[2,1032,128]{2,1,0:T(8,128)} %get-tuple-element.30), channel_id=1, source_target_pairs={{0,16},{8,24},{16,0},{24,8},{1,17},{9,25},{17,1},{25,9},{2,18},{10... | collective-permute-start | bytes 3170312 | tf_op jit(solution)/shard_map/ppermute | solution.py:362
  22.9 22.6 %copy-start.10 = (f32[2,1032,128]{2,1,0:T(8,128)S(1)}, f32[2,1032,128]{2,1,0:T(8,128)}, u32[]{:S(2)}) copy-start(f32[2,1032,128]{2,1,0:T(8,128)} %get-tuple-element.27.refs_0_) | copy-start | bytes 3170308
  22.9 71.2 %all-to-all-start = ((f32[8,96,512]{2,1,0:T(8,128)}), f32[8,96,512]{2,1,0:T(8,128)S(1)}, u32[]{:S(2)}, u32[]{:S(2)}) async-start(f32[8,96,512]{2,1,0:T(8,128)} %get-tuple-element.26), calls=%async_computation | async-start | bytes 3145728 | tf_op jit(solution)/shard_map/all_to_all | solution.py:421
  28.3 20.4 %copy-start.11 = (f32[2,1032,128]{2,1,0:T(8,128)S(1)}, f32[2,1032,128]{2,1,0:T(8,128)}, u32[]{:S(2)}) copy-start(f32[2,1032,128]{2,1,0:T(8,128)} %get-tuple-element.29.refs_3_) | copy-start | bytes 3170308
  46.6 13.7 %collective-permute-start.1 = (f32[1,1032,128]{2,1,0:T(8,128)S(1)}, f32[1,1032,128]{2,1,0:T(8,128)S(1)}, u32[]{:S(2)}, u32[]{:S(2)}) collective-permute-start(f32[1,1032,128]{2,1,0:T(8,128)S(1)} %slice_add_fusion.1), channel_id=1, source_target_pairs={{0,16},{8,24},{16,0},{24,8},{1,17},{9,25},{17,1},{25,9},{2,18},{10... | collective-permute-start | bytes 1585160 | tf_op jit(solution)/shard_map/ppermute | solution.py:362
  49.8 13.2 %collective-permute-start.3 = (f32[1,1032,128]{2,1,0:T(8,128)S(1)}, f32[1,1032,128]{2,1,0:T(8,128)S(1)}, u32[]{:S(2)}, u32[]{:S(2)}) collective-permute-start(f32[1,1032,128]{2,1,0:T(8,128)S(1)} %slice_add_fusion), channel_id=1, source_target_pairs={{0,8},{8,0},{16,24},{24,16},{1,9},{9,1},{17,25},{25,17},{2,10},{10... | collective-permute-start | bytes 1585160 | tf_op jit(solution)/shard_map/ppermute | solution.py:362
  60.3 2.7 %copy-start.12 = (f32[1,1032,128]{2,1,0:T(8,128)}, f32[1,1032,128]{2,1,0:T(8,128)S(1)}, u32[]{:S(2)}) copy-start(f32[1,1032,128]{2,1,0:T(8,128)S(1)} %collective-permute-done.1.refs_2_) | copy-start | bytes 1585156
  67.8 6.0 %collective-permute-start.4 = (f32[288,128]{1,0:T(8,128)}, f32[288,128]{1,0:T(8,128)S(1)}, u32[]{:S(2)}, u32[]{:S(2)}) collective-permute-start(f32[288,128]{1,0:T(8,128)} %get-tuple-element.32), channel_id=1, source_target_pairs={{0,1},{1,0},{2,3},{3,2},{4,5},{5,4},{6,7},{7,6},{8,9},{9,8},{10,11... | collective-permute-start | bytes 442376 | tf_op jit(solution)/shard_map/ppermute | solution.py:472
  67.8 12.0 %collective-permute-start.5 = (f32[288,128]{1,0:T(8,128)}, f32[288,128]{1,0:T(8,128)S(1)}, u32[]{:S(2)}, u32[]{:S(2)}) collective-permute-start(f32[288,128]{1,0:T(8,128)} %get-tuple-element.33), channel_id=1, source_target_pairs={{0,2},{1,3},{2,0},{3,1},{4,6},{5,7},{6,4},{7,5},{8,10},{9,11},{10,... | collective-permute-start | bytes 442376 | tf_op jit(solution)/shard_map/ppermute | solution.py:472
  68.3 13.6 %collective-permute-start.6 = (f32[288,128]{1,0:T(8,128)}, f32[288,128]{1,0:T(8,128)S(1)}, u32[]{:S(2)}, u32[]{:S(2)}) collective-permute-start(f32[288,128]{1,0:T(8,128)} %get-tuple-element.34), channel_id=1, source_target_pairs={{0,3},{1,2},{2,1},{3,0},{4,7},{5,6},{6,5},{7,4},{8,11},{9,10},{10,... | collective-permute-start | bytes 442376 | tf_op jit(solution)/shard_map/ppermute | solution.py:472
  69.6 13.0 %collective-permute-start.7 = (f32[288,128]{1,0:T(8,128)}, f32[288,128]{1,0:T(8,128)S(1)}, u32[]{:S(2)}, u32[]{:S(2)}) collective-permute-start(f32[288,128]{1,0:T(8,128)} %get-tuple-element.35), channel_id=1, source_target_pairs={{0,4},{1,5},{2,6},{3,7},{4,0},{5,1},{6,2},{7,3},{8,12},{9,13},{10,... | collective-permute-start | bytes 442376 | tf_op jit(solution)/shard_map/ppermute | solution.py:472
  71.5 20.6 %collective-permute-start.8 = (f32[288,128]{1,0:T(8,128)}, f32[288,128]{1,0:T(8,128)S(1)}, u32[]{:S(2)}, u32[]{:S(2)}) collective-permute-start(f32[288,128]{1,0:T(8,128)} %get-tuple-element.36), channel_id=1, source_target_pairs={{0,5},{1,4},{2,7},{3,6},{4,1},{5,0},{6,3},{7,2},{8,13},{9,12},{10,... | collective-permute-start | bytes 442376 | tf_op jit(solution)/shard_map/ppermute | solution.py:472
  73.8 18.9 %collective-permute-start.9 = (f32[288,128]{1,0:T(8,128)}, f32[288,128]{1,0:T(8,128)S(1)}, u32[]{:S(2)}, u32[]{:S(2)}) collective-permute-start(f32[288,128]{1,0:T(8,128)} %get-tuple-element.37), channel_id=1, source_target_pairs={{0,6},{1,7},{2,4},{3,5},{4,2},{5,3},{6,0},{7,1},{8,14},{9,15},{10,... | collective-permute-start | bytes 442376 | tf_op jit(solution)/shard_map/ppermute | solution.py:472
  79.8 13.6 %collective-permute-start.10 = (f32[288,128]{1,0:T(8,128)}, f32[288,128]{1,0:T(8,128)S(1)}, u32[]{:S(2)}, u32[]{:S(2)}) collective-permute-start(f32[288,128]{1,0:T(8,128)} %get-tuple-element.38), channel_id=1, source_target_pairs={{0,7},{1,6},{2,5},{3,4},{4,3},{5,2},{6,1},{7,0},{8,15},{9,14},{10,... | collective-permute-start | bytes 442376 | tf_op jit(solution)/shard_map/ppermute | solution.py:472
  95.2 79.3 %all-to-all-start.1 = ((f32[8,160,512]{2,1,0:T(8,128)}), f32[8,160,512]{2,1,0:T(8,128)S(1)}, u32[]{:S(2)}, u32[]{:S(2)}) async-start(f32[8,160,512]{2,1,0:T(8,128)} %get-tuple-element.39), calls=%async_computation.1 | async-start | bytes 5242880 | tf_op jit(solution)/shard_map/all_to_all | solution.py:475
  103.6 47.5 %copy-start.6 = (f32[4,2,6]{2,1,0:T(2,128)S(1)}, f32[4,2,6]{2,1,0:T(2,128)}, u32[]{:S(2)}) copy-start(f32[4,2,6]{2,1,0:T(2,128)} %refs_5_.1) | copy-start | bytes 580
  103.6 28.6 %collective-permute-start.12 = (f32[8,288,128]{2,1,0:T(8,128)}, f32[8,288,128]{2,1,0:T(8,128)S(1)}, u32[]{:S(2)}, u32[]{:S(2)}) collective-permute-start(f32[8,288,128]{2,1,0:T(8,128)} %bitcast_dynamic-update-slice_fusion.refs_0_), channel_id=1, source_target_pairs={{0,16},{8,24},{16,0},{24,8},{1,17},{9,25},{17,1},{25,9},{2,18},{10... | collective-permute-start | bytes 3538952 | tf_op jit(solution)/shard_map/ppermute | solution.py:362
  104.8 29.5 %collective-permute-start.11 = (f32[8,288,128]{2,1,0:T(8,128)}, f32[8,288,128]{2,1,0:T(8,128)S(1)}, u32[]{:S(2)}, u32[]{:S(2)}) collective-permute-start(f32[8,288,128]{2,1,0:T(8,128)} %bitcast_dynamic-update-slice_fusion.refs_0_), channel_id=1, source_target_pairs={{0,8},{8,0},{16,24},{24,16},{1,9},{9,1},{17,25},{25,17},{2,10},{10... | collective-permute-start | bytes 3538952 | tf_op jit(solution)/shard_map/ppermute | solution.py:362
  132.2 3.0 %copy-start.2 = (f32[8,288,128]{2,1,0:T(8,128)}, f32[8,288,128]{2,1,0:T(8,128)S(1)}, u32[]{:S(2)}) copy-start(f32[8,288,128]{2,1,0:T(8,128)S(1)} %collective-permute-done.12.refs_2_) | copy-start | bytes 3538948
  133.1 15.0 %collective-permute-start.13 = (f32[4,288,128]{2,1,0:T(8,128)}, f32[4,288,128]{2,1,0:T(8,128)S(1)}, u32[]{:S(2)}, u32[]{:S(2)}) collective-permute-start(f32[4,288,128]{2,1,0:T(8,128)} %slice.26), channel_id=1, source_target_pairs={{0,8},{8,0},{16,24},{24,16},{1,9},{9,1},{17,25},{25,17},{2,10},{10... | collective-permute-start | bytes 1769480 | tf_op jit(solution)/shard_map/ppermute | solution.py:362
  136.2 14.8 %collective-permute-start.14 = (f32[4,288,128]{2,1,0:T(8,128)}, f32[4,288,128]{2,1,0:T(8,128)}, u32[]{:S(2)}, u32[]{:S(2)}) collective-permute-start(f32[4,288,128]{2,1,0:T(8,128)} %slice.27), channel_id=1, source_target_pairs={{0,16},{8,24},{16,0},{24,8},{1,17},{9,25},{17,1},{25,9},{2,18},{10... | collective-permute-start | bytes 1769480 | tf_op jit(solution)/shard_map/ppermute | solution.py:362
  151.1 1.4 copy-start.1
  152.5 1.3 copy-start.3
  (7 other events, 7.0 us)

commit v7 on v5

--- a/solution.py
+++ b/solution.py
@@ -52,7 +52,7 @@
 def warp_kernel(
     geom, kind_ref, heights_ref, invvar_ref, raw_ref, rmat_ref, cmat_ref,
     sci_a, sci_b, keep_a, send_a, keep_b, send_b,
-    sci_s, num_s, wt_s, rmat_s, cmat_s, chi_s, clo_s, top_s, ready_s, fetch_sems, sems, wt_sems,
+    sci_s, num_s, wt_s, wide_s, rmat_s, cmat_s, chi_s, clo_s, top_s, ready_s, fetch_sems, sems, wt_sems,
 ):
     epochs, nrow, share, orders, tiles = geom
     step = pl.program_id(0)
@@ -65,10 +65,11 @@
     block = lax.div(first_tile, per_col)
     offset_in = lax.rem(first_tile, per_col)
     kinds = cmat_ref.shape[0]
-    strips, rows_a, _ = sci_a.shape
+    strips = sci_a.shape[0]
+    rows_dev = nrow // strips
     rows_b = sci_b.shape[1]
+    rows_a = rows_dev - rows_b
     edge = rows_b // 2
-    rows_dev = rows_a + rows_b
     nhalf = nrow // 2
     bhalf = strips // 2 * rows_b
     outs = (keep_a, send_a), (keep_b, send_b)
@@ -82,7 +83,7 @@
     def strip_copies(s):
         base = s * rows_dev
         part = base // nhalf
-        pairs = [(sci_s.at[pl.ds(base + edge, rows_a)], sci_a.at[s])]
+        pairs = [(sci_s.at[pl.ds(base + edge, rows_a)], sci_a.at[s, pl.ds(0, rows_a)])]
         for i in range(2):
             source = pl.ds(base + i * (rows_dev - edge), edge)
             pairs.append((sci_s.at[source], sci_b.at[s, pl.ds(i * edge, edge)]))
@@ -186,6 +187,15 @@
                             wt_sems.at[len(copies)],
                         )
                     )
+        per_strip = rows_dev // share
+        wide_s[...] = jnp.zeros_like(wide_s)
+        for s in range(strips):
+            wide_s[s, pl.ds(0, per_strip), pl.ds(0, share)] = wt_s[pl.ds(s * per_strip, per_strip), :]
+            copies.append(
+                pltpu.make_async_copy(
+                    wide_s.at[s], sci_a.at[s, pl.ds(rows_a, wide_s.shape[1])], wt_sems.at[len(copies)]
+                )
+            )
         start_and_wait(copies)
         for s in range(strips):
             for copy in strip_copies(s):
@@ -235,41 +245,25 @@
         out_refs[k][...] = pad_s[pl.ds(pl.multiple_of(strip * rows_b, 8), long), :]
 
 
-def weigh_kernel(geom, heights_ref, invvar_ref, sci_ref, *refs):
+def weigh_kernel(geom, sci_ref, *refs):
     epochs, orders, share = geom
     outs, num_s = refs[:4], refs[4]
-    blocks, rows_a, _ = sci_ref.shape
-    per_col = heights_ref.shape[2]
-    tiles = invvar_ref.shape[1]
-    sources = per_col // tiles
-    me, strip = lax.axis_index("epoch"), lax.axis_index("strip")
-    first = strip * ROWS_DEV + EDGE
+    blocks = sci_ref.shape[0]
+    rows_a = ROWS_DEV - 2 * EDGE
+    per_strip = ROWS_DEV // share
+    me = lax.axis_index("epoch")
     half = blocks // 2
-    long = outs[0].shape[1]
-    flat_shape = (long - half * rows_a, share)
-    pitch = pl.cdiv(rows_a, share) * share
-    flat = lax.broadcasted_iota(jnp.int32, flat_shape, 0) * share + lax.broadcasted_iota(jnp.int32, flat_shape, 1)
-    row = lax.broadcasted_iota(jnp.int32, (rows_a, share), 0) + first
     for part in range(2):
-        wide = jnp.zeros(flat_shape, F32)
         for b in range(half):
             block = part * half + b
-            sky = flat - b * pitch
-            mine = (sky >= 0) & (sky < rows_a)
-            sky = sky + first
-            weight = jnp.zeros((rows_a, share), F32)
-            top = jnp.int32(0)
-            for t in range(per_col):
-                height = heights_ref[0, block, t]
-                value = invvar_ref[jnp.bitwise_xor(block * sources + t // tiles, strip), t % tiles]
-                weight = jnp.where((row >= top) & (row < top + height), value, weight)
-                wide = jnp.where(mine & (sky >= top) & (sky < top + height), value, wide)
-                top = top + height
+            lines = sci_ref[block, pl.ds(rows_a, 8), pl.ds(0, share)][:per_strip]
+            below = jnp.concatenate([upright(lines[i : i + 1], share) for i in range(per_strip)], axis=0)
+            weight = below[EDGE : EDGE + rows_a]
             for q in range(epochs):
-                piece = sci_ref[block, :, pl.ds(q * share, share)]
+                piece = sci_ref[block, pl.ds(0, rows_a), pl.ds(q * share, share)]
                 num_s[jnp.bitwise_xor(me, q), pl.ds(b * rows_a, rows_a), :] = weight * piece
-        for j in range(epochs):
-            num_s[j, pl.ds(half * rows_a, flat_shape[0]), :] = wide
+            for j in range(epochs):
+                num_s[j, pl.ds(half * rows_a + b * per_strip, per_strip), :] = lines
         for slots, out in zip(slot_order(epochs, orders[part]), outs[2 * part : 2 * part + 2]):
             for place, j in enumerate(slots):
                 out[place] = num_s[j]
@@ -288,12 +282,13 @@
     for part in range(2):
         own = term_refs[part * terms : (part + 1) * terms]
         weights = added(own, pl.ds(half * rows_a, own[0].shape[1] - half * rows_a))
-        lines = pl.cdiv(rows_a, share)
+        per_strip = ROWS_DEV // share
         for b in range(half):
             below = jnp.concatenate(
-                [upright(weights[b * lines + i : b * lines + i + 1, :], share) for i in range(lines)], axis=0
+                [upright(weights[b * per_strip + i : b * per_strip + i + 1, :], share) for i in range(per_strip)],
+                axis=0,
             )
-            value = added(own, pl.ds(b * rows_a, rows_a)) / below[:rows_a]
+            value = added(own, pl.ds(b * rows_a, rows_a)) / below[EDGE : EDGE + rows_a]
             out_ref[jnp.bitwise_xor(home, part * half + b), pl.ds(above, rows_a), :] = value
 
 
@@ -455,7 +450,7 @@
     vmem = pl.BlockSpec(memory_space=pltpu.VMEM)
     kinds = col_interp.shape[0]
 
-    sci_shapes = [jax.ShapeDtypeStruct((strips, rows, tile_cols), F32) for rows in (rows_a, rows_b)]
+    sci_shapes = [jax.ShapeDtypeStruct((strips, rows, tile_cols), F32) for rows in (rows_a + 8, rows_b)]
     send_shape = jax.ShapeDtypeStruct((epochs // 2, long_half, share), F32)
     together = 2 if tiles % 2 == 0 else 1
     sci_a, sci_b, keep_a, send_a, keep_b, send_b = pl.pallas_call(
@@ -475,6 +470,7 @@
             pltpu.VMEM((nrow, tile_cols), F32),
             pltpu.VMEM((epochs, nrow, share), F32),
             pltpu.VMEM((wrows, share), F32),
+            pltpu.VMEM((strips, 8, tile_cols), F32),
             pltpu.VMEM((kinds, tile_rows, tile_rows), F32),
             pltpu.VMEM((kinds, tile_cols, tile_cols), F32),
             pltpu.VMEM((kinds, tile_cols, tile_cols), BF16),
@@ -483,18 +479,13 @@
             pltpu.SMEM((kinds,), jnp.int32),
             pltpu.SemaphoreType.DMA((kinds, 2)),
             pltpu.SemaphoreType.DMA((strips, 3 + 2 * epochs)),
-            pltpu.SemaphoreType.DMA((2 * epochs,)),
+            pltpu.SemaphoreType.DMA((2 * epochs + strips,)),
         ],
         name="warp",
         cost_estimate=pl.CostEstimate(flops=8_000_000_000, bytes_accessed=20_000_000, transcendentals=0),
     )(tile_kind, tile_heights, tile_invvar, raw_tiles[0], row_interp, col_interp)
 
     got_a = lax.all_to_all(sci_a, "strip", split_axis=0, concat_axis=0, tiled=True)
-    invvars = [tile_invvar]
-    for k in range(1, strips):
-        invvars.append(lax.ppermute(tile_invvar, "strip", [(i, i ^ k) for i in range(strips)]))
-    invvars = jnp.concatenate(invvars, axis=0)
-
     basis, _, _ = psf_profiles.shape
     build_bands = pl.pallas_call(
         bands_kernel,
@@ -552,22 +543,20 @@
     side_a = got_a
     if sources > 1:
         side_a = jnp.sum(got_a.reshape((blocks, sources) + got_a.shape[1:]), axis=1)
-    long_a = blocks // 2 * rows_a + 8 * pl.cdiv(blocks // 2 * pl.cdiv(rows_a, share), 8)
+    long_a = blocks // 2 * (rows_a + ROWS_DEV // share)
     weighted_shape = jax.ShapeDtypeStruct((epochs // 2, long_a, share), F32)
     weigh = pl.pallas_call(
         functools.partial(weigh_kernel, (epochs, orders, share)),
-        in_specs=[smem, smem, vmem],
+        in_specs=[vmem],
         out_specs=[vmem] * 4,
         out_shape=[weighted_shape] * 4,
         scratch_shapes=[pltpu.VMEM((epochs, long_a, share), F32)],
         name="weigh",
         cost_estimate=pl.CostEstimate(flops=2_000_000, bytes_accessed=2_500_000, transcendentals=0),
     )
-    weighted = weigh(tile_heights, invvars, side_a)
+    weighted = weigh(side_a)
     middle_terms = reduced(weighted[0::2], weighted[1::2])
     outer = came[::sources]
-    for part in range(2):
-        sci_b, middle_terms[part][-1] = lax.optimization_barrier((sci_b, middle_terms[part][-1]))
     sci_b, got_a, *outer = lax.optimization_barrier((sci_b, got_a, *outer))
     merge = pl.pallas_call(
         functools.partial(middle_kernel, len(middle_terms[0])),

time: 213 us -> 193 us (0.906)
  the two profiles are of different devices: /device:TPU:9 before, /device:TPU:0 now
where the time goes in v7:
time: 193 us; the launch traced here: 192 us
  waiting for transfers between devices  81.5 us (42%)
  Pallas kernels  55.9 us (29%)
  starting transfers between devices  37.8 us (20%)
  local copies, waits for them, and re-layouts  14.6 us (8%)
  other arithmetic  2.3 us (1%)
    ppermute x12, waiting for transfers between devices, swap(): return lax.ppermute(value, axis, [(i, i ^ 1 << bit) for i in range(count)])  69.4 us
    pallas_call x1, Pallas kernels, shards(): pl.pallas_call(functools.partial(warp_kernel, (epochs, nrow, share, order...  19.5 us
    pallas_call x1, Pallas kernels, shards(): matched = convolve(*arrays, psf_poly, toep_hi, toep_lo, band, got_a)  18 us
    ppermute x12, starting transfers between devices, swap(): return lax.ppermute(value, axis, [(i, i ^ 1 << bit) for i in range(count)])  16.5 us
    unnamed x54, local copies, waits for them, and re-layouts  12.8 us
    ppermute x7, waiting for transfers between devices, shards(): lax.ppermute(parts[k], 'strip', [(i, i ^ k) for i in range(strips)])  12.1 us
    ppermute x7, starting transfers between devices, shards(): lax.ppermute(parts[k], 'strip', [(i, i ^ k) for i in range(strips)])  8.53 us
    pallas_call x1, Pallas kernels, shards(): pl.pallas_call(subtract_kernel, grid=(2 * outside,), in_specs=[vmem, rest...  6.79 us
  transfers between devices with their start and end apart: 21, of which 13 were waited for; matrix products, arithmetic and copies ran while one was open for 2% of the time, Pallas kernels for 15%

profile of v7, /device:TPU:0, one launch (start us, length us, event | category | flops | bytes accessed | tf_op | source)
XLA Modules:
  0.0 192.3 jit_solution(17352975813682574873)
XLA Ops:
  0.0 19.5 %warp.1 = (f32[8,104,512]{2,1,0:T(8,128)}, f32[8,160,512]{2,1,0:T(8,128)}, f32[2,648,128]{2,1,0:T(8,128)}, f32[2,648,128]{2,1,0:T(8,128)}, f32[2,648,128]{2,1,0:T(8,128)}, /*index=5*/f32[2,648,128]{2,1,0:T(8,128)}) custom-call(s32[1,12]{1,0:T(1,128)} %kind_ref.1, s32[1,8,12]{2,1,0:T(8,128)} %heights_ref.1, f32[1,12]{1,0:T(1,128)} %invvar_ref.1, ...), custom_call_target="tpu_custom_call" | custom-call | flops 8000000000 | bytes 20000000 | tf_op jit(solution)/shard_map/warp/pallas_call | solution.py:456
  19.5 6.4 %all-to-all-start = ((f32[8,104,512]{2,1,0:T(8,128)}), f32[8,104,512]{2,1,0:T(8,128)S(1)}, u32[]{:S(2)}, u32[]{:S(2)}) async-start(f32[8,104,512]{2,1,0:T(8,128)} %get-tuple-element.37), calls=%async_computation | async-start | bytes 3407872 | tf_op jit(solution)/shard_map/all_to_all | solution.py:488
  27.0 1.9 %collective-permute-start.2 = (f32[2,648,128]{2,1,0:T(8,128)}, f32[2,648,128]{2,1,0:T(8,128)S(1)}, u32[]{:S(2)}, u32[]{:S(2)}) collective-permute-start(f32[2,648,128]{2,1,0:T(8,128)} %get-tuple-element.41), channel_id=1, source_target_pairs={{0,16},{8,24},{16,0},{24,8},{1,17},{9,25},{17,1},{25,9},{2,18},{10... | collective-permute-start | bytes 1990664 | tf_op jit(solution)/shard_map/ppermute | solution.py:430
  29.0 14.5 %collective-permute-done.refs_1_ = f32[2,648,128]{2,1,0:T(8,128)S(1)} collective-permute-done((f32[2,648,128]{2,1,0:T(8,128)}, f32[2,648,128]{2,1,0:T(8,128)S(1)}, u32[]{:S(2)}, u32[]{:S(2)}) %collective-permute-start) | collective-permute-done | bytes 663584 | tf_op jit(solution)/shard_map/ppermute | solution.py:430
  44.9 1.8 collective-permute-start.3
  46.8 6.2 %collective-permute-done.1.refs_2_ = f32[1,648,128]{2,1,0:T(8,128)S(1)} collective-permute-done((f32[1,648,128]{2,1,0:T(8,128)S(1)}, f32[1,648,128]{2,1,0:T(8,128)S(1)}, u32[]{:S(2)}, u32[]{:S(2)}) %collective-permute-start.1) | collective-permute-done | bytes 331808 | tf_op jit(solution)/shard_map/ppermute | solution.py:430
  54.9 3.1 %template.1 = (f32[192,128]{1,0:T(8,128)}, f32[192,128]{1,0:T(8,128)}, f32[192,128]{1,0:T(8,128)}, f32[192,128]{1,0:T(8,128)}, f32[192,128]{1,0:T(8,128)}, /*ind...) custom-call(f32[2,648,128]{2,1,0:T(8,128)} %get-tuple-element.38.refs_0_, f32[2,648,128]{2,1,0:T(8,128)} %copy-done.13, ...), custom_call_target="tpu_custom_call" | custom-call | flops 2000000 | bytes 5000000 | tf_op jit(solution)/shard_map/template/pallas_call | solution.py:530
  59.9 2.1 %collective-permute-start.7 = (f32[192,128]{1,0:T(8,128)}, f32[192,128]{1,0:T(8,128)S(1)}, u32[]{:S(2)}, u32[]{:S(2)}) collective-permute-start(f32[192,128]{1,0:T(8,128)} %get-tuple-element.46), channel_id=1, source_target_pairs={{0,4},{1,5},{2,6},{3,7},{4,0},{5,1},{6,2},{7,3},{8,12},{9,13},{10,... | collective-permute-start | bytes 294920 | tf_op jit(solution)/shard_map/ppermute | solution.py:542
  62.5 3.0 %collective-permute-start.9 = (f32[192,128]{1,0:T(8,128)}, f32[192,128]{1,0:T(8,128)S(1)}, u32[]{:S(2)}, u32[]{:S(2)}) collective-permute-start(f32[192,128]{1,0:T(8,128)} %get-tuple-element.48), channel_id=1, source_target_pairs={{0,6},{1,7},{2,4},{3,5},{4,2},{5,3},{6,0},{7,1},{8,14},{9,15},{10,... | collective-permute-start | bytes 294920 | tf_op jit(solution)/shard_map/ppermute | solution.py:542
  65.5 3.9 %collective-permute-done.5.refs_8_ = f32[192,128]{1,0:T(8,128)S(1)} collective-permute-done((f32[192,128]{1,0:T(8,128)}, f32[192,128]{1,0:T(8,128)S(1)}, u32[]{:S(2)}, u32[]{:S(2)}) %collective-permute-start.5) | collective-permute-done | bytes 98336 | tf_op jit(solution)/shard_map/ppermute | solution.py:542
  71.4 6.3 %collective-permute-done.7.refs_10_ = f32[192,128]{1,0:T(8,128)S(1)} collective-permute-done((f32[192,128]{1,0:T(8,128)}, f32[192,128]{1,0:T(8,128)S(1)}, u32[]{:S(2)}, u32[]{:S(2)}) %collective-permute-start.7) | collective-permute-done | bytes 98336 | tf_op jit(solution)/shard_map/ppermute | solution.py:542
  79.9 6.3 %all-to-all-start.1 = ((f32[8,160,512]{2,1,0:T(8,128)}), f32[8,160,512]{2,1,0:T(8,128)S(1)}, u32[]{:S(2)}, u32[]{:S(2)}) async-start(f32[8,160,512]{2,1,0:T(8,128)} %get-tuple-element.50), calls=%async_computation.1 | async-start | bytes 5242880 | tf_op jit(solution)/shard_map/all_to_all | solution.py:570
  86.3 3.0 %weigh.1 = (f32[2,392,128]{2,1,0:T(8,128)}, f32[2,392,128]{2,1,0:T(8,128)}, f32[2,392,128]{2,1,0:T(8,128)}, f32[2,392,128]{2,1,0:T(8,128)}) custom-call(f32[8,104,512]{2,1,0:T(8,128)} %copy-done), custom_call_target="tpu_custom_call" | custom-call | flops 2000000 | bytes 2500000 | tf_op jit(solution)/shard_map/weigh/pallas_call | solution.py:557
  90.1 2.2 %collective-permute-start.13 = (f32[2,392,128]{2,1,0:T(8,128)}, f32[2,392,128]{2,1,0:T(8,128)S(1)}, u32[]{:S(2)}, u32[]{:S(2)}) collective-permute-start(f32[2,392,128]{2,1,0:T(8,128)} %get-tuple-element.54), channel_id=1, source_target_pairs={{0,16},{8,24},{16,0},{24,8},{1,17},{9,25},{17,1},{25,9},{2,18},{10... | collective-permute-start | bytes 1204232 | tf_op jit(solution)/shard_map/ppermute | solution.py:430
  92.3 8.9 %collective-permute-done.11.refs_1_ = f32[2,392,128]{2,1,0:T(8,128)S(1)} collective-permute-done((f32[2,392,128]{2,1,0:T(8,128)}, f32[2,392,128]{2,1,0:T(8,128)S(1)}, u32[]{:S(2)}, u32[]{:S(2)}) %collective-permute-start.11) | collective-permute-done | bytes 401440 | tf_op jit(solution)/shard_map/ppermute | solution.py:430
  104.7 1.8 collective-permute-start.14
  106.5 2.3 %collective-permute-done.12.refs_2_ = f32[1,392,128]{2,1,0:T(8,128)S(1)} collective-permute-done((f32[1,392,128]{2,1,0:T(8,128)S(1)}, f32[1,392,128]{2,1,0:T(8,128)S(1)}, u32[]{:S(2)}, u32[]{:S(2)}) %collective-permute-start.12) | collective-permute-done | bytes 200736 | tf_op jit(solution)/shard_map/ppermute | solution.py:430
  111.2 3.1 %middle.1.refs_0_ = f32[8,288,128]{2,1,0:T(8,128)} custom-call(f32[2,392,128]{2,1,0:T(8,128)} %get-tuple-element.51.refs_0_, f32[2,392,128]{2,1,0:T(8,128)} %copy-done.15, f32[1,392,128]{2,1,0:T(8,128)} %copy-done.19, f32[2,392,128]{2,1,0:T(8,128)} %get-tuple-element.53.refs_3_, f32[2,392,128]{2,1,0:T(8,128)} %copy-done.16, ...), custom_call_target="tpu_custom_call" | custom-call | flops 500000 | bytes 4000000 | tf_op jit(solution)/shard_map/middle/pallas_call | solution.py:569
  116.3 24.7 %collective-permute-done.16.refs_2_ = f32[8,288,128]{2,1,0:T(8,128)S(1)} collective-permute-done((f32[8,288,128]{2,1,0:T(8,128)}, f32[8,288,128]{2,1,0:T(8,128)S(1)}, u32[]{:S(2)}, u32[]{:S(2)}) %collective-permute-start.16) | collective-permute-done | bytes 1179680 | tf_op jit(solution)/shard_map/ppermute | solution.py:430
  147.1 2.4 %bands.1 = (bf16[256,256]{1,0:T(8,128)(2,1)}, bf16[256,256]{1,0:T(8,128)(2,1)}, bf16[2,256,160]{2,1,0:T(8,128)(2,1)}) custom-call(f32[2,2,31]{2,1,0:T(2,128)} %psf_ref.1), custom_call_target="tpu_custom_call" | custom-call | flops 10000000 | bytes 500000 | tf_op jit(solution)/shard_map/bands/pallas_call | solution.py:502
  149.4 6.6 %collective-permute-done.17.refs_3_ = f32[4,288,128]{2,1,0:T(8,128)S(1)} collective-permute-done((f32[4,288,128]{2,1,0:T(8,128)}, f32[4,288,128]{2,1,0:T(8,128)S(1)}, u32[]{:S(2)}, u32[]{:S(2)}) %collective-permute-start.17) | collective-permute-done | bytes 589856 | tf_op jit(solution)/shard_map/ppermute | solution.py:430
  156.0 3.3 %collective-permute-done.18.refs_4_ = f32[4,288,128]{2,1,0:T(8,128)} collective-permute-done((f32[4,288,128]{2,1,0:T(8,128)}, f32[4,288,128]{2,1,0:T(8,128)}, u32[]{:S(2)}, u32[]{:S(2)}) %collective-permute-start.18) | collective-permute-done | bytes 589856 | tf_op jit(solution)/shard_map/ppermute | solution.py:430
  167.4 18.0 %convolve.1 = f32[256,4096]{1,0:T(8,128)} custom-call(f32[8,288,128]{2,1,0:T(8,128)S(1)} %copy-done.2, f32[8,288,128]{2,1,0:T(8,128)S(1)} %copy-done.6, f32[8,288,128]{2,1,0:T(8,128)S(1)} %copy-done.4, f32[4,288,128]{2,1,0:T(8,128)S(1)} %collective-permute-done.17.refs_3_, f32[4,288,128]{2,1,0:T(8,128)} %collective-permute-done.18.refs_4_, ...), custom_call_target="tpu_custom_call" | custom-call | flops 15000000512 | bytes 10000000 | tf_op jit(solution)/shard_map/convolve/pallas_call | solution.py:620
  185.5 6.8 %subtract.1 = f32[1,256,4096]{2,1,0:T(8,128)} custom-call(f32[8,160,512]{2,1,0:T(8,128)S(1)} %all-to-all-done.1.sci_ref, f32[1,256,4096]{2,1,0:T(8,128)} %bitcast.2), custom_call_target="tpu_custom_call", output_to_operand_aliasing={{}: (1, {})} | custom-call | flops 1000000 | bytes 6000000 | tf_op jit(solution)/shard_map/subtract/pallas_call | solution.py:626
  (85 shorter events, 33.9 us)
Async XLA Ops:
  19.5 25.4 %copy-start.12 = (f32[2,648,128]{2,1,0:T(8,128)S(1)}, f32[2,648,128]{2,1,0:T(8,128)}, u32[]{:S(2)}) copy-start(f32[2,648,128]{2,1,0:T(8,128)} %get-tuple-element.40.refs_3_) | copy-start | bytes 1990660
  19.5 59.2 %all-to-all-start = ((f32[8,104,512]{2,1,0:T(8,128)}), f32[8,104,512]{2,1,0:T(8,128)S(1)}, u32[]{:S(2)}, u32[]{:S(2)}) async-start(f32[8,104,512]{2,1,0:T(8,128)} %get-tuple-element.37), calls=%async_computation | async-start | bytes 3407872 | tf_op jit(solution)/shard_map/all_to_all | solution.py:488
  26.0 17.5 %collective-permute-start = (f32[2,648,128]{2,1,0:T(8,128)}, f32[2,648,128]{2,1,0:T(8,128)S(1)}, u32[]{:S(2)}, u32[]{:S(2)}) collective-permute-start(f32[2,648,128]{2,1,0:T(8,128)} %get-tuple-element.39), channel_id=1, source_target_pairs={{0,8},{8,0},{16,24},{24,16},{1,9},{9,1},{17,25},{25,17},{2,10},{10... | collective-permute-start | bytes 1990664 | tf_op jit(solution)/shard_map/ppermute | solution.py:430
  27.0 17.9 %collective-permute-start.2 = (f32[2,648,128]{2,1,0:T(8,128)}, f32[2,648,128]{2,1,0:T(8,128)S(1)}, u32[]{:S(2)}, u32[]{:S(2)}) collective-permute-start(f32[2,648,128]{2,1,0:T(8,128)} %get-tuple-element.41), channel_id=1, source_target_pairs={{0,16},{8,24},{16,0},{24,8},{1,17},{9,25},{17,1},{25,9},{2,18},{10... | collective-permute-start | bytes 1990664 | tf_op jit(solution)/shard_map/ppermute | solution.py:430
  43.5 9.4 %collective-permute-start.1 = (f32[1,648,128]{2,1,0:T(8,128)S(1)}, f32[1,648,128]{2,1,0:T(8,128)S(1)}, u32[]{:S(2)}, u32[]{:S(2)}) collective-permute-start(f32[1,648,128]{2,1,0:T(8,128)S(1)} %slice_add_fusion.1), channel_id=1, source_target_pairs={{0,16},{8,24},{16,0},{24,8},{1,17},{9,25},{17,1},{25,9},{2,18},{10... | collective-permute-start | bytes 995336 | tf_op jit(solution)/shard_map/ppermute | solution.py:430
  44.9 9.2 %collective-permute-start.3 = (f32[1,648,128]{2,1,0:T(8,128)S(1)}, f32[1,648,128]{2,1,0:T(8,128)S(1)}, u32[]{:S(2)}, u32[]{:S(2)}) collective-permute-start(f32[1,648,128]{2,1,0:T(8,128)S(1)} %slice_add_fusion), channel_id=1, source_target_pairs={{0,8},{8,0},{16,24},{24,16},{1,9},{9,1},{17,25},{25,17},{2,10},{10... | collective-permute-start | bytes 995336 | tf_op jit(solution)/shard_map/ppermute | solution.py:430
  58.0 4.5 %collective-permute-start.4 = (f32[192,128]{1,0:T(8,128)}, f32[192,128]{1,0:T(8,128)S(1)}, u32[]{:S(2)}, u32[]{:S(2)}) collective-permute-start(f32[192,128]{1,0:T(8,128)} %get-tuple-element.43), channel_id=1, source_target_pairs={{0,1},{1,0},{2,3},{3,2},{4,5},{5,4},{6,7},{7,6},{8,9},{9,8},{10,11... | collective-permute-start | bytes 294920 | tf_op jit(solution)/shard_map/ppermute | solution.py:542
  58.0 11.4 %collective-permute-start.5 = (f32[192,128]{1,0:T(8,128)}, f32[192,128]{1,0:T(8,128)S(1)}, u32[]{:S(2)}, u32[]{:S(2)}) collective-permute-start(f32[192,128]{1,0:T(8,128)} %get-tuple-element.44), channel_id=1, source_target_pairs={{0,2},{1,3},{2,0},{3,1},{4,6},{5,7},{6,4},{7,5},{8,10},{9,11},{10,... | collective-permute-start | bytes 294920 | tf_op jit(solution)/shard_map/ppermute | solution.py:542
  59.3 12.1 %collective-permute-start.6 = (f32[192,128]{1,0:T(8,128)}, f32[192,128]{1,0:T(8,128)S(1)}, u32[]{:S(2)}, u32[]{:S(2)}) collective-permute-start(f32[192,128]{1,0:T(8,128)} %get-tuple-element.45), channel_id=1, source_target_pairs={{0,3},{1,2},{2,1},{3,0},{4,7},{5,6},{6,5},{7,4},{8,11},{9,10},{10,... | collective-permute-start | bytes 294920 | tf_op jit(solution)/shard_map/ppermute | solution.py:542
  59.9 17.8 %collective-permute-start.7 = (f32[192,128]{1,0:T(8,128)}, f32[192,128]{1,0:T(8,128)S(1)}, u32[]{:S(2)}, u32[]{:S(2)}) collective-permute-start(f32[192,128]{1,0:T(8,128)} %get-tuple-element.46), channel_id=1, source_target_pairs={{0,4},{1,5},{2,6},{3,7},{4,0},{5,1},{6,2},{7,3},{8,12},{9,13},{10,... | collective-permute-start | bytes 294920 | tf_op jit(solution)/shard_map/ppermute | solution.py:542
  62.0 16.7 %collective-permute-start.8 = (f32[192,128]{1,0:T(8,128)}, f32[192,128]{1,0:T(8,128)S(1)}, u32[]{:S(2)}, u32[]{:S(2)}) collective-permute-start(f32[192,128]{1,0:T(8,128)} %get-tuple-element.47), channel_id=1, source_target_pairs={{0,5},{1,4},{2,7},{3,6},{4,1},{5,0},{6,3},{7,2},{8,13},{9,12},{10,... | collective-permute-start | bytes 294920 | tf_op jit(solution)/shard_map/ppermute | solution.py:542
  62.5 48.8 %copy-start.20 = (f32[192,128]{1,0:T(8,128)}, f32[192,128]{1,0:T(8,128)S(1)}, u32[]{:S(2)}) copy-start(f32[192,128]{1,0:T(8,128)S(1)} %collective-permute-done.4.refs_7_) | copy-start | bytes 294916
  62.5 16.2 %collective-permute-start.9 = (f32[192,128]{1,0:T(8,128)}, f32[192,128]{1,0:T(8,128)S(1)}, u32[]{:S(2)}, u32[]{:S(2)}) collective-permute-start(f32[192,128]{1,0:T(8,128)} %get-tuple-element.48), channel_id=1, source_target_pairs={{0,6},{1,7},{2,4},{3,5},{4,2},{5,3},{6,0},{7,1},{8,14},{9,15},{10,... | collective-permute-start | bytes 294920 | tf_op jit(solution)/shard_map/ppermute | solution.py:542
  69.4 9.3 %collective-permute-start.10 = (f32[192,128]{1,0:T(8,128)}, f32[192,128]{1,0:T(8,128)S(1)}, u32[]{:S(2)}, u32[]{:S(2)}) collective-permute-start(f32[192,128]{1,0:T(8,128)} %get-tuple-element.49), channel_id=1, source_target_pairs={{0,7},{1,6},{2,5},{3,4},{4,3},{5,2},{6,1},{7,0},{8,15},{9,14},{10,... | collective-permute-start | bytes 294920 | tf_op jit(solution)/shard_map/ppermute | solution.py:542
  79.9 105.5 %all-to-all-start.1 = ((f32[8,160,512]{2,1,0:T(8,128)}), f32[8,160,512]{2,1,0:T(8,128)S(1)}, u32[]{:S(2)}, u32[]{:S(2)}) async-start(f32[8,160,512]{2,1,0:T(8,128)} %get-tuple-element.50), calls=%async_computation.1 | async-start | bytes 5242880 | tf_op jit(solution)/shard_map/all_to_all | solution.py:570
  89.2 11.9 %collective-permute-start.11 = (f32[2,392,128]{2,1,0:T(8,128)}, f32[2,392,128]{2,1,0:T(8,128)S(1)}, u32[]{:S(2)}, u32[]{:S(2)}) collective-permute-start(f32[2,392,128]{2,1,0:T(8,128)} %get-tuple-element.52), channel_id=1, source_target_pairs={{0,8},{8,0},{16,24},{24,16},{1,9},{9,1},{17,25},{25,17},{2,10},{10... | collective-permute-start | bytes 1204232 | tf_op jit(solution)/shard_map/ppermute | solution.py:430
  90.1 13.5 %collective-permute-start.13 = (f32[2,392,128]{2,1,0:T(8,128)}, f32[2,392,128]{2,1,0:T(8,128)S(1)}, u32[]{:S(2)}, u32[]{:S(2)}) collective-permute-start(f32[2,392,128]{2,1,0:T(8,128)} %get-tuple-element.54), channel_id=1, source_target_pairs={{0,16},{8,24},{16,0},{24,8},{1,17},{9,25},{17,1},{25,9},{2,18},{10... | collective-permute-start | bytes 1204232 | tf_op jit(solution)/shard_map/ppermute | solution.py:430
  102.3 6.6 %collective-permute-start.12 = (f32[1,392,128]{2,1,0:T(8,128)S(1)}, f32[1,392,128]{2,1,0:T(8,128)S(1)}, u32[]{:S(2)}, u32[]{:S(2)}) collective-permute-start(f32[1,392,128]{2,1,0:T(8,128)S(1)} %slice_add_fusion.3), channel_id=1, source_target_pairs={{0,16},{8,24},{16,0},{24,8},{1,17},{9,25},{17,1},{25,9},{2,18},{10... | collective-permute-start | bytes 602120 | tf_op jit(solution)/shard_map/ppermute | solution.py:430
  104.7 54.7 %copy-start.7 = (f32[4,2,6]{2,1,0:T(2,128)S(1)}, f32[4,2,6]{2,1,0:T(2,128)}, u32[]{:S(2)}) copy-start(f32[4,2,6]{2,1,0:T(2,128)} %refs_5_.1) | copy-start | bytes 580
  104.7 6.5 %collective-permute-start.14 = (f32[1,392,128]{2,1,0:T(8,128)S(1)}, f32[1,392,128]{2,1,0:T(8,128)}, u32[]{:S(2)}, u32[]{:S(2)}) collective-permute-start(f32[1,392,128]{2,1,0:T(8,128)S(1)} %slice_add_fusion.2), channel_id=1, source_target_pairs={{0,8},{8,0},{16,24},{24,16},{1,9},{9,1},{17,25},{25,17},{2,10},{10... | collective-permute-start | bytes 602120 | tf_op jit(solution)/shard_map/ppermute | solution.py:430
  114.3 26.7 %collective-permute-start.16 = (f32[8,288,128]{2,1,0:T(8,128)}, f32[8,288,128]{2,1,0:T(8,128)S(1)}, u32[]{:S(2)}, u32[]{:S(2)}) collective-permute-start(f32[8,288,128]{2,1,0:T(8,128)} %middle.1.refs_0_), channel_id=1, source_target_pairs={{0,16},{8,24},{16,0},{24,8},{1,17},{9,25},{17,1},{25,9},{2,18},{10... | collective-permute-start | bytes 3538952 | tf_op jit(solution)/shard_map/ppermute | solution.py:430
  115.0 29.5 %collective-permute-start.15 = (f32[8,288,128]{2,1,0:T(8,128)}, f32[8,288,128]{2,1,0:T(8,128)S(1)}, u32[]{:S(2)}, u32[]{:S(2)}) collective-permute-start(f32[8,288,128]{2,1,0:T(8,128)} %middle.1.refs_0_), channel_id=1, source_target_pairs={{0,8},{8,0},{16,24},{24,16},{1,9},{9,1},{17,25},{25,17},{2,10},{10... | collective-permute-start | bytes 3538952 | tf_op jit(solution)/shard_map/ppermute | solution.py:430
  142.9 13.2 %collective-permute-start.17 = (f32[4,288,128]{2,1,0:T(8,128)}, f32[4,288,128]{2,1,0:T(8,128)S(1)}, u32[]{:S(2)}, u32[]{:S(2)}) collective-permute-start(f32[4,288,128]{2,1,0:T(8,128)} %slice.44), channel_id=1, source_target_pairs={{0,8},{8,0},{16,24},{24,16},{1,9},{9,1},{17,25},{25,17},{2,10},{10... | collective-permute-start | bytes 1769480 | tf_op jit(solution)/shard_map/ppermute | solution.py:430
  146.5 12.9 %collective-permute-start.18 = (f32[4,288,128]{2,1,0:T(8,128)}, f32[4,288,128]{2,1,0:T(8,128)}, u32[]{:S(2)}, u32[]{:S(2)}) collective-permute-start(f32[4,288,128]{2,1,0:T(8,128)} %slice.45), channel_id=1, source_target_pairs={{0,16},{8,24},{16,0},{24,8},{1,17},{9,25},{17,1},{25,9},{2,18},{10... | collective-permute-start | bytes 1769480 | tf_op jit(solution)/shard_map/ppermute | solution.py:430
  (24 other events, 78.7 us)

commit v8 on v3

--- a/solution.py
+++ b/solution.py
@@ -243,7 +243,7 @@
     slots, nrow, ncol = geom
     count = max(len(slots), 1) + (len(slots) > 1)
     tile_refs = refs[:count]
-    poly_ref, toep_hi, toep_lo, band_ref, sci_ref, out_ref, pad_s, row_s, sems = refs[count:]
+    poly_ref, toep_hi, toep_lo, band_ref, sci_ref, out_ref, pad_s, row_s = refs[count:]
     step = pl.program_id(0)
     blocks = pl.num_programs(0)
     tiles = pad_s.shape[0] - 2
@@ -256,32 +256,25 @@
         if not slots:
             for i in range(per_step):
                 place = b * per_step + i
-                pltpu.make_async_copy(tile_refs[0].at[place], pad_s.at[1 + place], sems.at[b, i]).start()
+                pad_s[1 + place] = tile_refs[0][place]
             return
         at = jnp.bitwise_xor(strip, b)
-        for n, slot in enumerate(slots):
-            target = pad_s.at[1 + b * per_step + jnp.bitwise_xor(me, slot)]
-            if n < len(slots) - 1:
-                pltpu.make_async_copy(tile_refs[n].at[at], target, sems.at[b, n]).start()
-                continue
-            cut = tile_refs[n].shape[0]
-
-            @pl.when(at < cut)
-            def _():
-                pltpu.make_async_copy(tile_refs[n].at[at], target, sems.at[b, n]).start()
-
-            @pl.when(at >= cut)
-            def _():
-                pltpu.make_async_copy(tile_refs[n + 1].at[at - cut], target, sems.at[b, n]).start()
-
-    def await_block(b):
-        for i in range(per_step):
-            pltpu.make_async_copy(tile_refs[0].at[0], pad_s.at[1], sems.at[b, i]).wait()
+        for n, slot in enumerate(slots[:-1]):
+            pad_s[1 + b * per_step + jnp.bitwise_xor(me, slot)] = tile_refs[n][at]
+        place = 1 + b * per_step + jnp.bitwise_xor(me, slots[-1])
+        cut = tile_refs[-1].shape[0]
+
+        @pl.when(at < cut)
+        def _():
+            pad_s[place] = tile_refs[-2][at]
+
+        @pl.when(at >= cut)
+        def _():
+            pad_s[place] = tile_refs[-1][at - cut]
 
     @pl.when(step == 0)
     def _():
-        for b in range(tiles // per_step):
-            bring(b)
+        bring(0)
         pad_s[0] = jnp.zeros(pad_s.shape[1:], F32)
         pad_s[tiles + 1] = jnp.zeros(pad_s.shape[1:], F32)
         shape = (rows_dev, LANES)
@@ -291,11 +284,10 @@
             p = [poly_ref[me, k, i] for i in range(6)]
             row_s[k, 0] = p[0] + u * (p[1] + p[3] * u)
             row_s[k, 1] = p[2] + p[4] * u
-        await_block(0)
 
     @pl.when(step < blocks - 1)
     def _():
-        await_block(step + 1)
+        bring(step + 1)
 
     lane = lax.broadcasted_iota(jnp.int32, pad_s.shape[1:], 1)
     base = step * per_step
@@ -494,7 +486,7 @@
     convolve = pl.pallas_call(
         functools.partial(match_kernel, (held, nrow, ncol)),
         grid=(blocks,),
-        in_specs=[hbm] * len(arrays)
+        in_specs=[vmem] * len(arrays)
         + [
             smem,
             pl.BlockSpec(toep_hi.shape, const),
@@ -507,12 +499,12 @@
         scratch_shapes=[
             pltpu.VMEM((blocks * per_block + 2, long, LANES), F32),
             pltpu.VMEM((2, 2, ROWS_DEV, LANES), F32),
-            pltpu.SemaphoreType.DMA((blocks, per_block)),
         ],
         name="convolve",
-        compiler_params=pltpu.CompilerParams(vmem_limit_bytes=32 << 20),
+        compiler_params=pltpu.CompilerParams(vmem_limit_bytes=28 << 20),
         cost_estimate=pl.CostEstimate(flops=15_000_000_000, bytes_accessed=10_000_000, transcendentals=0),
     )
+    arrays = [pltpu.with_memory_space_constraint(x, pltpu.VMEM) for x in arrays]
     matched = convolve(*arrays, psf_poly, toep_hi, toep_lo, band, got_a)
     unit = ROWS_DEV // 8
     rest = pl.BlockSpec((1, unit, ncol), lambda i: (0, FIRST_PART + i, 0))

time: 180 us -> 178 us (0.989)
  Pallas kernels: 47.1 us -> 44.1 us
    pallas_call x1, Pallas kernels: 16.7 us -> 13.7 us  [shards(): matched = convolve(*arrays, psf_poly, toep_hi, toep_lo, band, got_a)]
  transfers between devices with their start and end apart: 17 -> 17, of which waited for: 9 -> 9; matrix products, arithmetic and copies ran while one was open for 6% -> 6% of each run, Pallas kernels for 13% -> 11%
where the time goes in v8:
time: 178 us; the launch traced here: 177 us
  waiting for transfers between devices  80.7 us (45%)
  Pallas kernels  44.1 us (25%)
  starting transfers between devices  32 us (18%)
  local copies, waits for them, and re-layouts  17.8 us (10%)
  other arithmetic  2.19 us (1%)
    ppermute x8, waiting for transfers between devices, swap(): return lax.ppermute(value, axis, [(i, i ^ 1 << bit) for i in range(count)])  68.2 us
    pallas_call x1, Pallas kernels, shards(): pl.pallas_call(functools.partial(warp_kernel, (epochs, nrow, share, order...  19.3 us
    unnamed x35, local copies, waits for them, and re-layouts  15.3 us
    pallas_call x1, Pallas kernels, shards(): matched = convolve(*arrays, psf_poly, toep_hi, toep_lo, band, got_a)  13.7 us
    ppermute x7, waiting for transfers between devices, shards(): lax.ppermute(parts[k], 'strip', [(i, i ^ k) for i in range(strips)])  12.5 us
    ppermute x8, starting transfers between devices, swap(): return lax.ppermute(value, axis, [(i, i ^ 1 << bit) for i in range(count)])  10.6 us
    all_to_all x1, starting transfers between devices, shards(): lax.all_to_all(sci_b, 'strip', split_axis=0, concat_axis=0, tiled=True)  8.49 us
    ppermute x7, starting transfers between devices, shards(): lax.ppermute(parts[k], 'strip', [(i, i ^ k) for i in range(strips)])  7.52 us
  transfers between devices with their start and end apart: 17, of which 9 were waited for; matrix products, arithmetic and copies ran while one was open for 6% of the time, Pallas kernels for 11%

profile of v8, /device:TPU:0, one launch (start us, length us, event | category | flops | bytes accessed | tf_op | source)
XLA Modules:
  0.0 176.8 jit_solution(17703189129391712076)
XLA Ops:
  0.0 19.3 %warp.1 = (f32[8,96,512]{2,1,0:T(8,128)}, f32[8,160,512]{2,1,0:T(8,128)}, f32[2,1032,128]{2,1,0:T(8,128)}, f32[2,1032,128]{2,1,0:T(8,128)}, f32[2,1032,128]{2,1,0:T(8,128)}, /*index=5*/f32[2,1032,128]{2,1,0:T(8,128)}) custom-call(s32[1,12]{1,0:T(1,128)} %kind_ref.1, s32[1,8,12]{2,1,0:T(8,128)} %heights_ref.1, f32[1,12]{1,0:T(1,128)} %invvar_ref.1, ...), custom_call_target="tpu_custom_call" | custom-call | flops 8000000000 | bytes 20000000 | tf_op jit(solution)/shard_map/warp/pallas_call | solution.py:373
  19.4 2.6 %collective-permute-start = (f32[2,1032,128]{2,1,0:T(8,128)}, f32[2,1032,128]{2,1,0:T(8,128)}, u32[]{:S(2)}, u32[]{:S(2)}) collective-permute-start(f32[2,1032,128]{2,1,0:T(8,128)} %get-tuple-element.28), channel_id=1, source_target_pairs={{0,8},{8,0},{16,24},{24,16},{1,9},{9,1},{17,25},{25,17},{2,10},{10... | collective-permute-start | bytes 3170312 | tf_op jit(solution)/shard_map/ppermute | solution.py:345
  22.0 1.5 collective-permute-start.2
  23.4 5.4 %all-to-all-start = ((f32[8,96,512]{2,1,0:T(8,128)}), f32[8,96,512]{2,1,0:T(8,128)S(1)}, u32[]{:S(2)}, u32[]{:S(2)}) async-start(f32[8,96,512]{2,1,0:T(8,128)} %get-tuple-element.26), calls=%async_computation | async-start | bytes 3145728 | tf_op jit(solution)/shard_map/all_to_all | solution.py:404
  28.9 17.3 %collective-permute-done.refs_1_ = f32[2,1032,128]{2,1,0:T(8,128)} collective-permute-done((f32[2,1032,128]{2,1,0:T(8,128)}, f32[2,1032,128]{2,1,0:T(8,128)}, u32[]{:S(2)}, u32[]{:S(2)}) %collective-permute-start) | collective-permute-done | bytes 1056800 | tf_op jit(solution)/shard_map/ppermute | solution.py:345
  47.3 2.0 %collective-permute-start.1 = (f32[1,1032,128]{2,1,0:T(8,128)S(1)}, f32[1,1032,128]{2,1,0:T(8,128)S(1)}, u32[]{:S(2)}, u32[]{:S(2)}) collective-permute-start(f32[1,1032,128]{2,1,0:T(8,128)S(1)} %slice_add_fusion.1), channel_id=1, source_target_pairs={{0,16},{8,24},{16,0},{24,8},{1,17},{9,25},{17,1},{25,9},{2,18},{10... | collective-permute-start | bytes 1585160 | tf_op jit(solution)/shard_map/ppermute | solution.py:345
  50.4 1.6 collective-permute-start.3
  51.9 9.1 %collective-permute-done.1.refs_2_ = f32[1,1032,128]{2,1,0:T(8,128)S(1)} collective-permute-done((f32[1,1032,128]{2,1,0:T(8,128)S(1)}, f32[1,1032,128]{2,1,0:T(8,128)S(1)}, u32[]{:S(2)}, u32[]{:S(2)}) %collective-permute-start.1) | collective-permute-done | bytes 528416 | tf_op jit(solution)/shard_map/ppermute | solution.py:345
  61.0 2.5 %collective-permute-done.3.refs_5_ = f32[1,1032,128]{2,1,0:T(8,128)S(1)} collective-permute-done((f32[1,1032,128]{2,1,0:T(8,128)S(1)}, f32[1,1032,128]{2,1,0:T(8,128)S(1)}, u32[]{:S(2)}, u32[]{:S(2)}) %collective-permute-start.3) | collective-permute-done | bytes 528416 | tf_op jit(solution)/shard_map/ppermute | solution.py:345
  64.4 3.9 %template.1 = (f32[288,128]{1,0:T(8,128)}, f32[288,128]{1,0:T(8,128)}, f32[288,128]{1,0:T(8,128)}, f32[288,128]{1,0:T(8,128)}, f32[288,128]{1,0:T(8,128)}, /*ind...) custom-call(f32[2,1032,128]{2,1,0:T(8,128)} %get-tuple-element.27.refs_0_, ...), custom_call_target="tpu_custom_call" | custom-call | flops 2000000 | bytes 5000000 | tf_op jit(solution)/shard_map/template/pallas_call | solution.py:443
  70.2 1.9 %collective-permute-start.7 = (f32[288,128]{1,0:T(8,128)}, f32[288,128]{1,0:T(8,128)S(1)}, u32[]{:S(2)}, u32[]{:S(2)}) collective-permute-start(f32[288,128]{1,0:T(8,128)} %get-tuple-element.35), channel_id=1, source_target_pairs={{0,4},{1,5},{2,6},{3,7},{4,0},{5,1},{6,2},{7,3},{8,12},{9,13},{10,... | collective-permute-start | bytes 442376 | tf_op jit(solution)/shard_map/ppermute | solution.py:455
  72.8 1.6 bitcast_dynamic-update-slice_fusion.7
  74.4 3.1 %collective-permute-start.9 = (f32[288,128]{1,0:T(8,128)}, f32[288,128]{1,0:T(8,128)S(1)}, u32[]{:S(2)}, u32[]{:S(2)}) collective-permute-start(f32[288,128]{1,0:T(8,128)} %get-tuple-element.37), channel_id=1, source_target_pairs={{0,6},{1,7},{2,4},{3,5},{4,2},{5,3},{6,0},{7,1},{8,14},{9,15},{10,... | collective-permute-start | bytes 442376 | tf_op jit(solution)/shard_map/ppermute | solution.py:455
  78.1 2.3 %collective-permute-done.5 = f32[288,128]{1,0:T(8,128)S(1)} collective-permute-done((f32[288,128]{1,0:T(8,128)}, f32[288,128]{1,0:T(8,128)S(1)}, u32[]{:S(2)}, u32[]{:S(2)}) %collective-permute-start.5) | collective-permute-done | bytes 147488 | tf_op jit(solution)/shard_map/ppermute | solution.py:455
  81.1 1.4 collective-permute-done.6
  83.9 8.7 %collective-permute-done.8 = f32[288,128]{1,0:T(8,128)S(1)} collective-permute-done((f32[288,128]{1,0:T(8,128)}, f32[288,128]{1,0:T(8,128)S(1)}, u32[]{:S(2)}, u32[]{:S(2)}) %collective-permute-start.8) | collective-permute-done | bytes 147488 | tf_op jit(solution)/shard_map/ppermute | solution.py:455
  95.8 8.5 %all-to-all-start.1 = ((f32[8,160,512]{2,1,0:T(8,128)}), f32[8,160,512]{2,1,0:T(8,128)S(1)}, u32[]{:S(2)}, u32[]{:S(2)}) async-start(f32[8,160,512]{2,1,0:T(8,128)} %get-tuple-element.39), calls=%async_computation.1 | async-start | bytes 5242880 | tf_op jit(solution)/shard_map/all_to_all | solution.py:458
  105.8 27.1 %collective-permute-done.12.refs_2_ = f32[8,288,128]{2,1,0:T(8,128)S(1)} collective-permute-done((f32[8,288,128]{2,1,0:T(8,128)}, f32[8,288,128]{2,1,0:T(8,128)S(1)}, u32[]{:S(2)}, u32[]{:S(2)}) %collective-permute-start.12) | collective-permute-done | bytes 1179680 | tf_op jit(solution)/shard_map/ppermute | solution.py:345
  137.1 2.4 %bands.1 = (bf16[256,256]{1,0:T(8,128)(2,1)}, bf16[256,256]{1,0:T(8,128)(2,1)}, bf16[2,256,160]{2,1,0:T(8,128)(2,1)}) custom-call(f32[2,2,31]{2,1,0:T(2,128)} %psf_ref.1), custom_call_target="tpu_custom_call" | custom-call | flops 10000000 | bytes 500000 | tf_op jit(solution)/shard_map/bands/pallas_call | solution.py:419
  139.5 9.3 %collective-permute-done.13.refs_3_ = f32[4,288,128]{2,1,0:T(8,128)S(1)} collective-permute-done((f32[4,288,128]{2,1,0:T(8,128)}, f32[4,288,128]{2,1,0:T(8,128)S(1)}, u32[]{:S(2)}, u32[]{:S(2)}) %collective-permute-start.13) | collective-permute-done | bytes 589856 | tf_op jit(solution)/shard_map/ppermute | solution.py:345
  148.8 2.9 %collective-permute-done.14.refs_4_ = f32[4,288,128]{2,1,0:T(8,128)} collective-permute-done((f32[4,288,128]{2,1,0:T(8,128)}, f32[4,288,128]{2,1,0:T(8,128)}, u32[]{:S(2)}, u32[]{:S(2)}) %collective-permute-start.14) | collective-permute-done | bytes 589856 | tf_op jit(solution)/shard_map/ppermute | solution.py:345
  151.6 1.4 copy-done.1
  158.3 13.7 %convolve.1 = f32[256,4096]{1,0:T(8,128)} custom-call(f32[8,288,128]{2,1,0:T(8,128)} %bitcast_dynamic-update-slice_fusion.refs_0_, f32[8,288,128]{2,1,0:T(8,128)S(1)} %copy-done.5, f32[8,288,128]{2,1,0:T(8,128)S(1)} %copy-done.3, f32[4,288,128]{2,1,0:T(8,128)S(1)} %collective-permute-done.13.refs_3_, f32[4,288,128]{2,1,0:T(8,128)} %collective-permute-done.14.refs_4_, ...), custom_call_target="tpu_custom_call" | custom-call | flops 15000000512 | bytes 10000000 | tf_op jit(solution)/shard_map/convolve/pallas_call | solution.py:508
  172.1 4.7 %subtract.1 = f32[1,256,4096]{2,1,0:T(8,128)} custom-call(f32[8,160,512]{2,1,0:T(8,128)S(1)} %all-to-all-done.1.sci_ref, f32[1,256,4096]{2,1,0:T(8,128)} %bitcast.18), custom_call_target="tpu_custom_call", output_to_operand_aliasing={{}: (1, {})} | custom-call | flops 1000000 | bytes 6000000 | tf_op jit(solution)/shard_map/subtract/pallas_call | solution.py:511
  (55 shorter events, 22.5 us)
Async XLA Ops:
  19.4 26.8 %collective-permute-start = (f32[2,1032,128]{2,1,0:T(8,128)}, f32[2,1032,128]{2,1,0:T(8,128)}, u32[]{:S(2)}, u32[]{:S(2)}) collective-permute-start(f32[2,1032,128]{2,1,0:T(8,128)} %get-tuple-element.28), channel_id=1, source_target_pairs={{0,8},{8,0},{16,24},{24,16},{1,9},{9,1},{17,25},{25,17},{2,10},{10... | collective-permute-start | bytes 3170312 | tf_op jit(solution)/shard_map/ppermute | solution.py:345
  22.0 27.3 %collective-permute-start.2 = (f32[2,1032,128]{2,1,0:T(8,128)}, f32[2,1032,128]{2,1,0:T(8,128)}, u32[]{:S(2)}, u32[]{:S(2)}) collective-permute-start(f32[2,1032,128]{2,1,0:T(8,128)} %get-tuple-element.30), channel_id=1, source_target_pairs={{0,16},{8,24},{16,0},{24,8},{1,17},{9,25},{17,1},{25,9},{2,18},{10... | collective-permute-start | bytes 3170312 | tf_op jit(solution)/shard_map/ppermute | solution.py:345
  23.4 22.7 %copy-start.10 = (f32[2,1032,128]{2,1,0:T(8,128)S(1)}, f32[2,1032,128]{2,1,0:T(8,128)}, u32[]{:S(2)}) copy-start(f32[2,1032,128]{2,1,0:T(8,128)} %get-tuple-element.27.refs_0_) | copy-start | bytes 3170308
  23.4 71.2 %all-to-all-start = ((f32[8,96,512]{2,1,0:T(8,128)}), f32[8,96,512]{2,1,0:T(8,128)S(1)}, u32[]{:S(2)}, u32[]{:S(2)}) async-start(f32[8,96,512]{2,1,0:T(8,128)} %get-tuple-element.26), calls=%async_computation | async-start | bytes 3145728 | tf_op jit(solution)/shard_map/all_to_all | solution.py:404
  28.9 20.4 %copy-start.11 = (f32[2,1032,128]{2,1,0:T(8,128)S(1)}, f32[2,1032,128]{2,1,0:T(8,128)}, u32[]{:S(2)}) copy-start(f32[2,1032,128]{2,1,0:T(8,128)} %get-tuple-element.29.refs_3_) | copy-start | bytes 3170308
  47.3 13.8 %collective-permute-start.1 = (f32[1,1032,128]{2,1,0:T(8,128)S(1)}, f32[1,1032,128]{2,1,0:T(8,128)S(1)}, u32[]{:S(2)}, u32[]{:S(2)}) collective-permute-start(f32[1,1032,128]{2,1,0:T(8,128)S(1)} %slice_add_fusion.1), channel_id=1, source_target_pairs={{0,16},{8,24},{16,0},{24,8},{1,17},{9,25},{17,1},{25,9},{2,18},{10... | collective-permute-start | bytes 1585160 | tf_op jit(solution)/shard_map/ppermute | solution.py:345
  50.4 13.2 %collective-permute-start.3 = (f32[1,1032,128]{2,1,0:T(8,128)S(1)}, f32[1,1032,128]{2,1,0:T(8,128)S(1)}, u32[]{:S(2)}, u32[]{:S(2)}) collective-permute-start(f32[1,1032,128]{2,1,0:T(8,128)S(1)} %slice_add_fusion), channel_id=1, source_target_pairs={{0,8},{8,0},{16,24},{24,16},{1,9},{9,1},{17,25},{25,17},{2,10},{10... | collective-permute-start | bytes 1585160 | tf_op jit(solution)/shard_map/ppermute | solution.py:345
  61.0 2.5 %copy-start.12 = (f32[1,1032,128]{2,1,0:T(8,128)}, f32[1,1032,128]{2,1,0:T(8,128)S(1)}, u32[]{:S(2)}) copy-start(f32[1,1032,128]{2,1,0:T(8,128)S(1)} %collective-permute-done.1.refs_2_) | copy-start | bytes 1585156
  68.3 6.0 %collective-permute-start.4 = (f32[288,128]{1,0:T(8,128)}, f32[288,128]{1,0:T(8,128)S(1)}, u32[]{:S(2)}, u32[]{:S(2)}) collective-permute-start(f32[288,128]{1,0:T(8,128)} %get-tuple-element.32), channel_id=1, source_target_pairs={{0,1},{1,0},{2,3},{3,2},{4,5},{5,4},{6,7},{7,6},{8,9},{9,8},{10,11... | collective-permute-start | bytes 442376 | tf_op jit(solution)/shard_map/ppermute | solution.py:455
  68.4 12.1 %collective-permute-start.5 = (f32[288,128]{1,0:T(8,128)}, f32[288,128]{1,0:T(8,128)S(1)}, u32[]{:S(2)}, u32[]{:S(2)}) collective-permute-start(f32[288,128]{1,0:T(8,128)} %get-tuple-element.33), channel_id=1, source_target_pairs={{0,2},{1,3},{2,0},{3,1},{4,6},{5,7},{6,4},{7,5},{8,10},{9,11},{10,... | collective-permute-start | bytes 442376 | tf_op jit(solution)/shard_map/ppermute | solution.py:455
  68.8 13.8 %collective-permute-start.6 = (f32[288,128]{1,0:T(8,128)}, f32[288,128]{1,0:T(8,128)S(1)}, u32[]{:S(2)}, u32[]{:S(2)}) collective-permute-start(f32[288,128]{1,0:T(8,128)} %get-tuple-element.34), channel_id=1, source_target_pairs={{0,3},{1,2},{2,1},{3,0},{4,7},{5,6},{6,5},{7,4},{8,11},{9,10},{10,... | collective-permute-start | bytes 442376 | tf_op jit(solution)/shard_map/ppermute | solution.py:455
  70.2 13.0 %collective-permute-start.7 = (f32[288,128]{1,0:T(8,128)}, f32[288,128]{1,0:T(8,128)S(1)}, u32[]{:S(2)}, u32[]{:S(2)}) collective-permute-start(f32[288,128]{1,0:T(8,128)} %get-tuple-element.35), channel_id=1, source_target_pairs={{0,4},{1,5},{2,6},{3,7},{4,0},{5,1},{6,2},{7,3},{8,12},{9,13},{10,... | collective-permute-start | bytes 442376 | tf_op jit(solution)/shard_map/ppermute | solution.py:455
  72.1 20.5 %collective-permute-start.8 = (f32[288,128]{1,0:T(8,128)}, f32[288,128]{1,0:T(8,128)S(1)}, u32[]{:S(2)}, u32[]{:S(2)}) collective-permute-start(f32[288,128]{1,0:T(8,128)} %get-tuple-element.36), channel_id=1, source_target_pairs={{0,5},{1,4},{2,7},{3,6},{4,1},{5,0},{6,3},{7,2},{8,13},{9,12},{10,... | collective-permute-start | bytes 442376 | tf_op jit(solution)/shard_map/ppermute | solution.py:455
  74.4 18.9 %collective-permute-start.9 = (f32[288,128]{1,0:T(8,128)}, f32[288,128]{1,0:T(8,128)S(1)}, u32[]{:S(2)}, u32[]{:S(2)}) collective-permute-start(f32[288,128]{1,0:T(8,128)} %get-tuple-element.37), channel_id=1, source_target_pairs={{0,6},{1,7},{2,4},{3,5},{4,2},{5,3},{6,0},{7,1},{8,14},{9,15},{10,... | collective-permute-start | bytes 442376 | tf_op jit(solution)/shard_map/ppermute | solution.py:455
  80.4 13.5 %collective-permute-start.10 = (f32[288,128]{1,0:T(8,128)}, f32[288,128]{1,0:T(8,128)S(1)}, u32[]{:S(2)}, u32[]{:S(2)}) collective-permute-start(f32[288,128]{1,0:T(8,128)} %get-tuple-element.38), channel_id=1, source_target_pairs={{0,7},{1,6},{2,5},{3,4},{4,3},{5,2},{6,1},{7,0},{8,15},{9,14},{10,... | collective-permute-start | bytes 442376 | tf_op jit(solution)/shard_map/ppermute | solution.py:455
  95.8 76.3 %all-to-all-start.1 = ((f32[8,160,512]{2,1,0:T(8,128)}), f32[8,160,512]{2,1,0:T(8,128)S(1)}, u32[]{:S(2)}, u32[]{:S(2)}) async-start(f32[8,160,512]{2,1,0:T(8,128)} %get-tuple-element.39), calls=%async_computation.1 | async-start | bytes 5242880 | tf_op jit(solution)/shard_map/all_to_all | solution.py:458
  104.3 47.4 %copy-start.6 = (f32[4,2,6]{2,1,0:T(2,128)S(1)}, f32[4,2,6]{2,1,0:T(2,128)}, u32[]{:S(2)}) copy-start(f32[4,2,6]{2,1,0:T(2,128)} %refs_5_.1) | copy-start | bytes 580
  104.3 28.6 %collective-permute-start.12 = (f32[8,288,128]{2,1,0:T(8,128)}, f32[8,288,128]{2,1,0:T(8,128)S(1)}, u32[]{:S(2)}, u32[]{:S(2)}) collective-permute-start(f32[8,288,128]{2,1,0:T(8,128)} %bitcast_dynamic-update-slice_fusion.refs_0_), channel_id=1, source_target_pairs={{0,16},{8,24},{16,0},{24,8},{1,17},{9,25},{17,1},{25,9},{2,18},{10... | collective-permute-start | bytes 3538952 | tf_op jit(solution)/shard_map/ppermute | solution.py:345
  105.3 29.5 %collective-permute-start.11 = (f32[8,288,128]{2,1,0:T(8,128)}, f32[8,288,128]{2,1,0:T(8,128)S(1)}, u32[]{:S(2)}, u32[]{:S(2)}) collective-permute-start(f32[8,288,128]{2,1,0:T(8,128)} %bitcast_dynamic-update-slice_fusion.refs_0_), channel_id=1, source_target_pairs={{0,8},{8,0},{16,24},{24,16},{1,9},{9,1},{17,25},{25,17},{2,10},{10... | collective-permute-start | bytes 3538952 | tf_op jit(solution)/shard_map/ppermute | solution.py:345
  132.9 2.9 %copy-start.2 = (f32[8,288,128]{2,1,0:T(8,128)}, f32[8,288,128]{2,1,0:T(8,128)S(1)}, u32[]{:S(2)}) copy-start(f32[8,288,128]{2,1,0:T(8,128)S(1)} %collective-permute-done.12.refs_2_) | copy-start | bytes 3538948
  133.8 15.0 %collective-permute-start.13 = (f32[4,288,128]{2,1,0:T(8,128)}, f32[4,288,128]{2,1,0:T(8,128)S(1)}, u32[]{:S(2)}, u32[]{:S(2)}) collective-permute-start(f32[4,288,128]{2,1,0:T(8,128)} %slice.26), channel_id=1, source_target_pairs={{0,8},{8,0},{16,24},{24,16},{1,9},{9,1},{17,25},{25,17},{2,10},{10... | collective-permute-start | bytes 1769480 | tf_op jit(solution)/shard_map/ppermute | solution.py:345
  136.8 14.8 %collective-permute-start.14 = (f32[4,288,128]{2,1,0:T(8,128)}, f32[4,288,128]{2,1,0:T(8,128)}, u32[]{:S(2)}, u32[]{:S(2)}) collective-permute-start(f32[4,288,128]{2,1,0:T(8,128)} %slice.27), channel_id=1, source_target_pairs={{0,16},{8,24},{16,0},{24,8},{1,17},{9,25},{17,1},{25,9},{2,18},{10... | collective-permute-start | bytes 1769480 | tf_op jit(solution)/shard_map/ppermute | solution.py:345
  151.6 1.4 copy-start.1
  153.0 1.3 copy-start.3
  (7 other events, 7.0 us)

commit v9 on v8

--- a/solution.py
+++ b/solution.py
@@ -50,10 +50,14 @@
 
 
 def warp_kernel(
-    geom, kind_ref, heights_ref, invvar_ref, raw_ref, rmat_ref, cmat_ref,
-    sci_a, sci_b, keep_a, send_a, keep_b, send_b,
-    sci_s, num_s, wt_s, rmat_s, cmat_s, chi_s, clo_s, top_s, ready_s, fetch_sems, sems, wt_sems,
+    geom, kind_ref, heights_ref, invvar_ref, raw_ref, rmat_ref, cmat_ref, *refs
 ):
+    strips = lax.axis_size("strip")
+    sci_a, sci_b = refs[:strips], refs[strips : 2 * strips]
+    keep_a, send_a, keep_b, send_b = refs[2 * strips : 2 * strips + 4]
+    (
+        sci_s, num_s, wt_s, rmat_s, cmat_s, chi_s, clo_s, top_s, ready_s, fetch_sems, sems, sci_sems, wt_sems
+    ) = refs[2 * strips + 4 :]
     epochs, nrow, share, orders, tiles = geom
     step = pl.program_id(0)
     together, tile_rows, tile_cols = raw_ref.shape
@@ -65,8 +69,8 @@
     block = lax.div(first_tile, per_col)
     offset_in = lax.rem(first_tile, per_col)
     kinds = cmat_ref.shape[0]
-    strips, rows_a, _ = sci_a.shape
-    rows_dev = rows_a + sci_b.shape[1]
+    rows_a, rows_b = sci_a[0].shape[0], sci_b[0].shape[0]
+    rows_dev = rows_a + rows_b
     nhalf = nrow // 2
     outs = (keep_a, send_a), (keep_b, send_b)
 
@@ -79,16 +83,23 @@
     def strip_copies(s):
         base = s * rows_dev
         part = base // nhalf
-        pairs = [
-            (sci_s.at[pl.ds(base, rows_a)], sci_a.at[s]),
-            (sci_s.at[pl.ds(base + rows_a, rows_dev - rows_a)], sci_b.at[s]),
-        ]
+        pairs = []
         for slots, out in zip(slot_order(epochs, orders[part]), outs[part]):
             for place, j in enumerate(slots):
                 pairs.append(
                     (num_s.at[j, pl.ds(base, rows_dev)], out.at[place, pl.ds(base - part * nhalf, rows_dev)])
                 )
         return [pltpu.make_async_copy(a, b, sems.at[s, n]) for n, (a, b) in enumerate(pairs)]
+
+    def partner(k):
+        return jnp.bitwise_xor(lax.axis_index("strip"), k)
+
+    def sci_copies(k):
+        base = pl.multiple_of(partner(k) * rows_dev, rows_dev)
+        return [
+            pltpu.make_async_copy(sci_s.at[pl.ds(base, rows_a)], sci_a[k], sci_sems.at[k, 0]),
+            pltpu.make_async_copy(sci_s.at[pl.ds(base + rows_a, rows_b)], sci_b[k], sci_sems.at[k, 1]),
+        ]
 
     @pl.when(step == 0)
     def _():
@@ -168,6 +179,14 @@
         @pl.when((before < end) & (end <= final))
         def _():
             for copy in strip_copies(s):
+                copy.start()
+
+    for k in range(strips):
+        edge = (partner(k) + 1) * rows_dev
+
+        @pl.when((before < edge) & (edge <= final))
+        def _():
+            for copy in sci_copies(k):
                 copy.start()
 
     @pl.when(step == last)
@@ -186,7 +205,7 @@
                     )
         start_and_wait(copies)
         for s in range(strips):
-            for copy in strip_copies(s):
+            for copy in strip_copies(s) + sci_copies(s):
                 copy.wait()
         for k in range(kinds):
 
@@ -243,7 +262,7 @@
     slots, nrow, ncol = geom
     count = max(len(slots), 1) + (len(slots) > 1)
     tile_refs = refs[:count]
-    poly_ref, toep_hi, toep_lo, band_ref, sci_ref, out_ref, pad_s, row_s = refs[count:]
+    poly_ref, toep_hi, toep_lo, band_ref, *sci_refs, out_ref, pad_s, row_s = refs[count:]
     step = pl.program_id(0)
     blocks = pl.num_programs(0)
     tiles = pad_s.shape[0] - 2
@@ -321,22 +340,25 @@
                 two = jnp.concatenate([row_s[k, 1, place, :]] * 2, axis=1)
                 coeff = one + v * (two + poly_ref[me, k, 5] * v)
                 total = total + coeff * done
-            columns = pl.ds(pair * width, width)
-            ready = min(max(sci_ref.shape[1] - part * LANES, 0), LANES)
-            if ready:
-                here = pl.ds(part * LANES, ready)
-                out_ref[here, columns] = sci_ref[0, here, columns] - total[:ready]
-            if ready < LANES:
-                out_ref[pl.ds(part * LANES + ready, LANES - ready), columns] = total[ready:]
-
-
-def subtract_kernel(sci_ref, matched_ref, out_ref):
+            out_ref[pl.ds(part * LANES, LANES), pl.ds(pair * width, width)] = total
+
+    home = lax.div(strip, lax.axis_size("strip") // blocks)
+    for k, ref in enumerate(sci_refs):
+
+        @pl.when(jnp.bitwise_xor(home, step) == k)
+        def _():
+            ready = pl.ds(0, ref.shape[0])
+            out_ref[ready, :] = ref[...] - out_ref[ready, :]
+
+
+def subtract_kernel(*refs):
+    *sci_refs, matched_ref, out_ref = refs
     i = pl.program_id(0)
-    blocks, _, width = sci_ref.shape
-    rows = out_ref.shape[1]
-    for b in range(blocks):
-        columns = pl.ds(b * width, width)
-        science = sci_ref[b, pl.ds(pl.multiple_of(i * rows, rows), rows), :]
+    rows, width = out_ref.shape[1], sci_refs[0].shape[1]
+    home = lax.div(lax.axis_index("strip"), lax.axis_size("strip") // len(sci_refs))
+    for k, ref in enumerate(sci_refs):
+        columns = pl.ds(pl.multiple_of(jnp.bitwise_xor(home, k) * width, width), width)
+        science = ref[pl.ds(pl.multiple_of(i * rows, rows), rows), :]
         out_ref[0, :, columns] = science - matched_ref[0, :, columns]
 
 
@@ -366,11 +388,11 @@
 
     first_rows = ROWS_DEV * FIRST_PART // 8
     sci_shapes = [
-        jax.ShapeDtypeStruct((strips, rows, tile_cols), F32) for rows in (first_rows, ROWS_DEV - first_rows)
+        jax.ShapeDtypeStruct((rows, tile_cols), F32) for rows in (first_rows, ROWS_DEV - first_rows)
     ]
     send_shape = jax.ShapeDtypeStruct((epochs // 2, long_half, share), F32)
     together = 2 if tiles % 2 == 0 else 1
-    sci_a, sci_b, keep_a, send_a, keep_b, send_b = pl.pallas_call(
+    warped = pl.pallas_call(
         functools.partial(warp_kernel, (epochs, nrow, share, orders, tiles)),
         grid=(tiles // together,),
         in_specs=[
@@ -381,8 +403,8 @@
             hbm,
             hbm,
         ],
-        out_specs=[hbm] * 6,
-        out_shape=sci_shapes + [send_shape] * 4,
+        out_specs=[hbm] * (2 * strips + 4),
+        out_shape=[sci_shapes[0]] * strips + [sci_shapes[1]] * strips + [send_shape] * 4,
         scratch_shapes=[
             pltpu.VMEM((nrow, tile_cols), F32),
             pltpu.VMEM((epochs, nrow, share), F32),
@@ -394,14 +416,29 @@
             pltpu.SMEM((2,), jnp.int32),
             pltpu.SMEM((kinds,), jnp.int32),
             pltpu.SemaphoreType.DMA((kinds, 2)),
-            pltpu.SemaphoreType.DMA((strips, 2 + epochs)),
+            pltpu.SemaphoreType.DMA((strips, epochs)),
+            pltpu.SemaphoreType.DMA((strips, 2)),
             pltpu.SemaphoreType.DMA((2 * epochs,)),
         ],
         name="warp",
         cost_estimate=pl.CostEstimate(flops=8_000_000_000, bytes_accessed=20_000_000, transcendentals=0),
     )(tile_kind, tile_heights, tile_invvar, raw_tiles[0], row_interp, col_interp)
 
-    got_a = lax.all_to_all(sci_a, "strip", split_axis=0, concat_axis=0, tiled=True)
+    sci_a, sci_b = warped[:strips], warped[strips : 2 * strips]
+    keep_a, send_a, keep_b, send_b = warped[2 * strips :]
+
+    def exchanged(arrays):
+        got = [arrays[0]] + [None] * (strips - 1)
+        for k in reversed(range(1, strips)):
+            got[k] = lax.ppermute(arrays[k], "strip", [(i, i ^ k) for i in range(strips)])
+        return got
+
+    def merged(got):
+        return [
+            functools.reduce(lambda a, b: a + b, got[k : k + sources]) for k in range(0, strips, sources)
+        ]
+
+    got_a = exchanged(sci_a)
 
     basis, _, _ = psf_profiles.shape
     build_bands = pl.pallas_call(
@@ -440,7 +477,7 @@
         terms = fixed
 
     long = ROWS_DEV + 2 * HALO
-    parts = pl.pallas_call(
+    build_strips = pl.pallas_call(
         functools.partial(template_kernel, len(terms[0])),
         in_specs=[vmem] * (2 * len(terms[0])),
         out_specs=[vmem] * strips,
@@ -448,17 +485,13 @@
         scratch_shapes=[pltpu.VMEM((nrow + 2 * HALO, share), F32)],
         name="template",
         cost_estimate=pl.CostEstimate(flops=2_000_000, bytes_accessed=5_000_000, transcendentals=0),
-    )(*terms[0], *terms[1])
-    came = [None] * strips
-    came[0] = parts[0]
-    for k in reversed(range(1, strips)):
-        came[k] = lax.ppermute(parts[k], "strip", [(i, i ^ k) for i in range(strips)])
+    )
+    parts = build_strips(*terms[0], *terms[1])
+    came = exchanged(parts)
     mine = jnp.stack(came[:: sources])
-    sci_b, got_a, mine = lax.optimization_barrier((sci_b, got_a, mine))
-    got_b = lax.all_to_all(sci_b, "strip", split_axis=0, concat_axis=0, tiled=True)
-    if sources > 1:
-        got_a = jnp.sum(got_a.reshape((blocks, sources) + got_a.shape[1:]), axis=1)
-        got_b = jnp.sum(got_b.reshape((blocks, sources) + got_b.shape[1:]), axis=1)
+    mine, *sci_b = lax.optimization_barrier((mine, *sci_b))
+    got_b = merged(exchanged(sci_b))
+    got_a = merged(got_a)
 
     per_block = tile_cols // LANES
     if epochs == 4 and share == LANES:
@@ -492,8 +525,8 @@
             pl.BlockSpec(toep_hi.shape, const),
             pl.BlockSpec(toep_lo.shape, const),
             pl.BlockSpec(band.shape, lambda b: (0, 0, 0)),
-            pl.BlockSpec((1,) + got_a.shape[1:], lambda b: (b, 0, 0)),
-        ],
+        ]
+        + [vmem] * blocks,
         out_specs=pl.BlockSpec((ROWS_DEV, tile_cols), lambda b: (0, b)),
         out_shape=jax.ShapeDtypeStruct((ROWS_DEV, ncol), F32),
         scratch_shapes=[
@@ -505,20 +538,20 @@
         cost_estimate=pl.CostEstimate(flops=15_000_000_000, bytes_accessed=10_000_000, transcendentals=0),
     )
     arrays = [pltpu.with_memory_space_constraint(x, pltpu.VMEM) for x in arrays]
-    matched = convolve(*arrays, psf_poly, toep_hi, toep_lo, band, got_a)
+    matched = convolve(*arrays, psf_poly, toep_hi, toep_lo, band, *got_a)
     unit = ROWS_DEV // 8
     rest = pl.BlockSpec((1, unit, ncol), lambda i: (0, FIRST_PART + i, 0))
     return pl.pallas_call(
         subtract_kernel,
         grid=(8 - FIRST_PART,),
-        in_specs=[vmem, rest],
+        in_specs=[vmem] * blocks + [rest],
         out_specs=rest,
         out_shape=jax.ShapeDtypeStruct((1, ROWS_DEV, ncol), F32),
-        input_output_aliases={1: 0},
+        input_output_aliases={blocks: 0},
         name="subtract",
         compiler_params=pltpu.CompilerParams(vmem_limit_bytes=16 << 20),
         cost_estimate=pl.CostEstimate(flops=1_000_000, bytes_accessed=6_000_000, transcendentals=0),
-    )(pltpu.with_memory_space_constraint(got_b, pltpu.VMEM), matched[None])
+    )(*[pltpu.with_memory_space_constraint(x, pltpu.VMEM) for x in got_b], matched[None])
 
 
 def solution(mesh):

time: 178 us -> 233 us (1.31)
  the two profiles are of different devices: /device:TPU:0 before, /device:TPU:9 now
where the time goes in v9:
time: 233 us; the launch traced here: 231 us
  waiting for transfers between devices  109 us (47%)
  starting transfers between devices  61.5 us (26%)
  Pallas kernels  43.9 us (19%)
  local copies, waits for them, and re-layouts  15 us (6%)
    ppermute x8, waiting for transfers between devices, swap(): return lax.ppermute(value, axis, [(i, i ^ 1 << bit) for i in range(count)])  54.6 us
    ppermute x21, waiting for transfers between devices, exchanged(): lax.ppermute(arrays[k], 'strip', [(i, i ^ k) for i in range(strips)])  54.2 us
    ppermute x21, starting transfers between devices, exchanged(): lax.ppermute(arrays[k], 'strip', [(i, i ^ k) for i in range(strips)])  51.6 us
    pallas_call x1, Pallas kernels, shards(): pl.pallas_call(functools.partial(warp_kernel, (epochs, nrow, share, order...  18.8 us
    pallas_call x1, Pallas kernels, shards(): matched = convolve(*arrays, psf_poly, toep_hi, toep_lo, band, *got_a)  14 us
    unnamed x59, local copies, waits for them, and re-layouts  13.3 us
    ppermute x8, starting transfers between devices, swap(): return lax.ppermute(value, axis, [(i, i ^ 1 << bit) for i in range(count)])  9.95 us
    pallas_call x1, Pallas kernels, shards(): pl.pallas_call(subtract_kernel, grid=(8 - FIRST_PART,), in_specs=[vmem] *...  4.87 us
  transfers between devices with their start and end apart: 29, of which 16 were waited for; matrix products, arithmetic and copies ran while one was open for 2% of the time, Pallas kernels for 7%

profile of v9, /device:TPU:9, one launch (start us, length us, event | category | flops | bytes accessed | tf_op | source)
XLA Modules:
  0.0 230.9 jit_solution(6701387895809429307)
XLA Ops:
  0.0 18.8 %warp.1 = (f32[96,512]{1,0:T(8,128)}, f32[96,512]{1,0:T(8,128)}, f32[96,512]{1,0:T(8,128)}, f32[96,512]{1,0:T(8,128)}, f32[96,512]{1,0:T(8,128)}, /*index=5*/f32...) custom-call(s32[1,12]{1,0:T(1,128)} %kind_ref.1, ...), custom_call_target="tpu_custom_call" | custom-call | flops 8000000000 | bytes 20000000 | tf_op jit(solution)/shard_map/warp/pallas_call | solution.py:395
  21.7 21.0 %collective-permute-done.refs_1_ = f32[2,1032,128]{2,1,0:T(8,128)S(1)} collective-permute-done((f32[2,1032,128]{2,1,0:T(8,128)}, f32[2,1032,128]{2,1,0:T(8,128)S(1)}, u32[]{:S(2)}, u32[]{:S(2)}) %collective-permute-start) | collective-permute-done | bytes 1056800 | tf_op jit(solution)/shard_map/ppermute | solution.py:367
  47.8 8.0 %collective-permute-done.1.refs_2_ = f32[1,1032,128]{2,1,0:T(8,128)} collective-permute-done((f32[1,1032,128]{2,1,0:T(8,128)S(1)}, f32[1,1032,128]{2,1,0:T(8,128)}, u32[]{:S(2)}, u32[]{:S(2)}) %collective-permute-start.1) | collective-permute-done | bytes 528416 | tf_op jit(solution)/shard_map/ppermute | solution.py:367
  55.8 2.4 %collective-permute-done.3.refs_5_ = f32[1,1032,128]{2,1,0:T(8,128)S(1)} collective-permute-done((f32[1,1032,128]{2,1,0:T(8,128)S(1)}, f32[1,1032,128]{2,1,0:T(8,128)S(1)}, u32[]{:S(2)}, u32[]{:S(2)}) %collective-permute-start.3) | collective-permute-done | bytes 528416 | tf_op jit(solution)/shard_map/ppermute | solution.py:367
  59.0 3.9 %template.1 = (f32[288,128]{1,0:T(8,128)}, f32[288,128]{1,0:T(8,128)}, f32[288,128]{1,0:T(8,128)}, f32[288,128]{1,0:T(8,128)}, f32[288,128]{1,0:T(8,128)}, /*ind...) custom-call(f32[2,1032,128]{2,1,0:T(8,128)} %get-tuple-element.45.refs_0_, f32[2,1032,128]{2,1,0:T(8,128)} %copy-done.17, ...), custom_call_target="tpu_custom_call" | custom-call | flops 2000000 | bytes 5000000 | tf_op jit(solution)/shard_map/template/pallas_call | solution.py:489
  62.9 2.6 %collective-permute-start.4 = (f32[288,128]{1,0:T(8,128)}, f32[288,128]{1,0:T(8,128)S(1)}, u32[]{:S(2)}, u32[]{:S(2)}) collective-permute-start(f32[288,128]{1,0:T(8,128)} %get-tuple-element.50), channel_id=1, source_target_pairs={{0,1},{1,0},{2,3},{3,2},{4,5},{5,4},{6,7},{7,6},{8,9},{9,8},{10,11... | collective-permute-start | bytes 442376 | tf_op jit(solution)/shard_map/ppermute | solution.py:433
  67.1 2.9 %collective-permute-start.7 = (f32[288,128]{1,0:T(8,128)}, f32[288,128]{1,0:T(8,128)S(1)}, u32[]{:S(2)}, u32[]{:S(2)}) collective-permute-start(f32[288,128]{1,0:T(8,128)} %get-tuple-element.53), channel_id=1, source_target_pairs={{0,4},{1,5},{2,6},{3,7},{4,0},{5,1},{6,2},{7,3},{8,12},{9,13},{10,... | collective-permute-start | bytes 442376 | tf_op jit(solution)/shard_map/ppermute | solution.py:433
  72.6 3.6 %collective-permute-start.10 = (f32[288,128]{1,0:T(8,128)}, f32[288,128]{1,0:T(8,128)S(1)}, u32[]{:S(2)}, u32[]{:S(2)}) collective-permute-start(f32[288,128]{1,0:T(8,128)} %get-tuple-element.56), channel_id=1, source_target_pairs={{0,7},{1,6},{2,5},{3,4},{4,3},{5,2},{6,1},{7,0},{8,15},{9,14},{10,... | collective-permute-start | bytes 442376 | tf_op jit(solution)/shard_map/ppermute | solution.py:433
  79.1 10.1 %collective-permute-done.8 = f32[288,128]{1,0:T(8,128)S(1)} collective-permute-done((f32[288,128]{1,0:T(8,128)}, f32[288,128]{1,0:T(8,128)S(1)}, u32[]{:S(2)}, u32[]{:S(2)}) %collective-permute-start.8) | collective-permute-done | bytes 147488 | tf_op jit(solution)/shard_map/ppermute | solution.py:433
  89.2 3.4 %collective-permute-done.9 = f32[288,128]{1,0:T(8,128)S(1)} collective-permute-done((f32[288,128]{1,0:T(8,128)}, f32[288,128]{1,0:T(8,128)S(1)}, u32[]{:S(2)}, u32[]{:S(2)}) %collective-permute-start.9) | collective-permute-done | bytes 147488 | tf_op jit(solution)/shard_map/ppermute | solution.py:433
  92.6 3.5 %collective-permute-done.10 = f32[288,128]{1,0:T(8,128)S(1)} collective-permute-done((f32[288,128]{1,0:T(8,128)}, f32[288,128]{1,0:T(8,128)S(1)}, u32[]{:S(2)}, u32[]{:S(2)}) %collective-permute-start.10) | collective-permute-done | bytes 147488 | tf_op jit(solution)/shard_map/ppermute | solution.py:433
  100.1 23.2 %collective-permute-done.19.refs_2_ = f32[8,288,128]{2,1,0:T(8,128)S(1)} collective-permute-done((f32[8,288,128]{2,1,0:T(8,128)S(1)}, f32[8,288,128]{2,1,0:T(8,128)S(1)}, u32[]{:S(2)}, u32[]{:S(2)}) %collective-permute-start.19) | collective-permute-done | bytes 1179680 | tf_op jit(solution)/shard_map/ppermute | solution.py:367
  127.0 3.9 %collective-permute-start.26 = (f32[96,512]{1,0:T(8,128)S(1)}, f32[96,512]{1,0:T(8,128)S(1)}, u32[]{:S(2)}, u32[]{:S(2)}) collective-permute-start(f32[96,512]{1,0:T(8,128)S(1)} %copy-done.21), channel_id=1, source_target_pairs={{0,5},{1,4},{2,7},{3,6},{4,1},{5,0},{6,3},{7,2},{8,13},{9,12},{10,... | collective-permute-start | bytes 589832 | tf_op jit(solution)/shard_map/ppermute | solution.py:433
  133.6 13.4 %collective-permute-start.11 = (f32[160,512]{1,0:T(8,128)}, f32[160,512]{1,0:T(8,128)S(1)}, u32[]{:S(2)}, u32[]{:S(2)}) collective-permute-start(f32[160,512]{1,0:T(8,128)} %get-tuple-element.66), channel_id=1, source_target_pairs={{0,1},{1,0},{2,3},{3,2},{4,5},{5,4},{6,7},{7,6},{8,9},{9,8},{10,11... | collective-permute-start | bytes 983048 | tf_op jit(solution)/shard_map/ppermute | solution.py:433
  147.6 5.6 %collective-permute-start.12 = (f32[160,512]{1,0:T(8,128)}, f32[160,512]{1,0:T(8,128)S(1)}, u32[]{:S(2)}, u32[]{:S(2)}) collective-permute-start(f32[160,512]{1,0:T(8,128)} %get-tuple-element.67), channel_id=1, source_target_pairs={{0,2},{1,3},{2,0},{3,1},{4,6},{5,7},{6,4},{7,5},{8,10},{9,11},{10,... | collective-permute-start | bytes 983048 | tf_op jit(solution)/shard_map/ppermute | solution.py:433
  155.9 2.4 %bands.1 = (bf16[256,256]{1,0:T(8,128)(2,1)}, bf16[256,256]{1,0:T(8,128)(2,1)}, bf16[2,256,160]{2,1,0:T(8,128)(2,1)}) custom-call(f32[2,2,31]{2,1,0:T(2,128)} %psf_ref.1), custom_call_target="tpu_custom_call" | custom-call | flops 10000000 | bytes 500000 | tf_op jit(solution)/shard_map/bands/pallas_call | solution.py:456
  158.3 2.8 %collective-permute-done.28.refs_16_ = f32[96,512]{1,0:T(8,128)} collective-permute-done((f32[96,512]{1,0:T(8,128)}, f32[96,512]{1,0:T(8,128)}, u32[]{:S(2)}, u32[]{:S(2)}) %collective-permute-start.28) | collective-permute-done | bytes 196640 | tf_op jit(solution)/shard_map/ppermute | solution.py:433
  161.1 6.7 %collective-permute-start.13 = (f32[160,512]{1,0:T(8,128)}, f32[160,512]{1,0:T(8,128)S(1)}, u32[]{:S(2)}, u32[]{:S(2)}) collective-permute-start(f32[160,512]{1,0:T(8,128)} %get-tuple-element.68), channel_id=1, source_target_pairs={{0,3},{1,2},{2,1},{3,0},{4,7},{5,6},{6,5},{7,4},{8,11},{9,10},{10,... | collective-permute-start | bytes 983048 | tf_op jit(solution)/shard_map/ppermute | solution.py:433
  180.8 14.0 %convolve.1 = f32[256,4096]{1,0:T(8,128)} custom-call(f32[8,288,128]{2,1,0:T(8,128)S(1)} %copy-done.2, f32[8,288,128]{2,1,0:T(8,128)S(1)} %collective-permute-done.18.refs_1_, f32[8,288,128]{2,1,0:T(8,128)S(1)} %collective-permute-done.19.refs_2_, f32[4,288,128]{2,1,0:T(8,128)} %collective-permute-done.20.refs_3_, ...), custom_call_target="tpu_custom_call" | custom-call | flops 15000000512 | bytes 10000000 | tf_op jit(solution)/shard_map/convolve/pallas_call | solution.py:541
  194.9 9.2 %collective-permute-done.14.refs_4_ = f32[160,512]{1,0:T(8,128)S(1)} collective-permute-done((f32[160,512]{1,0:T(8,128)}, f32[160,512]{1,0:T(8,128)S(1)}, u32[]{:S(2)}, u32[]{:S(2)}) %collective-permute-start.14) | collective-permute-done | bytes 327712 | tf_op jit(solution)/shard_map/ppermute | solution.py:433
  204.1 7.0 %collective-permute-done.15.refs_5_ = f32[160,512]{1,0:T(8,128)S(1)} collective-permute-done((f32[160,512]{1,0:T(8,128)}, f32[160,512]{1,0:T(8,128)S(1)}, u32[]{:S(2)}, u32[]{:S(2)}) %collective-permute-start.15) | collective-permute-done | bytes 327712 | tf_op jit(solution)/shard_map/ppermute | solution.py:433
  211.1 7.3 %collective-permute-done.16.refs_6_ = f32[160,512]{1,0:T(8,128)S(1)} collective-permute-done((f32[160,512]{1,0:T(8,128)}, f32[160,512]{1,0:T(8,128)S(1)}, u32[]{:S(2)}, u32[]{:S(2)}) %collective-permute-start.16) | collective-permute-done | bytes 327712 | tf_op jit(solution)/shard_map/ppermute | solution.py:433
  218.5 7.6 %collective-permute-done.17.refs_7_ = f32[160,512]{1,0:T(8,128)S(1)} collective-permute-done((f32[160,512]{1,0:T(8,128)}, f32[160,512]{1,0:T(8,128)S(1)}, u32[]{:S(2)}, u32[]{:S(2)}) %collective-permute-start.17) | collective-permute-done | bytes 327712 | tf_op jit(solution)/shard_map/ppermute | solution.py:433
  226.1 4.9 %subtract.1 = f32[1,256,4096]{2,1,0:T(8,128)} custom-call(f32[160,512]{1,0:T(8,128)S(1)} %copy-done, f32[160,512]{1,0:T(8,128)S(1)} %collective-permute-done.11.refs_1_, f32[160,512]{1,0:T(8,128)S(1)} %collective-permute-done.12.refs_2_, f32[160,512]{1,0:T(8,128)S(1)} %collective-permute-done.13.refs_3_, ...), custom_call_target="tpu_custom_call", output_to_operand_aliasing={{}: (8, {})} | custom-call | flops 1000000 | bytes 6000000 | tf_op jit(solution)/shard_map/subtract/pallas_call | solution.py:544
  (103 shorter events, 42.6 us)
Async XLA Ops:
  18.8 23.9 %collective-permute-start = (f32[2,1032,128]{2,1,0:T(8,128)}, f32[2,1032,128]{2,1,0:T(8,128)S(1)}, u32[]{:S(2)}, u32[]{:S(2)}) collective-permute-start(f32[2,1032,128]{2,1,0:T(8,128)} %get-tuple-element.46), channel_id=1, source_target_pairs={{0,8},{8,0},{16,24},{24,16},{1,9},{9,1},{17,25},{25,17},{2,10},{10... | collective-permute-start | bytes 3170312 | tf_op jit(solution)/shard_map/ppermute | solution.py:367
  20.1 25.5 %collective-permute-start.2 = (f32[2,1032,128]{2,1,0:T(8,128)}, f32[2,1032,128]{2,1,0:T(8,128)S(1)}, u32[]{:S(2)}, u32[]{:S(2)}) collective-permute-start(f32[2,1032,128]{2,1,0:T(8,128)} %get-tuple-element.48), channel_id=1, source_target_pairs={{0,16},{8,24},{16,0},{24,8},{1,17},{9,25},{17,1},{25,9},{2,18},{10... | collective-permute-start | bytes 3170312 | tf_op jit(solution)/shard_map/ppermute | solution.py:367
  45.7 12.5 %collective-permute-start.3 = (f32[1,1032,128]{2,1,0:T(8,128)S(1)}, f32[1,1032,128]{2,1,0:T(8,128)S(1)}, u32[]{:S(2)}, u32[]{:S(2)}) collective-permute-start(f32[1,1032,128]{2,1,0:T(8,128)S(1)} %slice_add_fusion), channel_id=1, source_target_pairs={{0,8},{8,0},{16,24},{24,16},{1,9},{9,1},{17,25},{25,17},{2,10},{10... | collective-permute-start | bytes 1585160 | tf_op jit(solution)/shard_map/ppermute | solution.py:367
  66.7 11.7 %collective-permute-start.6 = (f32[288,128]{1,0:T(8,128)}, f32[288,128]{1,0:T(8,128)S(1)}, u32[]{:S(2)}, u32[]{:S(2)}) collective-permute-start(f32[288,128]{1,0:T(8,128)} %get-tuple-element.52), channel_id=1, source_target_pairs={{0,3},{1,2},{2,1},{3,0},{4,7},{5,6},{6,5},{7,4},{8,11},{9,10},{10,... | collective-permute-start | bytes 442376 | tf_op jit(solution)/shard_map/ppermute | solution.py:433
  67.1 11.9 %collective-permute-start.7 = (f32[288,128]{1,0:T(8,128)}, f32[288,128]{1,0:T(8,128)S(1)}, u32[]{:S(2)}, u32[]{:S(2)}) collective-permute-start(f32[288,128]{1,0:T(8,128)} %get-tuple-element.53), channel_id=1, source_target_pairs={{0,4},{1,5},{2,6},{3,7},{4,0},{5,1},{6,2},{7,3},{8,12},{9,13},{10,... | collective-permute-start | bytes 442376 | tf_op jit(solution)/shard_map/ppermute | solution.py:433
  70.0 19.2 %collective-permute-start.8 = (f32[288,128]{1,0:T(8,128)}, f32[288,128]{1,0:T(8,128)S(1)}, u32[]{:S(2)}, u32[]{:S(2)}) collective-permute-start(f32[288,128]{1,0:T(8,128)} %get-tuple-element.54), channel_id=1, source_target_pairs={{0,5},{1,4},{2,7},{3,6},{4,1},{5,0},{6,3},{7,2},{8,13},{9,12},{10,... | collective-permute-start | bytes 442376 | tf_op jit(solution)/shard_map/ppermute | solution.py:433
  71.1 21.5 %collective-permute-start.9 = (f32[288,128]{1,0:T(8,128)}, f32[288,128]{1,0:T(8,128)S(1)}, u32[]{:S(2)}, u32[]{:S(2)}) collective-permute-start(f32[288,128]{1,0:T(8,128)} %get-tuple-element.55), channel_id=1, source_target_pairs={{0,6},{1,7},{2,4},{3,5},{4,2},{5,3},{6,0},{7,1},{8,14},{9,15},{10,... | collective-permute-start | bytes 442376 | tf_op jit(solution)/shard_map/ppermute | solution.py:433
  72.6 23.5 %collective-permute-start.10 = (f32[288,128]{1,0:T(8,128)}, f32[288,128]{1,0:T(8,128)S(1)}, u32[]{:S(2)}, u32[]{:S(2)}) collective-permute-start(f32[288,128]{1,0:T(8,128)} %get-tuple-element.56), channel_id=1, source_target_pairs={{0,7},{1,6},{2,5},{3,4},{4,3},{5,2},{6,1},{7,0},{8,15},{9,14},{10,... | collective-permute-start | bytes 442376 | tf_op jit(solution)/shard_map/ppermute | solution.py:433
  96.1 27.1 %collective-permute-start.19 = (f32[8,288,128]{2,1,0:T(8,128)S(1)}, f32[8,288,128]{2,1,0:T(8,128)S(1)}, u32[]{:S(2)}, u32[]{:S(2)}) collective-permute-start(f32[8,288,128]{2,1,0:T(8,128)S(1)} %bitcast_dynamic-update-slice_fusion.refs_0_), channel_id=1, source_target_pairs={{0,16},{8,24},{16,0},{24,8},{1,17},{9,25},{17,1},{25,9},{2,18},{10... | collective-permute-start | bytes 3538952 | tf_op jit(solution)/shard_map/ppermute | solution.py:367
  96.3 29.7 %collective-permute-start.18 = (f32[8,288,128]{2,1,0:T(8,128)S(1)}, f32[8,288,128]{2,1,0:T(8,128)S(1)}, u32[]{:S(2)}, u32[]{:S(2)}) collective-permute-start(f32[8,288,128]{2,1,0:T(8,128)S(1)} %bitcast_dynamic-update-slice_fusion.refs_0_), channel_id=1, source_target_pairs={{0,8},{8,0},{16,24},{24,16},{1,9},{9,1},{17,25},{25,17},{2,10},{10... | collective-permute-start | bytes 3538952 | tf_op jit(solution)/shard_map/ppermute | solution.py:367
  97.7 29.2 %collective-permute-start.22 = (f32[96,512]{1,0:T(8,128)S(1)}, f32[96,512]{1,0:T(8,128)S(1)}, u32[]{:S(2)}, u32[]{:S(2)}) collective-permute-start(f32[96,512]{1,0:T(8,128)S(1)} %copy-done.25), channel_id=1, source_target_pairs={{0,1},{1,0},{2,3},{3,2},{4,5},{5,4},{6,7},{7,6},{8,9},{9,8},{10,11... | collective-permute-start | bytes 589832 | tf_op jit(solution)/shard_map/ppermute | solution.py:433
  98.3 28.6 %collective-permute-start.23 = (f32[96,512]{1,0:T(8,128)S(1)}, f32[96,512]{1,0:T(8,128)S(1)}, u32[]{:S(2)}, u32[]{:S(2)}) collective-permute-start(f32[96,512]{1,0:T(8,128)S(1)} %copy-done.24), channel_id=1, source_target_pairs={{0,2},{1,3},{2,0},{3,1},{4,6},{5,7},{6,4},{7,5},{8,10},{9,11},{10,... | collective-permute-start | bytes 589832 | tf_op jit(solution)/shard_map/ppermute | solution.py:433
  98.4 32.5 %collective-permute-start.24 = (f32[96,512]{1,0:T(8,128)S(1)}, f32[96,512]{1,0:T(8,128)S(1)}, u32[]{:S(2)}, u32[]{:S(2)}) collective-permute-start(f32[96,512]{1,0:T(8,128)S(1)} %copy-done.23), channel_id=1, source_target_pairs={{0,3},{1,2},{2,1},{3,0},{4,7},{5,6},{6,5},{7,4},{8,11},{9,10},{10,... | collective-permute-start | bytes 589832 | tf_op jit(solution)/shard_map/ppermute | solution.py:433
  124.1 46.3 %collective-permute-start.20 = (f32[4,288,128]{2,1,0:T(8,128)}, f32[4,288,128]{2,1,0:T(8,128)}, u32[]{:S(2)}, u32[]{:S(2)}) collective-permute-start(f32[4,288,128]{2,1,0:T(8,128)} %slice.26), channel_id=1, source_target_pairs={{0,8},{8,0},{16,24},{24,16},{1,9},{9,1},{17,25},{25,17},{2,10},{10... | collective-permute-start | bytes 1769480 | tf_op jit(solution)/shard_map/ppermute | solution.py:367
  126.8 44.2 %collective-permute-start.21 = (f32[4,288,128]{2,1,0:T(8,128)}, f32[4,288,128]{2,1,0:T(8,128)}, u32[]{:S(2)}, u32[]{:S(2)}) collective-permute-start(f32[4,288,128]{2,1,0:T(8,128)} %slice.27), channel_id=1, source_target_pairs={{0,16},{8,24},{16,0},{24,8},{1,17},{9,25},{17,1},{25,9},{2,18},{10... | collective-permute-start | bytes 1769480 | tf_op jit(solution)/shard_map/ppermute | solution.py:367
  127.0 20.0 %collective-permute-start.26 = (f32[96,512]{1,0:T(8,128)S(1)}, f32[96,512]{1,0:T(8,128)S(1)}, u32[]{:S(2)}, u32[]{:S(2)}) collective-permute-start(f32[96,512]{1,0:T(8,128)S(1)} %copy-done.21), channel_id=1, source_target_pairs={{0,5},{1,4},{2,7},{3,6},{4,1},{5,0},{6,3},{7,2},{8,13},{9,12},{10,... | collective-permute-start | bytes 589832 | tf_op jit(solution)/shard_map/ppermute | solution.py:433
  131.6 21.9 %collective-permute-start.27 = (f32[96,512]{1,0:T(8,128)S(1)}, f32[96,512]{1,0:T(8,128)S(1)}, u32[]{:S(2)}, u32[]{:S(2)}) collective-permute-start(f32[96,512]{1,0:T(8,128)S(1)} %copy-done.20), channel_id=1, source_target_pairs={{0,6},{1,7},{2,4},{3,5},{4,2},{5,3},{6,0},{7,1},{8,14},{9,15},{10,... | collective-permute-start | bytes 589832 | tf_op jit(solution)/shard_map/ppermute | solution.py:433
  133.6 34.1 %collective-permute-start.11 = (f32[160,512]{1,0:T(8,128)}, f32[160,512]{1,0:T(8,128)S(1)}, u32[]{:S(2)}, u32[]{:S(2)}) collective-permute-start(f32[160,512]{1,0:T(8,128)} %get-tuple-element.66), channel_id=1, source_target_pairs={{0,1},{1,0},{2,3},{3,2},{4,5},{5,4},{6,7},{7,6},{8,9},{9,8},{10,11... | collective-permute-start | bytes 983048 | tf_op jit(solution)/shard_map/ppermute | solution.py:433
  147.6 21.1 %collective-permute-start.12 = (f32[160,512]{1,0:T(8,128)}, f32[160,512]{1,0:T(8,128)S(1)}, u32[]{:S(2)}, u32[]{:S(2)}) collective-permute-start(f32[160,512]{1,0:T(8,128)} %get-tuple-element.67), channel_id=1, source_target_pairs={{0,2},{1,3},{2,0},{3,1},{4,6},{5,7},{6,4},{7,5},{8,10},{9,11},{10,... | collective-permute-start | bytes 983048 | tf_op jit(solution)/shard_map/ppermute | solution.py:433
  161.1 33.8 %collective-permute-start.13 = (f32[160,512]{1,0:T(8,128)}, f32[160,512]{1,0:T(8,128)S(1)}, u32[]{:S(2)}, u32[]{:S(2)}) collective-permute-start(f32[160,512]{1,0:T(8,128)} %get-tuple-element.68), channel_id=1, source_target_pairs={{0,3},{1,2},{2,1},{3,0},{4,7},{5,6},{6,5},{7,4},{8,11},{9,10},{10,... | collective-permute-start | bytes 983048 | tf_op jit(solution)/shard_map/ppermute | solution.py:433
  167.8 36.3 %collective-permute-start.14 = (f32[160,512]{1,0:T(8,128)}, f32[160,512]{1,0:T(8,128)S(1)}, u32[]{:S(2)}, u32[]{:S(2)}) collective-permute-start(f32[160,512]{1,0:T(8,128)} %get-tuple-element.69), channel_id=1, source_target_pairs={{0,4},{1,5},{2,6},{3,7},{4,0},{5,1},{6,2},{7,3},{8,12},{9,13},{10,... | collective-permute-start | bytes 983048 | tf_op jit(solution)/shard_map/ppermute | solution.py:433
  168.7 42.4 %collective-permute-start.15 = (f32[160,512]{1,0:T(8,128)}, f32[160,512]{1,0:T(8,128)S(1)}, u32[]{:S(2)}, u32[]{:S(2)}) collective-permute-start(f32[160,512]{1,0:T(8,128)} %get-tuple-element.70), channel_id=1, source_target_pairs={{0,5},{1,4},{2,7},{3,6},{4,1},{5,0},{6,3},{7,2},{8,13},{9,12},{10,... | collective-permute-start | bytes 983048 | tf_op jit(solution)/shard_map/ppermute | solution.py:433
  170.4 48.1 %collective-permute-start.16 = (f32[160,512]{1,0:T(8,128)}, f32[160,512]{1,0:T(8,128)S(1)}, u32[]{:S(2)}, u32[]{:S(2)}) collective-permute-start(f32[160,512]{1,0:T(8,128)} %get-tuple-element.71), channel_id=1, source_target_pairs={{0,6},{1,7},{2,4},{3,5},{4,2},{5,3},{6,0},{7,1},{8,14},{9,15},{10,... | collective-permute-start | bytes 983048 | tf_op jit(solution)/shard_map/ppermute | solution.py:433
  171.1 55.0 %collective-permute-start.17 = (f32[160,512]{1,0:T(8,128)}, f32[160,512]{1,0:T(8,128)S(1)}, u32[]{:S(2)}, u32[]{:S(2)}) collective-permute-start(f32[160,512]{1,0:T(8,128)} %get-tuple-element.72), channel_id=1, source_target_pairs={{0,7},{1,6},{2,5},{3,4},{4,3},{5,2},{6,1},{7,0},{8,15},{9,14},{10,... | collective-permute-start | bytes 983048 | tf_op jit(solution)/shard_map/ppermute | solution.py:433
  (31 other events, 418.8 us)

commit v10 on v8

--- a/solution.py
+++ b/solution.py
@@ -440,10 +440,15 @@
         terms = fixed
 
     long = ROWS_DEV + 2 * HALO
+    first_slot = pl.BlockSpec((1, long_half, share), lambda i: (0, 0, 0))
+    kinds_of_term = [first_slot] * (len(terms[0]) - 1) + [vmem]
+    for own in terms:
+        own[-1] = pltpu.with_memory_space_constraint(own[-1], pltpu.VMEM)
     parts = pl.pallas_call(
         functools.partial(template_kernel, len(terms[0])),
-        in_specs=[vmem] * (2 * len(terms[0])),
-        out_specs=[vmem] * strips,
+        grid=(1,),
+        in_specs=kinds_of_term * 2,
+        out_specs=[pl.BlockSpec((long, share), lambda i: (0, 0))] * strips,
         out_shape=[jax.ShapeDtypeStruct((long, share), F32)] * strips,
         scratch_shapes=[pltpu.VMEM((nrow + 2 * HALO, share), F32)],
         name="template",
@@ -453,8 +458,9 @@
     came[0] = parts[0]
     for k in reversed(range(1, strips)):
         came[k] = lax.ppermute(parts[k], "strip", [(i, i ^ k) for i in range(strips)])
+    came[strips // 2], got_a = lax.optimization_barrier((came[strips // 2], got_a))
     mine = jnp.stack(came[:: sources])
-    sci_b, got_a, mine = lax.optimization_barrier((sci_b, got_a, mine))
+    sci_b, mine = lax.optimization_barrier((sci_b, mine))
     got_b = lax.all_to_all(sci_b, "strip", split_axis=0, concat_axis=0, tiled=True)
     if sources > 1:
         got_a = jnp.sum(got_a.reshape((blocks, sources) + got_a.shape[1:]), axis=1)
@@ -506,11 +512,11 @@
     )
     arrays = [pltpu.with_memory_space_constraint(x, pltpu.VMEM) for x in arrays]
     matched = convolve(*arrays, psf_poly, toep_hi, toep_lo, band, got_a)
-    unit = ROWS_DEV // 8
-    rest = pl.BlockSpec((1, unit, ncol), lambda i: (0, FIRST_PART + i, 0))
+    unit = ROWS_DEV // 16
+    rest = pl.BlockSpec((1, unit, ncol), lambda i: (0, 2 * FIRST_PART + i, 0))
     return pl.pallas_call(
         subtract_kernel,
-        grid=(8 - FIRST_PART,),
+        grid=(2 * (8 - FIRST_PART),),
         in_specs=[vmem, rest],
         out_specs=rest,
         out_shape=jax.ShapeDtypeStruct((1, ROWS_DEV, ncol), F32),

time: 178 us -> 178 us (level)
  local copies, waits for them, and re-layouts: 17.8 us -> 14 us
  waiting for transfers between devices: 80.7 us -> 82.7 us
    unnamed x35, local copies, waits for them, and re-layouts: 15.3 us -> 12.2 us
    ppermute x7, waiting for transfers between devices: 12.5 us -> 14.5 us  [shards(): lax.ppermute(parts[k], 'strip', [(i, i ^ k) for i in range(strips)])]
  transfers between devices with their start and end apart: 17 -> 17, of which waited for: 9 -> 9; matrix products, arithmetic and copies ran while one was open for 6% -> 3% of each run, Pallas kernels for 11% -> 11%
where the time goes in v10:
time: 178 us; the launch traced here: 177 us
  waiting for transfers between devices  82.7 us (46%)
  Pallas kernels  44.8 us (25%)
  starting transfers between devices  33.3 us (19%)
  local copies, waits for them, and re-layouts  14 us (8%)
  other arithmetic  2.19 us (1%)
    ppermute x8, waiting for transfers between devices, swap(): return lax.ppermute(value, axis, [(i, i ^ 1 << bit) for i in range(count)])  68.2 us
    pallas_call x1, Pallas kernels, shards(): pl.pallas_call(functools.partial(warp_kernel, (epochs, nrow, share, order...  19.3 us
    ppermute x7, waiting for transfers between devices, shards(): lax.ppermute(parts[k], 'strip', [(i, i ^ k) for i in range(strips)])  14.5 us
    pallas_call x1, Pallas kernels, shards(): matched = convolve(*arrays, psf_poly, toep_hi, toep_lo, band, got_a)  13.3 us
    unnamed x35, local copies, waits for them, and re-layouts  12.2 us
    ppermute x8, starting transfers between devices, swap(): return lax.ppermute(value, axis, [(i, i ^ 1 << bit) for i in range(count)])  10.6 us
    all_to_all x1, starting transfers between devices, shards(): lax.all_to_all(sci_b, 'strip', split_axis=0, concat_axis=0, tiled=True)  9.79 us
    ppermute x7, starting transfers between devices, shards(): lax.ppermute(parts[k], 'strip', [(i, i ^ k) for i in range(strips)])  7.56 us
  transfers between devices with their start and end apart: 17, of which 9 were waited for; matrix products, arithmetic and copies ran while one was open for 3% of the time, Pallas kernels for 11%

profile of v10, /device:TPU:0, one launch (start us, length us, event | category | flops | bytes accessed | tf_op | source)
XLA Modules:
  0.0 177.1 jit_solution(13166426416591988754)
XLA Ops:
  0.0 19.3 %warp.1 = (f32[8,96,512]{2,1,0:T(8,128)}, f32[8,160,512]{2,1,0:T(8,128)}, f32[2,1032,128]{2,1,0:T(8,128)}, f32[2,1032,128]{2,1,0:T(8,128)}, f32[2,1032,128]{2,1,0:T(8,128)}, /*index=5*/f32[2,1032,128]{2,1,0:T(8,128)}) custom-call(s32[1,12]{1,0:T(1,128)} %kind_ref.1, s32[1,8,12]{2,1,0:T(8,128)} %heights_ref.1, f32[1,12]{1,0:T(1,128)} %invvar_ref.1, ...), custom_call_target="tpu_custom_call" | custom-call | flops 8000000000 | bytes 20000000 | tf_op jit(solution)/shard_map/warp/pallas_call | solution.py:373
  19.4 2.6 %collective-permute-start = (f32[2,1032,128]{2,1,0:T(8,128)}, f32[2,1032,128]{2,1,0:T(8,128)}, u32[]{:S(2)}, u32[]{:S(2)}) collective-permute-start(f32[2,1032,128]{2,1,0:T(8,128)} %get-tuple-element.28), channel_id=1, source_target_pairs={{0,8},{8,0},{16,24},{24,16},{1,9},{9,1},{17,25},{25,17},{2,10},{10... | collective-permute-start | bytes 3170312 | tf_op jit(solution)/shard_map/ppermute | solution.py:345
  22.0 1.5 collective-permute-start.2
  23.4 5.4 %all-to-all-start = ((f32[8,96,512]{2,1,0:T(8,128)}), f32[8,96,512]{2,1,0:T(8,128)S(1)}, u32[]{:S(2)}, u32[]{:S(2)}) async-start(f32[8,96,512]{2,1,0:T(8,128)} %get-tuple-element.36), calls=%async_computation | async-start | bytes 3145728 | tf_op jit(solution)/shard_map/all_to_all | solution.py:404
  28.9 17.3 %collective-permute-done.refs_1_ = f32[2,1032,128]{2,1,0:T(8,128)} collective-permute-done((f32[2,1032,128]{2,1,0:T(8,128)}, f32[2,1032,128]{2,1,0:T(8,128)}, u32[]{:S(2)}, u32[]{:S(2)}) %collective-permute-start) | collective-permute-done | bytes 1056800 | tf_op jit(solution)/shard_map/ppermute | solution.py:345
  47.3 2.0 %collective-permute-start.1 = (f32[1,1032,128]{2,1,0:T(8,128)S(1)}, f32[1,1032,128]{2,1,0:T(8,128)S(1)}, u32[]{:S(2)}, u32[]{:S(2)}) collective-permute-start(f32[1,1032,128]{2,1,0:T(8,128)S(1)} %slice_add_fusion.1), channel_id=1, source_target_pairs={{0,16},{8,24},{16,0},{24,8},{1,17},{9,25},{17,1},{25,9},{2,18},{10... | collective-permute-start | bytes 1585160 | tf_op jit(solution)/shard_map/ppermute | solution.py:345
  50.4 1.6 collective-permute-start.3
  51.9 9.1 %collective-permute-done.1.refs_2_ = f32[1,1032,128]{2,1,0:T(8,128)S(1)} collective-permute-done((f32[1,1032,128]{2,1,0:T(8,128)S(1)}, f32[1,1032,128]{2,1,0:T(8,128)S(1)}, u32[]{:S(2)}, u32[]{:S(2)}) %collective-permute-start.1) | collective-permute-done | bytes 528416 | tf_op jit(solution)/shard_map/ppermute | solution.py:345
  61.0 2.5 %collective-permute-done.3.refs_5_ = f32[1,1032,128]{2,1,0:T(8,128)S(1)} collective-permute-done((f32[1,1032,128]{2,1,0:T(8,128)S(1)}, f32[1,1032,128]{2,1,0:T(8,128)S(1)}, u32[]{:S(2)}, u32[]{:S(2)}) %collective-permute-start.3) | collective-permute-done | bytes 528416 | tf_op jit(solution)/shard_map/ppermute | solution.py:345
  63.6 3.0 %template.1 = (f32[288,128]{1,0:T(8,128)}, f32[288,128]{1,0:T(8,128)}, f32[288,128]{1,0:T(8,128)}, f32[288,128]{1,0:T(8,128)}, f32[288,128]{1,0:T(8,128)}, /*ind...) custom-call(f32[2,1032,128]{2,1,0:T(8,128)} %get-tuple-element.27.refs_0_, ...), custom_call_target="tpu_custom_call" | custom-call | flops 2000000 | bytes 5000000 | tf_op jit(solution)/shard_map/template/pallas_call | solution.py:447
  67.0 1.4 collective-permute-start.6
  68.4 1.9 %collective-permute-start.7 = (f32[288,128]{1,0:T(8,128)}, f32[288,128]{1,0:T(8,128)S(1)}, u32[]{:S(2)}, u32[]{:S(2)}) collective-permute-start(f32[288,128]{1,0:T(8,128)} %get-tuple-element.35), channel_id=1, source_target_pairs={{0,4},{1,5},{2,6},{3,7},{4,0},{5,1},{6,2},{7,3},{8,12},{9,13},{10,... | collective-permute-start | bytes 442376 | tf_op jit(solution)/shard_map/ppermute | solution.py:460
  71.9 3.1 %collective-permute-start.9 = (f32[288,128]{1,0:T(8,128)}, f32[288,128]{1,0:T(8,128)S(1)}, u32[]{:S(2)}, u32[]{:S(2)}) collective-permute-start(f32[288,128]{1,0:T(8,128)} %get-tuple-element.39), channel_id=1, source_target_pairs={{0,6},{1,7},{2,4},{3,5},{4,2},{5,3},{6,0},{7,1},{8,14},{9,15},{10,... | collective-permute-start | bytes 442376 | tf_op jit(solution)/shard_map/ppermute | solution.py:460
  75.1 3.6 %collective-permute-done.5 = f32[288,128]{1,0:T(8,128)S(1)} collective-permute-done((f32[288,128]{1,0:T(8,128)}, f32[288,128]{1,0:T(8,128)S(1)}, u32[]{:S(2)}, u32[]{:S(2)}) %collective-permute-start.5) | collective-permute-done | bytes 147488 | tf_op jit(solution)/shard_map/ppermute | solution.py:460
  78.7 2.1 %collective-permute-done.6 = f32[288,128]{1,0:T(8,128)S(1)} collective-permute-done((f32[288,128]{1,0:T(8,128)}, f32[288,128]{1,0:T(8,128)S(1)}, u32[]{:S(2)}, u32[]{:S(2)}) %collective-permute-start.6) | collective-permute-done | bytes 147488 | tf_op jit(solution)/shard_map/ppermute | solution.py:460
  82.0 8.8 %collective-permute-done.8 = f32[288,128]{1,0:T(8,128)S(1)} collective-permute-done((f32[288,128]{1,0:T(8,128)}, f32[288,128]{1,0:T(8,128)S(1)}, u32[]{:S(2)}, u32[]{:S(2)}) %collective-permute-start.8) | collective-permute-done | bytes 147488 | tf_op jit(solution)/shard_map/ppermute | solution.py:460
  91.9 9.8 %all-to-all-start.1 = ((f32[8,160,512]{2,1,0:T(8,128)}), f32[8,160,512]{2,1,0:T(8,128)S(1)}, u32[]{:S(2)}, u32[]{:S(2)}) async-start(f32[8,160,512]{2,1,0:T(8,128)} %get-tuple-element.41), calls=%async_computation.1 | async-start | bytes 5242880 | tf_op jit(solution)/shard_map/all_to_all | solution.py:464
  103.2 27.1 %collective-permute-done.12.refs_2_ = f32[8,288,128]{2,1,0:T(8,128)S(1)} collective-permute-done((f32[8,288,128]{2,1,0:T(8,128)}, f32[8,288,128]{2,1,0:T(8,128)S(1)}, u32[]{:S(2)}, u32[]{:S(2)}) %collective-permute-start.12) | collective-permute-done | bytes 1179680 | tf_op jit(solution)/shard_map/ppermute | solution.py:345
  134.6 2.4 %bands.1 = (bf16[256,256]{1,0:T(8,128)(2,1)}, bf16[256,256]{1,0:T(8,128)(2,1)}, bf16[2,256,160]{2,1,0:T(8,128)(2,1)}) custom-call(f32[2,2,31]{2,1,0:T(2,128)} %psf_ref.1), custom_call_target="tpu_custom_call" | custom-call | flops 10000000 | bytes 500000 | tf_op jit(solution)/shard_map/bands/pallas_call | solution.py:419
  137.0 9.2 %collective-permute-done.13.refs_3_ = f32[4,288,128]{2,1,0:T(8,128)S(1)} collective-permute-done((f32[4,288,128]{2,1,0:T(8,128)}, f32[4,288,128]{2,1,0:T(8,128)S(1)}, u32[]{:S(2)}, u32[]{:S(2)}) %collective-permute-start.13) | collective-permute-done | bytes 589856 | tf_op jit(solution)/shard_map/ppermute | solution.py:345
  146.2 2.9 %collective-permute-done.14.refs_4_ = f32[4,288,128]{2,1,0:T(8,128)} collective-permute-done((f32[4,288,128]{2,1,0:T(8,128)}, f32[4,288,128]{2,1,0:T(8,128)}, u32[]{:S(2)}, u32[]{:S(2)}) %collective-permute-start.14) | collective-permute-done | bytes 589856 | tf_op jit(solution)/shard_map/ppermute | solution.py:345
  149.1 1.4 copy-done.1
  157.1 13.3 %convolve.1 = f32[256,4096]{1,0:T(8,128)} custom-call(f32[8,288,128]{2,1,0:T(8,128)S(1)} %copy-done.7, f32[8,288,128]{2,1,0:T(8,128)S(1)} %copy-done.5, f32[8,288,128]{2,1,0:T(8,128)S(1)} %copy-done.3, f32[4,288,128]{2,1,0:T(8,128)S(1)} %collective-permute-done.13.refs_3_, f32[4,288,128]{2,1,0:T(8,128)} %collective-permute-done.14.refs_4_, ...), custom_call_target="tpu_custom_call" | custom-call | flops 15000000512 | bytes 10000000 | tf_op jit(solution)/shard_map/convolve/pallas_call | solution.py:514
  170.4 6.8 %subtract.1 = f32[1,256,4096]{2,1,0:T(8,128)} custom-call(f32[8,160,512]{2,1,0:T(8,128)S(1)} %all-to-all-done.1.sci_ref, f32[1,256,4096]{2,1,0:T(8,128)} %bitcast.18), custom_call_target="tpu_custom_call", output_to_operand_aliasing={{}: (1, {})} | custom-call | flops 1000000 | bytes 6000000 | tf_op jit(solution)/shard_map/subtract/pallas_call | solution.py:517
  (55 shorter events, 18.9 us)
Async XLA Ops:
  19.4 26.8 %collective-permute-start = (f32[2,1032,128]{2,1,0:T(8,128)}, f32[2,1032,128]{2,1,0:T(8,128)}, u32[]{:S(2)}, u32[]{:S(2)}) collective-permute-start(f32[2,1032,128]{2,1,0:T(8,128)} %get-tuple-element.28), channel_id=1, source_target_pairs={{0,8},{8,0},{16,24},{24,16},{1,9},{9,1},{17,25},{25,17},{2,10},{10... | collective-permute-start | bytes 3170312 | tf_op jit(solution)/shard_map/ppermute | solution.py:345
  22.0 27.3 %collective-permute-start.2 = (f32[2,1032,128]{2,1,0:T(8,128)}, f32[2,1032,128]{2,1,0:T(8,128)}, u32[]{:S(2)}, u32[]{:S(2)}) collective-permute-start(f32[2,1032,128]{2,1,0:T(8,128)} %get-tuple-element.30), channel_id=1, source_target_pairs={{0,16},{8,24},{16,0},{24,8},{1,17},{9,25},{17,1},{25,9},{2,18},{10... | collective-permute-start | bytes 3170312 | tf_op jit(solution)/shard_map/ppermute | solution.py:345
  23.4 22.7 %copy-start.12 = (f32[2,1032,128]{2,1,0:T(8,128)S(1)}, f32[2,1032,128]{2,1,0:T(8,128)}, u32[]{:S(2)}) copy-start(f32[2,1032,128]{2,1,0:T(8,128)} %get-tuple-element.27.refs_0_) | copy-start | bytes 3170308
  23.4 57.4 %all-to-all-start = ((f32[8,96,512]{2,1,0:T(8,128)}), f32[8,96,512]{2,1,0:T(8,128)S(1)}, u32[]{:S(2)}, u32[]{:S(2)}) async-start(f32[8,96,512]{2,1,0:T(8,128)} %get-tuple-element.36), calls=%async_computation | async-start | bytes 3145728 | tf_op jit(solution)/shard_map/all_to_all | solution.py:404
  28.9 20.4 %copy-start.13 = (f32[2,1032,128]{2,1,0:T(8,128)S(1)}, f32[2,1032,128]{2,1,0:T(8,128)}, u32[]{:S(2)}) copy-start(f32[2,1032,128]{2,1,0:T(8,128)} %get-tuple-element.29.refs_3_) | copy-start | bytes 3170308
  47.3 13.8 %collective-permute-start.1 = (f32[1,1032,128]{2,1,0:T(8,128)S(1)}, f32[1,1032,128]{2,1,0:T(8,128)S(1)}, u32[]{:S(2)}, u32[]{:S(2)}) collective-permute-start(f32[1,1032,128]{2,1,0:T(8,128)S(1)} %slice_add_fusion.1), channel_id=1, source_target_pairs={{0,16},{8,24},{16,0},{24,8},{1,17},{9,25},{17,1},{25,9},{2,18},{10... | collective-permute-start | bytes 1585160 | tf_op jit(solution)/shard_map/ppermute | solution.py:345
  50.4 13.2 %collective-permute-start.3 = (f32[1,1032,128]{2,1,0:T(8,128)S(1)}, f32[1,1032,128]{2,1,0:T(8,128)S(1)}, u32[]{:S(2)}, u32[]{:S(2)}) collective-permute-start(f32[1,1032,128]{2,1,0:T(8,128)S(1)} %slice_add_fusion), channel_id=1, source_target_pairs={{0,8},{8,0},{16,24},{24,16},{1,9},{9,1},{17,25},{25,17},{2,10},{10... | collective-permute-start | bytes 1585160 | tf_op jit(solution)/shard_map/ppermute | solution.py:345
  66.6 5.4 %collective-permute-start.4 = (f32[288,128]{1,0:T(8,128)}, f32[288,128]{1,0:T(8,128)S(1)}, u32[]{:S(2)}, u32[]{:S(2)}) collective-permute-start(f32[288,128]{1,0:T(8,128)} %get-tuple-element.32), channel_id=1, source_target_pairs={{0,1},{1,0},{2,3},{3,2},{4,5},{5,4},{6,7},{7,6},{8,9},{9,8},{10,11... | collective-permute-start | bytes 442376 | tf_op jit(solution)/shard_map/ppermute | solution.py:460
  66.6 12.1 %collective-permute-start.5 = (f32[288,128]{1,0:T(8,128)}, f32[288,128]{1,0:T(8,128)S(1)}, u32[]{:S(2)}, u32[]{:S(2)}) collective-permute-start(f32[288,128]{1,0:T(8,128)} %get-tuple-element.33), channel_id=1, source_target_pairs={{0,2},{1,3},{2,0},{3,1},{4,6},{5,7},{6,4},{7,5},{8,10},{9,11},{10,... | collective-permute-start | bytes 442376 | tf_op jit(solution)/shard_map/ppermute | solution.py:460
  67.0 13.8 %collective-permute-start.6 = (f32[288,128]{1,0:T(8,128)}, f32[288,128]{1,0:T(8,128)S(1)}, u32[]{:S(2)}, u32[]{:S(2)}) collective-permute-start(f32[288,128]{1,0:T(8,128)} %get-tuple-element.34), channel_id=1, source_target_pairs={{0,3},{1,2},{2,1},{3,0},{4,7},{5,6},{6,5},{7,4},{8,11},{9,10},{10,... | collective-permute-start | bytes 442376 | tf_op jit(solution)/shard_map/ppermute | solution.py:460
  68.4 12.4 %collective-permute-start.7 = (f32[288,128]{1,0:T(8,128)}, f32[288,128]{1,0:T(8,128)S(1)}, u32[]{:S(2)}, u32[]{:S(2)}) collective-permute-start(f32[288,128]{1,0:T(8,128)} %get-tuple-element.35), channel_id=1, source_target_pairs={{0,4},{1,5},{2,6},{3,7},{4,0},{5,1},{6,2},{7,3},{8,12},{9,13},{10,... | collective-permute-start | bytes 442376 | tf_op jit(solution)/shard_map/ppermute | solution.py:460
  70.3 20.5 %collective-permute-start.8 = (f32[288,128]{1,0:T(8,128)}, f32[288,128]{1,0:T(8,128)S(1)}, u32[]{:S(2)}, u32[]{:S(2)}) collective-permute-start(f32[288,128]{1,0:T(8,128)} %get-tuple-element.38), channel_id=1, source_target_pairs={{0,5},{1,4},{2,7},{3,6},{4,1},{5,0},{6,3},{7,2},{8,13},{9,12},{10,... | collective-permute-start | bytes 442376 | tf_op jit(solution)/shard_map/ppermute | solution.py:460
  71.9 18.9 %collective-permute-start.9 = (f32[288,128]{1,0:T(8,128)}, f32[288,128]{1,0:T(8,128)S(1)}, u32[]{:S(2)}, u32[]{:S(2)}) collective-permute-start(f32[288,128]{1,0:T(8,128)} %get-tuple-element.39), channel_id=1, source_target_pairs={{0,6},{1,7},{2,4},{3,5},{4,2},{5,3},{6,0},{7,1},{8,14},{9,15},{10,... | collective-permute-start | bytes 442376 | tf_op jit(solution)/shard_map/ppermute | solution.py:460
  78.7 12.2 %collective-permute-start.10 = (f32[288,128]{1,0:T(8,128)}, f32[288,128]{1,0:T(8,128)S(1)}, u32[]{:S(2)}, u32[]{:S(2)}) collective-permute-start(f32[288,128]{1,0:T(8,128)} %get-tuple-element.40), channel_id=1, source_target_pairs={{0,7},{1,6},{2,5},{3,4},{4,3},{5,2},{6,1},{7,0},{8,15},{9,14},{10,... | collective-permute-start | bytes 442376 | tf_op jit(solution)/shard_map/ppermute | solution.py:460
  91.9 78.4 %all-to-all-start.1 = ((f32[8,160,512]{2,1,0:T(8,128)}), f32[8,160,512]{2,1,0:T(8,128)S(1)}, u32[]{:S(2)}, u32[]{:S(2)}) async-start(f32[8,160,512]{2,1,0:T(8,128)} %get-tuple-element.41), calls=%async_computation.1 | async-start | bytes 5242880 | tf_op jit(solution)/shard_map/all_to_all | solution.py:464
  101.7 47.4 %copy-start.8 = (f32[4,2,6]{2,1,0:T(2,128)S(1)}, f32[4,2,6]{2,1,0:T(2,128)}, u32[]{:S(2)}) copy-start(f32[4,2,6]{2,1,0:T(2,128)} %refs_5_.1) | copy-start | bytes 580
  101.7 28.6 %collective-permute-start.12 = (f32[8,288,128]{2,1,0:T(8,128)}, f32[8,288,128]{2,1,0:T(8,128)S(1)}, u32[]{:S(2)}, u32[]{:S(2)}) collective-permute-start(f32[8,288,128]{2,1,0:T(8,128)} %copy-done.6), channel_id=1, source_target_pairs={{0,16},{8,24},{16,0},{24,8},{1,17},{9,25},{17,1},{25,9},{2,18},{10... | collective-permute-start | bytes 3538952 | tf_op jit(solution)/shard_map/ppermute | solution.py:345
  102.8 29.6 %collective-permute-start.11 = (f32[8,288,128]{2,1,0:T(8,128)}, f32[8,288,128]{2,1,0:T(8,128)S(1)}, u32[]{:S(2)}, u32[]{:S(2)}) collective-permute-start(f32[8,288,128]{2,1,0:T(8,128)} %copy-done.6), channel_id=1, source_target_pairs={{0,8},{8,0},{16,24},{24,16},{1,9},{9,1},{17,25},{25,17},{2,10},{10... | collective-permute-start | bytes 3538952 | tf_op jit(solution)/shard_map/ppermute | solution.py:345
  130.3 2.9 %copy-start.2 = (f32[8,288,128]{2,1,0:T(8,128)}, f32[8,288,128]{2,1,0:T(8,128)S(1)}, u32[]{:S(2)}) copy-start(f32[8,288,128]{2,1,0:T(8,128)S(1)} %collective-permute-done.12.refs_2_) | copy-start | bytes 3538948
  131.2 15.0 %collective-permute-start.13 = (f32[4,288,128]{2,1,0:T(8,128)}, f32[4,288,128]{2,1,0:T(8,128)S(1)}, u32[]{:S(2)}, u32[]{:S(2)}) collective-permute-start(f32[4,288,128]{2,1,0:T(8,128)} %slice.26), channel_id=1, source_target_pairs={{0,8},{8,0},{16,24},{24,16},{1,9},{9,1},{17,25},{25,17},{2,10},{10... | collective-permute-start | bytes 1769480 | tf_op jit(solution)/shard_map/ppermute | solution.py:345
  134.3 14.8 %collective-permute-start.14 = (f32[4,288,128]{2,1,0:T(8,128)}, f32[4,288,128]{2,1,0:T(8,128)}, u32[]{:S(2)}, u32[]{:S(2)}) collective-permute-start(f32[4,288,128]{2,1,0:T(8,128)} %slice.27), channel_id=1, source_target_pairs={{0,16},{8,24},{16,0},{24,8},{1,17},{9,25},{17,1},{25,9},{2,18},{10... | collective-permute-start | bytes 1769480 | tf_op jit(solution)/shard_map/ppermute | solution.py:345
  149.1 1.4 copy-start.1
  150.5 1.3 copy-start.3
  153.1 1.3 copy-start.7
  (7 other events, 7.3 us)

commit v11 on v10

--- a/solution.py
+++ b/solution.py
@@ -106,19 +106,6 @@
             num_s[...] = jnp.zeros_like(num_s)
             wt_s[...] = jnp.zeros_like(wt_s)
 
-    def warped(i, top):
-        t = step * together + i
-        kind = kind_ref[0, t]
-        height = heights_ref[0, block, offset_in + t]
-        start = pl.multiple_of(jnp.minimum(lax.div(top, 8) * 8, nrow - span), 8)
-        off = top - start
-        across = dot3(split(raw_ref[i]), (chi_s[kind], clo_s[kind]), trans_b=True)
-        live = lax.broadcasted_iota(jnp.int32, (tile_rows, tile_rows), 1) < height
-        rows = jnp.concatenate(
-            [jnp.where(live, rmat_s[kind], 0.0), jnp.zeros((8, tile_rows), F32)], axis=0
-        )
-        return t, height, start, off, dot3(split(pltpu.roll(rows, off, 0)), split(across))
-
     for i in range(together):
         kind = kind_ref[0, step * together + i]
 
@@ -136,28 +123,57 @@
             lax.fori_loop(0, 8, divide, 0)
 
     top = top_s[0]
-    results = []
+    local = lax.broadcasted_iota(jnp.int32, (span, share), 0)
+    flat = lax.broadcasted_iota(jnp.int32, wt_s.shape, 0) * share + lax.broadcasted_iota(
+        jnp.int32, wt_s.shape, 1
+    )
+    live = lax.broadcasted_iota(jnp.int32, (tile_rows, tile_rows), 1)
+    tops, heights, kind_of = [], [], []
     for i in range(together):
-        results.append((top, warped(i, top)))
-        top = top + results[-1][1][1]
+        t = step * together + i
+        tops.append(top)
+        heights.append(heights_ref[0, block, offset_in + t])
+        kind_of.append(kind_ref[0, t])
+        top = top + heights[i]
     top_s[0] = top
     after = top
-
-    for top, (t, height, start, off, placed) in results:
-        weight = invvar_ref[0, t]
-        local = lax.broadcasted_iota(jnp.int32, (span, share), 0) - off
-        own = (local >= 0) & (local < height)
-        here = pl.ds(start, span)
+    starts = [pl.multiple_of(jnp.minimum(lax.div(x, 8) * 8, nrow - span), 8) for x in tops]
+    images, wides, mixes, halves, placed = [{} for _ in range(5)]
+
+    def load(i):
+        images[i] = split(raw_ref[i])
+
+    def across(i):
+        wides[i] = dot3(images[i], (chi_s[kind_of[i]], clo_s[kind_of[i]]), trans_b=True)
+
+    def divide_half(i):
+        rows = jnp.concatenate(
+            [jnp.where(live < heights[i], rmat_s[kind_of[i]], 0.0), jnp.zeros((8, tile_rows), F32)], axis=0
+        )
+        mixes[i] = split(pltpu.roll(rows, tops[i] - starts[i], 0))
+        halves[i] = split(wides[i])
+
+    def down(i):
+        placed[i] = dot3(mixes[i], halves[i])
+
+    def store(i):
+        weight = invvar_ref[0, step * together + i]
+        inside = local - (tops[i] - starts[i])
+        own = (inside >= 0) & (inside < heights[i])
+        here = pl.ds(starts[i], span)
         for q in range(epochs):
             columns = pl.ds(q * share, share)
-            piece = placed[:, q * share : (q + 1) * share]
+            piece = placed[i][:, q * share : (q + 1) * share]
             slot = jnp.bitwise_xor(me, q)
             sci_s[here, columns] = jnp.where(own, piece, sci_s[here, columns])
             num_s[slot, here, :] = jnp.where(own, weight * piece, num_s[slot, here, :])
-        flat = lax.broadcasted_iota(jnp.int32, wt_s.shape, 0) * share + lax.broadcasted_iota(
-            jnp.int32, wt_s.shape, 1
-        )
-        wt_s[...] = jnp.where((flat >= top) & (flat < top + height), weight, wt_s[...])
+        wt_s[...] = jnp.where((flat >= tops[i]) & (flat < tops[i] + heights[i]), weight, wt_s[...])
+
+    phases = (load, across, divide_half, down, store)
+    for n in range(len(phases) + together - 1):
+        for i in range(together):
+            if 0 <= n - i < len(phases):
+                phases[n - i](i)
 
     before = top_s[1]
     final = jnp.where(step == last, nrow, jnp.minimum(lax.div(after, 8) * 8, nrow - span))
@@ -512,11 +528,11 @@
     )
     arrays = [pltpu.with_memory_space_constraint(x, pltpu.VMEM) for x in arrays]
     matched = convolve(*arrays, psf_poly, toep_hi, toep_lo, band, got_a)
-    unit = ROWS_DEV // 16
-    rest = pl.BlockSpec((1, unit, ncol), lambda i: (0, 2 * FIRST_PART + i, 0))
+    unit = ROWS_DEV // 8
+    rest = pl.BlockSpec((1, unit, ncol), lambda i: (0, FIRST_PART + i, 0))
     return pl.pallas_call(
         subtract_kernel,
-        grid=(2 * (8 - FIRST_PART),),
+        grid=(8 - FIRST_PART,),
         in_specs=[vmem, rest],
         out_specs=rest,
         out_shape=jax.ShapeDtypeStruct((1, ROWS_DEV, ncol), F32),

time: 178 us -> 174 us (0.978)
  Pallas kernels: 44.8 us -> 40.6 us
    pallas_call x1, Pallas kernels: 19.3 us -> 17.2 us  [shards(): pl.pallas_call(functools.partial(warp_kernel, (epochs, nrow, share, order...]
    pallas_call x1, Pallas kernels: 6.77 us -> 4.73 us  [shards(): pl.pallas_call(subtract_kernel, grid=(8 - FIRST_PART,), in_specs=[vmem, r...]
where the time goes in v11:
time: 174 us; the launch traced here: 173 us
  waiting for transfers between devices  82.7 us (48%)
  Pallas kernels  40.6 us (23%)
  starting transfers between devices  33.3 us (19%)
  local copies, waits for them, and re-layouts  14 us (8%)
  other arithmetic  2.19 us (1%)
    ppermute x8, waiting for transfers between devices, swap(): return lax.ppermute(value, axis, [(i, i ^ 1 << bit) for i in range(count)])  68.2 us
    pallas_call x1, Pallas kernels, shards(): pl.pallas_call(functools.partial(warp_kernel, (epochs, nrow, share, order...  17.2 us
    ppermute x7, waiting for transfers between devices, shards(): lax.ppermute(parts[k], 'strip', [(i, i ^ k) for i in range(strips)])  14.5 us
    pallas_call x1, Pallas kernels, shards(): matched = convolve(*arrays, psf_poly, toep_hi, toep_lo, band, got_a)  13.3 us
    unnamed x35, local copies, waits for them, and re-layouts  12.2 us
    ppermute x8, starting transfers between devices, swap(): return lax.ppermute(value, axis, [(i, i ^ 1 << bit) for i in range(count)])  10.6 us
    all_to_all x1, starting transfers between devices, shards(): lax.all_to_all(sci_b, 'strip', split_axis=0, concat_axis=0, tiled=True)  9.79 us
    ppermute x7, starting transfers between devices, shards(): lax.ppermute(parts[k], 'strip', [(i, i ^ k) for i in range(strips)])  7.56 us
  transfers between devices with their start and end apart: 17, of which 9 were waited for; matrix products, arithmetic and copies ran while one was open for 3% of the time, Pallas kernels for 11%

profile of v11, /device:TPU:0, one launch (start us, length us, event | category | flops | bytes accessed | tf_op | source)
XLA Modules:
  0.0 173.0 jit_solution(18122696979818039664)
XLA Ops:
  0.0 17.2 %warp.1 = (f32[8,96,512]{2,1,0:T(8,128)}, f32[8,160,512]{2,1,0:T(8,128)}, f32[2,1032,128]{2,1,0:T(8,128)}, f32[2,1032,128]{2,1,0:T(8,128)}, f32[2,1032,128]{2,1,0:T(8,128)}, /*index=5*/f32[2,1032,128]{2,1,0:T(8,128)}) custom-call(s32[1,12]{1,0:T(1,128)} %kind_ref.1, s32[1,8,12]{2,1,0:T(8,128)} %heights_ref.1, f32[1,12]{1,0:T(1,128)} %invvar_ref.1, ...), custom_call_target="tpu_custom_call" | custom-call | flops 8000000000 | bytes 20000000 | tf_op jit(solution)/shard_map/warp/pallas_call | solution.py:389
  17.2 2.6 %collective-permute-start = (f32[2,1032,128]{2,1,0:T(8,128)}, f32[2,1032,128]{2,1,0:T(8,128)}, u32[]{:S(2)}, u32[]{:S(2)}) collective-permute-start(f32[2,1032,128]{2,1,0:T(8,128)} %get-tuple-element.28), channel_id=1, source_target_pairs={{0,8},{8,0},{16,24},{24,16},{1,9},{9,1},{17,25},{25,17},{2,10},{10... | collective-permute-start | bytes 3170312 | tf_op jit(solution)/shard_map/ppermute | solution.py:361
  19.9 1.5 collective-permute-start.2
  21.3 5.4 %all-to-all-start = ((f32[8,96,512]{2,1,0:T(8,128)}), f32[8,96,512]{2,1,0:T(8,128)S(1)}, u32[]{:S(2)}, u32[]{:S(2)}) async-start(f32[8,96,512]{2,1,0:T(8,128)} %get-tuple-element.36), calls=%async_computation | async-start | bytes 3145728 | tf_op jit(solution)/shard_map/all_to_all | solution.py:420
  26.8 17.3 %collective-permute-done.refs_1_ = f32[2,1032,128]{2,1,0:T(8,128)} collective-permute-done((f32[2,1032,128]{2,1,0:T(8,128)}, f32[2,1032,128]{2,1,0:T(8,128)}, u32[]{:S(2)}, u32[]{:S(2)}) %collective-permute-start) | collective-permute-done | bytes 1056800 | tf_op jit(solution)/shard_map/ppermute | solution.py:361
  45.1 2.0 %collective-permute-start.1 = (f32[1,1032,128]{2,1,0:T(8,128)S(1)}, f32[1,1032,128]{2,1,0:T(8,128)S(1)}, u32[]{:S(2)}, u32[]{:S(2)}) collective-permute-start(f32[1,1032,128]{2,1,0:T(8,128)S(1)} %slice_add_fusion.1), channel_id=1, source_target_pairs={{0,16},{8,24},{16,0},{24,8},{1,17},{9,25},{17,1},{25,9},{2,18},{10... | collective-permute-start | bytes 1585160 | tf_op jit(solution)/shard_map/ppermute | solution.py:361
  48.3 1.6 collective-permute-start.3
  49.9 9.1 %collective-permute-done.1.refs_2_ = f32[1,1032,128]{2,1,0:T(8,128)S(1)} collective-permute-done((f32[1,1032,128]{2,1,0:T(8,128)S(1)}, f32[1,1032,128]{2,1,0:T(8,128)S(1)}, u32[]{:S(2)}, u32[]{:S(2)}) %collective-permute-start.1) | collective-permute-done | bytes 528416 | tf_op jit(solution)/shard_map/ppermute | solution.py:361
  58.9 2.6 %collective-permute-done.3.refs_5_ = f32[1,1032,128]{2,1,0:T(8,128)S(1)} collective-permute-done((f32[1,1032,128]{2,1,0:T(8,128)S(1)}, f32[1,1032,128]{2,1,0:T(8,128)S(1)}, u32[]{:S(2)}, u32[]{:S(2)}) %collective-permute-start.3) | collective-permute-done | bytes 528416 | tf_op jit(solution)/shard_map/ppermute | solution.py:361
  61.5 3.0 %template.1 = (f32[288,128]{1,0:T(8,128)}, f32[288,128]{1,0:T(8,128)}, f32[288,128]{1,0:T(8,128)}, f32[288,128]{1,0:T(8,128)}, f32[288,128]{1,0:T(8,128)}, /*ind...) custom-call(f32[2,1032,128]{2,1,0:T(8,128)} %get-tuple-element.27.refs_0_, ...), custom_call_target="tpu_custom_call" | custom-call | flops 2000000 | bytes 5000000 | tf_op jit(solution)/shard_map/template/pallas_call | solution.py:463
  65.0 1.3 collective-permute-start.6
  66.4 1.9 %collective-permute-start.7 = (f32[288,128]{1,0:T(8,128)}, f32[288,128]{1,0:T(8,128)S(1)}, u32[]{:S(2)}, u32[]{:S(2)}) collective-permute-start(f32[288,128]{1,0:T(8,128)} %get-tuple-element.35), channel_id=1, source_target_pairs={{0,4},{1,5},{2,6},{3,7},{4,0},{5,1},{6,2},{7,3},{8,12},{9,13},{10,... | collective-permute-start | bytes 442376 | tf_op jit(solution)/shard_map/ppermute | solution.py:476
  69.8 3.1 %collective-permute-start.9 = (f32[288,128]{1,0:T(8,128)}, f32[288,128]{1,0:T(8,128)S(1)}, u32[]{:S(2)}, u32[]{:S(2)}) collective-permute-start(f32[288,128]{1,0:T(8,128)} %get-tuple-element.39), channel_id=1, source_target_pairs={{0,6},{1,7},{2,4},{3,5},{4,2},{5,3},{6,0},{7,1},{8,14},{9,15},{10,... | collective-permute-start | bytes 442376 | tf_op jit(solution)/shard_map/ppermute | solution.py:476
  73.0 3.6 %collective-permute-done.5 = f32[288,128]{1,0:T(8,128)S(1)} collective-permute-done((f32[288,128]{1,0:T(8,128)}, f32[288,128]{1,0:T(8,128)S(1)}, u32[]{:S(2)}, u32[]{:S(2)}) %collective-permute-start.5) | collective-permute-done | bytes 147488 | tf_op jit(solution)/shard_map/ppermute | solution.py:476
  76.6 2.1 %collective-permute-done.6 = f32[288,128]{1,0:T(8,128)S(1)} collective-permute-done((f32[288,128]{1,0:T(8,128)}, f32[288,128]{1,0:T(8,128)S(1)}, u32[]{:S(2)}, u32[]{:S(2)}) %collective-permute-start.6) | collective-permute-done | bytes 147488 | tf_op jit(solution)/shard_map/ppermute | solution.py:476
  80.0 8.8 %collective-permute-done.8 = f32[288,128]{1,0:T(8,128)S(1)} collective-permute-done((f32[288,128]{1,0:T(8,128)}, f32[288,128]{1,0:T(8,128)S(1)}, u32[]{:S(2)}, u32[]{:S(2)}) %collective-permute-start.8) | collective-permute-done | bytes 147488 | tf_op jit(solution)/shard_map/ppermute | solution.py:476
  89.8 9.8 %all-to-all-start.1 = ((f32[8,160,512]{2,1,0:T(8,128)}), f32[8,160,512]{2,1,0:T(8,128)S(1)}, u32[]{:S(2)}, u32[]{:S(2)}) async-start(f32[8,160,512]{2,1,0:T(8,128)} %get-tuple-element.41), calls=%async_computation.1 | async-start | bytes 5242880 | tf_op jit(solution)/shard_map/all_to_all | solution.py:480
  101.1 27.1 %collective-permute-done.12.refs_2_ = f32[8,288,128]{2,1,0:T(8,128)S(1)} collective-permute-done((f32[8,288,128]{2,1,0:T(8,128)}, f32[8,288,128]{2,1,0:T(8,128)S(1)}, u32[]{:S(2)}, u32[]{:S(2)}) %collective-permute-start.12) | collective-permute-done | bytes 1179680 | tf_op jit(solution)/shard_map/ppermute | solution.py:361
  132.5 2.4 %bands.1 = (bf16[256,256]{1,0:T(8,128)(2,1)}, bf16[256,256]{1,0:T(8,128)(2,1)}, bf16[2,256,160]{2,1,0:T(8,128)(2,1)}) custom-call(f32[2,2,31]{2,1,0:T(2,128)} %psf_ref.1), custom_call_target="tpu_custom_call" | custom-call | flops 10000000 | bytes 500000 | tf_op jit(solution)/shard_map/bands/pallas_call | solution.py:435
  134.9 9.3 %collective-permute-done.13.refs_3_ = f32[4,288,128]{2,1,0:T(8,128)S(1)} collective-permute-done((f32[4,288,128]{2,1,0:T(8,128)}, f32[4,288,128]{2,1,0:T(8,128)S(1)}, u32[]{:S(2)}, u32[]{:S(2)}) %collective-permute-start.13) | collective-permute-done | bytes 589856 | tf_op jit(solution)/shard_map/ppermute | solution.py:361
  144.1 2.9 %collective-permute-done.14.refs_4_ = f32[4,288,128]{2,1,0:T(8,128)} collective-permute-done((f32[4,288,128]{2,1,0:T(8,128)}, f32[4,288,128]{2,1,0:T(8,128)}, u32[]{:S(2)}, u32[]{:S(2)}) %collective-permute-start.14) | collective-permute-done | bytes 589856 | tf_op jit(solution)/shard_map/ppermute | solution.py:361
  147.0 1.4 copy-done.1
  155.0 13.3 %convolve.1 = f32[256,4096]{1,0:T(8,128)} custom-call(f32[8,288,128]{2,1,0:T(8,128)S(1)} %copy-done.7, f32[8,288,128]{2,1,0:T(8,128)S(1)} %copy-done.5, f32[8,288,128]{2,1,0:T(8,128)S(1)} %copy-done.3, f32[4,288,128]{2,1,0:T(8,128)S(1)} %collective-permute-done.13.refs_3_, f32[4,288,128]{2,1,0:T(8,128)} %collective-permute-done.14.refs_4_, ...), custom_call_target="tpu_custom_call" | custom-call | flops 15000000512 | bytes 10000000 | tf_op jit(solution)/shard_map/convolve/pallas_call | solution.py:530
  168.2 4.7 %subtract.1 = f32[1,256,4096]{2,1,0:T(8,128)} custom-call(f32[8,160,512]{2,1,0:T(8,128)S(1)} %all-to-all-done.1.sci_ref, f32[1,256,4096]{2,1,0:T(8,128)} %bitcast.18), custom_call_target="tpu_custom_call", output_to_operand_aliasing={{}: (1, {})} | custom-call | flops 1000000 | bytes 6000000 | tf_op jit(solution)/shard_map/subtract/pallas_call | solution.py:533
  (55 shorter events, 18.9 us)
Async XLA Ops:
  17.2 26.8 %collective-permute-start = (f32[2,1032,128]{2,1,0:T(8,128)}, f32[2,1032,128]{2,1,0:T(8,128)}, u32[]{:S(2)}, u32[]{:S(2)}) collective-permute-start(f32[2,1032,128]{2,1,0:T(8,128)} %get-tuple-element.28), channel_id=1, source_target_pairs={{0,8},{8,0},{16,24},{24,16},{1,9},{9,1},{17,25},{25,17},{2,10},{10... | collective-permute-start | bytes 3170312 | tf_op jit(solution)/shard_map/ppermute | solution.py:361
  19.9 27.3 %collective-permute-start.2 = (f32[2,1032,128]{2,1,0:T(8,128)}, f32[2,1032,128]{2,1,0:T(8,128)}, u32[]{:S(2)}, u32[]{:S(2)}) collective-permute-start(f32[2,1032,128]{2,1,0:T(8,128)} %get-tuple-element.30), channel_id=1, source_target_pairs={{0,16},{8,24},{16,0},{24,8},{1,17},{9,25},{17,1},{25,9},{2,18},{10... | collective-permute-start | bytes 3170312 | tf_op jit(solution)/shard_map/ppermute | solution.py:361
  21.3 22.7 %copy-start.12 = (f32[2,1032,128]{2,1,0:T(8,128)S(1)}, f32[2,1032,128]{2,1,0:T(8,128)}, u32[]{:S(2)}) copy-start(f32[2,1032,128]{2,1,0:T(8,128)} %get-tuple-element.27.refs_0_) | copy-start | bytes 3170308
  21.3 57.5 %all-to-all-start = ((f32[8,96,512]{2,1,0:T(8,128)}), f32[8,96,512]{2,1,0:T(8,128)S(1)}, u32[]{:S(2)}, u32[]{:S(2)}) async-start(f32[8,96,512]{2,1,0:T(8,128)} %get-tuple-element.36), calls=%async_computation | async-start | bytes 3145728 | tf_op jit(solution)/shard_map/all_to_all | solution.py:420
  26.8 20.4 %copy-start.13 = (f32[2,1032,128]{2,1,0:T(8,128)S(1)}, f32[2,1032,128]{2,1,0:T(8,128)}, u32[]{:S(2)}) copy-start(f32[2,1032,128]{2,1,0:T(8,128)} %get-tuple-element.29.refs_3_) | copy-start | bytes 3170308
  45.1 13.8 %collective-permute-start.1 = (f32[1,1032,128]{2,1,0:T(8,128)S(1)}, f32[1,1032,128]{2,1,0:T(8,128)S(1)}, u32[]{:S(2)}, u32[]{:S(2)}) collective-permute-start(f32[1,1032,128]{2,1,0:T(8,128)S(1)} %slice_add_fusion.1), channel_id=1, source_target_pairs={{0,16},{8,24},{16,0},{24,8},{1,17},{9,25},{17,1},{25,9},{2,18},{10... | collective-permute-start | bytes 1585160 | tf_op jit(solution)/shard_map/ppermute | solution.py:361
  48.3 13.2 %collective-permute-start.3 = (f32[1,1032,128]{2,1,0:T(8,128)S(1)}, f32[1,1032,128]{2,1,0:T(8,128)S(1)}, u32[]{:S(2)}, u32[]{:S(2)}) collective-permute-start(f32[1,1032,128]{2,1,0:T(8,128)S(1)} %slice_add_fusion), channel_id=1, source_target_pairs={{0,8},{8,0},{16,24},{24,16},{1,9},{9,1},{17,25},{25,17},{2,10},{10... | collective-permute-start | bytes 1585160 | tf_op jit(solution)/shard_map/ppermute | solution.py:361
  64.5 5.4 %collective-permute-start.4 = (f32[288,128]{1,0:T(8,128)}, f32[288,128]{1,0:T(8,128)S(1)}, u32[]{:S(2)}, u32[]{:S(2)}) collective-permute-start(f32[288,128]{1,0:T(8,128)} %get-tuple-element.32), channel_id=1, source_target_pairs={{0,1},{1,0},{2,3},{3,2},{4,5},{5,4},{6,7},{7,6},{8,9},{9,8},{10,11... | collective-permute-start | bytes 442376 | tf_op jit(solution)/shard_map/ppermute | solution.py:476
  64.5 12.1 %collective-permute-start.5 = (f32[288,128]{1,0:T(8,128)}, f32[288,128]{1,0:T(8,128)S(1)}, u32[]{:S(2)}, u32[]{:S(2)}) collective-permute-start(f32[288,128]{1,0:T(8,128)} %get-tuple-element.33), channel_id=1, source_target_pairs={{0,2},{1,3},{2,0},{3,1},{4,6},{5,7},{6,4},{7,5},{8,10},{9,11},{10,... | collective-permute-start | bytes 442376 | tf_op jit(solution)/shard_map/ppermute | solution.py:476
  65.0 13.7 %collective-permute-start.6 = (f32[288,128]{1,0:T(8,128)}, f32[288,128]{1,0:T(8,128)S(1)}, u32[]{:S(2)}, u32[]{:S(2)}) collective-permute-start(f32[288,128]{1,0:T(8,128)} %get-tuple-element.34), channel_id=1, source_target_pairs={{0,3},{1,2},{2,1},{3,0},{4,7},{5,6},{6,5},{7,4},{8,11},{9,10},{10,... | collective-permute-start | bytes 442376 | tf_op jit(solution)/shard_map/ppermute | solution.py:476
  66.4 12.4 %collective-permute-start.7 = (f32[288,128]{1,0:T(8,128)}, f32[288,128]{1,0:T(8,128)S(1)}, u32[]{:S(2)}, u32[]{:S(2)}) collective-permute-start(f32[288,128]{1,0:T(8,128)} %get-tuple-element.35), channel_id=1, source_target_pairs={{0,4},{1,5},{2,6},{3,7},{4,0},{5,1},{6,2},{7,3},{8,12},{9,13},{10,... | collective-permute-start | bytes 442376 | tf_op jit(solution)/shard_map/ppermute | solution.py:476
  68.2 20.5 %collective-permute-start.8 = (f32[288,128]{1,0:T(8,128)}, f32[288,128]{1,0:T(8,128)S(1)}, u32[]{:S(2)}, u32[]{:S(2)}) collective-permute-start(f32[288,128]{1,0:T(8,128)} %get-tuple-element.38), channel_id=1, source_target_pairs={{0,5},{1,4},{2,7},{3,6},{4,1},{5,0},{6,3},{7,2},{8,13},{9,12},{10,... | collective-permute-start | bytes 442376 | tf_op jit(solution)/shard_map/ppermute | solution.py:476
  69.8 18.9 %collective-permute-start.9 = (f32[288,128]{1,0:T(8,128)}, f32[288,128]{1,0:T(8,128)S(1)}, u32[]{:S(2)}, u32[]{:S(2)}) collective-permute-start(f32[288,128]{1,0:T(8,128)} %get-tuple-element.39), channel_id=1, source_target_pairs={{0,6},{1,7},{2,4},{3,5},{4,2},{5,3},{6,0},{7,1},{8,14},{9,15},{10,... | collective-permute-start | bytes 442376 | tf_op jit(solution)/shard_map/ppermute | solution.py:476
  76.6 12.2 %collective-permute-start.10 = (f32[288,128]{1,0:T(8,128)}, f32[288,128]{1,0:T(8,128)S(1)}, u32[]{:S(2)}, u32[]{:S(2)}) collective-permute-start(f32[288,128]{1,0:T(8,128)} %get-tuple-element.40), channel_id=1, source_target_pairs={{0,7},{1,6},{2,5},{3,4},{4,3},{5,2},{6,1},{7,0},{8,15},{9,14},{10,... | collective-permute-start | bytes 442376 | tf_op jit(solution)/shard_map/ppermute | solution.py:476
  89.8 78.4 %all-to-all-start.1 = ((f32[8,160,512]{2,1,0:T(8,128)}), f32[8,160,512]{2,1,0:T(8,128)S(1)}, u32[]{:S(2)}, u32[]{:S(2)}) async-start(f32[8,160,512]{2,1,0:T(8,128)} %get-tuple-element.41), calls=%async_computation.1 | async-start | bytes 5242880 | tf_op jit(solution)/shard_map/all_to_all | solution.py:480
  99.6 47.4 %copy-start.8 = (f32[4,2,6]{2,1,0:T(2,128)S(1)}, f32[4,2,6]{2,1,0:T(2,128)}, u32[]{:S(2)}) copy-start(f32[4,2,6]{2,1,0:T(2,128)} %refs_5_.1) | copy-start | bytes 580
  99.6 28.6 %collective-permute-start.12 = (f32[8,288,128]{2,1,0:T(8,128)}, f32[8,288,128]{2,1,0:T(8,128)S(1)}, u32[]{:S(2)}, u32[]{:S(2)}) collective-permute-start(f32[8,288,128]{2,1,0:T(8,128)} %copy-done.6), channel_id=1, source_target_pairs={{0,16},{8,24},{16,0},{24,8},{1,17},{9,25},{17,1},{25,9},{2,18},{10... | collective-permute-start | bytes 3538952 | tf_op jit(solution)/shard_map/ppermute | solution.py:361
  100.7 29.5 %collective-permute-start.11 = (f32[8,288,128]{2,1,0:T(8,128)}, f32[8,288,128]{2,1,0:T(8,128)S(1)}, u32[]{:S(2)}, u32[]{:S(2)}) collective-permute-start(f32[8,288,128]{2,1,0:T(8,128)} %copy-done.6), channel_id=1, source_target_pairs={{0,8},{8,0},{16,24},{24,16},{1,9},{9,1},{17,25},{25,17},{2,10},{10... | collective-permute-start | bytes 3538952 | tf_op jit(solution)/shard_map/ppermute | solution.py:361
  128.2 2.9 %copy-start.2 = (f32[8,288,128]{2,1,0:T(8,128)}, f32[8,288,128]{2,1,0:T(8,128)S(1)}, u32[]{:S(2)}) copy-start(f32[8,288,128]{2,1,0:T(8,128)S(1)} %collective-permute-done.12.refs_2_) | copy-start | bytes 3538948
  129.1 15.0 %collective-permute-start.13 = (f32[4,288,128]{2,1,0:T(8,128)}, f32[4,288,128]{2,1,0:T(8,128)S(1)}, u32[]{:S(2)}, u32[]{:S(2)}) collective-permute-start(f32[4,288,128]{2,1,0:T(8,128)} %slice.26), channel_id=1, source_target_pairs={{0,8},{8,0},{16,24},{24,16},{1,9},{9,1},{17,25},{25,17},{2,10},{10... | collective-permute-start | bytes 1769480 | tf_op jit(solution)/shard_map/ppermute | solution.py:361
  132.1 14.8 %collective-permute-start.14 = (f32[4,288,128]{2,1,0:T(8,128)}, f32[4,288,128]{2,1,0:T(8,128)}, u32[]{:S(2)}, u32[]{:S(2)}) collective-permute-start(f32[4,288,128]{2,1,0:T(8,128)} %slice.27), channel_id=1, source_target_pairs={{0,16},{8,24},{16,0},{24,8},{1,17},{9,25},{17,1},{25,9},{2,18},{10... | collective-permute-start | bytes 1769480 | tf_op jit(solution)/shard_map/ppermute | solution.py:361
  147.0 1.4 copy-start.1
  148.4 1.3 copy-start.3
  149.7 1.3 copy-start.5
  (7 other events, 7.3 us)

commit v12 on v11

--- a/solution.py
+++ b/solution.py
@@ -80,8 +80,8 @@
         base = s * rows_dev
         part = base // nhalf
         pairs = [
-            (sci_s.at[pl.ds(base, rows_a)], sci_a.at[s]),
-            (sci_s.at[pl.ds(base + rows_a, rows_dev - rows_a)], sci_b.at[s]),
+            (sci_s.at[pl.ds(base + rows_dev - rows_a, rows_a)], sci_a.at[s]),
+            (sci_s.at[pl.ds(base, rows_dev - rows_a)], sci_b.at[s]),
         ]
         for slots, out in zip(slot_order(epochs, orders[part]), outs[part]):
             for place, j in enumerate(slots):
@@ -338,12 +338,14 @@
                 coeff = one + v * (two + poly_ref[me, k, 5] * v)
                 total = total + coeff * done
             columns = pl.ds(pair * width, width)
-            ready = min(max(sci_ref.shape[1] - part * LANES, 0), LANES)
-            if ready:
-                here = pl.ds(part * LANES, ready)
-                out_ref[here, columns] = sci_ref[0, here, columns] - total[:ready]
-            if ready < LANES:
-                out_ref[pl.ds(part * LANES + ready, LANES - ready), columns] = total[ready:]
+            first = rows_dev - sci_ref.shape[1]
+            late = min(max(first - part * LANES, 0), LANES)
+            if late:
+                out_ref[pl.ds(part * LANES, late), columns] = total[:late]
+            if late < LANES:
+                here = pl.ds(part * LANES + late, LANES - late)
+                own = pl.ds(part * LANES + late - first, LANES - late)
+                out_ref[here, columns] = sci_ref[0, own, columns] - total[late:]
 
 
 def subtract_kernel(sci_ref, matched_ref, out_ref):
@@ -475,8 +477,11 @@
     for k in reversed(range(1, strips)):
         came[k] = lax.ppermute(parts[k], "strip", [(i, i ^ k) for i in range(strips)])
     came[strips // 2], got_a = lax.optimization_barrier((came[strips // 2], got_a))
+    far = range(strips // 2, strips, sources)
+    sci_b, got_a, *arrived = lax.optimization_barrier((sci_b, got_a, *[came[k] for k in far]))
+    for k, value in zip(far, arrived):
+        came[k] = value
     mine = jnp.stack(came[:: sources])
-    sci_b, mine = lax.optimization_barrier((sci_b, mine))
     got_b = lax.all_to_all(sci_b, "strip", split_axis=0, concat_axis=0, tiled=True)
     if sources > 1:
         got_a = jnp.sum(got_a.reshape((blocks, sources) + got_a.shape[1:]), axis=1)
@@ -528,13 +533,13 @@
     )
     arrays = [pltpu.with_memory_space_constraint(x, pltpu.VMEM) for x in arrays]
     matched = convolve(*arrays, psf_poly, toep_hi, toep_lo, band, got_a)
-    unit = ROWS_DEV // 8
-    rest = pl.BlockSpec((1, unit, ncol), lambda i: (0, FIRST_PART + i, 0))
+    unit = (ROWS_DEV - first_rows) // 2
+    late_rows = pl.BlockSpec((1, unit, ncol), lambda i: (0, i, 0))
     return pl.pallas_call(
         subtract_kernel,
-        grid=(8 - FIRST_PART,),
-        in_specs=[vmem, rest],
-        out_specs=rest,
+        grid=(2,),
+        in_specs=[vmem, late_rows],
+        out_specs=late_rows,
         out_shape=jax.ShapeDtypeStruct((1, ROWS_DEV, ncol), F32),
         input_output_aliases={1: 0},
         name="subtract",

time: 174 us -> 175 us (level)
  local copies, waits for them, and re-layouts: 14 us -> 19.1 us
  Pallas kernels: 40.6 us -> 38.7 us
    unnamed x35, local copies, waits for them, and re-layouts: 12.2 us -> 16.7 us
    ppermute x8, waiting for transfers between devices: 68.2 us -> 71.8 us  [swap(): return lax.ppermute(value, axis, [(i, i ^ 1 << bit) for i in range(count)])]
    ppermute x7, waiting for transfers between devices: 14.5 us -> 11.3 us  [shards(): lax.ppermute(parts[k], 'strip', [(i, i ^ k) for i in range(strips)])]
    pallas_call x1, Pallas kernels: 4.73 us -> 2.94 us  [shards(): pl.pallas_call(subtract_kernel, grid=(2,), in_specs=[vmem, late_rows], ou...]
  transfers between devices with their start and end apart: 17 -> 17, of which waited for: 9 -> 9; matrix products, arithmetic and copies ran while one was open for 3% -> 6% of each run, Pallas kernels for 11% -> 11%
where the time goes in v12:
time: 175 us; the launch traced here: 174 us
  waiting for transfers between devices  83 us (47%)
  Pallas kernels  38.7 us (22%)
  starting transfers between devices  32.4 us (19%)
  local copies, waits for them, and re-layouts  19.1 us (11%)
    ppermute x8, waiting for transfers between devices, swap(): return lax.ppermute(value, axis, [(i, i ^ 1 << bit) for i in range(count)])  71.8 us
    pallas_call x1, Pallas kernels, shards(): pl.pallas_call(functools.partial(warp_kernel, (epochs, nrow, share, order...  17.2 us
    unnamed x35, local copies, waits for them, and re-layouts  16.7 us
    pallas_call x1, Pallas kernels, shards(): matched = convolve(*arrays, psf_poly, toep_hi, toep_lo, band, got_a)  13.2 us
    ppermute x8, starting transfers between devices, swap(): return lax.ppermute(value, axis, [(i, i ^ 1 << bit) for i in range(count)])  11.3 us
    ppermute x7, waiting for transfers between devices, shards(): lax.ppermute(parts[k], 'strip', [(i, i ^ k) for i in range(strips)])  11.3 us
    all_to_all x1, starting transfers between devices, shards(): lax.all_to_all(sci_b, 'strip', split_axis=0, concat_axis=0, tiled=True)  9.59 us
    ppermute x7, starting transfers between devices, shards(): lax.ppermute(parts[k], 'strip', [(i, i ^ k) for i in range(strips)])  6.59 us
  transfers between devices with their start and end apart: 17, of which 9 were waited for; matrix products, arithmetic and copies ran while one was open for 6% of the time, Pallas kernels for 11%

profile of v12, /device:TPU:0, one launch (start us, length us, event | category | flops | bytes accessed | tf_op | source)
XLA Modules:
  0.0 174.5 jit_solution(17117035607553821985)
XLA Ops:
  0.0 17.2 %warp.1 = (f32[8,96,512]{2,1,0:T(8,128)}, f32[8,160,512]{2,1,0:T(8,128)}, f32[2,1032,128]{2,1,0:T(8,128)}, f32[2,1032,128]{2,1,0:T(8,128)}, f32[2,1032,128]{2,1,0:T(8,128)}, /*index=5*/f32[2,1032,128]{2,1,0:T(8,128)}) custom-call(s32[1,12]{1,0:T(1,128)} %kind_ref.1, s32[1,8,12]{2,1,0:T(8,128)} %heights_ref.1, f32[1,12]{1,0:T(1,128)} %invvar_ref.1, ...), custom_call_target="tpu_custom_call" | custom-call | flops 8000000000 | bytes 20000000 | tf_op jit(solution)/shard_map/warp/pallas_call | solution.py:391
  17.2 2.6 %collective-permute-start = (f32[2,1032,128]{2,1,0:T(8,128)}, f32[2,1032,128]{2,1,0:T(8,128)}, u32[]{:S(2)}, u32[]{:S(2)}) collective-permute-start(f32[2,1032,128]{2,1,0:T(8,128)} %get-tuple-element.32), channel_id=1, source_target_pairs={{0,8},{8,0},{16,24},{24,16},{1,9},{9,1},{17,25},{25,17},{2,10},{10... | collective-permute-start | bytes 3170312 | tf_op jit(solution)/shard_map/ppermute | solution.py:363
  19.9 5.0 %all-to-all-start = ((f32[8,96,512]{2,1,0:T(8,128)}), f32[8,96,512]{2,1,0:T(8,128)S(1)}, u32[]{:S(2)}, u32[]{:S(2)}) async-start(f32[8,96,512]{2,1,0:T(8,128)} %get-tuple-element.36), calls=%async_computation | async-start | bytes 3145728 | tf_op jit(solution)/shard_map/all_to_all | solution.py:422
  24.8 2.0 %collective-permute-start.2 = (f32[2,1032,128]{2,1,0:T(8,128)}, f32[2,1032,128]{2,1,0:T(8,128)S(1)}, u32[]{:S(2)}, u32[]{:S(2)}) collective-permute-start(f32[2,1032,128]{2,1,0:T(8,128)} %get-tuple-element.34), channel_id=1, source_target_pairs={{0,16},{8,24},{16,0},{24,8},{1,17},{9,25},{17,1},{25,9},{2,18},{10... | collective-permute-start | bytes 3170312 | tf_op jit(solution)/shard_map/ppermute | solution.py:363
  26.8 17.2 %collective-permute-done.refs_1_ = f32[2,1032,128]{2,1,0:T(8,128)} collective-permute-done((f32[2,1032,128]{2,1,0:T(8,128)}, f32[2,1032,128]{2,1,0:T(8,128)}, u32[]{:S(2)}, u32[]{:S(2)}) %collective-permute-start) | collective-permute-done | bytes 1056800 | tf_op jit(solution)/shard_map/ppermute | solution.py:363
  45.1 2.0 %collective-permute-start.1 = (f32[1,1032,128]{2,1,0:T(8,128)S(1)}, f32[1,1032,128]{2,1,0:T(8,128)S(1)}, u32[]{:S(2)}, u32[]{:S(2)}) collective-permute-start(f32[1,1032,128]{2,1,0:T(8,128)S(1)} %slice_add_fusion.1), channel_id=1, source_target_pairs={{0,16},{8,24},{16,0},{24,8},{1,17},{9,25},{17,1},{25,9},{2,18},{10... | collective-permute-start | bytes 1585160 | tf_op jit(solution)/shard_map/ppermute | solution.py:363
  47.2 4.1 %collective-permute-done.2.refs_4_ = f32[2,1032,128]{2,1,0:T(8,128)S(1)} collective-permute-done((f32[2,1032,128]{2,1,0:T(8,128)}, f32[2,1032,128]{2,1,0:T(8,128)S(1)}, u32[]{:S(2)}, u32[]{:S(2)}) %collective-permute-start.2) | collective-permute-done | bytes 1056800 | tf_op jit(solution)/shard_map/ppermute | solution.py:363
  52.4 9.9 %collective-permute-done.1.refs_2_ = f32[1,1032,128]{2,1,0:T(8,128)S(1)} collective-permute-done((f32[1,1032,128]{2,1,0:T(8,128)S(1)}, f32[1,1032,128]{2,1,0:T(8,128)S(1)}, u32[]{:S(2)}, u32[]{:S(2)}) %collective-permute-start.1) | collective-permute-done | bytes 528416 | tf_op jit(solution)/shard_map/ppermute | solution.py:363
  62.3 2.5 %collective-permute-done.3.refs_5_ = f32[1,1032,128]{2,1,0:T(8,128)S(1)} collective-permute-done((f32[1,1032,128]{2,1,0:T(8,128)S(1)}, f32[1,1032,128]{2,1,0:T(8,128)S(1)}, u32[]{:S(2)}, u32[]{:S(2)}) %collective-permute-start.3) | collective-permute-done | bytes 528416 | tf_op jit(solution)/shard_map/ppermute | solution.py:363
  64.8 2.9 %template.1 = (f32[288,128]{1,0:T(8,128)}, f32[288,128]{1,0:T(8,128)}, f32[288,128]{1,0:T(8,128)}, f32[288,128]{1,0:T(8,128)}, f32[288,128]{1,0:T(8,128)}, /*ind...) custom-call(f32[2,1032,128]{2,1,0:T(8,128)} %get-tuple-element.31.refs_0_, ...), custom_call_target="tpu_custom_call" | custom-call | flops 2000000 | bytes 5000000 | tf_op jit(solution)/shard_map/template/pallas_call | solution.py:465
  67.8 2.2 %collective-permute-start.4 = (f32[288,128]{1,0:T(8,128)}, f32[288,128]{1,0:T(8,128)S(1)}, u32[]{:S(2)}, u32[]{:S(2)}) collective-permute-start(f32[288,128]{1,0:T(8,128)} %get-tuple-element.35), channel_id=1, source_target_pairs={{0,4},{1,5},{2,6},{3,7},{4,0},{5,1},{6,2},{7,3},{8,12},{9,13},{10,... | collective-permute-start | bytes 442376 | tf_op jit(solution)/shard_map/ppermute | solution.py:478
  70.0 1.5 collective-permute-start.6
  71.4 2.5 %collective-permute-start.7 = (f32[288,128]{1,0:T(8,128)}, f32[288,128]{1,0:T(8,128)S(1)}, u32[]{:S(2)}, u32[]{:S(2)}) collective-permute-start(f32[288,128]{1,0:T(8,128)} %get-tuple-element.41), channel_id=1, source_target_pairs={{0,7},{1,6},{2,5},{3,4},{4,3},{5,2},{6,1},{7,0},{8,15},{9,14},{10,... | collective-permute-start | bytes 442376 | tf_op jit(solution)/shard_map/ppermute | solution.py:478
  74.0 1.6 bitcast_dynamic-update-slice_fusion.7
  75.5 11.1 %collective-permute-done.4 = f32[288,128]{1,0:T(8,128)S(1)} collective-permute-done((f32[288,128]{1,0:T(8,128)}, f32[288,128]{1,0:T(8,128)S(1)}, u32[]{:S(2)}, u32[]{:S(2)}) %collective-permute-start.4) | collective-permute-done | bytes 147488 | tf_op jit(solution)/shard_map/ppermute | solution.py:478
  88.3 9.6 %all-to-all-start.1 = ((f32[8,160,512]{2,1,0:T(8,128)}), f32[8,160,512]{2,1,0:T(8,128)S(1)}, u32[]{:S(2)}, u32[]{:S(2)}) async-start(f32[8,160,512]{2,1,0:T(8,128)} %get-tuple-element.42), calls=%async_computation.1 | async-start | bytes 5242880 | tf_op jit(solution)/shard_map/all_to_all | solution.py:485
  99.3 1.6 bitcast_dynamic-update-slice_fusion.4
  103.5 1.5 collective-permute-start.12
  105.3 26.8 %collective-permute-done.12.refs_2_ = f32[8,288,128]{2,1,0:T(8,128)S(1)} collective-permute-done((f32[8,288,128]{2,1,0:T(8,128)}, f32[8,288,128]{2,1,0:T(8,128)S(1)}, u32[]{:S(2)}, u32[]{:S(2)}) %collective-permute-start.12) | collective-permute-done | bytes 1179680 | tf_op jit(solution)/shard_map/ppermute | solution.py:363
  136.7 2.4 %bands.1 = (bf16[256,256]{1,0:T(8,128)(2,1)}, bf16[256,256]{1,0:T(8,128)(2,1)}, bf16[2,256,160]{2,1,0:T(8,128)(2,1)}) custom-call(f32[2,2,31]{2,1,0:T(2,128)} %psf_ref.1), custom_call_target="tpu_custom_call" | custom-call | flops 10000000 | bytes 500000 | tf_op jit(solution)/shard_map/bands/pallas_call | solution.py:437
  139.2 8.9 %collective-permute-done.13.refs_3_ = f32[4,288,128]{2,1,0:T(8,128)S(1)} collective-permute-done((f32[4,288,128]{2,1,0:T(8,128)}, f32[4,288,128]{2,1,0:T(8,128)S(1)}, u32[]{:S(2)}, u32[]{:S(2)}) %collective-permute-start.13) | collective-permute-done | bytes 589856 | tf_op jit(solution)/shard_map/ppermute | solution.py:363
  148.1 2.3 %collective-permute-done.14.refs_4_ = f32[4,288,128]{2,1,0:T(8,128)} collective-permute-done((f32[4,288,128]{2,1,0:T(8,128)}, f32[4,288,128]{2,1,0:T(8,128)}, u32[]{:S(2)}, u32[]{:S(2)}) %collective-permute-start.14) | collective-permute-done | bytes 589856 | tf_op jit(solution)/shard_map/ppermute | solution.py:363
  158.3 13.2 %convolve.1 = f32[256,4096]{1,0:T(8,128)} custom-call(f32[8,288,128]{2,1,0:T(8,128)S(1)} %copy-done.6, f32[8,288,128]{2,1,0:T(8,128)S(1)} %copy-done.5, f32[8,288,128]{2,1,0:T(8,128)S(1)} %copy-done.3, f32[4,288,128]{2,1,0:T(8,128)S(1)} %collective-permute-done.13.refs_3_, f32[4,288,128]{2,1,0:T(8,128)} %collective-permute-done.14.refs_4_, ...), custom_call_target="tpu_custom_call" | custom-call | flops 15000000512 | bytes 10000000 | tf_op jit(solution)/shard_map/convolve/pallas_call | solution.py:535
  171.5 2.9 %subtract.1 = f32[1,256,4096]{2,1,0:T(8,128)} custom-call(f32[8,160,512]{2,1,0:T(8,128)S(1)} %all-to-all-done.1.sci_ref, f32[1,256,4096]{2,1,0:T(8,128)} %bitcast.18), custom_call_target="tpu_custom_call", output_to_operand_aliasing={{}: (1, {})} | custom-call | flops 1000000 | bytes 6000000 | tf_op jit(solution)/shard_map/subtract/pallas_call | solution.py:538
  (55 shorter events, 20.8 us)
Async XLA Ops:
  17.2 26.8 %collective-permute-start = (f32[2,1032,128]{2,1,0:T(8,128)}, f32[2,1032,128]{2,1,0:T(8,128)}, u32[]{:S(2)}, u32[]{:S(2)}) collective-permute-start(f32[2,1032,128]{2,1,0:T(8,128)} %get-tuple-element.32), channel_id=1, source_target_pairs={{0,8},{8,0},{16,24},{24,16},{1,9},{9,1},{17,25},{25,17},{2,10},{10... | collective-permute-start | bytes 3170312 | tf_op jit(solution)/shard_map/ppermute | solution.py:363
  19.8 24.2 %copy-start.11 = (f32[2,1032,128]{2,1,0:T(8,128)S(1)}, f32[2,1032,128]{2,1,0:T(8,128)}, u32[]{:S(2)}) copy-start(f32[2,1032,128]{2,1,0:T(8,128)} %get-tuple-element.31.refs_0_) | copy-start | bytes 3170308
  19.9 67.2 %all-to-all-start = ((f32[8,96,512]{2,1,0:T(8,128)}), f32[8,96,512]{2,1,0:T(8,128)S(1)}, u32[]{:S(2)}, u32[]{:S(2)}) async-start(f32[8,96,512]{2,1,0:T(8,128)} %get-tuple-element.36), calls=%async_computation | async-start | bytes 3145728 | tf_op jit(solution)/shard_map/all_to_all | solution.py:422
  24.8 26.5 %copy-start.12 = (f32[2,1032,128]{2,1,0:T(8,128)S(1)}, f32[2,1032,128]{2,1,0:T(8,128)}, u32[]{:S(2)}) copy-start(f32[2,1032,128]{2,1,0:T(8,128)} %get-tuple-element.33.refs_3_) | copy-start | bytes 3170308
  24.8 26.5 %collective-permute-start.2 = (f32[2,1032,128]{2,1,0:T(8,128)}, f32[2,1032,128]{2,1,0:T(8,128)S(1)}, u32[]{:S(2)}, u32[]{:S(2)}) collective-permute-start(f32[2,1032,128]{2,1,0:T(8,128)} %get-tuple-element.34), channel_id=1, source_target_pairs={{0,16},{8,24},{16,0},{24,8},{1,17},{9,25},{17,1},{25,9},{2,18},{10... | collective-permute-start | bytes 3170312 | tf_op jit(solution)/shard_map/ppermute | solution.py:363
  45.1 17.2 %collective-permute-start.1 = (f32[1,1032,128]{2,1,0:T(8,128)S(1)}, f32[1,1032,128]{2,1,0:T(8,128)S(1)}, u32[]{:S(2)}, u32[]{:S(2)}) collective-permute-start(f32[1,1032,128]{2,1,0:T(8,128)S(1)} %slice_add_fusion.1), channel_id=1, source_target_pairs={{0,16},{8,24},{16,0},{24,8},{1,17},{9,25},{17,1},{25,9},{2,18},{10... | collective-permute-start | bytes 1585160 | tf_op jit(solution)/shard_map/ppermute | solution.py:363
  51.3 11.0 %copy-start.13 = (f32[2,1032,128]{2,1,0:T(8,128)}, f32[2,1032,128]{2,1,0:T(8,128)S(1)}, u32[]{:S(2)}) copy-start(f32[2,1032,128]{2,1,0:T(8,128)S(1)} %collective-permute-done.2.refs_4_) | copy-start | bytes 3170308
  51.4 13.5 %collective-permute-start.3 = (f32[1,1032,128]{2,1,0:T(8,128)S(1)}, f32[1,1032,128]{2,1,0:T(8,128)S(1)}, u32[]{:S(2)}, u32[]{:S(2)}) collective-permute-start(f32[1,1032,128]{2,1,0:T(8,128)S(1)} %slice_add_fusion), channel_id=1, source_target_pairs={{0,8},{8,0},{16,24},{24,16},{1,9},{9,1},{17,25},{25,17},{2,10},{10... | collective-permute-start | bytes 1585160 | tf_op jit(solution)/shard_map/ppermute | solution.py:363
  67.8 18.9 %collective-permute-start.4 = (f32[288,128]{1,0:T(8,128)}, f32[288,128]{1,0:T(8,128)S(1)}, u32[]{:S(2)}, u32[]{:S(2)}) collective-permute-start(f32[288,128]{1,0:T(8,128)} %get-tuple-element.35), channel_id=1, source_target_pairs={{0,4},{1,5},{2,6},{3,7},{4,0},{5,1},{6,2},{7,3},{8,12},{9,13},{10,... | collective-permute-start | bytes 442376 | tf_op jit(solution)/shard_map/ppermute | solution.py:478
  70.0 18.3 %collective-permute-start.5 = (f32[288,128]{1,0:T(8,128)}, f32[288,128]{1,0:T(8,128)S(1)}, u32[]{:S(2)}, u32[]{:S(2)}) collective-permute-start(f32[288,128]{1,0:T(8,128)} %get-tuple-element.39), channel_id=1, source_target_pairs={{0,5},{1,4},{2,7},{3,6},{4,1},{5,0},{6,3},{7,2},{8,13},{9,12},{10,... | collective-permute-start | bytes 442376 | tf_op jit(solution)/shard_map/ppermute | solution.py:478
  70.0 18.3 %collective-permute-start.6 = (f32[288,128]{1,0:T(8,128)}, f32[288,128]{1,0:T(8,128)S(1)}, u32[]{:S(2)}, u32[]{:S(2)}) collective-permute-start(f32[288,128]{1,0:T(8,128)} %get-tuple-element.40), channel_id=1, source_target_pairs={{0,6},{1,7},{2,4},{3,5},{4,2},{5,3},{6,0},{7,1},{8,14},{9,15},{10,... | collective-permute-start | bytes 442376 | tf_op jit(solution)/shard_map/ppermute | solution.py:478
  71.4 16.9 %collective-permute-start.7 = (f32[288,128]{1,0:T(8,128)}, f32[288,128]{1,0:T(8,128)S(1)}, u32[]{:S(2)}, u32[]{:S(2)}) collective-permute-start(f32[288,128]{1,0:T(8,128)} %get-tuple-element.41), channel_id=1, source_target_pairs={{0,7},{1,6},{2,5},{3,4},{4,3},{5,2},{6,1},{7,0},{8,15},{9,14},{10,... | collective-permute-start | bytes 442376 | tf_op jit(solution)/shard_map/ppermute | solution.py:478
  74.0 24.0 %collective-permute-start.8 = (f32[288,128]{1,0:T(8,128)}, f32[288,128]{1,0:T(8,128)S(1)}, u32[]{:S(2)}, u32[]{:S(2)}) collective-permute-start(f32[288,128]{1,0:T(8,128)} %get-tuple-element.44), channel_id=1, source_target_pairs={{0,1},{1,0},{2,3},{3,2},{4,5},{5,4},{6,7},{7,6},{8,9},{9,8},{10,11... | collective-permute-start | bytes 442376 | tf_op jit(solution)/shard_map/ppermute | solution.py:478
  86.7 11.9 %collective-permute-start.9 = (f32[288,128]{1,0:T(8,128)}, f32[288,128]{1,0:T(8,128)S(1)}, u32[]{:S(2)}, u32[]{:S(2)}) collective-permute-start(f32[288,128]{1,0:T(8,128)} %get-tuple-element.45), channel_id=1, source_target_pairs={{0,2},{1,3},{2,0},{3,1},{4,6},{5,7},{6,4},{7,5},{8,10},{9,11},{10,... | collective-permute-start | bytes 442376 | tf_op jit(solution)/shard_map/ppermute | solution.py:478
  88.3 11.0 %collective-permute-start.10 = (f32[288,128]{1,0:T(8,128)}, f32[288,128]{1,0:T(8,128)}, u32[]{:S(2)}, u32[]{:S(2)}) collective-permute-start(f32[288,128]{1,0:T(8,128)} %get-tuple-element.46), channel_id=1, source_target_pairs={{0,3},{1,2},{2,1},{3,0},{4,7},{5,6},{6,5},{7,4},{8,11},{9,10},{10,... | collective-permute-start | bytes 442376 | tf_op jit(solution)/shard_map/ppermute | solution.py:478
  88.3 83.2 %all-to-all-start.1 = ((f32[8,160,512]{2,1,0:T(8,128)}), f32[8,160,512]{2,1,0:T(8,128)S(1)}, u32[]{:S(2)}, u32[]{:S(2)}) async-start(f32[8,160,512]{2,1,0:T(8,128)} %get-tuple-element.42), calls=%async_computation.1 | async-start | bytes 5242880 | tf_op jit(solution)/shard_map/all_to_all | solution.py:485
  103.5 46.8 %copy-start.7 = (f32[4,2,6]{2,1,0:T(2,128)S(1)}, f32[4,2,6]{2,1,0:T(2,128)}, u32[]{:S(2)}) copy-start(f32[4,2,6]{2,1,0:T(2,128)} %refs_5_.1) | copy-start | bytes 580
  103.5 28.6 %collective-permute-start.12 = (f32[8,288,128]{2,1,0:T(8,128)}, f32[8,288,128]{2,1,0:T(8,128)S(1)}, u32[]{:S(2)}, u32[]{:S(2)}) collective-permute-start(f32[8,288,128]{2,1,0:T(8,128)} %bitcast_dynamic-update-slice_fusion.refs_0_), channel_id=1, source_target_pairs={{0,16},{8,24},{16,0},{24,8},{1,17},{9,25},{17,1},{25,9},{2,18},{10... | collective-permute-start | bytes 3538952 | tf_op jit(solution)/shard_map/ppermute | solution.py:363
  105.0 28.5 %collective-permute-start.11 = (f32[8,288,128]{2,1,0:T(8,128)}, f32[8,288,128]{2,1,0:T(8,128)S(1)}, u32[]{:S(2)}, u32[]{:S(2)}) collective-permute-start(f32[8,288,128]{2,1,0:T(8,128)} %bitcast_dynamic-update-slice_fusion.refs_0_), channel_id=1, source_target_pairs={{0,8},{8,0},{16,24},{24,16},{1,9},{9,1},{17,25},{25,17},{2,10},{10... | collective-permute-start | bytes 3538952 | tf_op jit(solution)/shard_map/ppermute | solution.py:363
  132.1 2.3 %copy-start.2 = (f32[8,288,128]{2,1,0:T(8,128)}, f32[8,288,128]{2,1,0:T(8,128)S(1)}, u32[]{:S(2)}) copy-start(f32[8,288,128]{2,1,0:T(8,128)S(1)} %collective-permute-done.12.refs_2_) | copy-start | bytes 3538948
  133.0 15.1 %collective-permute-start.13 = (f32[4,288,128]{2,1,0:T(8,128)}, f32[4,288,128]{2,1,0:T(8,128)S(1)}, u32[]{:S(2)}, u32[]{:S(2)}) collective-permute-start(f32[4,288,128]{2,1,0:T(8,128)} %slice.26), channel_id=1, source_target_pairs={{0,8},{8,0},{16,24},{24,16},{1,9},{9,1},{17,25},{25,17},{2,10},{10... | collective-permute-start | bytes 1769480 | tf_op jit(solution)/shard_map/ppermute | solution.py:363
  135.4 14.9 %collective-permute-start.14 = (f32[4,288,128]{2,1,0:T(8,128)}, f32[4,288,128]{2,1,0:T(8,128)}, u32[]{:S(2)}, u32[]{:S(2)}) collective-permute-start(f32[4,288,128]{2,1,0:T(8,128)} %slice.27), channel_id=1, source_target_pairs={{0,16},{8,24},{16,0},{24,8},{1,17},{9,25},{17,1},{25,9},{2,18},{10... | collective-permute-start | bytes 1769480 | tf_op jit(solution)/shard_map/ppermute | solution.py:363
  150.3 1.4 copy-start.1
  153.0 1.3 copy-start.5
  (7 other events, 7.5 us)

commit v13 on v12

--- a/solution.py
+++ b/solution.py
@@ -477,11 +477,8 @@
     for k in reversed(range(1, strips)):
         came[k] = lax.ppermute(parts[k], "strip", [(i, i ^ k) for i in range(strips)])
     came[strips // 2], got_a = lax.optimization_barrier((came[strips // 2], got_a))
-    far = range(strips // 2, strips, sources)
-    sci_b, got_a, *arrived = lax.optimization_barrier((sci_b, got_a, *[came[k] for k in far]))
-    for k, value in zip(far, arrived):
-        came[k] = value
     mine = jnp.stack(came[:: sources])
+    sci_b, mine = lax.optimization_barrier((sci_b, mine))
     got_b = lax.all_to_all(sci_b, "strip", split_axis=0, concat_axis=0, tiled=True)
     if sources > 1:
         got_a = jnp.sum(got_a.reshape((blocks, sources) + got_a.shape[1:]), axis=1)
@@ -531,7 +528,7 @@
         compiler_params=pltpu.CompilerParams(vmem_limit_bytes=28 << 20),
         cost_estimate=pl.CostEstimate(flops=15_000_000_000, bytes_accessed=10_000_000, transcendentals=0),
     )
-    arrays = [pltpu.with_memory_space_constraint(x, pltpu.VMEM) for x in arrays]
+    arrays = arrays[:1] + [pltpu.with_memory_space_constraint(x, pltpu.VMEM) for x in arrays[1:]]
     matched = convolve(*arrays, psf_poly, toep_hi, toep_lo, band, got_a)
     unit = (ROWS_DEV - first_rows) // 2
     late_rows = pl.BlockSpec((1, unit, ncol), lambda i: (0, i, 0))

time: 175 us -> 172 us (0.983)
  local copies, waits for them, and re-layouts: 19.1 us -> 14 us
    unnamed x35, local copies, waits for them, and re-layouts: 16.7 us -> 12.2 us
    ppermute x8, waiting for transfers between devices: 71.8 us -> 68.2 us  [swap(): return lax.ppermute(value, axis, [(i, i ^ 1 << bit) for i in range(count)])]
    ppermute x7, waiting for transfers between devices: 11.3 us -> 14.5 us  [shards(): lax.ppermute(parts[k], 'strip', [(i, i ^ k) for i in range(strips)])]
  transfers between devices with their start and end apart: 17 -> 17, of which waited for: 9 -> 9; matrix products, arithmetic and copies ran while one was open for 6% -> 3% of each run, Pallas kernels for 11% -> 11%
where the time goes in v13:
time: 172 us; the launch traced here: 171 us
  waiting for transfers between devices  82.7 us (48%)
  Pallas kernels  38.7 us (23%)
  starting transfers between devices  33.3 us (19%)
  local copies, waits for them, and re-layouts  14 us (8%)
  other arithmetic  2.19 us (1%)
    ppermute x8, waiting for transfers between devices, swap(): return lax.ppermute(value, axis, [(i, i ^ 1 << bit) for i in range(count)])  68.2 us
    pallas_call x1, Pallas kernels, shards(): pl.pallas_call(functools.partial(warp_kernel, (epochs, nrow, share, order...  17.2 us
    ppermute x7, waiting for transfers between devices, shards(): lax.ppermute(parts[k], 'strip', [(i, i ^ k) for i in range(strips)])  14.5 us
    pallas_call x1, Pallas kernels, shards(): matched = convolve(*arrays, psf_poly, toep_hi, toep_lo, band, got_a)  13.2 us
    unnamed x35, local copies, waits for them, and re-layouts  12.2 us
    ppermute x8, starting transfers between devices, swap(): return lax.ppermute(value, axis, [(i, i ^ 1 << bit) for i in range(count)])  10.6 us
    all_to_all x1, starting transfers between devices, shards(): lax.all_to_all(sci_b, 'strip', split_axis=0, concat_axis=0, tiled=True)  9.79 us
    ppermute x7, starting transfers between devices, shards(): lax.ppermute(parts[k], 'strip', [(i, i ^ k) for i in range(strips)])  7.56 us
  transfers between devices with their start and end apart: 17, of which 9 were waited for; matrix products, arithmetic and copies ran while one was open for 3% of the time, Pallas kernels for 11%

profile of v13, /device:TPU:0, one launch (start us, length us, event | category | flops | bytes accessed | tf_op | source)
XLA Modules:
  0.0 171.1 jit_solution(13255454852100393994)
XLA Ops:
  0.0 17.2 %warp.1 = (f32[8,96,512]{2,1,0:T(8,128)}, f32[8,160,512]{2,1,0:T(8,128)}, f32[2,1032,128]{2,1,0:T(8,128)}, f32[2,1032,128]{2,1,0:T(8,128)}, f32[2,1032,128]{2,1,0:T(8,128)}, /*index=5*/f32[2,1032,128]{2,1,0:T(8,128)}) custom-call(s32[1,12]{1,0:T(1,128)} %kind_ref.1, s32[1,8,12]{2,1,0:T(8,128)} %heights_ref.1, f32[1,12]{1,0:T(1,128)} %invvar_ref.1, ...), custom_call_target="tpu_custom_call" | custom-call | flops 8000000000 | bytes 20000000 | tf_op jit(solution)/shard_map/warp/pallas_call | solution.py:391
  17.2 2.6 %collective-permute-start = (f32[2,1032,128]{2,1,0:T(8,128)}, f32[2,1032,128]{2,1,0:T(8,128)}, u32[]{:S(2)}, u32[]{:S(2)}) collective-permute-start(f32[2,1032,128]{2,1,0:T(8,128)} %get-tuple-element.28), channel_id=1, source_target_pairs={{0,8},{8,0},{16,24},{24,16},{1,9},{9,1},{17,25},{25,17},{2,10},{10... | collective-permute-start | bytes 3170312 | tf_op jit(solution)/shard_map/ppermute | solution.py:363
  19.9 1.5 collective-permute-start.2
  21.3 5.4 %all-to-all-start = ((f32[8,96,512]{2,1,0:T(8,128)}), f32[8,96,512]{2,1,0:T(8,128)S(1)}, u32[]{:S(2)}, u32[]{:S(2)}) async-start(f32[8,96,512]{2,1,0:T(8,128)} %get-tuple-element.36), calls=%async_computation | async-start | bytes 3145728 | tf_op jit(solution)/shard_map/all_to_all | solution.py:422
  26.8 17.3 %collective-permute-done.refs_1_ = f32[2,1032,128]{2,1,0:T(8,128)} collective-permute-done((f32[2,1032,128]{2,1,0:T(8,128)}, f32[2,1032,128]{2,1,0:T(8,128)}, u32[]{:S(2)}, u32[]{:S(2)}) %collective-permute-start) | collective-permute-done | bytes 1056800 | tf_op jit(solution)/shard_map/ppermute | solution.py:363
  45.1 2.0 %collective-permute-start.1 = (f32[1,1032,128]{2,1,0:T(8,128)S(1)}, f32[1,1032,128]{2,1,0:T(8,128)S(1)}, u32[]{:S(2)}, u32[]{:S(2)}) collective-permute-start(f32[1,1032,128]{2,1,0:T(8,128)S(1)} %slice_add_fusion.1), channel_id=1, source_target_pairs={{0,16},{8,24},{16,0},{24,8},{1,17},{9,25},{17,1},{25,9},{2,18},{10... | collective-permute-start | bytes 1585160 | tf_op jit(solution)/shard_map/ppermute | solution.py:363
  48.3 1.6 collective-permute-start.3
  49.9 9.1 %collective-permute-done.1.refs_2_ = f32[1,1032,128]{2,1,0:T(8,128)S(1)} collective-permute-done((f32[1,1032,128]{2,1,0:T(8,128)S(1)}, f32[1,1032,128]{2,1,0:T(8,128)S(1)}, u32[]{:S(2)}, u32[]{:S(2)}) %collective-permute-start.1) | collective-permute-done | bytes 528416 | tf_op jit(solution)/shard_map/ppermute | solution.py:363
  58.9 2.6 %collective-permute-done.3.refs_5_ = f32[1,1032,128]{2,1,0:T(8,128)S(1)} collective-permute-done((f32[1,1032,128]{2,1,0:T(8,128)S(1)}, f32[1,1032,128]{2,1,0:T(8,128)S(1)}, u32[]{:S(2)}, u32[]{:S(2)}) %collective-permute-start.3) | collective-permute-done | bytes 528416 | tf_op jit(solution)/shard_map/ppermute | solution.py:363
  61.5 3.0 %template.1 = (f32[288,128]{1,0:T(8,128)}, f32[288,128]{1,0:T(8,128)}, f32[288,128]{1,0:T(8,128)}, f32[288,128]{1,0:T(8,128)}, f32[288,128]{1,0:T(8,128)}, /*ind...) custom-call(f32[2,1032,128]{2,1,0:T(8,128)} %get-tuple-element.27.refs_0_, ...), custom_call_target="tpu_custom_call" | custom-call | flops 2000000 | bytes 5000000 | tf_op jit(solution)/shard_map/template/pallas_call | solution.py:465
  65.0 1.3 collective-permute-start.6
  66.4 1.9 %collective-permute-start.7 = (f32[288,128]{1,0:T(8,128)}, f32[288,128]{1,0:T(8,128)S(1)}, u32[]{:S(2)}, u32[]{:S(2)}) collective-permute-start(f32[288,128]{1,0:T(8,128)} %get-tuple-element.35), channel_id=1, source_target_pairs={{0,4},{1,5},{2,6},{3,7},{4,0},{5,1},{6,2},{7,3},{8,12},{9,13},{10,... | collective-permute-start | bytes 442376 | tf_op jit(solution)/shard_map/ppermute | solution.py:478
  69.8 3.1 %collective-permute-start.9 = (f32[288,128]{1,0:T(8,128)}, f32[288,128]{1,0:T(8,128)S(1)}, u32[]{:S(2)}, u32[]{:S(2)}) collective-permute-start(f32[288,128]{1,0:T(8,128)} %get-tuple-element.39), channel_id=1, source_target_pairs={{0,6},{1,7},{2,4},{3,5},{4,2},{5,3},{6,0},{7,1},{8,14},{9,15},{10,... | collective-permute-start | bytes 442376 | tf_op jit(solution)/shard_map/ppermute | solution.py:478
  73.0 3.6 %collective-permute-done.5 = f32[288,128]{1,0:T(8,128)S(1)} collective-permute-done((f32[288,128]{1,0:T(8,128)}, f32[288,128]{1,0:T(8,128)S(1)}, u32[]{:S(2)}, u32[]{:S(2)}) %collective-permute-start.5) | collective-permute-done | bytes 147488 | tf_op jit(solution)/shard_map/ppermute | solution.py:478
  76.6 2.1 %collective-permute-done.6 = f32[288,128]{1,0:T(8,128)S(1)} collective-permute-done((f32[288,128]{1,0:T(8,128)}, f32[288,128]{1,0:T(8,128)S(1)}, u32[]{:S(2)}, u32[]{:S(2)}) %collective-permute-start.6) | collective-permute-done | bytes 147488 | tf_op jit(solution)/shard_map/ppermute | solution.py:478
  80.0 8.8 %collective-permute-done.8 = f32[288,128]{1,0:T(8,128)S(1)} collective-permute-done((f32[288,128]{1,0:T(8,128)}, f32[288,128]{1,0:T(8,128)S(1)}, u32[]{:S(2)}, u32[]{:S(2)}) %collective-permute-start.8) | collective-permute-done | bytes 147488 | tf_op jit(solution)/shard_map/ppermute | solution.py:478
  89.8 9.8 %all-to-all-start.1 = ((f32[8,160,512]{2,1,0:T(8,128)}), f32[8,160,512]{2,1,0:T(8,128)S(1)}, u32[]{:S(2)}, u32[]{:S(2)}) async-start(f32[8,160,512]{2,1,0:T(8,128)} %get-tuple-element.41), calls=%async_computation.1 | async-start | bytes 5242880 | tf_op jit(solution)/shard_map/all_to_all | solution.py:482
  101.1 27.1 %collective-permute-done.12.refs_2_ = f32[8,288,128]{2,1,0:T(8,128)S(1)} collective-permute-done((f32[8,288,128]{2,1,0:T(8,128)}, f32[8,288,128]{2,1,0:T(8,128)S(1)}, u32[]{:S(2)}, u32[]{:S(2)}) %collective-permute-start.12) | collective-permute-done | bytes 1179680 | tf_op jit(solution)/shard_map/ppermute | solution.py:363
  132.5 2.4 %bands.1 = (bf16[256,256]{1,0:T(8,128)(2,1)}, bf16[256,256]{1,0:T(8,128)(2,1)}, bf16[2,256,160]{2,1,0:T(8,128)(2,1)}) custom-call(f32[2,2,31]{2,1,0:T(2,128)} %psf_ref.1), custom_call_target="tpu_custom_call" | custom-call | flops 10000000 | bytes 500000 | tf_op jit(solution)/shard_map/bands/pallas_call | solution.py:437
  134.9 9.3 %collective-permute-done.13.refs_3_ = f32[4,288,128]{2,1,0:T(8,128)S(1)} collective-permute-done((f32[4,288,128]{2,1,0:T(8,128)}, f32[4,288,128]{2,1,0:T(8,128)S(1)}, u32[]{:S(2)}, u32[]{:S(2)}) %collective-permute-start.13) | collective-permute-done | bytes 589856 | tf_op jit(solution)/shard_map/ppermute | solution.py:363
  144.1 2.9 %collective-permute-done.14.refs_4_ = f32[4,288,128]{2,1,0:T(8,128)} collective-permute-done((f32[4,288,128]{2,1,0:T(8,128)}, f32[4,288,128]{2,1,0:T(8,128)}, u32[]{:S(2)}, u32[]{:S(2)}) %collective-permute-start.14) | collective-permute-done | bytes 589856 | tf_op jit(solution)/shard_map/ppermute | solution.py:363
  147.0 1.4 copy-done.1
  155.0 13.2 %convolve.1 = f32[256,4096]{1,0:T(8,128)} custom-call(f32[8,288,128]{2,1,0:T(8,128)S(1)} %copy-done.7, f32[8,288,128]{2,1,0:T(8,128)S(1)} %copy-done.5, f32[8,288,128]{2,1,0:T(8,128)S(1)} %copy-done.3, f32[4,288,128]{2,1,0:T(8,128)S(1)} %collective-permute-done.13.refs_3_, f32[4,288,128]{2,1,0:T(8,128)} %collective-permute-done.14.refs_4_, ...), custom_call_target="tpu_custom_call" | custom-call | flops 15000000512 | bytes 10000000 | tf_op jit(solution)/shard_map/convolve/pallas_call | solution.py:532
  168.2 2.9 %subtract.1 = f32[1,256,4096]{2,1,0:T(8,128)} custom-call(f32[8,160,512]{2,1,0:T(8,128)S(1)} %all-to-all-done.1.sci_ref, f32[1,256,4096]{2,1,0:T(8,128)} %bitcast.18), custom_call_target="tpu_custom_call", output_to_operand_aliasing={{}: (1, {})} | custom-call | flops 1000000 | bytes 6000000 | tf_op jit(solution)/shard_map/subtract/pallas_call | solution.py:535
  (55 shorter events, 18.9 us)
Async XLA Ops:
  17.2 26.8 %collective-permute-start = (f32[2,1032,128]{2,1,0:T(8,128)}, f32[2,1032,128]{2,1,0:T(8,128)}, u32[]{:S(2)}, u32[]{:S(2)}) collective-permute-start(f32[2,1032,128]{2,1,0:T(8,128)} %get-tuple-element.28), channel_id=1, source_target_pairs={{0,8},{8,0},{16,24},{24,16},{1,9},{9,1},{17,25},{25,17},{2,10},{10... | collective-permute-start | bytes 3170312 | tf_op jit(solution)/shard_map/ppermute | solution.py:363
  19.9 27.3 %collective-permute-start.2 = (f32[2,1032,128]{2,1,0:T(8,128)}, f32[2,1032,128]{2,1,0:T(8,128)}, u32[]{:S(2)}, u32[]{:S(2)}) collective-permute-start(f32[2,1032,128]{2,1,0:T(8,128)} %get-tuple-element.30), channel_id=1, source_target_pairs={{0,16},{8,24},{16,0},{24,8},{1,17},{9,25},{17,1},{25,9},{2,18},{10... | collective-permute-start | bytes 3170312 | tf_op jit(solution)/shard_map/ppermute | solution.py:363
  21.3 22.7 %copy-start.12 = (f32[2,1032,128]{2,1,0:T(8,128)S(1)}, f32[2,1032,128]{2,1,0:T(8,128)}, u32[]{:S(2)}) copy-start(f32[2,1032,128]{2,1,0:T(8,128)} %get-tuple-element.27.refs_0_) | copy-start | bytes 3170308
  21.3 57.5 %all-to-all-start = ((f32[8,96,512]{2,1,0:T(8,128)}), f32[8,96,512]{2,1,0:T(8,128)S(1)}, u32[]{:S(2)}, u32[]{:S(2)}) async-start(f32[8,96,512]{2,1,0:T(8,128)} %get-tuple-element.36), calls=%async_computation | async-start | bytes 3145728 | tf_op jit(solution)/shard_map/all_to_all | solution.py:422
  26.8 20.4 %copy-start.13 = (f32[2,1032,128]{2,1,0:T(8,128)S(1)}, f32[2,1032,128]{2,1,0:T(8,128)}, u32[]{:S(2)}) copy-start(f32[2,1032,128]{2,1,0:T(8,128)} %get-tuple-element.29.refs_3_) | copy-start | bytes 3170308
  45.1 13.8 %collective-permute-start.1 = (f32[1,1032,128]{2,1,0:T(8,128)S(1)}, f32[1,1032,128]{2,1,0:T(8,128)S(1)}, u32[]{:S(2)}, u32[]{:S(2)}) collective-permute-start(f32[1,1032,128]{2,1,0:T(8,128)S(1)} %slice_add_fusion.1), channel_id=1, source_target_pairs={{0,16},{8,24},{16,0},{24,8},{1,17},{9,25},{17,1},{25,9},{2,18},{10... | collective-permute-start | bytes 1585160 | tf_op jit(solution)/shard_map/ppermute | solution.py:363
  48.3 13.2 %collective-permute-start.3 = (f32[1,1032,128]{2,1,0:T(8,128)S(1)}, f32[1,1032,128]{2,1,0:T(8,128)S(1)}, u32[]{:S(2)}, u32[]{:S(2)}) collective-permute-start(f32[1,1032,128]{2,1,0:T(8,128)S(1)} %slice_add_fusion), channel_id=1, source_target_pairs={{0,8},{8,0},{16,24},{24,16},{1,9},{9,1},{17,25},{25,17},{2,10},{10... | collective-permute-start | bytes 1585160 | tf_op jit(solution)/shard_map/ppermute | solution.py:363
  64.5 5.4 %collective-permute-start.4 = (f32[288,128]{1,0:T(8,128)}, f32[288,128]{1,0:T(8,128)S(1)}, u32[]{:S(2)}, u32[]{:S(2)}) collective-permute-start(f32[288,128]{1,0:T(8,128)} %get-tuple-element.32), channel_id=1, source_target_pairs={{0,1},{1,0},{2,3},{3,2},{4,5},{5,4},{6,7},{7,6},{8,9},{9,8},{10,11... | collective-permute-start | bytes 442376 | tf_op jit(solution)/shard_map/ppermute | solution.py:478
  64.5 12.1 %collective-permute-start.5 = (f32[288,128]{1,0:T(8,128)}, f32[288,128]{1,0:T(8,128)S(1)}, u32[]{:S(2)}, u32[]{:S(2)}) collective-permute-start(f32[288,128]{1,0:T(8,128)} %get-tuple-element.33), channel_id=1, source_target_pairs={{0,2},{1,3},{2,0},{3,1},{4,6},{5,7},{6,4},{7,5},{8,10},{9,11},{10,... | collective-permute-start | bytes 442376 | tf_op jit(solution)/shard_map/ppermute | solution.py:478
  65.0 13.7 %collective-permute-start.6 = (f32[288,128]{1,0:T(8,128)}, f32[288,128]{1,0:T(8,128)S(1)}, u32[]{:S(2)}, u32[]{:S(2)}) collective-permute-start(f32[288,128]{1,0:T(8,128)} %get-tuple-element.34), channel_id=1, source_target_pairs={{0,3},{1,2},{2,1},{3,0},{4,7},{5,6},{6,5},{7,4},{8,11},{9,10},{10,... | collective-permute-start | bytes 442376 | tf_op jit(solution)/shard_map/ppermute | solution.py:478
  66.4 12.4 %collective-permute-start.7 = (f32[288,128]{1,0:T(8,128)}, f32[288,128]{1,0:T(8,128)S(1)}, u32[]{:S(2)}, u32[]{:S(2)}) collective-permute-start(f32[288,128]{1,0:T(8,128)} %get-tuple-element.35), channel_id=1, source_target_pairs={{0,4},{1,5},{2,6},{3,7},{4,0},{5,1},{6,2},{7,3},{8,12},{9,13},{10,... | collective-permute-start | bytes 442376 | tf_op jit(solution)/shard_map/ppermute | solution.py:478
  68.2 20.5 %collective-permute-start.8 = (f32[288,128]{1,0:T(8,128)}, f32[288,128]{1,0:T(8,128)S(1)}, u32[]{:S(2)}, u32[]{:S(2)}) collective-permute-start(f32[288,128]{1,0:T(8,128)} %get-tuple-element.38), channel_id=1, source_target_pairs={{0,5},{1,4},{2,7},{3,6},{4,1},{5,0},{6,3},{7,2},{8,13},{9,12},{10,... | collective-permute-start | bytes 442376 | tf_op jit(solution)/shard_map/ppermute | solution.py:478
  69.8 18.9 %collective-permute-start.9 = (f32[288,128]{1,0:T(8,128)}, f32[288,128]{1,0:T(8,128)S(1)}, u32[]{:S(2)}, u32[]{:S(2)}) collective-permute-start(f32[288,128]{1,0:T(8,128)} %get-tuple-element.39), channel_id=1, source_target_pairs={{0,6},{1,7},{2,4},{3,5},{4,2},{5,3},{6,0},{7,1},{8,14},{9,15},{10,... | collective-permute-start | bytes 442376 | tf_op jit(solution)/shard_map/ppermute | solution.py:478
  76.6 12.2 %collective-permute-start.10 = (f32[288,128]{1,0:T(8,128)}, f32[288,128]{1,0:T(8,128)S(1)}, u32[]{:S(2)}, u32[]{:S(2)}) collective-permute-start(f32[288,128]{1,0:T(8,128)} %get-tuple-element.40), channel_id=1, source_target_pairs={{0,7},{1,6},{2,5},{3,4},{4,3},{5,2},{6,1},{7,0},{8,15},{9,14},{10,... | collective-permute-start | bytes 442376 | tf_op jit(solution)/shard_map/ppermute | solution.py:478
  89.8 78.4 %all-to-all-start.1 = ((f32[8,160,512]{2,1,0:T(8,128)}), f32[8,160,512]{2,1,0:T(8,128)S(1)}, u32[]{:S(2)}, u32[]{:S(2)}) async-start(f32[8,160,512]{2,1,0:T(8,128)} %get-tuple-element.41), calls=%async_computation.1 | async-start | bytes 5242880 | tf_op jit(solution)/shard_map/all_to_all | solution.py:482
  99.6 47.4 %copy-start.8 = (f32[4,2,6]{2,1,0:T(2,128)S(1)}, f32[4,2,6]{2,1,0:T(2,128)}, u32[]{:S(2)}) copy-start(f32[4,2,6]{2,1,0:T(2,128)} %refs_5_.1) | copy-start | bytes 580
  99.6 28.6 %collective-permute-start.12 = (f32[8,288,128]{2,1,0:T(8,128)}, f32[8,288,128]{2,1,0:T(8,128)S(1)}, u32[]{:S(2)}, u32[]{:S(2)}) collective-permute-start(f32[8,288,128]{2,1,0:T(8,128)} %copy-done.6), channel_id=1, source_target_pairs={{0,16},{8,24},{16,0},{24,8},{1,17},{9,25},{17,1},{25,9},{2,18},{10... | collective-permute-start | bytes 3538952 | tf_op jit(solution)/shard_map/ppermute | solution.py:363
  100.7 29.5 %collective-permute-start.11 = (f32[8,288,128]{2,1,0:T(8,128)}, f32[8,288,128]{2,1,0:T(8,128)S(1)}, u32[]{:S(2)}, u32[]{:S(2)}) collective-permute-start(f32[8,288,128]{2,1,0:T(8,128)} %copy-done.6), channel_id=1, source_target_pairs={{0,8},{8,0},{16,24},{24,16},{1,9},{9,1},{17,25},{25,17},{2,10},{10... | collective-permute-start | bytes 3538952 | tf_op jit(solution)/shard_map/ppermute | solution.py:363
  128.2 2.9 %copy-start.2 = (f32[8,288,128]{2,1,0:T(8,128)}, f32[8,288,128]{2,1,0:T(8,128)S(1)}, u32[]{:S(2)}) copy-start(f32[8,288,128]{2,1,0:T(8,128)S(1)} %collective-permute-done.12.refs_2_) | copy-start | bytes 3538948
  129.1 15.0 %collective-permute-start.13 = (f32[4,288,128]{2,1,0:T(8,128)}, f32[4,288,128]{2,1,0:T(8,128)S(1)}, u32[]{:S(2)}, u32[]{:S(2)}) collective-permute-start(f32[4,288,128]{2,1,0:T(8,128)} %slice.26), channel_id=1, source_target_pairs={{0,8},{8,0},{16,24},{24,16},{1,9},{9,1},{17,25},{25,17},{2,10},{10... | collective-permute-start | bytes 1769480 | tf_op jit(solution)/shard_map/ppermute | solution.py:363
  132.1 14.8 %collective-permute-start.14 = (f32[4,288,128]{2,1,0:T(8,128)}, f32[4,288,128]{2,1,0:T(8,128)}, u32[]{:S(2)}, u32[]{:S(2)}) collective-permute-start(f32[4,288,128]{2,1,0:T(8,128)} %slice.27), channel_id=1, source_target_pairs={{0,16},{8,24},{16,0},{24,8},{1,17},{9,25},{17,1},{25,9},{2,18},{10... | collective-permute-start | bytes 1769480 | tf_op jit(solution)/shard_map/ppermute | solution.py:363
  147.0 1.4 copy-start.1
  148.4 1.3 copy-start.3
  149.7 1.3 copy-start.5
  (7 other events, 7.3 us)
